TPU v7x, 32 devices: a whole 2x2x4 slice. The times are simulated.
32 devices in a mesh: wide: 8 (over z, core), narrow: 4 (over y, x).
Axes of the slice: x: 2, y: 2, z: 4, core: 2. Of those that a mesh axis runs over, the one named last changes fastest.
Arguments:
- tokens: bfloat16 [4096, 2048], P('wide'), may hold values from -6 to 6
- attn_gain: bfloat16 [2048], replicated, may hold values from 0.099609375 to 1.8984375
- w_query: bfloat16 [2048, 2048], P(None, 'narrow'), may hold values from -0.125 to 0.125
- w_key: bfloat16 [2048, 512], P(None, 'narrow'), may hold values from -0.125 to 0.125
- w_value: bfloat16 [2048, 512], P(None, 'narrow'), may hold values from -0.125 to 0.125
- w_out: bfloat16 [2048, 2048], P('narrow'), may hold values from -2 to 2
- ffn_gain: bfloat16 [2048], replicated, may hold values from 0.099609375 to 1.8984375
- w_gate: bfloat16 [2048, 8192], P(None, 'narrow'), may hold values from -0.125 to 0.125
- w_up: bfloat16 [2048, 8192], P(None, 'narrow'), may hold values from -0.125 to 0.125
- w_down: bfloat16 [8192, 2048], P('narrow'), may hold values from -0.0625 to 0.0625
- doc_lengths: int32 [12], replicated, may hold values from 1 to 2048, 4096 in all
- cotangent: bfloat16 [4096, 2048], P('wide'), may hold values from -6 to 6
Outputs:
- output: bfloat16 [4096, 2048], P('wide')
- input_grad: bfloat16 [4096, 2048], P('wide')
- grad_attn_gain: float32 [2048], P('wide')
- grad_query: float32 [2048, 2048], P('wide', 'narrow')
- grad_key: float32 [2048, 512], P('wide', 'narrow')
- grad_value: float32 [2048, 512], P('wide', 'narrow')
- grad_out: float32 [2048, 2048], P('narrow', 'wide')
- grad_ffn_gain: float32 [2048], P('wide')
- grad_gate: float32 [2048, 8192], P('wide', 'narrow')
- grad_up: float32 [2048, 8192], P('wide', 'narrow')
- grad_down: float32 [8192, 2048], P('narrow', 'wide')
Inputs may be any that keep to these rules, and one draw needn't show every extreme that they name: `doc_lengths`: the last entry is the padding at the row's end; the longest entry is exactly 2048.
All inputs are finite; a program needn't handle non-finite values.
Results may differ from a plain program's by a relative error of at most 0.02.
Values may be sent and summed in bfloat16 or wider, within the bound.
No kernel may reach another device: no remote copies, remote signals or barrier semaphores. Data moves between devices by JAX's collectives and lax.ppermute only.
A program may use at most 320 MiB of HBM per device.

v0:
```python
import math

import jax
import jax.numpy as jnp
import numpy as np
from jax import lax
from jax.sharding import PartitionSpec as P

HD = 64
QBLK = 512
DOCS = 12


NORM_EPS = 1e-05
MASKED_SCORE = -1e30


def inverse_frequencies(head_size):
    frequency = 1.0 / 500000.0 ** (np.arange(0, head_size, 2) / head_size)
    wavelength = 2 * math.pi / frequency
    smoothing = (8192.0 / wavelength - 1.0) / 3.0
    scaled_freq = np.where(wavelength > 8192.0, frequency / 32.0, frequency)
    middle_band = (wavelength <= 8192.0) & (wavelength >= 2048.0)
    scaled_freq = np.where(
        middle_band, (1 - smoothing) * frequency / 32.0 + smoothing * frequency, scaled_freq
    )
    return scaled_freq.astype(np.float32)


def doc_layout(doc_lengths, index):
    ends = jnp.cumsum(doc_lengths)
    passed = (index[:, None] >= ends[None, :]).astype(jnp.int32)
    segment = jnp.sum(passed, axis=1)
    offset = jnp.sum(passed * doc_lengths[None, :], axis=1)
    position = index - offset
    valid = index < ends[DOCS - 2]
    return (segment, position, valid)


def rotate(values, position, heads, direction):
    angle = position.astype(jnp.float32)[:, None] * jnp.asarray(inverse_frequencies(HD))[None, :]
    cosine = jnp.cos(angle)[:, None, :]
    sine = direction * jnp.sin(angle)[:, None, :]
    shaped = values.reshape(values.shape[0], heads, 2, HD // 2)
    first = shaped[:, :, 0]
    second = shaped[:, :, 1]
    return jnp.stack(
        [first * cosine - second * sine, second * cosine + first * sine], axis=2
    ).reshape(values.shape)


def contract_rows(left, right):
    return lax.dot_general(
        left, right, (((0,), (0,)), ((), ())), preferred_element_type=jnp.float32
    )


def contract_cols(left, right):
    return lax.dot_general(
        left, right, (((1,), (1,)), ((), ())), preferred_element_type=jnp.float32
    )


def head_scores(query_head, key_head, allowed):
    raw_scores = contract_cols(query_head, key_head)
    return jnp.where(allowed, raw_scores / math.sqrt(HD), MASKED_SCORE)


def norm_back(grad_normed, gain, values, inverse):
    scaled = grad_normed * gain
    return inverse * scaled - values * inverse**3 * jnp.mean(
        scaled * values, axis=-1, keepdims=True
    )


def body(
    tokens,
    attn_gain,
    w_query,
    w_key,
    w_value,
    w_out,
    ffn_gain,
    w_gate,
    w_up,
    w_down,
    doc_lengths,
    cotangent,
):
    rows = tokens.shape[0]
    total = rows * lax.axis_size("wide")
    heads = w_query.shape[1] // HD
    kv_heads = w_key.shape[1] // HD
    group = heads // kv_heads
    blocks = rows // QBLK
    local_index = lax.axis_index("wide") * rows + jnp.arange(rows, dtype=jnp.int32)
    segment, position, valid = doc_layout(doc_lengths, local_index)
    key_index = jnp.arange(total, dtype=jnp.int32)
    key_layout = doc_layout(doc_lengths, key_index)
    key_segment = key_layout[0]
    inputs = tokens.astype(jnp.float32)
    gain_one = attn_gain.astype(jnp.float32)
    gain_two = ffn_gain.astype(jnp.float32)
    inv_one = lax.rsqrt(jnp.mean(inputs * inputs, axis=-1, keepdims=True) + NORM_EPS)
    normed = (inputs * inv_one * gain_one).astype(jnp.bfloat16)
    query = jnp.dot(normed, w_query, preferred_element_type=jnp.float32)
    keys = jnp.dot(normed, w_key, preferred_element_type=jnp.float32)
    values = jnp.dot(normed, w_value, preferred_element_type=jnp.float32).astype(jnp.bfloat16)
    query_r = rotate(query, position, heads, 1.0).astype(jnp.bfloat16)
    keys_r = rotate(keys, position, kv_heads, 1.0).astype(jnp.bfloat16)
    packed = jnp.concatenate([keys_r, values], axis=1)
    gathered = lax.all_gather(packed, "wide", axis=0, tiled=True)
    width = kv_heads * HD
    all_keys = gathered[:, :width]
    all_values = gathered[:, width:]

    def block_mask(segment_block, index_block):
        return (segment_block[:, None] == key_segment[None, :]) & (
            index_block[:, None] >= key_index[None, :]
        )

    def attend(block_in):
        query_block, segment_block, index_block = block_in
        allowed = block_mask(segment_block, index_block)
        outputs = []
        totals = []
        for head in range(heads):
            column = head // group * HD
            scores = head_scores(
                query_block[:, head * HD : (head + 1) * HD],
                all_keys[:, column : column + HD],
                allowed,
            )
            row_max = jnp.max(scores, axis=1, keepdims=True)
            exponent = jnp.exp(scores - row_max)
            row_sum = jnp.sum(exponent, axis=1, keepdims=True)
            probs = (exponent / row_sum).astype(jnp.bfloat16)
            outputs.append(
                jnp.dot(
                    probs, all_values[:, column : column + HD], preferred_element_type=jnp.float32
                )
            )
            totals.append(row_max[:, 0] + jnp.log(row_sum[:, 0]))
        return (jnp.concatenate(outputs, axis=1), jnp.stack(totals, axis=1))

    query_blocks = query_r.reshape(blocks, QBLK, heads * HD)
    segment_blocks = segment.reshape(blocks, QBLK)
    index_blocks = local_index.reshape(blocks, QBLK)
    attended, log_sums = lax.map(attend, (query_blocks, segment_blocks, index_blocks))
    valid_rows = valid[:, None]
    mixed = jnp.where(valid_rows, attended.reshape(rows, heads * HD), 0.0).astype(jnp.bfloat16)
    attn_part = jnp.dot(mixed, w_out, preferred_element_type=jnp.float32)
    hidden_one = inputs + lax.psum(attn_part, "narrow")
    inv_two = lax.rsqrt(jnp.mean(hidden_one * hidden_one, axis=-1, keepdims=True) + NORM_EPS)
    normed_two = (hidden_one * inv_two * gain_two).astype(jnp.bfloat16)
    gate = jnp.dot(normed_two, w_gate, preferred_element_type=jnp.float32)
    up_proj = jnp.dot(normed_two, w_up, preferred_element_type=jnp.float32)
    sigmoid_gate = jax.nn.sigmoid(gate)
    silu_gate = gate * sigmoid_gate
    activ = (silu_gate * up_proj).astype(jnp.bfloat16)
    ffn_part = jnp.dot(activ, w_down, preferred_element_type=jnp.float32)
    grad_down = contract_rows(activ, cotangent)
    d_activ = contract_cols(cotangent, w_down)
    d_gate = (d_activ * up_proj * sigmoid_gate * (1.0 + gate * (1.0 - sigmoid_gate))).astype(
        jnp.bfloat16
    )
    d_up = (d_activ * silu_gate).astype(jnp.bfloat16)
    grad_gate = contract_rows(normed_two, d_gate)
    grad_up = contract_rows(normed_two, d_up)
    norm_two_part = contract_cols(d_gate, w_gate) + contract_cols(d_up, w_up)
    output = (
        hidden_one + lax.psum(ffn_part.astype(jnp.bfloat16), "narrow").astype(jnp.float32)
    ).astype(jnp.bfloat16)
    d_norm_two = lax.psum(norm_two_part.astype(jnp.bfloat16), "narrow").astype(jnp.float32)
    grad_ffn_gain = jnp.sum(d_norm_two * hidden_one * inv_two, axis=0)
    d_hidden = cotangent.astype(jnp.float32) + norm_back(d_norm_two, gain_two, hidden_one, inv_two)
    d_hidden_b = d_hidden.astype(jnp.bfloat16)
    grad_out = contract_rows(mixed, d_hidden_b)
    d_mixed = jnp.where(
        valid_rows,
        contract_cols(d_hidden_b, w_out).astype(jnp.bfloat16),
        jnp.zeros((), jnp.bfloat16),
    )

    def attend_back(carry, block_in):
        query_block, grad_block, lse_block, segment_block, index_block = block_in
        allowed = block_mask(segment_block, index_block)
        query_grads = []
        key_terms = [None] * kv_heads
        value_terms = [None] * kv_heads
        for head in range(heads):
            kv_index = head // group
            column = kv_index * HD
            query_head = query_block[:, head * HD : (head + 1) * HD]
            grad_head = grad_block[:, head * HD : (head + 1) * HD]
            key_head = all_keys[:, column : column + HD]
            value_head = all_values[:, column : column + HD]
            scores = head_scores(query_head, key_head, allowed)
            probs = jnp.where(allowed, jnp.exp(scores - lse_block[:, head : head + 1]), 0.0)
            prob_grad = contract_cols(grad_head, value_head)
            delta = jnp.sum(probs * prob_grad, axis=1, keepdims=True)
            d_scores = (probs * (prob_grad - delta)).astype(jnp.bfloat16)
            query_grads.append(
                jnp.dot(d_scores, key_head, preferred_element_type=jnp.float32) / math.sqrt(HD)
            )
            key_term = contract_rows(d_scores, query_head) / math.sqrt(HD)
            value_term = contract_rows(probs.astype(jnp.bfloat16), grad_head)
            if key_terms[kv_index] is None:
                key_terms[kv_index] = key_term
                value_terms[kv_index] = value_term
            else:
                key_terms[kv_index] = key_terms[kv_index] + key_term
                value_terms[kv_index] = value_terms[kv_index] + value_term
        update = jnp.concatenate(key_terms + value_terms, axis=1)
        return (carry + update, jnp.concatenate(query_grads, axis=1))

    start_terms = jnp.zeros((total, 2 * width), jnp.float32)
    grad_blocks = d_mixed.reshape(blocks, QBLK, heads * HD)
    kv_terms, query_grad_blocks = lax.scan(
        attend_back,
        start_terms,
        (query_blocks, grad_blocks, log_sums, segment_blocks, index_blocks),
    )
    d_kv = lax.psum_scatter(
        kv_terms.astype(jnp.bfloat16), "wide", scatter_dimension=0, tiled=True
    ).astype(jnp.float32)
    d_query = rotate(query_grad_blocks.reshape(rows, heads * HD), position, heads, -1.0).astype(
        jnp.bfloat16
    )
    d_keys = rotate(d_kv[:, :width], position, kv_heads, -1.0).astype(jnp.bfloat16)
    d_values = d_kv[:, width:].astype(jnp.bfloat16)
    grad_query = contract_rows(normed, d_query)
    grad_key = contract_rows(normed, d_keys)
    grad_value = contract_rows(normed, d_values)
    norm_one_part = (
        contract_cols(d_query, w_query)
        + contract_cols(d_keys, w_key)
        + contract_cols(d_values, w_value)
    )
    d_norm_one = lax.psum(norm_one_part.astype(jnp.bfloat16), "narrow").astype(jnp.float32)
    grad_attn_gain = jnp.sum(d_norm_one * inputs * inv_one, axis=0)
    input_grad = (d_hidden + norm_back(d_norm_one, gain_one, inputs, inv_one)).astype(jnp.bfloat16)
    summed = (
        lax.psum_scatter(
            grad_attn_gain.astype(jnp.bfloat16), "wide", scatter_dimension=0, tiled=True
        ).astype(jnp.float32),
        lax.psum_scatter(
            grad_query.astype(jnp.bfloat16), "wide", scatter_dimension=0, tiled=True
        ).astype(jnp.float32),
        lax.psum_scatter(
            grad_key.astype(jnp.bfloat16), "wide", scatter_dimension=0, tiled=True
        ).astype(jnp.float32),
        lax.psum_scatter(
            grad_value.astype(jnp.bfloat16), "wide", scatter_dimension=0, tiled=True
        ).astype(jnp.float32),
        lax.psum_scatter(
            grad_out.astype(jnp.bfloat16), "wide", scatter_dimension=1, tiled=True
        ).astype(jnp.float32),
        lax.psum_scatter(
            grad_ffn_gain.astype(jnp.bfloat16), "wide", scatter_dimension=0, tiled=True
        ).astype(jnp.float32),
        lax.psum_scatter(
            grad_gate.astype(jnp.bfloat16), "wide", scatter_dimension=0, tiled=True
        ).astype(jnp.float32),
        lax.psum_scatter(
            grad_up.astype(jnp.bfloat16), "wide", scatter_dimension=0, tiled=True
        ).astype(jnp.float32),
        lax.psum_scatter(
            grad_down.astype(jnp.bfloat16), "wide", scatter_dimension=1, tiled=True
        ).astype(jnp.float32),
    )
    gain_attn = summed[0]
    gain_ffn = summed[5]
    return (
        output,
        input_grad,
        gain_attn,
        summed[1],
        summed[2],
        summed[3],
        summed[4],
        gain_ffn,
        summed[6],
        summed[7],
        summed[8],
    )


def solution(mesh):
    in_specs = (
        P("wide", None),
        P(),
        P(None, "narrow"),
        P(None, "narrow"),
        P(None, "narrow"),
        P("narrow", None),
        P(),
        P(None, "narrow"),
        P(None, "narrow"),
        P("narrow", None),
        P(),
        P("wide", None),
    )
    out_specs = (
        P("wide", None),
        P("wide", None),
        P("wide"),
        P("wide", "narrow"),
        P("wide", "narrow"),
        P("wide", "narrow"),
        P("narrow", "wide"),
        P("wide"),
        P("wide", "narrow"),
        P("wide", "narrow"),
        P("narrow", "wide"),
    )
    return jax.shard_map(body, mesh=mesh, in_specs=in_specs, out_specs=out_specs, check_vma=False)
```

profile of v0, /device:TPU:0, one launch (start us, length us, event | category | flops | bytes accessed | tf_op | source)
XLA Modules:
  0.0 1095.6 jit_solution(12022537940424208202)
XLA Ops:
  24.5 25.3 %all-gather.2.cloned.1.call-done = bf16[4096,256]{0,1:T(8,128)(2,1)} async-done(((bf16[512,256]{0,1:T(8,128)(2,1)}), bf16[4096,256]{0,1:T(8,128)(2,1)}) %all-gather.2.cloned.1.call-update) | async-done | bytes 2097168 | tf_op jit(solution)/shard_map/all_gather | solution.py:112
  134.6 103.2 %all-reduce.8.cloned.1.call-done = f32[512,2048]{1,0:T(8,128)} async-done(((f32[512,2048]{1,0:T(8,128)}), f32[512,2048]{1,0:T(8,128)}) %all-reduce.8.cloned.1.call-update) | async-done | bytes 4194320 | tf_op jit(solution)/shard_map/psum | solution.py:153
  241.8 9.3 fusion.178
  257.5 12.0 %multiply_convert_fusion.8 = (bf16[512,2048]{1,0:T(8,128)(2,1)}, bf16[512,2048]{1,0:T(8,128)(2,1)}, bf16[512,2048]{1,0:T(8,128)(2,1)}) fusion(f32[512,2048]{1,0:T(8,128)} %fusion.177, f32[512,2048]{1,0:T(8,128)S(1)} %fusion.178, bf16[512,2048]{1,0:T(8,128)(2,1)S(1)} %copy-done.36, bf16[2048,2048]{1,0:T(8,128)(2,1)} %param.25), kind=kOutput, calls=%fused_computation.118 | convolution fusion | flops 4310695936 | bytes 25165824 | tf_op jit(solution)/shard_map/dot_general | solution.py:59
  269.5 7.8 fusion.179
  277.3 9.4 add_convert_fusion.1
  287.0 69.5 %all-reduce.10.cloned.1.call-done = bf16[512,2048]{1,0:T(8,128)(2,1)} async-done(((bf16[512,2048]{1,0:T(8,128)(2,1)}), bf16[512,2048]{1,0:T(8,128)(2,1)}) %all-reduce.10.cloned.1.call-update) | async-done | bytes 2097168 | tf_op jit(solution)/shard_map/psum | solution.py:174
  415.0 26.5 %multiply_reduce_fusion = (f32[512]{0:T(512)S(1)}, f32[512]{0:T(512)S(1)}, f32[512]{0:T(512)S(1)}, f32[512]{0:T(512)S(1)}, f32[512]{0:T(512)S(1)}, /*index=5*/f32[512,4096]{1,0:T(8,128)}) fusion(f32[512,4096]{1,0:T(8,128)} %copy-done.7, f32[512]{0:T(512)S(1)} %log_add_fusion, s32[512]{0:T(512)S(1)} %iota_add_fusion, s32[4096]{0:T(1024)S(1)} %convert_reduce_fusion, ...), kind=kOutput, calls=%fused_computation.7 | convolution fusion | flops 316667392 | bytes 84516864 | tf_op jit(solution)/shard_map/while/body/eval_jaxpr/dot_general | solution.py:59
  441.5 25.5 %multiply_reduce_fusion.1 = (f32[512]{0:T(512)S(1)}, f32[512]{0:T(512)S(1)}, f32[512]{0:T(512)S(1)}, bf16[512,4096]{1,0:T(8,128)(2,1)}, f32[512,4096]{1,0:T(8,128)}) fusion(f32[512,4096]{1,0:T(8,128)} %copy-done.4, f32[512]{0:T(512)S(1)} %get-tuple-element.145, s32[512]{0:T(512)S(1)} %iota_add_fusion, s32[4096]{0:T(1024)S(1)} %convert_reduce_fusion, ...), kind=kOutput, calls=%fused_computation.10 | convolution fusion | flops 310376960 | bytes 71929856 | tf_op jit(solution)/shard_map/while/body/eval_jaxpr/dot_general | solution.py:59
  467.1 21.2 %multiply_convert_fusion.2 = (bf16[512,4096]{1,0:T(8,128)(2,1)}, bf16[512,4096]{1,0:T(8,128)(2,1)}, bf16[512,4096]{1,0:T(8,128)(2,1)S(1)}) fusion(f32[512,4096]{1,0:T(8,128)} %fusion.78, f32[512]{0:T(512)S(1)} %get-tuple-element.88, f32[512,4096]{1,0:T(8,128)} %copy-done.8, f32[512]{0:T(512)S(1)} %get-tuple-element.146, s32[512]{0:T(512)S(1)} %iota_add_fusion, ...), kind=kLoop, calls=%fused_computation.12 | loop fusion | flops 37748736 | bytes 62947328 | tf_op jit(solution)/shard_map/while/body/eval_jaxpr/convert_element_type | solution.py:202
  492.1 27.3 %multiply_convert_fusion.1 = (bf16[512,4096]{1,0:T(8,128)(2,1)}, bf16[512,4096]{1,0:T(8,128)(2,1)}, bf16[512,4096]{1,0:T(8,128)(2,1)}, bf16[512,4096]{1,0:T(8,128)(2,1)}) fusion(f32[512,4096]{1,0:T(8,128)} %get-tuple-element.140, f32[512]{0:T(512)S(1)} %get-tuple-element.74, f32[512,4096]{1,0:T(8,128)} %copy-done.4, f32[512]{0:T(512)S(1)} %get-tuple-element.145, ...), kind=kLoop, calls=%fused_computation.9 | loop fusion | flops 48234496 | bytes 83922944 | tf_op jit(solution)/shard_map/while/body/eval_jaxpr/convert_element_type | solution.py:202
  558.3 11.5 %reduce-scatter.9.cloned.1.call-done = bf16[512,256]{0,1:T(8,128)(2,1)} async-done(((bf16[4096,256]{0,1:T(8,128)(2,1)}), bf16[512,256]{0,1:T(8,128)(2,1)}) %reduce-scatter.9.cloned.1.call-update) | async-done | bytes 262160 | tf_op jit(solution)/shard_map/reduce_scatter | solution.py:224
  572.9 10.0 convolution_convert_fusion.5
  591.0 10.1 convolution_convert_fusion.1
  601.3 10.1 convolution_convert_fusion.2
  611.5 10.2 convolution_convert_fusion
  625.4 17.6 %reduce-scatter.11.cloned.1.call-done = bf16[256,512]{1,0:T(8,128)(2,1)} async-done(((bf16[2048,512]{1,0:T(8,128)(2,1)}), bf16[256,512]{1,0:T(8,128)(2,1)}) %reduce-scatter.11.cloned.1.call-update) | async-done | bytes 262160 | tf_op jit(solution)/shard_map/reduce_scatter | solution.py:247
  644.9 30.1 %reduce-scatter.13.cloned.1.call-done = bf16[256,128]{1,0:T(8,128)(2,1)} async-done(((bf16[2048,128]{1,0:T(8,128)(2,1)}), bf16[256,128]{1,0:T(8,128)(2,1)}) %reduce-scatter.13.cloned.1.call-update) | async-done | bytes 65552 | tf_op jit(solution)/shard_map/reduce_scatter | solution.py:250
  676.5 30.0 %reduce-scatter.15.cloned.1.call-done = bf16[256,128]{1,0:T(8,128)(2,1)} async-done(((bf16[2048,128]{1,0:T(8,128)(2,1)}), bf16[256,128]{1,0:T(8,128)(2,1)}) %reduce-scatter.15.cloned.1.call-update) | async-done | bytes 65552 | tf_op jit(solution)/shard_map/reduce_scatter | solution.py:253
  708.0 104.9 %all-reduce.12.cloned.1.call-done = (bf16[512,2048]{1,0:T(8,128)(2,1)}, bf16[512,2048]{1,0:T(8,128)(2,1)}) async-done(((bf16[512,2048]{1,0:T(8,128)(2,1)}, bf16[512,2048]{1,0:T(8,128)(2,1)}), (bf16[512,2048]{1,0:T(8,128)(2,1)}, bf16[512,2048]{1,0:T(8,128)(2,1)})) %all-reduce.12.cloned.1.call-update) | async-done | bytes 4194320 | tf_op jit(solution)/shard_map/psum | solution.py:172
  816.1 17.5 %all-reduce.2 = (bf16[2048]{0:T(1024)(128)(2,1)S(1)}, bf16[2048]{0:T(1024)(128)(2,1)S(1)}) all-reduce(bf16[2048]{0:T(1024)(128)(2,1)S(1)} %get-tuple-element.67, bf16[2048]{0:T(1024)(128)(2,1)S(1)} %copy-done.52), channel_id=3, replica_groups=mesh['wide'=8,'narrow'=4] {'wide'}, use_global_device_ids=true, to_apply=%region_38.39.clone | all-reduce | flops 4096 | bytes 16384
  843.6 61.7 %reduce-scatter.21.cloned.1.call-done = bf16[256,2048]{1,0:T(8,128)(2,1)} async-done(((bf16[2048,2048]{1,0:T(8,128)(2,1)}), bf16[256,2048]{1,0:T(8,128)(2,1)}) %reduce-scatter.21.cloned.1.call-update) | async-done | bytes 1048592 | tf_op jit(solution)/shard_map/reduce_scatter | solution.py:265
  908.1 87.4 %reduce-scatter.19.cloned.1.call-done = bf16[256,2048]{1,0:T(8,128)(2,1)} async-done(((bf16[2048,2048]{1,0:T(8,128)(2,1)}), bf16[256,2048]{1,0:T(8,128)(2,1)}) %reduce-scatter.19.cloned.1.call-update) | async-done | bytes 1048592 | tf_op jit(solution)/shard_map/reduce_scatter | solution.py:262
  998.3 87.4 %reduce-scatter.23.cloned.1.call-done = bf16[2048,256]{1,0:T(8,128)(2,1)} async-done(((bf16[2048,2048]{1,0:T(8,128)(2,1)}), bf16[2048,256]{1,0:T(8,128)(2,1)}) %reduce-scatter.23.cloned.1.call-update) | async-done | bytes 1048592 | tf_op jit(solution)/shard_map/reduce_scatter | solution.py:268
  (321 shorter events, 253.6 us)
Async XLA Ops:
  7.2 123.9 %copy-start = (bf16[512,2048]{1,0:T(8,128)(2,1)S(1)}, bf16[512,2048]{1,0:T(8,128)(2,1)}, u32[]{:S(2)}) copy-start(bf16[512,2048]{1,0:T(8,128)(2,1)} %param.21) | copy-start | bytes 6291460
  7.2 42.6 %all-gather.2.cloned.1.call-start = ((), (), s32[]{:S(2)}) async-start(), calls=%async_computation.8 | async-start | bytes 2359296 | tf_op jit(solution)/shard_map/all_gather | solution.py:112
  17.9 220.0 %all-reduce.8.cloned.1.call-start = ((), (), s32[]{:S(2)}) async-start(), calls=%async_computation.9 | async-start | bytes 8388608 | tf_op jit(solution)/shard_map/psum | solution.py:153
  19.7 345.4 %copy-start.53 = (pred[512]{0:T(512)(128)(4,1)}, pred[512]{0:T(512)(128)(4,1)S(1)}, u32[]{:S(2)}) copy-start(pred[512]{0:T(512)(128)(4,1)S(1)} %fusion.150) | copy-start | bytes 1540
  61.6 64.6 %copy-start.4 = (f32[512,4096]{1,0:T(8,128)}, f32[512,4096]{1,0:T(8,128)S(1)}, u32[]{:S(2)}) copy-start(f32[512,4096]{1,0:T(8,128)S(1)} %get-tuple-element.136) | copy-start | bytes 25165828
  88.9 25.7 %copy-start.5 = (f32[512,4096]{1,0:T(8,128)}, f32[512,4096]{1,0:T(8,128)S(1)}, u32[]{:S(2)}) copy-start(f32[512,4096]{1,0:T(8,128)S(1)} %get-tuple-element.128) | copy-start | bytes 25165828
  94.5 18.3 %copy-start.6 = (f32[512,4096]{1,0:T(8,128)}, f32[512,4096]{1,0:T(8,128)S(1)}, u32[]{:S(2)}) copy-start(f32[512,4096]{1,0:T(8,128)S(1)} %get-tuple-element.126) | copy-start | bytes 25165828
  134.4 222.1 %all-reduce.10.cloned.1.call-start = ((), (), s32[]{:S(2)}) async-start(), calls=%async_computation.10 | async-start | bytes 4194304 | tf_op jit(solution)/shard_map/psum | solution.py:174
  286.7 283.1 %reduce-scatter.9.cloned.1.call-start = ((), (), s32[]{:S(2)}) async-start(), calls=%async_computation.11 | async-start | bytes 2359296 | tf_op jit(solution)/shard_map/reduce_scatter | solution.py:224
  356.5 10.7 slice-start.14
  467.1 23.3 %copy-start.34 = (bf16[512,8,2,32]{0,3,2,1:T(8,128)(2,1)S(1)}, bf16[512,8,2,32]{0,3,2,1:T(8,128)(2,1)}, u32[]{:S(2)}) copy-start(bf16[512,8,2,32]{0,3,2,1:T(8,128)(2,1)} %pad_maximum_fusion.1) | copy-start | bytes 1572868
  533.8 89.9 %reduce-scatter.17.cloned.1.call-start = ((), (), s32[]{:S(2)}) async-start(), calls=%async_computation.15 | async-start | bytes 2359296 | tf_op jit(solution)/shard_map/reduce_scatter | solution.py:256
  538.6 104.4 %reduce-scatter.11.cloned.1.call-start = ((), (), s32[]{:S(2)}) async-start(), calls=%async_computation.12 | async-start | bytes 2359296 | tf_op jit(solution)/shard_map/reduce_scatter | solution.py:247
  555.3 15.5 %copy-start.28 = (bf16[512,2048]{1,0:T(8,128)(2,1)S(1)}, bf16[512,2048]{1,0:T(8,128)(2,1)}, u32[]{:S(2)}) copy-start(bf16[512,2048]{1,0:T(8,128)(2,1)} %param.16) | copy-start | bytes 6291460
  558.2 116.8 %reduce-scatter.13.cloned.1.call-start = ((), (), s32[]{:S(2)}) async-start(), calls=%async_computation.13 | async-start | bytes 589824 | tf_op jit(solution)/shard_map/reduce_scatter | solution.py:250
  572.6 133.8 %reduce-scatter.15.cloned.1.call-start = ((), (), s32[]{:S(2)}) async-start(), calls=%async_computation.14 | async-start | bytes 589824 | tf_op jit(solution)/shard_map/reduce_scatter | solution.py:253
  572.9 10.0 copy-start.47
  584.7 228.2 %all-reduce.12.cloned.1.call-start = ((), (), s32[]{:S(2)}) async-start(), calls=%async_computation.19 | async-start | bytes 8388608 | tf_op jit(solution)/shard_map/psum | solution.py:172
  590.9 314.4 %reduce-scatter.21.cloned.1.call-start = ((), (), s32[]{:S(2)}) async-start(), calls=%async_computation.17 | async-start | bytes 9437184 | tf_op jit(solution)/shard_map/reduce_scatter | solution.py:265
  601.1 394.4 %reduce-scatter.19.cloned.1.call-start = ((), (), s32[]{:S(2)}) async-start(), calls=%async_computation.16 | async-start | bytes 9437184 | tf_op jit(solution)/shard_map/reduce_scatter | solution.py:262
  611.4 474.3 %reduce-scatter.23.cloned.1.call-start = ((), (), s32[]{:S(2)}) async-start(), calls=%async_computation.18 | async-start | bytes 9437184 | tf_op jit(solution)/shard_map/reduce_scatter | solution.py:268
  621.8 194.3 %copy-start.52 = (bf16[2048]{0:T(1024)(128)(2,1)S(1)}, bf16[2048]{0:T(1024)(128)(2,1)}, u32[]{:S(2)}) copy-start(bf16[2048]{0:T(1024)(128)(2,1)} %get-tuple-element.65) | copy-start | bytes 12292
  643.1 196.8 %copy-start.55 = (f32[512]{0:T(512)S(1)}, f32[512]{0:T(512)}, u32[]{:S(2)}) copy-start(f32[512]{0:T(512)} %get-tuple-element.119) | copy-start | bytes 6148
  841.0 247.4 %copy-start.1 = (bf16[512,2048]{1,0:T(8,128)(2,1)S(1)}, bf16[512,2048]{1,0:T(8,128)(2,1)}, u32[]{:S(2)}) copy-start(bf16[512,2048]{1,0:T(8,128)(2,1)} %param.21) | copy-start | bytes 6291460
  (72 other events, 313.3 us)
Sparse Core Ops, SparseCore 0:
  18.0 31.7 all-gather.1
  134.5 103.3 all-reduce.7
  286.8 69.6 all-reduce.9
  533.9 35.8 reduce-scatter.8
  571.9 34.4 reduce-scatter.16
  608.6 34.4 reduce-scatter.10
  645.3 29.6 reduce-scatter.12
  677.3 29.0 reduce-scatter.14
  710.5 102.3 all-reduce.11
  815.1 90.1 reduce-scatter.20
  907.7 87.7 reduce-scatter.18
  997.8 87.9 reduce-scatter.22
where the time goes:
time: 1100 us
  waiting for transfers between devices  629 us (57%)
  matrix products  293 us (27%)
  other arithmetic  112 us (10%)
  local copies, waits for them, and re-layouts  25.3 us (2%)
  blocking collectives  17.5 us (2%)
  between operations  16.4 us (1%)
    dot_general x23, matrix products, contract_cols(): lax.dot_general(left, right, (((1,), (1,)), ((), ())), preferred_element_...  146 us
    psum x1, waiting for transfers between devices, body(): lax.psum(ffn_part.astype(jnp.bfloat16), 'narrow').astype(jnp.float32)  105 us
    psum x1, waiting for transfers between devices, body(): hidden_one = inputs + lax.psum(attn_part, 'narrow')  103 us
    reduce_scatter x1, waiting for transfers between devices, body(): lax.psum_scatter(grad_down.astype(jnp.bfloat16), 'wide', scatter_dimensio...  87.4 us
    reduce_scatter x1, waiting for transfers between devices, body(): lax.psum_scatter(grad_gate.astype(jnp.bfloat16), 'wide', scatter_dimensio...  87.4 us
    dot_general x23, matrix products, contract_rows(): lax.dot_general(left, right, (((0,), (0,)), ((), ())), preferred_element_...  73.4 us
    psum x1, waiting for transfers between devices, body(): lax.psum(norm_two_part.astype(jnp.bfloat16), 'narrow').astype(jnp.float32)  69.5 us
    reduce_scatter x1, waiting for transfers between devices, body(): lax.psum_scatter(grad_up.astype(jnp.bfloat16), 'wide', scatter_dimension=...  61.7 us
  transfers between devices with their start and end apart: 12, of which 11 were waited for; matrix products, arithmetic and copies ran while one was open for 10% of the time, Pallas kernels for 0%

commit v1 on v0

v1 whole, which is shorter than its diff:
```python
import functools
import math

import jax
import jax.numpy as jnp
import numpy as np
from jax import lax
from jax.experimental import pallas as pl
from jax.experimental.pallas import tpu as pltpu
from jax.sharding import PartitionSpec as P

HD = 64
DOCS = 12
NORM_EPS = 1e-05
MASKED_SCORE = -1e30
LOG2E = math.log2(math.e)
SCALE2 = LOG2E / math.sqrt(HD)
QT = 256
KT = 256
BF = jnp.bfloat16
F32 = jnp.float32


def inverse_frequencies(head_size):
    frequency = 1.0 / 500000.0 ** (np.arange(0, head_size, 2) / head_size)
    wavelength = 2 * math.pi / frequency
    smoothing = (8192.0 / wavelength - 1.0) / 3.0
    scaled_freq = np.where(wavelength > 8192.0, frequency / 32.0, frequency)
    middle_band = (wavelength <= 8192.0) & (wavelength >= 2048.0)
    scaled_freq = np.where(
        middle_band, (1 - smoothing) * frequency / 32.0 + smoothing * frequency, scaled_freq
    )
    return scaled_freq.astype(np.float32)


def doc_offsets(doc_lengths, index):
    ends = jnp.cumsum(doc_lengths)
    passed = (index[None, :] >= ends[:, None]).astype(jnp.int32)
    start = jnp.sum(passed * doc_lengths[:, None], axis=0)
    valid = index < ends[DOCS - 2]
    return start, valid


def rotate_t(values, cosine, sine):
    heads = values.shape[0] // HD
    shaped = values.reshape(heads, 2, HD // 2, values.shape[1])
    first = shaped[:, 0]
    second = shaped[:, 1]
    return jnp.stack(
        [first * cosine - second * sine, second * cosine + first * sine], axis=1
    ).reshape(values.shape)


def dims(left, right, a, b):
    return lax.dot_general(left, right, (((a,), (b,)), ((), ())), preferred_element_type=F32)


def tile_active(info_ref, tiles, tile, q_tile):
    key_base = info_ref[tile]
    q_base = info_ref[tiles] + q_tile * QT
    first_key = info_ref[tiles + 1 + q_tile]
    return (key_base <= q_base + QT - 1) & (key_base + KT > first_key), key_base, q_base


def tile_mask(key_base, q_base, start_row):
    keys = key_base + lax.broadcasted_iota(jnp.int32, (KT, QT), 0)
    queries = q_base + lax.broadcasted_iota(jnp.int32, (KT, QT), 1)
    return (keys <= queries) & (keys >= start_row)


def attend_kernel(slots, group, info_ref, start_ref, valid_ref, q_ref, *refs):
    k_refs = refs[:slots]
    v_refs = refs[slots : 2 * slots]
    o_ref, mixed_ref, lse_ref, keys_s, values_s, top_s, sum_s, acc_s = refs[2 * slots :]
    rows = q_ref.shape[1]
    per = rows // KT
    tiles = slots * per
    for slot in range(slots):
        for part in range(per):
            cut = slice(part * KT, (part + 1) * KT)
            keys_s[slot * per + part] = k_refs[slot][:, cut].T
            values_s[slot * per + part] = v_refs[slot][:, cut]
    for q_tile in range(rows // QT):
        q_cut = slice(q_tile * QT, (q_tile + 1) * QT)
        top_s[...] = jnp.full_like(top_s, MASKED_SCORE)
        sum_s[...] = jnp.zeros_like(sum_s)
        acc_s[...] = jnp.zeros_like(acc_s)
        start_row = start_ref[:, q_cut]

        def step(tile, carry, q_tile=q_tile, q_cut=q_cut, start_row=start_row):
            active, key_base, q_base = tile_active(info_ref, tiles, tile, q_tile)

            @pl.when(active)
            def _():
                allowed = tile_mask(key_base, q_base, start_row)
                keys = keys_s[tile]
                values = values_s[tile]
                for head in range(group):
                    scores = jnp.dot(
                        keys, q_ref[head * HD : (head + 1) * HD, q_cut], preferred_element_type=F32
                    )
                    scores = jnp.where(allowed, scores, MASKED_SCORE)
                    old = top_s[head : head + 1, :]
                    new = jnp.maximum(old, jnp.max(scores, axis=0, keepdims=True))
                    weight = jnp.exp2((scores - new) * SCALE2)
                    decay = jnp.exp2((old - new) * SCALE2)
                    top_s[head : head + 1, :] = new
                    sum_s[head : head + 1, :] = sum_s[head : head + 1, :] * decay + jnp.sum(
                        weight, axis=0, keepdims=True
                    )
                    acc_s[head] = acc_s[head] * decay + jnp.dot(
                        values, weight.astype(BF), preferred_element_type=F32
                    )

            return carry

        lax.fori_loop(0, tiles, step, 0)
        for head in range(group):
            h_cut = slice(head * HD, (head + 1) * HD)
            total = sum_s[head : head + 1, :]
            out = acc_s[head] / total
            o_ref[h_cut, q_cut] = out
            mixed_ref[h_cut, q_cut] = jnp.where(valid_ref[:, q_cut] != 0, out, 0.0).astype(BF)
            lse_ref[0, head : head + 1, q_cut] = (
                top_s[head : head + 1, :] * SCALE2 + jnp.log(total) * LOG2E
            )


def attend(info, start, valid, q_t, blocks, kv_heads):
    slots = len(blocks)
    heads = q_t.shape[0] // HD
    group = heads // kv_heads
    rows = q_t.shape[1]
    tiles = slots * (rows // KT)
    row_spec = pl.BlockSpec((1, rows), lambda g: (0, 0))
    q_spec = pl.BlockSpec((group * HD, rows), lambda g: (g, 0))
    return pl.pallas_call(
        functools.partial(attend_kernel, slots, group),
        grid=(kv_heads,),
        in_specs=[pl.BlockSpec(memory_space=pltpu.SMEM), row_spec, row_spec, q_spec]
        + [pl.BlockSpec((HD, rows), lambda g: (g, 0))] * slots
        + [pl.BlockSpec((HD, rows), lambda g: (kv_heads + g, 0))] * slots,
        out_specs=[q_spec, q_spec, pl.BlockSpec((1, group, rows), lambda g: (g, 0, 0))],
        out_shape=[
            jax.ShapeDtypeStruct(q_t.shape, F32),
            jax.ShapeDtypeStruct(q_t.shape, BF),
            jax.ShapeDtypeStruct((kv_heads, group, rows), F32),
        ],
        scratch_shapes=[
            pltpu.VMEM((tiles, KT, HD), BF),
            pltpu.VMEM((tiles, HD, KT), BF),
            pltpu.VMEM((group, QT), F32),
            pltpu.VMEM((group, QT), F32),
            pltpu.VMEM((group, HD, QT), F32),
        ],
        name="attend",
        cost_estimate=pl.CostEstimate(
            flops=4 * heads * rows * rows * 4 * HD,
            transcendentals=heads * rows * rows * 4,
            bytes_accessed=8 * rows * heads * HD,
        ),
    )(info, start, valid, q_t, *blocks, *blocks)


def attend_back_kernel(slots, group, info_ref, start_ref, q_ref, do_ref, o_ref, lse_ref, *refs):
    k_refs = refs[:slots]
    v_refs = refs[slots : 2 * slots]
    dq_ref, dkv_ref, keys_s, values_s, keys_t_s, dk_s, dv_s, q_s, do_s, dq_s, delta_s = refs[
        2 * slots :
    ]
    rows = q_ref.shape[1]
    per = rows // KT
    tiles = slots * per
    for slot in range(slots):
        for part in range(per):
            cut = slice(part * KT, (part + 1) * KT)
            tile = slot * per + part
            keys_s[tile] = k_refs[slot][:, cut].T
            keys_t_s[tile] = k_refs[slot][:, cut]
            values_s[tile] = v_refs[slot][:, cut].T
    dk_s[...] = jnp.zeros_like(dk_s)
    dv_s[...] = jnp.zeros_like(dv_s)
    for q_tile in range(rows // QT):
        q_cut = slice(q_tile * QT, (q_tile + 1) * QT)
        for head in range(group):
            h_cut = slice(head * HD, (head + 1) * HD)
            q_s[head] = q_ref[h_cut, q_cut].T
            do_s[head] = do_ref[h_cut, q_cut].T
            delta_s[head : head + 1, :] = jnp.sum(
                do_ref[h_cut, q_cut].astype(F32) * o_ref[h_cut, q_cut], axis=0, keepdims=True
            )
        dq_s[...] = jnp.zeros_like(dq_s)
        start_row = start_ref[:, q_cut]

        def step(tile, carry, q_tile=q_tile, q_cut=q_cut, start_row=start_row):
            active, key_base, q_base = tile_active(info_ref, tiles, tile, q_tile)

            @pl.when(active)
            def _():
                allowed = tile_mask(key_base, q_base, start_row)
                keys = keys_s[tile]
                values = values_s[tile]
                keys_t = keys_t_s[tile]
                dk = dk_s[tile]
                dv = dv_s[tile]
                for head in range(group):
                    h_cut = slice(head * HD, (head + 1) * HD)
                    scores = jnp.dot(keys, q_ref[h_cut, q_cut], preferred_element_type=F32)
                    scores = jnp.where(allowed, scores * SCALE2, MASKED_SCORE)
                    prob = jnp.exp2(scores - lse_ref[0, head : head + 1, q_cut])
                    prob_grad = jnp.dot(values, do_ref[h_cut, q_cut], preferred_element_type=F32)
                    d_scores = (prob * (prob_grad - delta_s[head : head + 1, :])).astype(BF)
                    dv = dv + jnp.dot(prob.astype(BF), do_s[head], preferred_element_type=F32)
                    dk = dk + jnp.dot(d_scores, q_s[head], preferred_element_type=F32)
                    dq_s[head] += jnp.dot(keys_t, d_scores, preferred_element_type=F32)
                dk_s[tile] = dk
                dv_s[tile] = dv

            return carry

        lax.fori_loop(0, tiles, step, 0)
        for head in range(group):
            dq_ref[head * HD : (head + 1) * HD, q_cut] = dq_s[head]
    for slot in range(slots):
        for part in range(per):
            cut = slice(part * KT, (part + 1) * KT)
            tile = slot * per + part
            dkv_ref[slot, 0, :, cut] = (dk_s[tile].T * (1.0 / math.sqrt(HD))).astype(BF)
            dkv_ref[slot, 1, :, cut] = dv_s[tile].T.astype(BF)


def attend_back(info, start, q_t, do_t, o_t, lse, blocks, kv_heads):
    slots = len(blocks)
    heads = q_t.shape[0] // HD
    group = heads // kv_heads
    rows = q_t.shape[1]
    tiles = slots * (rows // KT)
    row_spec = pl.BlockSpec((1, rows), lambda g: (0, 0))
    q_spec = pl.BlockSpec((group * HD, rows), lambda g: (g, 0))
    return pl.pallas_call(
        functools.partial(attend_back_kernel, slots, group),
        grid=(kv_heads,),
        in_specs=[pl.BlockSpec(memory_space=pltpu.SMEM), row_spec, q_spec, q_spec, q_spec]
        + [pl.BlockSpec((1, group, rows), lambda g: (g, 0, 0))]
        + [pl.BlockSpec((HD, rows), lambda g: (g, 0))] * slots
        + [pl.BlockSpec((HD, rows), lambda g: (kv_heads + g, 0))] * slots,
        out_specs=[q_spec, pl.BlockSpec((slots, 2, HD, rows), lambda g: (0, 0, g, 0))],
        out_shape=[
            jax.ShapeDtypeStruct(q_t.shape, F32),
            jax.ShapeDtypeStruct((slots, 2, kv_heads * HD, rows), BF),
        ],
        scratch_shapes=[
            pltpu.VMEM((tiles, KT, HD), BF),
            pltpu.VMEM((tiles, KT, HD), BF),
            pltpu.VMEM((tiles, HD, KT), BF),
            pltpu.VMEM((tiles, KT, HD), F32),
            pltpu.VMEM((tiles, KT, HD), F32),
            pltpu.VMEM((group, QT, HD), BF),
            pltpu.VMEM((group, QT, HD), BF),
            pltpu.VMEM((group, HD, QT), F32),
            pltpu.VMEM((group, QT), F32),
        ],
        name="attend_back",
        cost_estimate=pl.CostEstimate(
            flops=10 * heads * rows * rows * 4 * HD,
            transcendentals=heads * rows * rows * 4,
            bytes_accessed=16 * rows * heads * HD,
        ),
    )(info, start, q_t, do_t, o_t, lse, *blocks, *blocks)


def ffn_kernel(n_ref, da_ref, wg_ref, wu_ref, act_ref, dg_ref, du_ref):
    normed = n_ref[...]
    gate = jnp.dot(normed, wg_ref[...], preferred_element_type=F32)
    up = jnp.dot(normed, wu_ref[...], preferred_element_type=F32)
    sig = jax.nn.sigmoid(gate)
    silu = gate * sig
    act_ref[...] = (silu * up).astype(BF)
    d_act = da_ref[...]
    dg_ref[...] = (d_act * up * sig * (1.0 + gate * (1.0 - sig))).astype(BF)
    du_ref[...] = (d_act * silu).astype(BF)


def ffn_forward(normed, d_act, w_gate, w_up):
    rows, width = normed.shape
    units = w_gate.shape[1]
    step = min(512, units)
    tile = pl.BlockSpec((rows, step), lambda j: (0, j))
    weight = pl.BlockSpec((width, step), lambda j: (0, j))
    return pl.pallas_call(
        ffn_kernel,
        grid=(units // step,),
        in_specs=[pl.BlockSpec((rows, width), lambda j: (0, 0)), tile, weight, weight],
        out_specs=[tile, tile, tile],
        out_shape=[jax.ShapeDtypeStruct((rows, units), BF)] * 3,
        name="gate_up",
        cost_estimate=pl.CostEstimate(
            flops=4 * rows * width * units,
            transcendentals=rows * units,
            bytes_accessed=4 * width * units + 2 * rows * width + 10 * rows * units,
        ),
    )(normed, d_act, w_gate, w_up)


def pair_nt_kernel(a_ref, b_ref, wa_ref, wb_ref, o_ref):
    o_ref[...] = (
        dims(a_ref[...], wa_ref[...], 1, 1) + dims(b_ref[...], wb_ref[...], 1, 1)
    ).astype(BF)


def pair_nt(a, b, w_a, w_b):
    rows, units = a.shape
    width = w_a.shape[0]
    step = min(512, width)
    full = pl.BlockSpec((rows, units), lambda j: (0, 0))
    weight = pl.BlockSpec((step, units), lambda j: (j, 0))
    return pl.pallas_call(
        pair_nt_kernel,
        grid=(width // step,),
        in_specs=[full, full, weight, weight],
        out_specs=pl.BlockSpec((rows, step), lambda j: (0, j)),
        out_shape=jax.ShapeDtypeStruct((rows, width), BF),
        name="d_normed_two",
        cost_estimate=pl.CostEstimate(
            flops=4 * rows * width * units,
            transcendentals=0,
            bytes_accessed=4 * width * units + 4 * rows * units + 2 * rows * width,
        ),
    )(a, b, w_a, w_b)


def grad_down_kernel(a_ref, b_ref, ca_ref, cb_ref, o_ref):
    o_ref[...] = (
        dims(a_ref[...], ca_ref[...], 0, 0) + dims(b_ref[...], cb_ref[...], 0, 0)
    ).astype(BF)


def grad_down_of(act, act_other, cot, cot_other):
    rows, units = act.shape
    width = cot.shape[1]
    step = min(512, units)
    tile = pl.BlockSpec((rows, step), lambda j: (0, j))
    full = pl.BlockSpec((rows, width), lambda j: (0, 0))
    return pl.pallas_call(
        grad_down_kernel,
        grid=(units // step,),
        in_specs=[tile, tile, full, full],
        out_specs=pl.BlockSpec((step, width), lambda j: (j, 0)),
        out_shape=jax.ShapeDtypeStruct((units, width), BF),
        name="grad_down",
        cost_estimate=pl.CostEstimate(
            flops=4 * rows * width * units,
            transcendentals=0,
            bytes_accessed=4 * rows * units + 4 * rows * width + 2 * width * units,
        ),
    )(act, act_other, cot, cot_other)


def grad_in_kernel(half, n_ref, m_ref, ga_ref, gb_ref, ua_ref, ub_ref, o_ref):
    def of(a_ref, b_ref):
        o_ref[...] = (
            dims(n_ref[...], a_ref[...], 0, 0) + dims(m_ref[...], b_ref[...], 0, 0)
        ).astype(BF)

    pl.when(pl.program_id(0) < half)(lambda: of(ga_ref, gb_ref))
    pl.when(pl.program_id(0) >= half)(lambda: of(ua_ref, ub_ref))


def grad_in_of(normed, normed_other, dg, dg_other, du, du_other):
    rows, width = normed.shape
    units = dg.shape[1]
    step = min(512, units)
    half = units // step
    full = pl.BlockSpec((rows, width), lambda j: (0, 0))
    first = pl.BlockSpec((rows, step), lambda j: (0, jnp.minimum(j, half - 1)))
    second = pl.BlockSpec((rows, step), lambda j: (0, jnp.maximum(j - half, 0)))
    return pl.pallas_call(
        functools.partial(grad_in_kernel, half),
        grid=(2 * half,),
        in_specs=[full, full, first, first, second, second],
        out_specs=pl.BlockSpec((width, step), lambda j: (0, j)),
        out_shape=jax.ShapeDtypeStruct((width, 2 * units), BF),
        name="grad_gate_up",
        cost_estimate=pl.CostEstimate(
            flops=8 * rows * width * units,
            transcendentals=0,
            bytes_accessed=8 * rows * units + 4 * rows * width + 4 * width * units,
        ),
    )(normed, normed_other, dg, dg_other, du, du_other)


def norm_back(grad_normed, gain, values, inverse):
    scaled = grad_normed * gain
    return inverse * scaled - values * inverse**3 * jnp.mean(
        scaled * values, axis=-1, keepdims=True
    )


def body(
    tokens,
    attn_gain,
    w_query,
    w_key,
    w_value,
    w_out,
    ffn_gain,
    w_gate,
    w_up,
    w_down,
    doc_lengths,
    cotangent,
):
    rows, width = tokens.shape
    wide = lax.axis_size("wide")
    narrow = lax.axis_size("narrow")
    me_wide = lax.axis_index("wide")
    me = lax.axis_index("narrow")
    core = me_wide % 2
    kv_heads = w_key.shape[1] // HD
    shard = rows // narrow
    part = width // wide
    hops = wide // 4
    half_groups = [list(range(0, wide, 2)), list(range(1, wide, 2))]

    def other_core(value):
        return lax.ppermute(value, "wide", [(i, i ^ 1) for i in range(wide)])

    def chips_up(value, hop):
        return lax.ppermute(value, "wide", [(i, i + 2 * hop) for i in range(wide - 2 * hop)])

    def chips_down(value, hop):
        return lax.ppermute(value, "wide", [(i + 2 * hop, i) for i in range(wide - 2 * hop)])

    def swap(value, distance):
        return lax.ppermute(value, "narrow", [(i, i ^ distance) for i in range(narrow)])

    def rows_of(value, distance):
        return lax.dynamic_slice_in_dim(value, (me ^ distance) * shard, shard, 0)

    def sum_pieces(pieces):
        total = pieces[0].astype(F32)
        for distance in range(1, narrow):
            total = total + swap(pieces[distance], distance).astype(F32)
        return total

    def gather_near(piece):
        return [piece] + [swap(piece, distance) for distance in range(1, narrow)]

    def in_order(pieces):
        out = jnp.zeros((rows, width), pieces[0].dtype)
        for distance in range(narrow):
            out = lax.dynamic_update_slice_in_dim(
                out, pieces[distance], (me ^ distance) * shard, 0
            )
        return out

    def columns_of(value, which):
        return jnp.concatenate(
            [
                lax.dynamic_slice_in_dim(value, (2 * chip + which) * part, part, 1)
                for chip in range(wide // 2)
            ],
            axis=1,
        )

    def both_cores(value):
        return columns_of(value, core), other_core(columns_of(value, 1 - core))

    def scatter(value, dimension):
        return lax.psum_scatter(
            value,
            "wide",
            scatter_dimension=dimension,
            axis_index_groups=half_groups,
            tiled=True,
        )

    gain_one = attn_gain.astype(F32)
    gain_two = ffn_gain.astype(F32)

    base = me_wide * rows
    index = base + jnp.arange(rows, dtype=jnp.int32)
    start, valid = doc_offsets(doc_lengths, index)
    angle = jnp.asarray(inverse_frequencies(HD))[:, None] * (index - start).astype(F32)[None, :]
    cosine = jnp.cos(angle)
    sine = jnp.sin(angle)
    first_key = jnp.where(valid, start, index)
    key_tiles = []
    for hop in range(hops + 1):
        for side in range(2):
            block = ((me_wide // 2 - hop) * 2 + (core ^ side)) * rows
            key_tiles += [block + tile * KT for tile in range(rows // KT)]
    info = jnp.concatenate(
        [jnp.stack(key_tiles).astype(jnp.int32), base[None].astype(jnp.int32), first_key[::QT]]
    )
    start_row = first_key[None, :]
    valid_row = valid.astype(jnp.int32)[None, :]

    inputs = tokens.astype(F32)
    inv_one = lax.rsqrt(jnp.mean(inputs * inputs, axis=-1, keepdims=True) + NORM_EPS)
    normed = (inputs * inv_one * gain_one).astype(BF)
    keys_t = rotate_t(dims(w_key, normed, 0, 1), cosine, sine).astype(BF)
    values_t = dims(w_value, normed, 0, 1).astype(BF)
    packed = jnp.concatenate([keys_t, values_t], axis=0)
    blocks = [packed, other_core(packed)]
    for hop in range(1, hops + 1):
        near = chips_up(packed, hop)
        blocks += [near, other_core(near)]
    query_t = rotate_t(dims(w_query, normed, 0, 1), cosine, sine).astype(BF)
    o_t, mixed_t, lse = attend(info, start_row, valid_row, query_t, blocks, kv_heads)

    attn_part = dims(mixed_t, w_out, 0, 0).astype(BF)
    attn_sum = sum_pieces([rows_of(attn_part, d) for d in range(narrow)])
    inputs_mine = rows_of(tokens, 0).astype(F32)
    hidden_one = inputs_mine + attn_sum
    inv_two = lax.rsqrt(jnp.mean(hidden_one * hidden_one, axis=-1, keepdims=True) + NORM_EPS)
    normed_two_mine = (hidden_one * inv_two * gain_two).astype(BF)

    cot_near = jnp.concatenate([rows_of(cotangent, d) for d in range(narrow)], axis=0)
    cot_mine = cot_near[:shard].astype(F32)
    d_act = dims(cot_near, w_down, 1, 1)
    normed_two = jnp.concatenate(gather_near(normed_two_mine), axis=0)
    act, d_gate, d_up = ffn_forward(normed_two, d_act, w_gate, w_up)
    cot_cols, cot_cols_other = both_cores(cot_near)
    normed_two_cols, normed_two_cols_other = both_cores(normed_two)
    act_other = other_core(act)
    d_gate_other = other_core(d_gate)
    d_up_other = other_core(d_up)
    grad_down = scatter(grad_down_of(act, act_other, cot_cols, cot_cols_other), 1)

    d_norm_part = pair_nt(d_gate, d_up, w_gate, w_up)
    d_norm_two = sum_pieces([d_norm_part[d * shard : (d + 1) * shard] for d in range(narrow)])
    grad_gate_up = scatter(
        grad_in_of(
            normed_two_cols, normed_two_cols_other, d_gate, d_gate_other, d_up, d_up_other
        ),
        0,
    )
    units = w_gate.shape[1]
    grad_gate = grad_gate_up[:, :units].astype(F32)
    grad_up = grad_gate_up[:, units:].astype(F32)

    ffn_part = jnp.dot(act, w_down, preferred_element_type=F32).astype(BF)
    ffn_sum = sum_pieces([ffn_part[d * shard : (d + 1) * shard] for d in range(narrow)])
    output = in_order(gather_near((hidden_one + ffn_sum).astype(BF)))

    gain_two_part = jnp.sum(d_norm_two * hidden_one * inv_two, axis=0)
    d_hidden = cot_mine + norm_back(d_norm_two, gain_two, hidden_one, inv_two)
    d_hidden_b = in_order(gather_near(d_hidden.astype(BF)))

    d_mixed_t = jnp.where(valid[None, :], dims(w_out, d_hidden_b, 1, 1), 0.0).astype(BF)
    d_query_r, d_blocks = attend_back(
        info, start_row, query_t, d_mixed_t, o_t, lse, blocks, kv_heads
    )
    d_blocks = d_blocks.reshape(2 * (hops + 1), 2 * kv_heads * HD, rows)
    for_other = other_core(d_blocks[1::2])
    d_kv = d_blocks[0].astype(F32) + for_other[0].astype(F32)
    for hop in range(1, hops + 1):
        both = (d_blocks[2 * hop].astype(F32) + for_other[hop].astype(F32)).astype(BF)
        d_kv = d_kv + chips_down(both, hop).astype(F32)
    d_query = rotate_t(d_query_r * (1.0 / math.sqrt(HD)), cosine, -sine).astype(BF)
    d_keys = rotate_t(d_kv[: kv_heads * HD], cosine, -sine).astype(BF)
    d_values = d_kv[kv_heads * HD :].astype(BF)

    d_proj = jnp.concatenate([d_query, d_keys, d_values], axis=0)
    d_proj_other = other_core(d_proj)
    normed_cols, normed_cols_other = both_cores(normed)
    d_hidden_cols, d_hidden_cols_other = both_cores(d_hidden_b)
    mixed_other = other_core(mixed_t)
    grad_out = jnp.dot(mixed_t, d_hidden_cols, preferred_element_type=F32) + jnp.dot(
        mixed_other, d_hidden_cols_other, preferred_element_type=F32
    )
    grad_proj = jnp.dot(d_proj, normed_cols, preferred_element_type=F32) + jnp.dot(
        d_proj_other, normed_cols_other, preferred_element_type=F32
    )
    grad_out = scatter(grad_out.astype(BF), 1).astype(F32)
    grad_proj = scatter(grad_proj.astype(BF), 1).astype(F32)
    q_width = w_query.shape[1]
    k_width = w_key.shape[1]
    grad_query = grad_proj[:q_width].T
    grad_key = grad_proj[q_width : q_width + k_width].T
    grad_value = grad_proj[q_width + k_width :].T

    norm_one_part = dims(d_query, w_query, 0, 1) + dims(d_keys, w_key, 0, 1) + dims(
        d_values, w_value, 0, 1
    )
    norm_one_part = norm_one_part.astype(BF)
    d_norm_one = sum_pieces([rows_of(norm_one_part, d) for d in range(narrow)])
    inv_one_mine = rows_of(inv_one, 0)
    gain_one_part = jnp.sum(d_norm_one * inputs_mine * inv_one_mine, axis=0)
    input_mine = d_hidden + norm_back(d_norm_one, gain_one, inputs_mine, inv_one_mine)
    input_grad = in_order(gather_near(input_mine.astype(BF)))

    gains = lax.psum(jnp.stack([gain_one_part, gain_two_part]), ("wide", "narrow"))
    gains = lax.dynamic_slice_in_dim(gains, me_wide * part, part, 1)
    return (
        output,
        input_grad,
        gains[0],
        grad_query,
        grad_key,
        grad_value,
        grad_out,
        gains[1],
        grad_gate,
        grad_up,
        grad_down.astype(F32),
    )


def solution(mesh):
    in_specs = (
        P("wide", None),
        P(),
        P(None, "narrow"),
        P(None, "narrow"),
        P(None, "narrow"),
        P("narrow", None),
        P(),
        P(None, "narrow"),
        P(None, "narrow"),
        P("narrow", None),
        P(),
        P("wide", None),
    )
    out_specs = (
        P("wide", None),
        P("wide", None),
        P("wide"),
        P("wide", "narrow"),
        P("wide", "narrow"),
        P("wide", "narrow"),
        P("narrow", "wide"),
        P("wide"),
        P("wide", "narrow"),
        P("wide", "narrow"),
        P("narrow", "wide"),
    )
    return jax.shard_map(body, mesh=mesh, in_specs=in_specs, out_specs=out_specs, check_vma=False)
```

time: 1100 us -> 579 us (0.53)
  waiting for transfers between devices: 629 us -> 231 us
  matrix products: 293 us -> 38.7 us
  Pallas kernels: 0 us -> 77.3 us
  other arithmetic: 112 us -> 41.4 us
  blocking collectives: 17.5 us -> 78 us
  starting transfers between devices: 1.8 us -> 47 us
  local copies, waits for them, and re-layouts: 25.3 us -> 43.6 us
    psum x3 -> x0, waiting for transfers between devices: 278 us -> none  [the longest x1 105 us: body(): lax.psum(ffn_part.astype(jnp.bfloat16), 'narrow').astype(jnp.float32)]
    dot_general x69 -> x14, matrix products: 293 us -> 38.7 us  [the longest x9 22.6 us: dims(): lax.dot_general(left, right, (((a,), (b,)), ((), ())), preferred_element_...]
    reduce_scatter x8 -> x4, waiting for transfers between devices: 326 us -> 76.9 us  [scatter(): lax.psum_scatter(value, 'wide', scatter_dimension=dimension, axis_index_g...]
    ppermute x0 -> x41, waiting for transfers between devices: none -> 154 us  [the longest x24 125 us: swap(): lax.ppermute(value, 'narrow', [(i, i ^ distance) for i in range(narrow)])]
    psum x0 -> x1, blocking collectives: none -> 78 us  [body(): lax.psum(jnp.stack([gain_one_part, gain_two_part]), ('wide', 'narrow'))]
    pallas_call x0 -> x6, Pallas kernels: none -> 77.3 us  [the longest x1 15.9 us: ffn_forward(): pl.pallas_call(ffn_kernel, grid=(units // step,), in_specs=[pl.BlockSpec(...]
    convert_element_type x17 -> x11, other arithmetic: 73.4 us -> 14.1 us  [the longest x1 4.08 us: body(): grad_up = grad_gate_up[:, units:].astype(F32)]
    ppermute x0 -> x41, starting transfers between devices: none -> 46.7 us  [the longest x24 28.7 us: swap(): lax.ppermute(value, 'narrow', [(i, i ^ distance) for i in range(narrow)])]
  transfers between devices with their start and end apart: 12 -> 45, of which waited for: 11 -> 24; matrix products, arithmetic and copies ran while one was open for 10% -> 14% of each run, Pallas kernels for 0% -> 6%
where the time goes in v1:
time: 579 us; the launch traced here: 572 us
  waiting for transfers between devices  231 us (40%)
  blocking collectives  78 us (13%)
  Pallas kernels  77.3 us (13%)
  starting transfers between devices  47 us (8%)
  local copies, waits for them, and re-layouts  43.6 us (8%)
  other arithmetic  41.4 us (7%)
  matrix products  38.7 us (7%)
  between operations  14.8 us (3%)
    ppermute x24, waiting for transfers between devices, swap(): lax.ppermute(value, 'narrow', [(i, i ^ distance) for i in range(narrow)])  125 us
    psum x1, blocking collectives, body(): lax.psum(jnp.stack([gain_one_part, gain_two_part]), ('wide', 'narrow'))  78 us
    reduce_scatter x4, waiting for transfers between devices, scatter(): lax.psum_scatter(value, 'wide', scatter_dimension=dimension, axis_index_g...  76.9 us
    ppermute x24, starting transfers between devices, swap(): lax.ppermute(value, 'narrow', [(i, i ^ distance) for i in range(narrow)])  28.7 us
    dot_general x9, matrix products, dims(): lax.dot_general(left, right, (((a,), (b,)), ((), ())), preferred_element_...  22.6 us
    ppermute x2, waiting for transfers between devices, chips_down(): lax.ppermute(value, 'wide', [(i + 2 * hop, i) for i in range(wide - 2 * h...  17.9 us
    pallas_call x1, Pallas kernels, ffn_forward(): pl.pallas_call(ffn_kernel, grid=(units // step,), in_specs=[pl.BlockSpec(...  15.9 us
    pallas_call x1, Pallas kernels, grad_in_of(): pl.pallas_call(functools.partial(grad_in_kernel, half), grid=(2 * half,),...  14.8 us
  transfers between devices with their start and end apart: 45, of which 24 were waited for; matrix products, arithmetic and copies ran while one was open for 14% of the time, Pallas kernels for 6%

profile of v1, /device:TPU:0, one launch (start us, length us, event | category | flops | bytes accessed | tf_op | source)
XLA Modules:
  0.0 572.2 jit_solution(7346973454688839585)
XLA Ops:
  16.6 5.7 collective-permute-start.1
  36.7 10.9 %attend.1 = (f32[512,512]{1,0:T(8,128)}, bf16[512,512]{1,0:T(8,128)(2,1)}, f32[2,4,512]{2,1,0:T(4,128)}) custom-call(s32[15]{0:T(128)} %concatenate.39.info_ref, s32[1,512]{1,0:T(1,128)} %compare_select_fusion.start_ref, s32[1,512]{1,0:T(1,128)} %compare_convert_fusion.valid_ref, bf16[512,512]{1,0:T(8,128)(2,1)} %bitcast.106, bf16[256,512]{1,0:T(8,128)(2,1)} %copy-done.42, ...), custom_call_target="tpu_custom_call" | custom-call | flops 2147483648 | bytes 2097152 | tf_op jit(solution)/shard_map/attend/pallas_call | solution.py:137
  57.3 7.9 %collective-permute-done.5 = bf16[128,2048]{1,0:T(8,128)(2,1)} collective-permute-done((bf16[128,2048]{1,0:T(8,128)(2,1)}, bf16[128,2048]{1,0:T(8,128)(2,1)}, u32[]{:S(2)}, u32[]{:S(2)}) %collective-permute-start.5) | collective-permute-done | bytes 524320 | tf_op jit(solution)/shard_map/ppermute | solution.py:435
  67.4 10.1 %collective-permute-done.7 = bf16[128,2048]{1,0:T(8,128)(2,1)} collective-permute-done((bf16[128,2048]{1,0:T(8,128)(2,1)S(1)}, bf16[128,2048]{1,0:T(8,128)(2,1)}, u32[]{:S(2)}, u32[]{:S(2)}) %collective-permute-start.7) | collective-permute-done | bytes 524320 | tf_op jit(solution)/shard_map/ppermute | solution.py:435
  83.6 10.9 %fusion.38.da_ref = f32[512,2048]{1,0:T(8,128)} fusion(bf16[2048,2048]{1,0:T(8,128)(2,1)} %param.22, bf16[128,2048]{1,0:T(8,128)(2,1)S(1)} %get-tuple-element.109, bf16[128,2048]{1,0:T(8,128)(2,1)S(1)} %get-tuple-element.110, bf16[128,2048]{1,0:T(8,128)(2,1)S(1)} %get-tuple-element.108, bf16[128,2048]{1,0:T(8,128)(2,1)S(1)} %get-tuple-element.107), kind=kOutput, calls=%fused_computation.164 | convolution fusion | flops 4303355904 | bytes 14680064 | tf_op jit(solution)/shard_map/dot_general | solution.py:55
  94.8 9.2 %collective-permute-done.8 = bf16[128,2048]{1,0:T(8,128)(2,1)S(1)} collective-permute-done((bf16[128,2048]{1,0:T(8,128)(2,1)S(1)}, bf16[128,2048]{1,0:T(8,128)(2,1)S(1)}, u32[]{:S(2)}, u32[]{:S(2)}) %collective-permute-start.8) | collective-permute-done | bytes 524320 | tf_op jit(solution)/shard_map/ppermute | solution.py:435
  108.3 15.9 %gate_up.1 = (bf16[512,2048]{1,0:T(8,128)(2,1)}, bf16[512,2048]{1,0:T(8,128)(2,1)}, bf16[512,2048]{1,0:T(8,128)(2,1)}) custom-call(bf16[512,2048]{1,0:T(8,128)(2,1)} %pad_maximum_fusion.n_ref, f32[512,2048]{1,0:T(8,128)} %fusion.38.da_ref, bf16[2048,2048]{1,0:T(8,128)(2,1)} %wa_ref.1, bf16[2048,2048]{1,0:T(8,128)(2,1)} %wb_ref.1), custom_call_target="tpu_custom_call" | custom-call | flops 8589934592 | bytes 29360128 | tf_op jit(solution)/shard_map/gate_up/pallas_call | solution.py:290
  124.3 14.2 %d_normed_two.1 = bf16[512,2048]{1,0:T(8,128)(2,1)} custom-call(bf16[512,2048]{1,0:T(8,128)(2,1)} %get-tuple-element.21.a_ref.ga_ref, bf16[512,2048]{1,0:T(8,128)(2,1)} %get-tuple-element.22.b_ref.ua_ref, bf16[2048,2048]{1,0:T(8,128)(2,1)} %wa_ref.1, bf16[2048,2048]{1,0:T(8,128)(2,1)} %wb_ref.1), custom_call_target="tpu_custom_call" | custom-call | flops 8589934592 | bytes 23068672 | tf_op jit(solution)/shard_map/d_normed_two/pallas_call | solution.py:317
  143.7 11.3 %collective-permute-done.17 = bf16[128,2048]{1,0:T(8,128)(2,1)S(1)} collective-permute-done((bf16[128,2048]{1,0:T(8,128)(2,1)S(1)}, bf16[128,2048]{1,0:T(8,128)(2,1)S(1)}, u32[]{:S(2)}, u32[]{:S(2)}) %collective-permute-start.17) | collective-permute-done | bytes 524320 | tf_op jit(solution)/shard_map/ppermute | solution.py:435
  155.0 11.6 %collective-permute-done.18 = bf16[128,2048]{1,0:T(8,128)(2,1)S(1)} collective-permute-done((bf16[128,2048]{1,0:T(8,128)(2,1)S(1)}, bf16[128,2048]{1,0:T(8,128)(2,1)S(1)}, u32[]{:S(2)}, u32[]{:S(2)}) %collective-permute-start.18) | collective-permute-done | bytes 524320 | tf_op jit(solution)/shard_map/ppermute | solution.py:435
  174.7 11.1 %collective-permute-done.20 = bf16[128,2048]{1,0:T(8,128)(2,1)} collective-permute-done((bf16[128,2048]{1,0:T(8,128)(2,1)}, bf16[128,2048]{1,0:T(8,128)(2,1)}, u32[]{:S(2)}, u32[]{:S(2)}) %collective-permute-start.20) | collective-permute-done | bytes 524320 | tf_op jit(solution)/shard_map/ppermute | solution.py:435
  187.7 7.7 %collective-permute-done.21 = bf16[128,2048]{1,0:T(8,128)(2,1)} collective-permute-done((bf16[128,2048]{1,0:T(8,128)(2,1)}, bf16[128,2048]{1,0:T(8,128)(2,1)}, u32[]{:S(2)}, u32[]{:S(2)}) %collective-permute-start.21) | collective-permute-done | bytes 524320 | tf_op jit(solution)/shard_map/ppermute | solution.py:435
  206.5 13.1 %attend_back.1 = (f32[512,512]{1,0:T(8,128)}, bf16[6,2,128,512]{3,2,1,0:T(8,128)(2,1)}) custom-call(s32[15]{0:T(128)} %concatenate.39.info_ref, s32[1,512]{1,0:T(1,128)} %compare_select_fusion.start_ref, bf16[512,512]{1,0:T(8,128)(2,1)} %bitcast.107, bf16[512,512]{1,0:T(8,128)(2,1)} %fusion.4.do_ref, f32[512,512]{1,0:T(8,128)} %get-tuple-element.23.o_ref, ...), custom_call_target="tpu_custom_call" | custom-call | flops 5368709120 | bytes 4194304 | tf_op jit(solution)/shard_map/attend_back/pallas_call | solution.py:240
  234.5 11.1 %collective-permute-done.24 = bf16[256,512]{1,0:T(8,128)(2,1)} collective-permute-done((bf16[256,512]{1,0:T(8,128)(2,1)}, bf16[256,512]{1,0:T(8,128)(2,1)}, u32[]{:S(2)}, u32[]{:S(2)}) %collective-permute-start.24) | collective-permute-done | bytes 262176 | tf_op jit(solution)/shard_map/ppermute | solution.py:432
  245.6 6.8 %collective-permute-done.25 = bf16[256,512]{1,0:T(8,128)(2,1)} collective-permute-done((bf16[256,512]{1,0:T(8,128)(2,1)}, bf16[256,512]{1,0:T(8,128)(2,1)}, u32[]{:S(2)}, u32[]{:S(2)}) %collective-permute-start.25) | collective-permute-done | bytes 262176 | tf_op jit(solution)/shard_map/ppermute | solution.py:432
  266.6 8.4 %grad_down.1 = bf16[2048,1024]{1,0:T(8,128)(2,1)} custom-call(bf16[512,2048]{1,0:T(8,128)(2,1)} %get-tuple-element.20.a_ref, bf16[512,2048]{1,0:T(8,128)(2,1)} %collective-permute-done.39.b_ref, bf16[512,1024]{1,0:T(8,128)(2,1)} %pad_maximum_fusion.6.ca_ref, bf16[512,1024]{1,0:T(8,128)(2,1)} %copy-done.49), custom_call_target="tpu_custom_call" | custom-call | flops 4294967296 | bytes 10485760 | tf_op jit(solution)/shard_map/grad_down/pallas_call | solution.py:344
  284.2 14.8 %grad_gate_up.1 = bf16[1024,4096]{1,0:T(8,128)(2,1)} custom-call(bf16[512,1024]{1,0:T(8,128)(2,1)} %pad_maximum_fusion.4.n_ref, bf16[512,1024]{1,0:T(8,128)(2,1)} %copy-done.48, bf16[512,2048]{1,0:T(8,128)(2,1)} %get-tuple-element.21.a_ref.ga_ref, bf16[512,2048]{1,0:T(8,128)(2,1)} %collective-permute-done.37.gb_ref, ...), custom_call_target="tpu_custom_call" | custom-call | flops 8589934592 | bytes 18874368 | tf_op jit(solution)/shard_map/grad_gate_up/pallas_call | solution.py:377
  300.6 8.1 %convolution_convert_fusion = bf16[512,2048]{1,0:T(8,128)(2,1)S(1)} fusion(bf16[512,2048]{1,0:T(8,128)(2,1)S(1)} %copy-done.47, bf16[2048,2048]{1,0:T(8,128)(2,1)} %param.22), kind=kOutput, calls=%fused_computation.7 | convolution fusion | flops 4296015872 | bytes 12582912 | tf_op jit(solution)/shard_map/dot_general | solution.py:543
  312.3 11.3 %collective-permute-done.11 = bf16[128,2048]{1,0:T(8,128)(2,1)S(1)} collective-permute-done((bf16[128,2048]{1,0:T(8,128)(2,1)S(1)}, bf16[128,2048]{1,0:T(8,128)(2,1)S(1)}, u32[]{:S(2)}, u32[]{:S(2)}) %collective-permute-start.11) | collective-permute-done | bytes 524320 | tf_op jit(solution)/shard_map/ppermute | solution.py:435
  323.6 9.8 %collective-permute-done.12 = bf16[128,2048]{1,0:T(8,128)(2,1)S(1)} collective-permute-done((bf16[128,2048]{1,0:T(8,128)(2,1)S(1)}, bf16[128,2048]{1,0:T(8,128)(2,1)S(1)}, u32[]{:S(2)}, u32[]{:S(2)}) %collective-permute-start.12) | collective-permute-done | bytes 524320 | tf_op jit(solution)/shard_map/ppermute | solution.py:435
  358.6 5.6 collective-permute-done.26
  364.2 19.5 %collective-permute-done.27 = bf16[128,2048]{1,0:T(8,128)(2,1)S(1)} collective-permute-done((bf16[128,2048]{1,0:T(8,128)(2,1)}, bf16[128,2048]{1,0:T(8,128)(2,1)S(1)}, u32[]{:S(2)}, u32[]{:S(2)}) %collective-permute-start.27) | collective-permute-done | bytes 524320 | tf_op jit(solution)/shard_map/ppermute | solution.py:435
  395.0 78.0 %psum.7 = f32[2,2048]{1,0:T(2,128)S(1)} all-reduce(f32[2,2048]{1,0:T(2,128)S(1)} %pad_maximum_fusion.14), channel_id=1, replica_groups=mesh['wide'=8,'narrow'=4] {'wide','narrow'}, use_global_device_ids=true, to_apply=%region_8.9 | all-reduce | flops 4096 | bytes 32768 | tf_op jit(solution)/shard_map/psum | solution.py:594
  484.6 76.8 %reduce-scatter.9.cloned.1.call-done = bf16[256,4096]{1,0:T(8,128)(2,1)} async-done(((bf16[1024,4096]{1,0:T(8,128)(2,1)}), bf16[256,4096]{1,0:T(8,128)(2,1)}) %reduce-scatter.9.cloned.1.call-update) | async-done | bytes 2097168 | tf_op jit(solution)/shard_map/reduce_scatter | solution.py:470
  (281 shorter events, 167.7 us)
Async XLA Ops:
  7.2 469.0 %reduce-scatter.7.cloned.1.call-start = ((), (), s32[]{:S(2)}) async-start(), calls=%async_computation.5 | async-start | bytes 1310720 | tf_op jit(solution)/shard_map/reduce_scatter | solution.py:470
  55.2 22.4 %collective-permute-start.7 = (bf16[128,2048]{1,0:T(8,128)(2,1)S(1)}, bf16[128,2048]{1,0:T(8,128)(2,1)}, u32[]{:S(2)}, u32[]{:S(2)}) collective-permute-start(bf16[128,2048]{1,0:T(8,128)(2,1)S(1)} %get-tuple-element.112), channel_id=1, source_target_pairs={{0,3},{1,2},{2,1},{3,0},{4,7},{5,6},{6,5},{7,4},{8,11},{9,10},{10,... | collective-permute-start | bytes 1572872 | tf_op jit(solution)/shard_map/ppermute | solution.py:435
  81.5 22.5 %collective-permute-start.8 = (bf16[128,2048]{1,0:T(8,128)(2,1)S(1)}, bf16[128,2048]{1,0:T(8,128)(2,1)S(1)}, u32[]{:S(2)}, u32[]{:S(2)}) collective-permute-start(bf16[128,2048]{1,0:T(8,128)(2,1)S(1)} %multiply_convert_fusion), channel_id=1, source_target_pairs={{0,1},{1,0},{2,3},{3,2},{4,5},{5,4},{6,7},{7,6},{8,9},{9,8},{10,11... | collective-permute-start | bytes 1572872 | tf_op jit(solution)/shard_map/ppermute | solution.py:435
  82.0 24.9 %collective-permute-start.9 = (bf16[128,2048]{1,0:T(8,128)(2,1)S(1)}, bf16[128,2048]{1,0:T(8,128)(2,1)S(1)}, u32[]{:S(2)}, u32[]{:S(2)}) collective-permute-start(bf16[128,2048]{1,0:T(8,128)(2,1)S(1)} %multiply_convert_fusion), channel_id=1, source_target_pairs={{0,2},{1,3},{2,0},{3,1},{4,6},{5,7},{6,4},{7,5},{8,10},{9,11},{10,... | collective-permute-start | bytes 1572872 | tf_op jit(solution)/shard_map/ppermute | solution.py:435
  141.7 24.9 %collective-permute-start.18 = (bf16[128,2048]{1,0:T(8,128)(2,1)S(1)}, bf16[128,2048]{1,0:T(8,128)(2,1)S(1)}, u32[]{:S(2)}, u32[]{:S(2)}) collective-permute-start(bf16[128,2048]{1,0:T(8,128)(2,1)S(1)} %get-tuple-element.103), channel_id=1, source_target_pairs={{0,2},{1,3},{2,0},{3,1},{4,6},{5,7},{6,4},{7,5},{8,10},{9,11},{10,... | collective-permute-start | bytes 1572872 | tf_op jit(solution)/shard_map/ppermute | solution.py:435
  142.3 24.3 %collective-permute-start.19 = (bf16[128,2048]{1,0:T(8,128)(2,1)S(1)}, bf16[128,2048]{1,0:T(8,128)(2,1)S(1)}, u32[]{:S(2)}, u32[]{:S(2)}) collective-permute-start(bf16[128,2048]{1,0:T(8,128)(2,1)S(1)} %get-tuple-element.102), channel_id=1, source_target_pairs={{0,3},{1,2},{2,1},{3,0},{4,7},{5,6},{6,5},{7,4},{8,11},{9,10},{10,... | collective-permute-start | bytes 1572872 | tf_op jit(solution)/shard_map/ppermute | solution.py:435
  171.2 24.2 %collective-permute-start.21 = (bf16[128,2048]{1,0:T(8,128)(2,1)}, bf16[128,2048]{1,0:T(8,128)(2,1)}, u32[]{:S(2)}, u32[]{:S(2)}) collective-permute-start(bf16[128,2048]{1,0:T(8,128)(2,1)} %get-tuple-element.58), channel_id=1, source_target_pairs={{0,2},{1,3},{2,0},{3,1},{4,6},{5,7},{6,4},{7,5},{8,10},{9,11},{10,... | collective-permute-start | bytes 1572872 | tf_op jit(solution)/shard_map/ppermute | solution.py:435
  172.4 24.9 %collective-permute-start.22 = (bf16[128,2048]{1,0:T(8,128)(2,1)}, bf16[128,2048]{1,0:T(8,128)(2,1)}, u32[]{:S(2)}, u32[]{:S(2)}) collective-permute-start(bf16[128,2048]{1,0:T(8,128)(2,1)} %get-tuple-element.58), channel_id=1, source_target_pairs={{0,3},{1,2},{2,1},{3,0},{4,7},{5,6},{6,5},{7,4},{8,11},{9,10},{10,... | collective-permute-start | bytes 1572872 | tf_op jit(solution)/shard_map/ppermute | solution.py:435
  202.8 27.7 %collective-permute-start.35 = (bf16[512,1024]{1,0:T(8,128)(2,1)}, bf16[512,1024]{1,0:T(8,128)(2,1)}, u32[]{:S(2)}, u32[]{:S(2)}) collective-permute-start(bf16[512,1024]{1,0:T(8,128)(2,1)} %pad_maximum_fusion.3), channel_id=1, source_target_pairs={{0,4},{4,0},{8,12},{12,8},{16,20},{20,16},{24,28},{28,24},{1,5},{5... | collective-permute-start | bytes 3145736 | tf_op jit(solution)/shard_map/ppermute | solution.py:426
  225.7 29.4 %collective-permute-start.33 = (bf16[512,1024]{1,0:T(8,128)(2,1)}, bf16[512,1024]{1,0:T(8,128)(2,1)}, u32[]{:S(2)}, u32[]{:S(2)}) collective-permute-start(bf16[512,1024]{1,0:T(8,128)(2,1)} %pad_maximum_fusion.2), channel_id=1, source_target_pairs={{0,4},{4,0},{8,12},{12,8},{16,20},{20,16},{24,28},{28,24},{1,5},{5... | collective-permute-start | bytes 3145736 | tf_op jit(solution)/shard_map/ppermute | solution.py:426
  229.2 23.2 %collective-permute-start.25 = (bf16[256,512]{1,0:T(8,128)(2,1)}, bf16[256,512]{1,0:T(8,128)(2,1)}, u32[]{:S(2)}, u32[]{:S(2)}) collective-permute-start(bf16[256,512]{1,0:T(8,128)(2,1)} %get-tuple-element.124), channel_id=1, source_target_pairs={{16,0},{20,4},{24,8},{28,12},{17,1},{21,5},{25,9},{29,13},{18,2},{... | collective-permute-start | bytes 786440 | tf_op jit(solution)/shard_map/ppermute | solution.py:432
  234.3 243.7 %reduce-scatter.5.cloned.1.call-start = ((), (), s32[]{:S(2)}) async-start(), calls=%async_computation.4 | async-start | bytes 1966080 | tf_op jit(solution)/shard_map/reduce_scatter | solution.py:470
  259.7 221.9 %reduce-scatter.11.cloned.1.call-start = ((), (), s32[]{:S(2)}) async-start(), calls=%async_computation.7 | async-start | bytes 5242880 | tf_op jit(solution)/shard_map/reduce_scatter | solution.py:470
  275.0 286.4 %reduce-scatter.9.cloned.1.call-start = ((), (), s32[]{:S(2)}) async-start(), calls=%async_computation.6 | async-start | bytes 10485760 | tf_op jit(solution)/shard_map/reduce_scatter | solution.py:470
  308.9 24.5 %collective-permute-start.12 = (bf16[128,2048]{1,0:T(8,128)(2,1)S(1)}, bf16[128,2048]{1,0:T(8,128)(2,1)S(1)}, u32[]{:S(2)}, u32[]{:S(2)}) collective-permute-start(bf16[128,2048]{1,0:T(8,128)(2,1)S(1)} %get-tuple-element.106), channel_id=1, source_target_pairs={{0,2},{1,3},{2,0},{3,1},{4,6},{5,7},{6,4},{7,5},{8,10},{9,11},{10,... | collective-permute-start | bytes 1572872 | tf_op jit(solution)/shard_map/ppermute | solution.py:435
  310.9 24.0 %collective-permute-start.13 = (bf16[128,2048]{1,0:T(8,128)(2,1)S(1)}, bf16[128,2048]{1,0:T(8,128)(2,1)S(1)}, u32[]{:S(2)}, u32[]{:S(2)}) collective-permute-start(bf16[128,2048]{1,0:T(8,128)(2,1)S(1)} %get-tuple-element.105), channel_id=1, source_target_pairs={{0,3},{1,2},{2,1},{3,0},{4,7},{5,6},{6,5},{7,4},{8,11},{9,10},{10,... | collective-permute-start | bytes 1572872 | tf_op jit(solution)/shard_map/ppermute | solution.py:435
  338.7 18.0 %collective-permute-start.15 = (bf16[128,2048]{1,0:T(8,128)(2,1)}, bf16[128,2048]{1,0:T(8,128)(2,1)}, u32[]{:S(2)}, u32[]{:S(2)}) collective-permute-start(bf16[128,2048]{1,0:T(8,128)(2,1)} %get-tuple-element.61), channel_id=1, source_target_pairs={{0,2},{1,3},{2,0},{3,1},{4,6},{5,7},{6,4},{7,5},{8,10},{9,11},{10,... | collective-permute-start | bytes 1572872 | tf_op jit(solution)/shard_map/ppermute | solution.py:435
  346.3 17.9 %collective-permute-start.26 = (bf16[128,2048]{1,0:T(8,128)(2,1)}, bf16[128,2048]{1,0:T(8,128)(2,1)S(1)}, u32[]{:S(2)}, u32[]{:S(2)}) collective-permute-start(bf16[128,2048]{1,0:T(8,128)(2,1)} %get-tuple-element.98), channel_id=1, source_target_pairs={{0,1},{1,0},{2,3},{3,2},{4,5},{5,4},{6,7},{7,6},{8,9},{9,8},{10,11... | collective-permute-start | bytes 1572872 | tf_op jit(solution)/shard_map/ppermute | solution.py:435
  346.6 37.2 %collective-permute-start.27 = (bf16[128,2048]{1,0:T(8,128)(2,1)}, bf16[128,2048]{1,0:T(8,128)(2,1)S(1)}, u32[]{:S(2)}, u32[]{:S(2)}) collective-permute-start(bf16[128,2048]{1,0:T(8,128)(2,1)} %get-tuple-element.100), channel_id=1, source_target_pairs={{0,2},{1,3},{2,0},{3,1},{4,6},{5,7},{6,4},{7,5},{8,10},{9,11},{10,... | collective-permute-start | bytes 1572872 | tf_op jit(solution)/shard_map/ppermute | solution.py:435
  347.7 36.0 %collective-permute-start.28 = (bf16[128,2048]{1,0:T(8,128)(2,1)}, bf16[128,2048]{1,0:T(8,128)(2,1)}, u32[]{:S(2)}, u32[]{:S(2)}) collective-permute-start(bf16[128,2048]{1,0:T(8,128)(2,1)} %get-tuple-element.99), channel_id=1, source_target_pairs={{0,3},{1,2},{2,1},{3,0},{4,7},{5,6},{6,5},{7,4},{8,11},{9,10},{10,... | collective-permute-start | bytes 1572872 | tf_op jit(solution)/shard_map/ppermute | solution.py:435
  353.1 38.8 %collective-permute-start.16 = (bf16[128,2048]{1,0:T(8,128)(2,1)}, bf16[128,2048]{1,0:T(8,128)(2,1)S(1)}, u32[]{:S(2)}, u32[]{:S(2)}) collective-permute-start(bf16[128,2048]{1,0:T(8,128)(2,1)} %get-tuple-element.61), channel_id=1, source_target_pairs={{0,3},{1,2},{2,1},{3,0},{4,7},{5,6},{6,5},{7,4},{8,11},{9,10},{10,... | collective-permute-start | bytes 1572872 | tf_op jit(solution)/shard_map/ppermute | solution.py:435
  390.7 83.0 %collective-permute-start.29 = (bf16[128,2048]{1,0:T(8,128)(2,1)}, bf16[128,2048]{1,0:T(8,128)(2,1)S(1)}, u32[]{:S(2)}, u32[]{:S(2)}) collective-permute-start(bf16[128,2048]{1,0:T(8,128)(2,1)} %get-tuple-element.54), channel_id=1, source_target_pairs={{0,1},{1,0},{2,3},{3,2},{4,5},{5,4},{6,7},{7,6},{8,9},{9,8},{10,11... | collective-permute-start | bytes 1572872 | tf_op jit(solution)/shard_map/ppermute | solution.py:435
  392.7 81.8 %collective-permute-start.30 = (bf16[128,2048]{1,0:T(8,128)(2,1)}, bf16[128,2048]{1,0:T(8,128)(2,1)S(1)}, u32[]{:S(2)}, u32[]{:S(2)}) collective-permute-start(bf16[128,2048]{1,0:T(8,128)(2,1)} %get-tuple-element.54), channel_id=1, source_target_pairs={{0,2},{1,3},{2,0},{3,1},{4,6},{5,7},{6,4},{7,5},{8,10},{9,11},{10,... | collective-permute-start | bytes 1572872 | tf_op jit(solution)/shard_map/ppermute | solution.py:435
  393.5 81.8 %collective-permute-start.31 = (bf16[128,2048]{1,0:T(8,128)(2,1)}, bf16[128,2048]{1,0:T(8,128)(2,1)S(1)}, u32[]{:S(2)}, u32[]{:S(2)}) collective-permute-start(bf16[128,2048]{1,0:T(8,128)(2,1)} %get-tuple-element.54), channel_id=1, source_target_pairs={{0,3},{1,2},{2,1},{3,0},{4,7},{5,6},{6,5},{7,4},{8,11},{9,10},{10,... | collective-permute-start | bytes 1572872 | tf_op jit(solution)/shard_map/ppermute | solution.py:435
  (74 other events, 737.5 us)
Sparse Core Ops, SparseCore 0:
  234.4 64.2 reduce-scatter.6
  301.0 33.9 reduce-scatter.4
  337.4 75.7 reduce-scatter.10
  415.4 145.9 reduce-scatter.8

commit v2 on v1

v2 whole, which is shorter than its diff:
```python
import functools
import math

import jax
import jax.numpy as jnp
import numpy as np
from jax import lax
from jax.experimental import pallas as pl
from jax.experimental.pallas import tpu as pltpu
from jax.sharding import PartitionSpec as P

HD = 64
DOCS = 12
NORM_EPS = 1e-05
MASKED_SCORE = -1e30
LOG2E = math.log2(math.e)
SCALE2 = LOG2E / math.sqrt(HD)
KT = 256
HALVES = 2
BF = jnp.bfloat16
F32 = jnp.float32


def inverse_frequencies(head_size):
    frequency = 1.0 / 500000.0 ** (np.arange(0, head_size, 2) / head_size)
    wavelength = 2 * math.pi / frequency
    smoothing = (8192.0 / wavelength - 1.0) / 3.0
    scaled_freq = np.where(wavelength > 8192.0, frequency / 32.0, frequency)
    middle_band = (wavelength <= 8192.0) & (wavelength >= 2048.0)
    scaled_freq = np.where(
        middle_band, (1 - smoothing) * frequency / 32.0 + smoothing * frequency, scaled_freq
    )
    return scaled_freq.astype(np.float32)


def doc_offsets(doc_lengths, index):
    ends = jnp.cumsum(doc_lengths)
    passed = (index[None, :] >= ends[:, None]).astype(jnp.int32)
    start = jnp.sum(passed * doc_lengths[:, None], axis=0)
    valid = index < ends[DOCS - 2]
    return start, valid


def rotate_t(values, cosine, sine):
    heads = values.shape[0] // HD
    shaped = values.reshape(heads, 2, HD // 2, values.shape[1])
    first = shaped[:, 0]
    second = shaped[:, 1]
    return jnp.stack(
        [first * cosine - second * sine, second * cosine + first * sine], axis=1
    ).reshape(values.shape)


def dims(left, right, a, b):
    return lax.dot_general(left, right, (((a,), (b,)), ((), ())), preferred_element_type=F32)


def tile_active(info_ref, tiles, tile, q_tile, q_rows):
    key_base = info_ref[tile]
    q_base = info_ref[tiles] + q_tile * q_rows
    first_key = info_ref[tiles + 1 + q_tile]
    return (key_base <= q_base + q_rows - 1) & (key_base + KT > first_key), key_base, q_base


def tile_mask(key_base, q_base, start_row):
    q_rows = start_row.shape[1]
    keys = key_base + lax.broadcasted_iota(jnp.int32, (KT, q_rows), 0)
    queries = q_base + lax.broadcasted_iota(jnp.int32, (KT, q_rows), 1)
    return (keys <= queries) & (keys >= start_row)


def attend_kernel(slots, group, half, info_ref, start_ref, valid_ref, q_ref, *refs):
    k_refs = refs[:slots]
    v_refs = refs[slots : 2 * slots]
    o_ref, mixed_ref, lse_ref, keys_s, values_s, top_s, sum_s, acc_s = refs[2 * slots :]
    q_rows = q_ref.shape[1]
    per = k_refs[0].shape[1] // KT
    tiles = slots * per
    for slot in range(slots):
        for part in range(per):
            tile = slot * per + part
            cut = slice(part * KT, (part + 1) * KT)

            @pl.when(tile_active(info_ref, tiles, tile, half, q_rows)[0])
            def _(tile=tile, slot=slot, cut=cut):
                keys_s[tile] = k_refs[slot][:, cut].T
                values_s[tile] = v_refs[slot][:, cut]

    top_s[...] = jnp.full_like(top_s, MASKED_SCORE)
    sum_s[...] = jnp.zeros_like(sum_s)
    acc_s[...] = jnp.zeros_like(acc_s)
    start_row = start_ref[...]

    def step(tile, carry):
        active, key_base, q_base = tile_active(info_ref, tiles, tile, half, q_rows)

        @pl.when(active)
        def _():
            allowed = tile_mask(key_base, q_base, start_row)
            keys = keys_s[tile]
            values = values_s[tile]
            for head in range(group):
                scores = jnp.dot(
                    keys, q_ref[head * HD : (head + 1) * HD, :], preferred_element_type=F32
                )
                scores = jnp.where(allowed, scores, MASKED_SCORE)
                old = top_s[head : head + 1, :]
                new = jnp.maximum(old, jnp.max(scores, axis=0, keepdims=True))
                weight = jnp.exp2((scores - new) * SCALE2)
                decay = jnp.exp2((old - new) * SCALE2)
                top_s[head : head + 1, :] = new
                sum_s[head : head + 1, :] = sum_s[head : head + 1, :] * decay + jnp.sum(
                    weight, axis=0, keepdims=True
                )
                acc_s[head] = acc_s[head] * decay + jnp.dot(
                    values, weight.astype(BF), preferred_element_type=F32
                )

        return carry

    lax.fori_loop(0, tiles, step, 0)
    for head in range(group):
        h_cut = slice(head * HD, (head + 1) * HD)
        total = sum_s[head : head + 1, :]
        out = acc_s[head] / total
        o_ref[h_cut, :] = out
        mixed_ref[h_cut, :] = jnp.where(valid_ref[...] != 0, out, 0.0).astype(BF)
        lse_ref[0, head : head + 1, :] = top_s[head : head + 1, :] * SCALE2 + jnp.log(total) * LOG2E


def attend(half, info, start, valid, q_t, blocks, kv_heads):
    slots = len(blocks)
    heads = q_t.shape[0] // HD
    group = heads // kv_heads
    rows = q_t.shape[1]
    q_rows = rows // HALVES
    tiles = slots * (rows // KT)
    row_spec = pl.BlockSpec((1, q_rows), lambda g: (0, half))
    out_spec = pl.BlockSpec((group * HD, q_rows), lambda g: (g, 0))
    return pl.pallas_call(
        functools.partial(attend_kernel, slots, group, half),
        grid=(kv_heads,),
        in_specs=[
            pl.BlockSpec(memory_space=pltpu.SMEM),
            row_spec,
            row_spec,
            pl.BlockSpec((group * HD, q_rows), lambda g: (g, half)),
        ]
        + [pl.BlockSpec((HD, rows), lambda g: (g, 0))] * slots
        + [pl.BlockSpec((HD, rows), lambda g: (kv_heads + g, 0))] * slots,
        out_specs=[out_spec, out_spec, pl.BlockSpec((1, group, q_rows), lambda g: (g, 0, 0))],
        out_shape=[
            jax.ShapeDtypeStruct((heads * HD, q_rows), F32),
            jax.ShapeDtypeStruct((heads * HD, q_rows), BF),
            jax.ShapeDtypeStruct((kv_heads, group, q_rows), F32),
        ],
        scratch_shapes=[
            pltpu.VMEM((tiles, KT, HD), BF),
            pltpu.VMEM((tiles, HD, KT), BF),
            pltpu.VMEM((group, q_rows), F32),
            pltpu.VMEM((group, q_rows), F32),
            pltpu.VMEM((group, HD, q_rows), F32),
        ],
        name="attend",
        cost_estimate=pl.CostEstimate(
            flops=4 * heads * q_rows * rows * 4 * HD,
            transcendentals=heads * q_rows * rows * 4,
            bytes_accessed=8 * rows * heads * HD,
        ),
    )(info, start, valid, q_t, *blocks, *blocks)


def attend_back_kernel(slots, group, info_ref, start_ref, q_ref, do_ref, *refs):
    o_refs = refs[:HALVES]
    lse_refs = refs[HALVES : 2 * HALVES]
    refs = refs[2 * HALVES :]
    k_refs = refs[:slots]
    v_refs = refs[slots : 2 * slots]
    dq_ref, dkv_ref, keys_s, values_s, keys_t_s, dk_s, dv_s, q_s, do_s, dq_s, delta_s = refs[
        2 * slots :
    ]
    rows = q_ref.shape[1]
    q_rows = rows // HALVES
    per = rows // KT
    tiles = slots * per

    def any_active(tile):
        found = tile_active(info_ref, tiles, tile, 0, q_rows)[0]
        for half in range(1, HALVES):
            found = found | tile_active(info_ref, tiles, tile, half, q_rows)[0]
        return found

    for slot in range(slots):
        for part in range(per):
            tile = slot * per + part
            cut = slice(part * KT, (part + 1) * KT)

            @pl.when(any_active(tile))
            def _(tile=tile, slot=slot, cut=cut):
                keys_s[tile] = k_refs[slot][:, cut].T
                keys_t_s[tile] = k_refs[slot][:, cut]
                values_s[tile] = v_refs[slot][:, cut].T
                dk_s[tile] = jnp.zeros((KT, HD), F32)
                dv_s[tile] = jnp.zeros((KT, HD), F32)

    for half in range(HALVES):
        q_cut = slice(half * q_rows, (half + 1) * q_rows)
        for head in range(group):
            h_cut = slice(head * HD, (head + 1) * HD)
            q_s[head] = q_ref[h_cut, q_cut].T
            do_s[head] = do_ref[h_cut, q_cut].T
            delta_s[head : head + 1, :] = jnp.sum(
                do_ref[h_cut, q_cut].astype(F32) * o_refs[half][h_cut, :], axis=0, keepdims=True
            )
        dq_s[...] = jnp.zeros_like(dq_s)
        start_row = start_ref[:, q_cut]

        def step(tile, carry, half=half, q_cut=q_cut, start_row=start_row):
            active, key_base, q_base = tile_active(info_ref, tiles, tile, half, q_rows)

            @pl.when(active)
            def _():
                allowed = tile_mask(key_base, q_base, start_row)
                keys = keys_s[tile]
                values = values_s[tile]
                keys_t = keys_t_s[tile]
                dk = dk_s[tile]
                dv = dv_s[tile]
                for head in range(group):
                    h_cut = slice(head * HD, (head + 1) * HD)
                    scores = jnp.dot(keys, q_ref[h_cut, q_cut], preferred_element_type=F32)
                    scores = jnp.where(allowed, scores * SCALE2, MASKED_SCORE)
                    prob = jnp.exp2(scores - lse_refs[half][0, head : head + 1, :])
                    prob_grad = jnp.dot(values, do_ref[h_cut, q_cut], preferred_element_type=F32)
                    d_scores = (prob * (prob_grad - delta_s[head : head + 1, :])).astype(BF)
                    dv = dv + jnp.dot(prob.astype(BF), do_s[head], preferred_element_type=F32)
                    dk = dk + jnp.dot(d_scores, q_s[head], preferred_element_type=F32)
                    dq_s[head] += jnp.dot(keys_t, d_scores, preferred_element_type=F32)
                dk_s[tile] = dk
                dv_s[tile] = dv

            return carry

        lax.fori_loop(0, tiles, step, 0)
        for head in range(group):
            dq_ref[head * HD : (head + 1) * HD, q_cut] = dq_s[head]
    for slot in range(slots):
        for part in range(per):
            cut = slice(part * KT, (part + 1) * KT)
            tile = slot * per + part
            active = any_active(tile)

            @pl.when(active)
            def _(tile=tile, slot=slot, cut=cut):
                dkv_ref[slot, 0, :, cut] = (dk_s[tile].T * (1.0 / math.sqrt(HD))).astype(BF)
                dkv_ref[slot, 1, :, cut] = dv_s[tile].T.astype(BF)

            @pl.when(jnp.logical_not(active))
            def _(slot=slot, cut=cut):
                dkv_ref[slot, 0, :, cut] = jnp.zeros((HD, KT), BF)
                dkv_ref[slot, 1, :, cut] = jnp.zeros((HD, KT), BF)


def attend_back(info, start, q_t, do_t, outs, lses, blocks, kv_heads):
    slots = len(blocks)
    heads = q_t.shape[0] // HD
    group = heads // kv_heads
    rows = q_t.shape[1]
    q_rows = rows // HALVES
    tiles = slots * (rows // KT)
    row_spec = pl.BlockSpec((1, rows), lambda g: (0, 0))
    q_spec = pl.BlockSpec((group * HD, rows), lambda g: (g, 0))
    return pl.pallas_call(
        functools.partial(attend_back_kernel, slots, group),
        grid=(kv_heads,),
        in_specs=[pl.BlockSpec(memory_space=pltpu.SMEM), row_spec, q_spec, q_spec]
        + [pl.BlockSpec((group * HD, q_rows), lambda g: (g, 0))] * HALVES
        + [pl.BlockSpec((1, group, q_rows), lambda g: (g, 0, 0))] * HALVES
        + [pl.BlockSpec((HD, rows), lambda g: (g, 0))] * slots
        + [pl.BlockSpec((HD, rows), lambda g: (kv_heads + g, 0))] * slots,
        out_specs=[q_spec, pl.BlockSpec((slots, 2, HD, rows), lambda g: (0, 0, g, 0))],
        out_shape=[
            jax.ShapeDtypeStruct(q_t.shape, F32),
            jax.ShapeDtypeStruct((slots, 2, kv_heads * HD, rows), BF),
        ],
        scratch_shapes=[
            pltpu.VMEM((tiles, KT, HD), BF),
            pltpu.VMEM((tiles, KT, HD), BF),
            pltpu.VMEM((tiles, HD, KT), BF),
            pltpu.VMEM((tiles, KT, HD), F32),
            pltpu.VMEM((tiles, KT, HD), F32),
            pltpu.VMEM((group, q_rows, HD), BF),
            pltpu.VMEM((group, q_rows, HD), BF),
            pltpu.VMEM((group, HD, q_rows), F32),
            pltpu.VMEM((group, q_rows), F32),
        ],
        name="attend_back",
        cost_estimate=pl.CostEstimate(
            flops=10 * heads * rows * rows * 4 * HD,
            transcendentals=heads * rows * rows * 4,
            bytes_accessed=16 * rows * heads * HD,
        ),
    )(info, start, q_t, do_t, *outs, *lses, *blocks, *blocks)


def vmem_call(kernel, out_shape, name, *operands, smem=0):
    whole = pl.BlockSpec(memory_space=pltpu.VMEM)
    moved = sum(math.prod(o.shape) * o.dtype.itemsize for o in operands)
    return pl.pallas_call(
        kernel,
        in_specs=[pl.BlockSpec(memory_space=pltpu.SMEM)] * smem + [whole] * (len(operands) - smem),
        out_specs=jax.tree.map(lambda _: whole, out_shape),
        out_shape=out_shape,
        name=name,
        cost_estimate=pl.CostEstimate(flops=moved, transcendentals=0, bytes_accessed=2 * moved),
    )(*operands)


def rms_scale(values):
    return lax.rsqrt(jnp.mean(values * values, axis=-1, keepdims=True) + NORM_EPS)


def row_sum(refs):
    total = refs[0][...].astype(F32)
    for ref in refs[1:]:
        total = total + ref[...].astype(F32)
    return total


def rows_call(kernel, out_shape, name, ids, narrow, rowed, halves, *operands):
    rows, width = rowed.shape
    piece = rows // (HALVES * narrow)
    mine = [
        pl.BlockSpec((piece, width), lambda i, ids, h=h: (h * narrow + ids[0], 0)) for h in halves
    ]

    def spec(shape):
        return pl.BlockSpec(shape.shape, lambda i, ids: (0, 0))

    moved = sum(math.prod(o.shape) * o.dtype.itemsize for o in operands)
    return pl.pallas_call(
        kernel,
        grid_spec=pltpu.PrefetchScalarGridSpec(
            num_scalar_prefetch=1,
            grid=(1,),
            in_specs=mine + [spec(o) for o in operands],
            out_specs=[spec(o) for o in out_shape],
        ),
        out_shape=out_shape,
        name=name,
        cost_estimate=pl.CostEstimate(flops=moved, transcendentals=0, bytes_accessed=2 * moved),
    )(ids, *([rowed] * len(mine)), *operands)


def norm_two_kernel(ids_ref, x_ref, gain_ref, *refs):
    hidden_ref, normed_ref = refs[-2:]
    hidden = x_ref[...].astype(F32) + row_sum(refs[:-2])
    hidden_ref[...] = hidden
    normed_ref[...] = (hidden * rms_scale(hidden) * gain_ref[...]).astype(BF)


def norm_back(grad_normed, gain, values, inverse):
    scaled = grad_normed * gain
    return inverse * scaled - values * inverse**3 * jnp.mean(
        scaled * values, axis=-1, keepdims=True
    )


def norm_two_back_kernel(ids_ref, *refs):
    cots, hiddens = refs[:HALVES], refs[HALVES : 2 * HALVES]
    gain_ref, pieces = refs[2 * HALVES], refs[2 * HALVES + 1 : -3]
    sum_ref, low_ref, part_ref = refs[-3:]
    piece = cots[0].shape[0]
    parts = 0.0
    for half in range(HALVES):
        cut = slice(half * piece, (half + 1) * piece)
        grad = row_sum([r.at[cut, :] for r in pieces])
        hidden = hiddens[half][...]
        inverse = rms_scale(hidden)
        parts = parts + jnp.sum(grad * hidden * inverse, axis=0, keepdims=True)
        total = cots[half][...].astype(F32) + norm_back(grad, gain_ref[...], hidden, inverse)
        sum_ref[cut, :] = total
        low_ref[cut, :] = total.astype(BF)
    part_ref[...] = parts


def norm_one_back_kernel(ids_ref, *refs):
    tokens = refs[:HALVES]
    add_ref, gain_ref, pieces = refs[HALVES], refs[HALVES + 1], refs[HALVES + 2 : -2]
    low_ref, part_ref = refs[-2:]
    piece = tokens[0].shape[0]
    parts = 0.0
    for half in range(HALVES):
        cut = slice(half * piece, (half + 1) * piece)
        grad = row_sum([r.at[cut, :] for r in pieces])
        values = tokens[half][...].astype(F32)
        inverse = rms_scale(values)
        parts = parts + jnp.sum(grad * values * inverse, axis=0, keepdims=True)
        low_ref[cut, :] = (
            add_ref[cut, :] + norm_back(grad, gain_ref[...], values, inverse)
        ).astype(BF)
    part_ref[...] = parts


def place_rows(me, out_ref, refs):
    rows = out_ref.shape[0]
    half_rows = rows // HALVES
    count = len(refs)
    part = half_rows // count
    for distance, ref in enumerate(refs):
        owner = me ^ distance
        for half in range(HALVES):
            at = pl.multiple_of(half * half_rows + owner * part, part)
            out_ref[pl.ds(at, part), :] = ref[half * part : (half + 1) * part, :]


def columns_to(core, part, in_ref, own_ref, send_ref):
    for block in range(own_ref.shape[1] // part):
        cut = slice(block * part, (block + 1) * part)
        own_at = pl.multiple_of((2 * block + core) * part, part)
        send_at = pl.multiple_of((2 * block + 1 - core) * part, part)
        own_ref[:, cut] = in_ref[:, pl.ds(own_at, part)]
        send_ref[:, cut] = in_ref[:, pl.ds(send_at, part)]


def in_order_kernel(ids_ref, *refs):
    place_rows(ids_ref[0], refs[-1], refs[:-1])


def in_order(ids, pieces):
    rows = pieces[0].shape[0] * len(pieces)
    return vmem_call(
        in_order_kernel,
        jax.ShapeDtypeStruct((rows, pieces[0].shape[1]), pieces[0].dtype),
        "token_order",
        ids,
        *pieces,
        smem=1,
    )


def near_order_kernel(part, members, ids_ref, in_ref, near_ref, own_ref, send_ref):
    half_rows = in_ref.shape[0] // HALVES
    piece = half_rows // members
    for half in range(HALVES):
        for distance in range(members):
            at = half * half_rows + distance * piece
            source = pl.multiple_of(half * half_rows + (ids_ref[0] ^ distance) * piece, piece)
            near_ref[at : at + piece, :] = in_ref[pl.ds(source, piece), :]
    columns_to(ids_ref[1], part, near_ref, own_ref, send_ref)


def near_order(ids, members, value, part):
    rows, width = value.shape
    half = jax.ShapeDtypeStruct((rows, width // 2), value.dtype)
    return vmem_call(
        functools.partial(near_order_kernel, part, members),
        [jax.ShapeDtypeStruct(value.shape, value.dtype), half, half],
        "near_order",
        ids,
        value,
        smem=1,
    )


def split_columns_kernel(part, ids_ref, in_ref, own_ref, send_ref):
    columns_to(ids_ref[1], part, in_ref, own_ref, send_ref)


def split_columns(ids, value, part):
    half = jax.ShapeDtypeStruct((value.shape[0], value.shape[1] // 2), value.dtype)
    return vmem_call(
        functools.partial(split_columns_kernel, part), [half, half], "columns", ids, value, smem=1
    )


def d_mixed_kernel(part, ids_ref, valid_ref, w_ref, *refs):
    out_ref, own_ref, send_ref, full_s = refs[-4:]
    place_rows(ids_ref[0], full_s, refs[:-4])
    columns_to(ids_ref[1], part, full_s, own_ref, send_ref)
    grad = dims(w_ref[...], full_s[...], 1, 1)
    out_ref[...] = jnp.where(valid_ref[...] != 0, grad, 0.0).astype(BF)


def d_mixed_of(ids, valid, w_out, pieces, part):
    rows = pieces[0].shape[0] * len(pieces)
    inner, width = w_out.shape
    whole = pl.BlockSpec(memory_space=pltpu.VMEM)
    return pl.pallas_call(
        functools.partial(d_mixed_kernel, part),
        in_specs=[pl.BlockSpec(memory_space=pltpu.SMEM)] + [whole] * (2 + len(pieces)),
        out_specs=[whole] * 3,
        out_shape=[
            jax.ShapeDtypeStruct((inner, rows), BF),
            jax.ShapeDtypeStruct((rows, width // 2), BF),
            jax.ShapeDtypeStruct((rows, width // 2), BF),
        ],
        scratch_shapes=[pltpu.VMEM((rows, width), BF)],
        name="d_mixed",
        cost_estimate=pl.CostEstimate(
            flops=2 * rows * inner * width,
            transcendentals=0,
            bytes_accessed=2 * (rows + inner) * width + 4 * rows * width,
        ),
    )(ids, valid, w_out, *pieces)


def ffn_kernel(part, ids_ref, da_ref, wg_ref, wu_ref, *refs):
    act_ref, dg_ref, du_ref, own_ref, send_ref, full_s = refs[-6:]
    pieces = refs[:-6]
    count = pieces[0].shape[0]

    @pl.when(pl.program_id(0) == 0)
    def _():
        for distance, ref in enumerate(pieces):
            full_s[distance * count : (distance + 1) * count, :] = ref[...]
        columns_to(ids_ref[1], part, full_s, own_ref, send_ref)

    normed = full_s[...]
    gate = jnp.dot(normed, wg_ref[...], preferred_element_type=F32)
    up = jnp.dot(normed, wu_ref[...], preferred_element_type=F32)
    sig = jax.nn.sigmoid(gate)
    silu = gate * sig
    act_ref[...] = (silu * up).astype(BF)
    d_act = da_ref[...]
    dg_ref[...] = (d_act * up * sig * (1.0 + gate * (1.0 - sig))).astype(BF)
    du_ref[...] = (d_act * silu).astype(BF)


def ffn_forward(half, ids, pieces, d_act, w_gate, w_up, part):
    count, width = pieces[0].shape
    rows = count * len(pieces)
    units = w_gate.shape[1]
    step = min(512, units)
    tile = pl.BlockSpec((rows, step), lambda j: (0, j))
    weight = pl.BlockSpec((width, step), lambda j: (0, j))
    cols = pl.BlockSpec((rows, width // 2), lambda j: (0, 0))
    return pl.pallas_call(
        functools.partial(ffn_kernel, part),
        grid=(units // step,),
        in_specs=[
            pl.BlockSpec(memory_space=pltpu.SMEM),
            pl.BlockSpec((rows, step), lambda j: (half, j)),
            weight,
            weight,
        ]
        + [pl.BlockSpec((count, width), lambda j: (0, 0))] * len(pieces),
        out_specs=[tile, tile, tile, cols, cols],
        out_shape=[jax.ShapeDtypeStruct((rows, units), BF)] * 3
        + [jax.ShapeDtypeStruct((rows, width // 2), BF)] * 2,
        scratch_shapes=[pltpu.VMEM((rows, width), BF)],
        name="gate_up",
        cost_estimate=pl.CostEstimate(
            flops=4 * rows * width * units,
            transcendentals=rows * units,
            bytes_accessed=4 * width * units + 2 * rows * width + 10 * rows * units,
        ),
    )(ids, d_act, w_gate, w_up, *pieces)


def store_pieces(members, out_ref, halves):
    part = halves[0].shape[0] // members
    for half, value in enumerate(halves):
        low = value.astype(BF)
        for distance in range(members):
            at = (distance * len(halves) + half) * part
            out_ref[at : at + part, :] = low[distance * part : (distance + 1) * part, :]


def pair_nt_kernel(members, *refs):
    wa_ref, wb_ref, o_ref = refs[-3:]
    halves = len(refs[:-3]) // 2
    store_pieces(
        members,
        o_ref,
        [
            dims(refs[h][...], wa_ref[...], 1, 1) + dims(refs[halves + h][...], wb_ref[...], 1, 1)
            for h in range(halves)
        ],
    )


def pair_nt(members, a_halves, b_halves, w_a, w_b):
    half_rows, units = a_halves[0].shape
    rows = half_rows * len(a_halves)
    width = w_a.shape[0]
    step = min(512, width)
    full = pl.BlockSpec((half_rows, units), lambda j: (0, 0))
    weight = pl.BlockSpec((step, units), lambda j: (j, 0))
    return pl.pallas_call(
        functools.partial(pair_nt_kernel, members),
        grid=(width // step,),
        in_specs=[full] * (2 * len(a_halves)) + [weight, weight],
        out_specs=pl.BlockSpec((rows, step), lambda j: (0, j)),
        out_shape=jax.ShapeDtypeStruct((rows, width), BF),
        name="d_normed_two",
        cost_estimate=pl.CostEstimate(
            flops=4 * rows * width * units,
            transcendentals=0,
            bytes_accessed=4 * width * units + 4 * rows * units + 2 * rows * width,
        ),
    )(*a_halves, *b_halves, w_a, w_b)


def down_kernel(members, *refs):
    w_ref, o_ref = refs[-2:]
    store_pieces(
        members,
        o_ref,
        [jnp.dot(ref[...], w_ref[...], preferred_element_type=F32) for ref in refs[:-2]],
    )


def down_of(members, act_halves, w_down):
    half_rows, units = act_halves[0].shape
    rows = half_rows * len(act_halves)
    width = w_down.shape[1]
    step = min(512, width)
    return pl.pallas_call(
        functools.partial(down_kernel, members),
        grid=(width // step,),
        in_specs=[pl.BlockSpec((half_rows, units), lambda j: (0, 0))] * len(act_halves)
        + [pl.BlockSpec((units, step), lambda j: (0, j))],
        out_specs=pl.BlockSpec((rows, step), lambda j: (0, j)),
        out_shape=jax.ShapeDtypeStruct((rows, width), BF),
        name="ffn_down",
        cost_estimate=pl.CostEstimate(
            flops=2 * rows * width * units,
            transcendentals=0,
            bytes_accessed=2 * width * units + 2 * rows * units + 2 * rows * width,
        ),
    )(*act_halves, w_down)


def contract_groups(lefts, rights):
    total = None
    for left, right in zip(lefts, rights, strict=True):
        term = dims(left, right, 0, 0)
        total = term if total is None else total + term
    return total.astype(BF)


def grad_down_kernel(groups, *refs):
    o_ref = refs[-1]
    o_ref[...] = contract_groups(
        [r[...] for r in refs[:groups]], [r[...] for r in refs[groups : 2 * groups]]
    )


def grad_down_of(acts, cots):
    rows, units = acts[0].shape
    width = cots[0].shape[1]
    step = min(512, units)
    groups = len(acts)
    return pl.pallas_call(
        functools.partial(grad_down_kernel, groups),
        grid=(units // step,),
        in_specs=[pl.BlockSpec((rows, step), lambda j: (0, j))] * groups
        + [pl.BlockSpec((rows, width), lambda j: (0, 0))] * groups,
        out_specs=pl.BlockSpec((step, width), lambda j: (j, 0)),
        out_shape=jax.ShapeDtypeStruct((units, width), BF),
        name="grad_down",
        cost_estimate=pl.CostEstimate(
            flops=2 * groups * rows * width * units,
            transcendentals=0,
            bytes_accessed=2 * groups * rows * (units + width) + 2 * width * units,
        ),
    )(*acts, *cots)


def grad_in_kernel(groups, half, *refs):
    o_ref = refs[-1]
    lefts = refs[:groups]

    def of(rights):
        o_ref[...] = contract_groups([r[...] for r in lefts], [r[...] for r in rights])

    pl.when(pl.program_id(0) < half)(lambda: of(refs[groups : 2 * groups]))
    pl.when(pl.program_id(0) >= half)(lambda: of(refs[2 * groups : 3 * groups]))


def grad_in_of(normeds, d_gates, d_ups):
    rows, width = normeds[0].shape
    units = d_gates[0].shape[1]
    step = min(512, units)
    half = units // step
    groups = len(normeds)
    full = pl.BlockSpec((rows, width), lambda j: (0, 0))
    first = pl.BlockSpec((rows, step), lambda j: (0, jnp.minimum(j, half - 1)))
    second = pl.BlockSpec((rows, step), lambda j: (0, jnp.maximum(j - half, 0)))
    return pl.pallas_call(
        functools.partial(grad_in_kernel, groups, half),
        grid=(2 * half,),
        in_specs=[full] * groups + [first] * groups + [second] * groups,
        out_specs=pl.BlockSpec((width, step), lambda j: (0, j)),
        out_shape=jax.ShapeDtypeStruct((width, 2 * units), BF),
        name="grad_gate_up",
        cost_estimate=pl.CostEstimate(
            flops=4 * groups * rows * width * units,
            transcendentals=0,
            bytes_accessed=2 * groups * rows * (2 * units + width) + 4 * width * units,
        ),
    )(*normeds, *d_gates, *d_ups)


def after(value, *others):
    return lax.optimization_barrier((value, *others))[0]


def body(
    tokens,
    attn_gain,
    w_query,
    w_key,
    w_value,
    w_out,
    ffn_gain,
    w_gate,
    w_up,
    w_down,
    doc_lengths,
    cotangent,
):
    rows, width = tokens.shape
    wide = lax.axis_size("wide")
    narrow = lax.axis_size("narrow")
    me_wide = lax.axis_index("wide")
    me = lax.axis_index("narrow")
    core = me_wide % 2
    kv_heads = w_key.shape[1] // HD
    half_rows = rows // HALVES
    piece = half_rows // narrow
    part = width // wide
    hops = wide // 4
    units = w_gate.shape[1]
    q_width = w_query.shape[1]
    k_width = w_key.shape[1]
    chip_groups = [list(range(0, wide, 2)), list(range(1, wide, 2))]
    ids = jnp.stack([me, core]).astype(jnp.int32)

    def other_core(value):
        return lax.ppermute(value, "wide", [(i, i ^ 1) for i in range(wide)])

    def chips_up(value, hop):
        return lax.ppermute(value, "wide", [(i, i + 2 * hop) for i in range(wide - 2 * hop)])

    def chips_down(value, hop):
        return lax.ppermute(value, "wide", [(i + 2 * hop, i) for i in range(wide - 2 * hop)])

    def swap(value, distance):
        return lax.ppermute(value, "narrow", [(i, i ^ distance) for i in range(narrow)])

    def half_piece(value, half, distance):
        return lax.dynamic_slice_in_dim(
            value, half * half_rows + (me ^ distance) * piece, piece, 0
        )

    def rows_of(value, distance):
        return jnp.concatenate([half_piece(value, h, distance) for h in range(HALVES)], axis=0)

    def exchange(pieces):
        return [pieces[0]] + [swap(pieces[d], d) for d in range(1, narrow)]

    def gather_near(value):
        return [value] + [swap(value, d) for d in range(1, narrow)]

    def split_pieces(value):
        size = value.shape[0] // narrow
        return [value[d * size : (d + 1) * size] for d in range(narrow)]

    def columns_of(value, which):
        return jnp.concatenate(
            [
                lax.dynamic_slice_in_dim(value, (2 * chip + which) * part, part, 1)
                for chip in range(wide // 2)
            ],
            axis=1,
        )

    def both_cores(value):
        return columns_of(value, core), other_core(columns_of(value, 1 - core))

    def scatter(value, dimension):
        return lax.psum_scatter(
            value,
            "wide",
            scatter_dimension=dimension,
            axis_index_groups=chip_groups,
            tiled=True,
        )

    gain_one = attn_gain.astype(F32)[None, :]
    gain_two = ffn_gain.astype(F32)[None, :]

    base = me_wide * rows
    index = base + jnp.arange(rows, dtype=jnp.int32)
    start, valid = doc_offsets(doc_lengths, index)
    angle = jnp.asarray(inverse_frequencies(HD))[:, None] * (index - start).astype(F32)[None, :]
    cosine = jnp.cos(angle)
    sine = jnp.sin(angle)
    first_key = jnp.where(valid, start, index)
    key_tiles = []
    for hop in range(hops + 1):
        for side in range(2):
            block = ((me_wide // 2 - hop) * 2 + (core ^ side)) * rows
            key_tiles += [block + tile * KT for tile in range(rows // KT)]
    info = jnp.concatenate(
        [
            jnp.stack(key_tiles).astype(jnp.int32),
            base[None].astype(jnp.int32),
            first_key[::half_rows],
        ]
    )
    start_row = first_key[None, :]
    valid_row = valid.astype(jnp.int32)[None, :]

    inputs = tokens.astype(F32)
    normed = (inputs * rms_scale(inputs) * gain_one).astype(BF)
    keys_t = rotate_t(dims(w_key, normed, 0, 1), cosine, sine).astype(BF)
    values_t = dims(w_value, normed, 0, 1).astype(BF)
    packed = jnp.concatenate([keys_t, values_t], axis=0)
    blocks = [packed, other_core(packed)]
    for hop in range(1, hops + 1):
        near = chips_up(packed, hop)
        blocks += [near, other_core(near)]
    query_t = rotate_t(dims(w_query, normed, 0, 1), cosine, sine).astype(BF)

    cot_near, cot_own, cot_send = near_order(ids, narrow, cotangent, part)
    cot_other = other_core(cot_send)
    query_t, start_row, valid_row, info, cot_own = lax.optimization_barrier(
        (query_t, start_row, valid_row, info, cot_own)
    )

    outs, mixes, lses, hiddens, normed_two = [], [], [], [], []

    def out_pieces(mixed):
        attn_part = dims(mixed, w_out, 0, 0).astype(BF)
        return [
            lax.dynamic_slice_in_dim(attn_part, (me ^ d) * piece, piece, 0) for d in range(narrow)
        ]

    def norm_two(half, pieces):
        return rows_call(
            norm_two_kernel,
            [
                jax.ShapeDtypeStruct((piece, width), F32),
                jax.ShapeDtypeStruct((piece, width), BF),
            ],
            "norm_two",
            ids,
            narrow,
            tokens,
            [half],
            gain_two,
            *pieces,
        )

    received = None
    for half in range(HALVES):
        out, mixed, lse = attend(half, info, start_row, valid_row, query_t, blocks, kv_heads)
        if received is not None:
            received, mixed = lax.optimization_barrier((received, mixed))
            hidden, low = norm_two(half - 1, received)
            hiddens.append(hidden)
            normed_two.append(gather_near(low))
            mixed, low = lax.optimization_barrier((mixed, low))
        outs.append(out)
        mixes.append(mixed)
        lses.append(lse)
        pieces = out_pieces(mixed)
        query_t, cot_near, pieces = lax.optimization_barrier((query_t, cot_near, pieces))
        received = exchange(pieces)
    d_act = dims(cot_near, w_down, 1, 1)
    received, d_act = lax.optimization_barrier((received, d_act))
    hidden, low = norm_two(HALVES - 1, received)
    hiddens.append(hidden)
    d_act, low = lax.optimization_barrier((d_act, low))
    normed_two.append(gather_near(low))

    acts, d_gates, d_ups, n_owns, n_sends = [], [], [], [], []
    for half in range(HALVES):
        act, d_gate, d_up, own, send = ffn_forward(
            half, ids, normed_two[half], d_act, w_gate, w_up, part
        )
        acts.append(act)
        d_gates.append(d_gate)
        d_ups.append(d_up)
        n_owns.append(own)
        n_sends.append(send)
    cots = [c[h * half_rows : (h + 1) * half_rows] for c in (cot_own, cot_other) for h in range(HALVES)]
    acts_all = acts + [other_core(a) for a in acts]
    d_gates_all = d_gates + [other_core(a) for a in d_gates]
    d_ups_all = d_ups + [other_core(a) for a in d_ups]
    n_all = n_owns + [other_core(a) for a in n_sends]

    normed_own, normed_send = split_columns(ids, normed, part)
    acts_all, normed_own, d_gates = lax.optimization_barrier((acts_all, normed_own, d_gates))
    grad_down = grad_down_of(acts_all, cots)
    d_gates_then, _ = lax.optimization_barrier((d_gates, grad_down))
    d_norm_part = pair_nt(narrow, d_gates_then, d_ups, w_gate, w_up)
    n_all, d_norm_part = lax.optimization_barrier((n_all, d_norm_part))
    d_norm_pieces = exchange(split_pieces(d_norm_part))
    grad_gate_up = grad_in_of(n_all, d_gates_all, d_ups_all)
    d_norm_pieces, _ = lax.optimization_barrier((d_norm_pieces, grad_gate_up))
    grad_down = scatter(grad_down, 1)

    shard = HALVES * piece
    d_hidden, d_hidden_b, gain_two_part = rows_call(
        norm_two_back_kernel,
        [
            jax.ShapeDtypeStruct((shard, width), F32),
            jax.ShapeDtypeStruct((shard, width), BF),
            jax.ShapeDtypeStruct((1, width), F32),
        ],
        "norm_two_back",
        ids,
        narrow,
        cotangent,
        range(HALVES),
        *hiddens,
        gain_two,
        *d_norm_pieces,
    )
    d_hidden_pieces = gather_near(d_hidden_b)
    ffn_part = down_of(narrow, acts, w_down)
    d_hidden_pieces, ffn_part = lax.optimization_barrier((d_hidden_pieces, ffn_part))
    grad_gate_up = scatter(grad_gate_up, 0)
    ffn_pieces = exchange(split_pieces(ffn_part))

    d_mixed_t, dh_own, dh_send = d_mixed_of(ids, valid_row, w_out, d_hidden_pieces, part)
    d_query_r, d_blocks = attend_back(
        info, start_row, query_t, d_mixed_t, outs, lses, blocks, kv_heads
    )
    d_blocks = d_blocks.reshape(2 * (hops + 1), 2 * k_width, rows)
    for_other = other_core(d_blocks[1::2])
    d_kv = d_blocks[0].astype(F32) + for_other[0].astype(F32)
    down = []
    for hop in range(1, hops + 1):
        both = (d_blocks[2 * hop].astype(F32) + for_other[hop].astype(F32)).astype(BF)
        down.append(chips_down(both, hop))
    d_query = rotate_t(d_query_r * (1.0 / math.sqrt(HD)), cosine, -sine).astype(BF)

    ffn_pieces, d_query = lax.optimization_barrier((ffn_pieces, d_query))
    ffn_sum = ffn_pieces[0].astype(F32)
    for other in ffn_pieces[1:]:
        ffn_sum = ffn_sum + other.astype(F32)
    output_pieces = gather_near((jnp.concatenate(hiddens, axis=0) + ffn_sum).astype(BF))
    normed_other = other_core(normed_send)
    dh_other = other_core(dh_send)
    mixed_others = [other_core(m) for m in mixes]
    d_query_other = other_core(d_query)
    grad_out = None
    for half in range(HALVES):
        cut = slice(half * half_rows, (half + 1) * half_rows)
        term = jnp.dot(mixes[half], dh_own[cut], preferred_element_type=F32) + jnp.dot(
            mixed_others[half], dh_other[cut], preferred_element_type=F32
        )
        grad_out = term if grad_out is None else grad_out + term
    grad_query = jnp.dot(d_query, normed_own, preferred_element_type=F32) + jnp.dot(
        d_query_other, normed_other, preferred_element_type=F32
    )
    grad_out, grad_query = grad_out.astype(BF), grad_query.astype(BF)

    down, grad_out, grad_query, grad_down = lax.optimization_barrier(
        (down, grad_out, grad_query, grad_down)
    )
    for value in down:
        d_kv = d_kv + value.astype(F32)
    d_keys = rotate_t(d_kv[:k_width], cosine, -sine).astype(BF)
    d_values = d_kv[k_width:].astype(BF)
    norm_one_part = (
        dims(d_query, w_query, 0, 1) + dims(d_keys, w_key, 0, 1) + dims(d_values, w_value, 0, 1)
    ).astype(BF)
    norm_one_pieces = exchange([rows_of(norm_one_part, d) for d in range(narrow)])
    d_pair = jnp.concatenate([d_keys, d_values], axis=0)
    d_pair_other = other_core(d_pair)
    grad_pair = jnp.dot(d_pair, normed_own, preferred_element_type=F32) + jnp.dot(
        d_pair_other, normed_other, preferred_element_type=F32
    )
    grad_pair = grad_pair.astype(BF)
    output = in_order(ids, output_pieces)

    input_mine, gain_one_part = rows_call(
        norm_one_back_kernel,
        [jax.ShapeDtypeStruct((shard, width), BF), jax.ShapeDtypeStruct((1, width), F32)],
        "norm_one_back",
        ids,
        narrow,
        tokens,
        range(HALVES),
        d_hidden,
        gain_one,
        *norm_one_pieces,
    )
    input_pieces = gather_near(input_mine)
    gains = jnp.concatenate([gain_one_part, gain_two_part], axis=0)
    gains = sum(gather_near(gains)[1:], gains)
    gains_own, gains_other = both_cores(gains)
    gain_rows = jnp.pad((gains_own + gains_other).astype(BF), ((0, 14), (0, 0)))
    grads = jnp.concatenate([grad_out, grad_query, grad_pair, gain_rows], axis=0)
    grads, grad_gate_up = lax.optimization_barrier((grads, grad_gate_up))
    grads = scatter(grads, 1)
    grad_gate = grad_gate_up[:, :units].astype(F32)
    grad_up = grad_gate_up[:, units:].astype(F32)
    grad_down = grad_down.astype(F32)
    grads, grad_gate, grad_up, grad_down = lax.optimization_barrier(
        (grads, grad_gate, grad_up, grad_down)
    )
    grads = grads.astype(F32)
    input_grad = in_order(ids, input_pieces)
    cuts = np.cumsum([0, w_out.shape[0], q_width, k_width, k_width])
    return (
        output,
        input_grad,
        grads[cuts[4]],
        grads[cuts[1] : cuts[2]].T,
        grads[cuts[2] : cuts[3]].T,
        grads[cuts[3] : cuts[4]].T,
        grads[: cuts[1]],
        grads[cuts[4] + 1],
        grad_gate,
        grad_up,
        grad_down,
    )


def solution(mesh):
    in_specs = (
        P("wide", None),
        P(),
        P(None, "narrow"),
        P(None, "narrow"),
        P(None, "narrow"),
        P("narrow", None),
        P(),
        P(None, "narrow"),
        P(None, "narrow"),
        P("narrow", None),
        P(),
        P("wide", None),
    )
    out_specs = (
        P("wide", None),
        P("wide", None),
        P("wide"),
        P("wide", "narrow"),
        P("wide", "narrow"),
        P("wide", "narrow"),
        P("narrow", "wide"),
        P("wide"),
        P("wide", "narrow"),
        P("wide", "narrow"),
        P("narrow", "wide"),
    )
    return jax.shard_map(body, mesh=mesh, in_specs=in_specs, out_specs=out_specs, check_vma=False)
```

time: 579 us -> 484 us (0.84); the launches traced: 572 us -> 486 us
  blocking collectives: 78 us -> 0 us
  Pallas kernels: 77.3 us -> 127 us
  waiting for transfers between devices: 231 us -> 198 us
  local copies, waits for them, and re-layouts: 43.6 us -> 27.3 us
  starting transfers between devices: 47 us -> 61.3 us
  other arithmetic: 41.4 us -> 27.2 us
  matrix products: 38.7 us -> 29.8 us
    psum x1 -> x0, blocking collectives: 78 us -> none  [body(): lax.psum(jnp.stack([gain_one_part, gain_two_part]), ('wide', 'narrow'))]
    reduce_scatter x4 -> x3, waiting for transfers between devices: 76.9 us -> 12.2 us  [scatter(): lax.psum_scatter(value, 'wide', scatter_dimension=dimension, axis_index_g...]
    ppermute x2, waiting for transfers between devices: 17.9 us -> 72.9 us  [chips_down(): lax.ppermute(value, 'wide', [(i + 2 * hop, i) for i in range(wide - 2 * h...]
    pallas_call x5 -> x17, Pallas kernels: 64.2 us -> 116 us  [the longest x2 23.3 us: ffn_forward(): pl.pallas_call(functools.partial(ffn_kernel, part), grid=(units // step,)...]
    ppermute x24 -> x33, waiting for transfers between devices: 125 us -> 108 us  [swap(): lax.ppermute(value, 'narrow', [(i, i ^ distance) for i in range(narrow)])]
    ppermute x24 -> x33, starting transfers between devices: 28.7 us -> 41.5 us  [swap(): lax.ppermute(value, 'narrow', [(i, i ^ distance) for i in range(narrow)])]
    dynamic_update_slice x9 -> x0, local copies, waits for them, and re-layouts: 12.8 us -> none  [in_order(): lax.dynamic_update_slice_in_dim(out, pieces[distance], (me ^ distance) *...]
    slice x6 -> x9, local copies, waits for them, and re-layouts: 2.55 us -> 11.9 us  [the longest x2 5.43 us: split_pieces(): return [value[d * size:(d + 1) * size] for d in range(narrow)]]
  transfers between devices with their start and end apart: 45 -> 60, of which waited for: 24 -> 25; matrix products, arithmetic and copies ran while one was open for 14% -> 11% of each run, Pallas kernels for 6% -> 23%
where the time goes in v2:
time: 484 us; the launch traced here: 486 us
  waiting for transfers between devices  198 us (41%)
  Pallas kernels  127 us (26%)
  starting transfers between devices  61.3 us (13%)
  matrix products  29.8 us (6%)
  local copies, waits for them, and re-layouts  27.3 us (6%)
  other arithmetic  27.2 us (6%)
  between operations  14.8 us (3%)
    ppermute x33, waiting for transfers between devices, swap(): lax.ppermute(value, 'narrow', [(i, i ^ distance) for i in range(narrow)])  108 us
    ppermute x2, waiting for transfers between devices, chips_down(): lax.ppermute(value, 'wide', [(i + 2 * hop, i) for i in range(wide - 2 * h...  72.9 us
    ppermute x33, starting transfers between devices, swap(): lax.ppermute(value, 'narrow', [(i, i ^ distance) for i in range(narrow)])  41.5 us
    pallas_call x2, Pallas kernels, ffn_forward(): pl.pallas_call(functools.partial(ffn_kernel, part), grid=(units // step,)...  23.3 us
    dot_general x9, matrix products, dims(): lax.dot_general(left, right, (((a,), (b,)), ((), ())), preferred_element_...  21.3 us
    pallas_call x4, Pallas kernels, rows_call(): pl.pallas_call(kernel, grid_spec=pltpu.PrefetchScalarGridSpec(num_scalar_...  15.4 us
    pallas_call x1, Pallas kernels, grad_in_of(): pl.pallas_call(functools.partial(grad_in_kernel, groups, half), grid=(2 *...  14.8 us
    pallas_call x1, Pallas kernels, pair_nt(): pl.pallas_call(functools.partial(pair_nt_kernel, members), grid=(width //...  13.7 us
  transfers between devices with their start and end apart: 60, of which 25 were waited for; matrix products, arithmetic and copies ran while one was open for 11% of the time, Pallas kernels for 23%

profile of v2, /device:TPU:0, one launch (start us, length us, event | category | flops | bytes accessed | tf_op | source)
XLA Modules:
  0.0 485.5 jit_solution(5174468607447215256)
XLA Ops:
  16.6 6.0 %collective-permute-start.3 = (bf16[256,512]{1,0:T(8,128)(2,1)S(1)}, bf16[256,512]{1,0:T(8,128)(2,1)S(1)}, u32[]{:S(2)}, u32[]{:S(2)}) collective-permute-start(bf16[256,512]{1,0:T(8,128)(2,1)S(1)} %pad_maximum_fusion.6.refs_0_.refs_6_.refs_4_.refs_10_), channel_id=1, source_target_pairs={{0,16},{4,20},{8,24},{12,28},{1,17},{5,21},{9,25},{13,29},{2,18},{... | collective-permute-start | bytes 786440 | tf_op jit(solution)/shard_map/ppermute | solution.py:745
  41.7 5.4 %attend.2 = (f32[512,256]{1,0:T(8,128)}, bf16[512,256]{1,0:T(8,128)(2,1)}, f32[2,4,256]{2,1,0:T(4,128)}) custom-call(s32[15]{0:T(128)} %concatenate.36.info_ref, s32[1,512]{1,0:T(1,128)} %compare_select_fusion.start_ref, s32[1,512]{1,0:T(1,128)} %compare_convert_fusion.valid_ref, bf16[512,512]{1,0:T(8,128)(2,1)} %bitcast.107, bf16[256,512]{1,0:T(8,128)(2,1)} %copy-done.33, ...), custom_call_target="tpu_custom_call" | custom-call | flops 1073741824 | bytes 2097152 | tf_op jit(solution)/shard_map/attend/pallas_call | solution.py:140
  54.4 7.7 %attend.3 = (f32[512,256]{1,0:T(8,128)}, bf16[512,256]{1,0:T(8,128)(2,1)}, f32[2,4,256]{2,1,0:T(4,128)}) custom-call(s32[15]{0:T(128)} %concatenate.36.info_ref, s32[1,512]{1,0:T(1,128)} %compare_select_fusion.start_ref, s32[1,512]{1,0:T(1,128)} %compare_convert_fusion.valid_ref, bf16[512,512]{1,0:T(8,128)(2,1)} %bitcast.108, bf16[256,512]{1,0:T(8,128)(2,1)} %copy-done.33, ...), custom_call_target="tpu_custom_call" | custom-call | flops 1073741824 | bytes 2097152 | tf_op jit(solution)/shard_map/attend/pallas_call | solution.py:140
  80.4 9.4 %fusion.31.da_ref = f32[512,2048]{1,0:T(8,128)} fusion(bf16[512,2048]{1,0:T(8,128)(2,1)S(1)} %copy-done.45, bf16[2048,2048]{1,0:T(8,128)(2,1)} %refs_2_.1), kind=kOutput, calls=%fused_computation.112 | convolution fusion | flops 4294967296 | bytes 14680064 | tf_op jit(solution)/shard_map/dot_general | solution.py:55
  89.8 7.2 %collective-permute-done.9.refs_2_ = bf16[64,2048]{1,0:T(8,128)(2,1)S(1)} collective-permute-done((bf16[64,2048]{1,0:T(8,128)(2,1)S(1)}, bf16[64,2048]{1,0:T(8,128)(2,1)S(1)}, u32[]{:S(2)}, u32[]{:S(2)}) %collective-permute-start.9) | collective-permute-done | bytes 262176 | tf_op jit(solution)/shard_map/ppermute | solution.py:751
  106.4 11.7 %gate_up.2 = (bf16[256,2048]{1,0:T(8,128)(2,1)}, bf16[256,2048]{1,0:T(8,128)(2,1)}, bf16[256,2048]{1,0:T(8,128)(2,1)}, bf16[256,1024]{1,0:T(8,128)(2,1)}, bf16[256,1024]{1,0:T(8,128)(2,1)}) custom-call(s32[2]{0:T(128)} %pad_add_fusion.ids_ref, f32[512,2048]{1,0:T(8,128)} %fusion.31.da_ref, bf16[2048,2048]{1,0:T(8,128)(2,1)} %refs_4_.1, ...), custom_call_target="tpu_custom_call" | custom-call | flops 4294967296 | bytes 23068672 | tf_op jit(solution)/shard_map/gate_up/pallas_call | solution.py:538
  118.2 11.6 %gate_up.3 = (bf16[256,2048]{1,0:T(8,128)(2,1)}, bf16[256,2048]{1,0:T(8,128)(2,1)}, bf16[256,2048]{1,0:T(8,128)(2,1)}, bf16[256,1024]{1,0:T(8,128)(2,1)}, bf16[256,1024]{1,0:T(8,128)(2,1)}) custom-call(s32[2]{0:T(128)} %pad_add_fusion.ids_ref, f32[512,2048]{1,0:T(8,128)} %fusion.31.da_ref, bf16[2048,2048]{1,0:T(8,128)(2,1)} %refs_4_.1, ...), custom_call_target="tpu_custom_call" | custom-call | flops 4294967296 | bytes 23068672 | tf_op jit(solution)/shard_map/gate_up/pallas_call | solution.py:538
  136.9 8.4 %grad_down.1 = bf16[2048,1024]{1,0:T(8,128)(2,1)} custom-call(bf16[256,2048]{1,0:T(8,128)(2,1)} %get-tuple-element.162.refs_0_, bf16[256,2048]{1,0:T(8,128)(2,1)} %get-tuple-element.163.refs_1_, bf16[256,2048]{1,0:T(8,128)(2,1)} %collective-permute-done.19.refs_2_, bf16[256,2048]{1,0:T(8,128)(2,1)} %collective-permute-done.20.refs_3_, ...), custom_call_target="tpu_custom_call" | custom-call | flops 4294967296 | bytes 10485760 | tf_op jit(solution)/shard_map/grad_down/pallas_call | solution.py:655
  148.3 13.7 %d_normed_two.1 = bf16[512,2048]{1,0:T(8,128)(2,1)} custom-call(bf16[256,2048]{1,0:T(8,128)(2,1)} %get-tuple-element.168.refs_0_.refs_4_, bf16[256,2048]{1,0:T(8,128)(2,1)} %get-tuple-element.169.refs_1_.refs_5_, bf16[256,2048]{1,0:T(8,128)(2,1)} %get-tuple-element.170.refs_2_.refs_8_, bf16[256,2048]{1,0:T(8,128)(2,1)} %get-tuple-element.171.refs_3_.refs_9_, ...), custom_call_target="tpu_custom_call" | custom-call | flops 8589934592 | bytes 23068672 | tf_op jit(solution)/shard_map/d_normed_two/pallas_call | solution.py:590
  162.1 14.8 %grad_gate_up.1 = bf16[1024,4096]{1,0:T(8,128)(2,1)} custom-call(bf16[256,1024]{1,0:T(8,128)(2,1)} %get-tuple-element.173.refs_0_, bf16[256,1024]{1,0:T(8,128)(2,1)} %get-tuple-element.174.refs_1_, bf16[256,1024]{1,0:T(8,128)(2,1)} %collective-permute-done.17.refs_2_, bf16[256,1024]{1,0:T(8,128)(2,1)} %collective-permute-done.18.refs_3_, ...), custom_call_target="tpu_custom_call" | custom-call | flops 8589934592 | bytes 18874368 | tf_op jit(solution)/shard_map/grad_gate_up/pallas_call | solution.py:691
  182.9 12.2 %collective-permute-done.24.refs_8_ = bf16[128,2048]{1,0:T(8,128)(2,1)S(1)} collective-permute-done((bf16[128,2048]{1,0:T(8,128)(2,1)S(1)}, bf16[128,2048]{1,0:T(8,128)(2,1)S(1)}, u32[]{:S(2)}, u32[]{:S(2)}) %collective-permute-start.24) | collective-permute-done | bytes 524320 | tf_op jit(solution)/shard_map/ppermute | solution.py:751
  195.1 10.6 %collective-permute-done.23.refs_7_ = bf16[128,2048]{1,0:T(8,128)(2,1)S(1)} collective-permute-done((bf16[128,2048]{1,0:T(8,128)(2,1)S(1)}, bf16[128,2048]{1,0:T(8,128)(2,1)S(1)}, u32[]{:S(2)}, u32[]{:S(2)}) %collective-permute-start.23) | collective-permute-done | bytes 524320 | tf_op jit(solution)/shard_map/ppermute | solution.py:751
  214.7 8.7 %ffn_down.1 = bf16[512,2048]{1,0:T(8,128)(2,1)} custom-call(bf16[256,2048]{1,0:T(8,128)(2,1)} %get-tuple-element.162.refs_0_, bf16[256,2048]{1,0:T(8,128)(2,1)} %get-tuple-element.163.refs_1_, bf16[2048,2048]{1,0:T(8,128)(2,1)} %refs_2_.1), custom_call_target="tpu_custom_call" | custom-call | flops 4294967296 | bytes 12582912 | tf_op jit(solution)/shard_map/ffn_down/pallas_call | solution.py:619
  227.1 10.4 %collective-permute-done.30.refs_2_ = bf16[128,2048]{1,0:T(8,128)(2,1)S(1)} collective-permute-done((bf16[128,2048]{1,0:T(8,128)(2,1)}, bf16[128,2048]{1,0:T(8,128)(2,1)S(1)}, u32[]{:S(2)}, u32[]{:S(2)}) %collective-permute-start.30) | collective-permute-done | bytes 524320 | tf_op jit(solution)/shard_map/ppermute | solution.py:751
  244.2 5.2 %d_mixed.1 = (bf16[512,512]{1,0:T(8,128)(2,1)}, bf16[512,1024]{1,0:T(8,128)(2,1)}, bf16[512,1024]{1,0:T(8,128)(2,1)}) custom-call(s32[2]{0:T(128)} %pad_add_fusion.ids_ref, s32[1,512]{1,0:T(1,128)} %compare_convert_fusion.valid_ref, bf16[512,2048]{1,0:T(8,128)(2,1)} %w_ref.1, bf16[128,2048]{1,0:T(8,128)(2,1)} %get-tuple-element.184.refs_0_, ...), custom_call_target="tpu_custom_call" | custom-call | flops 1073741824 | bytes 8388608 | tf_op jit(solution)/shard_map/d_mixed/pallas_call | solution.py:489
  249.3 11.7 %attend_back.1 = (f32[512,512]{1,0:T(8,128)}, bf16[6,2,128,512]{3,2,1,0:T(8,128)(2,1)}) custom-call(s32[15]{0:T(128)} %concatenate.36.info_ref, s32[1,512]{1,0:T(1,128)} %compare_select_fusion.start_ref, bf16[512,512]{1,0:T(8,128)(2,1)} %bitcast.109, bf16[512,512]{1,0:T(8,128)(2,1)} %get-tuple-element.188.do_ref, f32[512,256]{1,0:T(8,128)} %get-tuple-element.189.refs_0_, ...), custom_call_target="tpu_custom_call" | custom-call | flops 5368709120 | bytes 4194304 | tf_op jit(solution)/shard_map/attend_back/pallas_call | solution.py:273
  278.0 72.9 %collective-permute-done.40 = bf16[256,512]{1,0:T(8,128)(2,1)S(1)} collective-permute-done((bf16[256,512]{1,0:T(8,128)(2,1)S(1)}, bf16[256,512]{1,0:T(8,128)(2,1)S(1)}, u32[]{:S(2)}, u32[]{:S(2)}) %collective-permute-start.40) | collective-permute-done | bytes 262176 | tf_op jit(solution)/shard_map/ppermute | solution.py:748
  366.2 8.9 %collective-permute-done.46.refs_5_ = bf16[128,2048]{1,0:T(8,128)(2,1)} collective-permute-done((bf16[128,2048]{1,0:T(8,128)(2,1)}, bf16[128,2048]{1,0:T(8,128)(2,1)}, u32[]{:S(2)}, u32[]{:S(2)}) %collective-permute-start.46) | collective-permute-done | bytes 524320 | tf_op jit(solution)/shard_map/ppermute | solution.py:751
  375.1 13.1 %collective-permute-done.47.refs_6_ = bf16[128,2048]{1,0:T(8,128)(2,1)} collective-permute-done((bf16[128,2048]{1,0:T(8,128)(2,1)}, bf16[128,2048]{1,0:T(8,128)(2,1)}, u32[]{:S(2)}, u32[]{:S(2)}) %collective-permute-start.47) | collective-permute-done | bytes 524320 | tf_op jit(solution)/shard_map/ppermute | solution.py:751
  402.4 9.2 %reduce-scatter.6.cloned.1.call-done = bf16[256,4096]{1,0:T(8,128)(2,1)} async-done(((bf16[1024,4096]{1,0:T(8,128)(2,1)}), bf16[256,4096]{1,0:T(8,128)(2,1)}) %reduce-scatter.6.cloned.1.call-update) | async-done | bytes 2097168 | tf_op jit(solution)/shard_map/reduce_scatter | solution.py:784
  420.0 9.4 %collective-permute-done.37.refs_3_ = bf16[128,2048]{1,0:T(8,128)(2,1)S(1)} collective-permute-done((bf16[128,2048]{1,0:T(8,128)(2,1)S(1)}, bf16[128,2048]{1,0:T(8,128)(2,1)S(1)}, u32[]{:S(2)}, u32[]{:S(2)}) %collective-permute-start.37) | collective-permute-done | bytes 524320 | tf_op jit(solution)/shard_map/ppermute | solution.py:751
  430.9 9.8 %collective-permute-done.36.refs_2_ = bf16[128,2048]{1,0:T(8,128)(2,1)S(1)} collective-permute-done((bf16[128,2048]{1,0:T(8,128)(2,1)S(1)}, bf16[128,2048]{1,0:T(8,128)(2,1)S(1)}, u32[]{:S(2)}, u32[]{:S(2)}) %collective-permute-start.36) | collective-permute-done | bytes 524320 | tf_op jit(solution)/shard_map/ppermute | solution.py:751
  446.0 6.1 %collective-permute-done.51.refs_3_ = bf16[128,2048]{1,0:T(8,128)(2,1)} collective-permute-done((bf16[128,2048]{1,0:T(8,128)(2,1)}, bf16[128,2048]{1,0:T(8,128)(2,1)}, u32[]{:S(2)}, u32[]{:S(2)}) %collective-permute-start.51) | collective-permute-done | bytes 524320 | tf_op jit(solution)/shard_map/ppermute | solution.py:751
  452.0 9.8 %collective-permute-done.50.refs_2_ = bf16[128,2048]{1,0:T(8,128)(2,1)} collective-permute-done((bf16[128,2048]{1,0:T(8,128)(2,1)}, bf16[128,2048]{1,0:T(8,128)(2,1)}, u32[]{:S(2)}, u32[]{:S(2)}) %collective-permute-start.50) | collective-permute-done | bytes 524320 | tf_op jit(solution)/shard_map/ppermute | solution.py:751
  (297 shorter events, 176.7 us)
Async XLA Ops:
  7.2 343.7 %reduce-scatter.4.cloned.1.call-start = ((), (), s32[]{:S(2)}) async-start(), calls=%async_computation.3 | async-start | bytes 5242880 | tf_op jit(solution)/shard_map/reduce_scatter | solution.py:784
  71.9 32.6 %collective-permute-start.13 = (bf16[64,2048]{1,0:T(8,128)(2,1)S(1)}, bf16[64,2048]{1,0:T(8,128)(2,1)S(1)}, u32[]{:S(2)}, u32[]{:S(2)}) collective-permute-start(bf16[64,2048]{1,0:T(8,128)(2,1)S(1)} %copy-done.29), channel_id=1, source_target_pairs={{0,3},{1,2},{2,1},{3,0},{4,7},{5,6},{6,5},{7,4},{8,11},{9,10},{10,... | collective-permute-start | bytes 786440 | tf_op jit(solution)/shard_map/ppermute | solution.py:751
  72.5 32.6 %collective-permute-start.12 = (bf16[64,2048]{1,0:T(8,128)(2,1)S(1)}, bf16[64,2048]{1,0:T(8,128)(2,1)S(1)}, u32[]{:S(2)}, u32[]{:S(2)}) collective-permute-start(bf16[64,2048]{1,0:T(8,128)(2,1)S(1)} %copy-done.29), channel_id=1, source_target_pairs={{0,2},{1,3},{2,0},{3,1},{4,6},{5,7},{6,4},{7,5},{8,10},{9,11},{10,... | collective-permute-start | bytes 786440 | tf_op jit(solution)/shard_map/ppermute | solution.py:751
  74.0 31.6 %collective-permute-start.11 = (bf16[64,2048]{1,0:T(8,128)(2,1)S(1)}, bf16[64,2048]{1,0:T(8,128)(2,1)S(1)}, u32[]{:S(2)}, u32[]{:S(2)}) collective-permute-start(bf16[64,2048]{1,0:T(8,128)(2,1)S(1)} %copy-done.29), channel_id=1, source_target_pairs={{0,1},{1,0},{2,3},{3,2},{4,5},{5,4},{6,7},{7,6},{8,9},{9,8},{10,11... | collective-permute-start | bytes 786440 | tf_op jit(solution)/shard_map/ppermute | solution.py:751
  97.7 37.0 %collective-permute-start.21 = (bf16[512,1024]{1,0:T(8,128)(2,1)}, bf16[512,1024]{1,0:T(8,128)(2,1)}, u32[]{:S(2)}, u32[]{:S(2)}) collective-permute-start(bf16[512,1024]{1,0:T(8,128)(2,1)} %get-tuple-element.167), channel_id=1, source_target_pairs={{0,4},{4,0},{8,12},{12,8},{16,20},{20,16},{24,28},{28,24},{1,5},{5... | collective-permute-start | bytes 3145736 | tf_op jit(solution)/shard_map/ppermute | solution.py:742
  145.4 266.2 %reduce-scatter.6.cloned.1.call-start = ((), (), s32[]{:S(2)}) async-start(), calls=%async_computation.4 | async-start | bytes 10485760 | tf_op jit(solution)/shard_map/reduce_scatter | solution.py:784
  176.9 295.0 %reduce-scatter.8.cloned.1.call-start = ((), (), s32[]{:S(2)}) async-start(), calls=%async_computation.5 | async-start | bytes 3317760 | tf_op jit(solution)/shard_map/reduce_scatter | solution.py:784
  181.7 24.1 %collective-permute-start.23 = (bf16[128,2048]{1,0:T(8,128)(2,1)S(1)}, bf16[128,2048]{1,0:T(8,128)(2,1)S(1)}, u32[]{:S(2)}, u32[]{:S(2)}) collective-permute-start(bf16[128,2048]{1,0:T(8,128)(2,1)S(1)} %get-tuple-element.256), channel_id=1, source_target_pairs={{0,2},{1,3},{2,0},{3,1},{4,6},{5,7},{6,4},{7,5},{8,10},{9,11},{10,... | collective-permute-start | bytes 1572872 | tf_op jit(solution)/shard_map/ppermute | solution.py:751
  182.2 23.6 %collective-permute-start.22 = (bf16[128,2048]{1,0:T(8,128)(2,1)S(1)}, bf16[128,2048]{1,0:T(8,128)(2,1)}, u32[]{:S(2)}, u32[]{:S(2)}) collective-permute-start(bf16[128,2048]{1,0:T(8,128)(2,1)S(1)} %get-tuple-element.257), channel_id=1, source_target_pairs={{0,1},{1,0},{2,3},{3,2},{4,5},{5,4},{6,7},{7,6},{8,9},{9,8},{10,11... | collective-permute-start | bytes 1572872 | tf_op jit(solution)/shard_map/ppermute | solution.py:751
  213.0 24.6 %collective-permute-start.30 = (bf16[128,2048]{1,0:T(8,128)(2,1)}, bf16[128,2048]{1,0:T(8,128)(2,1)S(1)}, u32[]{:S(2)}, u32[]{:S(2)}) collective-permute-start(bf16[128,2048]{1,0:T(8,128)(2,1)} %get-tuple-element.184.refs_0_), channel_id=1, source_target_pairs={{0,2},{1,3},{2,0},{3,1},{4,6},{5,7},{6,4},{7,5},{8,10},{9,11},{10,... | collective-permute-start | bytes 1572872 | tf_op jit(solution)/shard_map/ppermute | solution.py:751
  214.0 23.6 %collective-permute-start.29 = (bf16[128,2048]{1,0:T(8,128)(2,1)}, bf16[128,2048]{1,0:T(8,128)(2,1)}, u32[]{:S(2)}, u32[]{:S(2)}) collective-permute-start(bf16[128,2048]{1,0:T(8,128)(2,1)} %get-tuple-element.184.refs_0_), channel_id=1, source_target_pairs={{0,1},{1,0},{2,3},{3,2},{4,5},{5,4},{6,7},{7,6},{8,9},{9,8},{10,11... | collective-permute-start | bytes 1572872 | tf_op jit(solution)/shard_map/ppermute | solution.py:751
  214.7 54.1 %collective-permute-start.45 = (bf16[512,1024]{1,0:T(8,128)(2,1)}, bf16[512,1024]{1,0:T(8,128)(2,1)}, u32[]{:S(2)}, u32[]{:S(2)}) collective-permute-start(bf16[512,1024]{1,0:T(8,128)(2,1)} %get-tuple-element.204), channel_id=1, source_target_pairs={{0,4},{4,0},{8,12},{12,8},{16,20},{20,16},{24,28},{28,24},{1,5},{5... | collective-permute-start | bytes 3145736 | tf_op jit(solution)/shard_map/ppermute | solution.py:742
  240.6 23.9 %collective-permute-start.34 = (bf16[128,2048]{1,0:T(8,128)(2,1)}, bf16[128,2048]{1,0:T(8,128)(2,1)}, u32[]{:S(2)}, u32[]{:S(2)}) collective-permute-start(bf16[128,2048]{1,0:T(8,128)(2,1)} %get-tuple-element.251), channel_id=1, source_target_pairs={{0,3},{1,2},{2,1},{3,0},{4,7},{5,6},{6,5},{7,4},{8,11},{9,10},{10,... | collective-permute-start | bytes 1572872 | tf_op jit(solution)/shard_map/ppermute | solution.py:751
  242.0 25.1 %collective-permute-start.33 = (bf16[128,2048]{1,0:T(8,128)(2,1)}, bf16[128,2048]{1,0:T(8,128)(2,1)}, u32[]{:S(2)}, u32[]{:S(2)}) collective-permute-start(bf16[128,2048]{1,0:T(8,128)(2,1)} %get-tuple-element.252), channel_id=1, source_target_pairs={{0,2},{1,3},{2,0},{3,1},{4,6},{5,7},{6,4},{7,5},{8,10},{9,11},{10,... | collective-permute-start | bytes 1572872 | tf_op jit(solution)/shard_map/ppermute | solution.py:751
  268.8 82.0 %collective-permute-start.40 = (bf16[256,512]{1,0:T(8,128)(2,1)S(1)}, bf16[256,512]{1,0:T(8,128)(2,1)S(1)}, u32[]{:S(2)}, u32[]{:S(2)}) collective-permute-start(bf16[256,512]{1,0:T(8,128)(2,1)S(1)} %get-tuple-element.280), channel_id=1, source_target_pairs={{16,0},{20,4},{24,8},{28,12},{17,1},{21,5},{25,9},{29,13},{18,2},{... | collective-permute-start | bytes 786440 | tf_op jit(solution)/shard_map/ppermute | solution.py:748
  270.5 80.4 %collective-permute-start.39 = (bf16[256,512]{1,0:T(8,128)(2,1)S(1)}, bf16[256,512]{1,0:T(8,128)(2,1)}, u32[]{:S(2)}, u32[]{:S(2)}) collective-permute-start(bf16[256,512]{1,0:T(8,128)(2,1)S(1)} %get-tuple-element.281), channel_id=1, source_target_pairs={{8,0},{12,4},{16,8},{20,12},{24,16},{28,20},{9,1},{13,5},{17,9},{2... | collective-permute-start | bytes 786440 | tf_op jit(solution)/shard_map/ppermute | solution.py:748
  362.9 25.3 %collective-permute-start.47 = (bf16[128,2048]{1,0:T(8,128)(2,1)}, bf16[128,2048]{1,0:T(8,128)(2,1)}, u32[]{:S(2)}, u32[]{:S(2)}) collective-permute-start(bf16[128,2048]{1,0:T(8,128)(2,1)} %pad_maximum_fusion.4), channel_id=1, source_target_pairs={{0,2},{1,3},{2,0},{3,1},{4,6},{5,7},{6,4},{7,5},{8,10},{9,11},{10,... | collective-permute-start | bytes 1572872 | tf_op jit(solution)/shard_map/ppermute | solution.py:751
  363.7 24.5 %collective-permute-start.48 = (bf16[128,2048]{1,0:T(8,128)(2,1)}, bf16[128,2048]{1,0:T(8,128)(2,1)}, u32[]{:S(2)}, u32[]{:S(2)}) collective-permute-start(bf16[128,2048]{1,0:T(8,128)(2,1)} %pad_maximum_fusion.5), channel_id=1, source_target_pairs={{0,3},{1,2},{2,1},{3,0},{4,7},{5,6},{6,5},{7,4},{8,11},{9,10},{10,... | collective-permute-start | bytes 1572872 | tf_op jit(solution)/shard_map/ppermute | solution.py:751
  365.3 32.0 %collective-permute-start.52 = (bf16[256,512]{1,0:T(8,128)(2,1)S(1)}, bf16[256,512]{1,0:T(8,128)(2,1)S(1)}, u32[]{:S(2)}, u32[]{:S(2)}) collective-permute-start(bf16[256,512]{1,0:T(8,128)(2,1)S(1)} %pad_maximum_fusion.7), channel_id=1, source_target_pairs={{0,4},{4,0},{8,12},{12,8},{16,20},{20,16},{24,28},{28,24},{1,5},{5... | collective-permute-start | bytes 786440 | tf_op jit(solution)/shard_map/ppermute | solution.py:742
  416.0 24.7 %collective-permute-start.36 = (bf16[128,2048]{1,0:T(8,128)(2,1)S(1)}, bf16[128,2048]{1,0:T(8,128)(2,1)S(1)}, u32[]{:S(2)}, u32[]{:S(2)}) collective-permute-start(bf16[128,2048]{1,0:T(8,128)(2,1)S(1)} %fusion.7.refs_0_), channel_id=1, source_target_pairs={{0,2},{1,3},{2,0},{3,1},{4,6},{5,7},{6,4},{7,5},{8,10},{9,11},{10,... | collective-permute-start | bytes 1572872 | tf_op jit(solution)/shard_map/ppermute | solution.py:751
  416.5 25.0 %collective-permute-start.35 = (bf16[128,2048]{1,0:T(8,128)(2,1)S(1)}, bf16[128,2048]{1,0:T(8,128)(2,1)}, u32[]{:S(2)}, u32[]{:S(2)}) collective-permute-start(bf16[128,2048]{1,0:T(8,128)(2,1)S(1)} %fusion.7.refs_0_), channel_id=1, source_target_pairs={{0,1},{1,0},{2,3},{3,2},{4,5},{5,4},{6,7},{7,6},{8,9},{9,8},{10,11... | collective-permute-start | bytes 1572872 | tf_op jit(solution)/shard_map/ppermute | solution.py:751
  417.1 34.9 %collective-permute-start.51 = (bf16[128,2048]{1,0:T(8,128)(2,1)}, bf16[128,2048]{1,0:T(8,128)(2,1)}, u32[]{:S(2)}, u32[]{:S(2)}) collective-permute-start(bf16[128,2048]{1,0:T(8,128)(2,1)} %get-tuple-element.207.refs_0_), channel_id=1, source_target_pairs={{0,3},{1,2},{2,1},{3,0},{4,7},{5,6},{6,5},{7,4},{8,11},{9,10},{10,... | collective-permute-start | bytes 1572872 | tf_op jit(solution)/shard_map/ppermute | solution.py:751
  419.5 42.3 %collective-permute-start.50 = (bf16[128,2048]{1,0:T(8,128)(2,1)}, bf16[128,2048]{1,0:T(8,128)(2,1)}, u32[]{:S(2)}, u32[]{:S(2)}) collective-permute-start(bf16[128,2048]{1,0:T(8,128)(2,1)} %get-tuple-element.207.refs_0_), channel_id=1, source_target_pairs={{0,2},{1,3},{2,0},{3,1},{4,6},{5,7},{6,4},{7,5},{8,10},{9,11},{10,... | collective-permute-start | bytes 1572872 | tf_op jit(solution)/shard_map/ppermute | solution.py:751
  429.4 32.5 %collective-permute-start.49 = (bf16[128,2048]{1,0:T(8,128)(2,1)}, bf16[128,2048]{1,0:T(8,128)(2,1)}, u32[]{:S(2)}, u32[]{:S(2)}) collective-permute-start(bf16[128,2048]{1,0:T(8,128)(2,1)} %get-tuple-element.207.refs_0_), channel_id=1, source_target_pairs={{0,1},{1,0},{2,3},{3,2},{4,5},{5,4},{6,7},{7,6},{8,9},{9,8},{10,11... | collective-permute-start | bytes 1572872 | tf_op jit(solution)/shard_map/ppermute | solution.py:751
  (87 other events, 991.1 us)
Sparse Core Ops, SparseCore 0:
  145.5 107.4 reduce-scatter.3
  255.4 156.1 reduce-scatter.5
  414.0 57.8 reduce-scatter.7

commit v3 on v1

v3 whole, which is shorter than its diff:
```python
import functools
import math

import jax
import jax.numpy as jnp
import numpy as np
from jax import lax
from jax.experimental import pallas as pl
from jax.experimental.pallas import tpu as pltpu
from jax.sharding import PartitionSpec as P

HD = 64
DOCS = 12
NORM_EPS = 1e-05
MASKED_SCORE = -1e30
LOG2E = math.log2(math.e)
SCALE2 = LOG2E / math.sqrt(HD)
KT = 256
HALVES = 2
BF = jnp.bfloat16
F32 = jnp.float32


def inverse_frequencies(head_size):
    frequency = 1.0 / 500000.0 ** (np.arange(0, head_size, 2) / head_size)
    wavelength = 2 * math.pi / frequency
    smoothing = (8192.0 / wavelength - 1.0) / 3.0
    scaled_freq = np.where(wavelength > 8192.0, frequency / 32.0, frequency)
    middle_band = (wavelength <= 8192.0) & (wavelength >= 2048.0)
    scaled_freq = np.where(
        middle_band, (1 - smoothing) * frequency / 32.0 + smoothing * frequency, scaled_freq
    )
    return scaled_freq.astype(np.float32)


def doc_offsets(doc_lengths, index):
    ends = jnp.cumsum(doc_lengths)
    passed = (index[None, :] >= ends[:, None]).astype(jnp.int32)
    return jnp.sum(passed * doc_lengths[:, None], axis=0)


def rotate_t(values, cosine, sine):
    heads = values.shape[0] // HD
    shaped = values.reshape(heads, 2, HD // 2, values.shape[1])
    first = shaped[:, 0]
    second = shaped[:, 1]
    return jnp.stack(
        [first * cosine - second * sine, second * cosine + first * sine], axis=1
    ).reshape(values.shape)


def dims(left, right, a, b):
    return lax.dot_general(left, right, (((a,), (b,)), ((), ())), preferred_element_type=F32)


def vmem_spec():
    return pl.BlockSpec(memory_space=pltpu.VMEM)


def smem_spec():
    return pl.BlockSpec(memory_space=pltpu.SMEM)


def any_spec():
    return pl.BlockSpec(memory_space=pl.ANY)


def cost(flops, moved, exps=0):
    return pl.CostEstimate(flops=int(flops), transcendentals=int(exps), bytes_accessed=int(moved))


def rms_scale(values):
    return lax.rsqrt(jnp.mean(values * values, axis=-1, keepdims=True) + NORM_EPS)


def keys_values_kernel(x_ref, gain_ref, wk_ref, wv_ref, cos_ref, sin_ref, normed_ref, packed_ref):
    rows = x_ref.shape[0]
    step = min(128, rows)
    for at in range(0, rows, step):
        values = x_ref[at : at + step, :].astype(F32)
        normed_ref[at : at + step, :] = (values * rms_scale(values) * gain_ref[...]).astype(BF)
    normed = normed_ref[...]
    keys = jnp.dot(normed, wk_ref[...], preferred_element_type=F32).T
    width = keys.shape[0]
    half = HD // 2
    for head in range(width // HD):
        first = keys[head * HD : head * HD + half]
        second = keys[head * HD + half : (head + 1) * HD]
        cosine, sine = cos_ref[...], sin_ref[...]
        packed_ref[head * HD : head * HD + half, :] = (first * cosine - second * sine).astype(BF)
        packed_ref[head * HD + half : (head + 1) * HD, :] = (
            second * cosine + first * sine
        ).astype(BF)
    packed_ref[width:, :] = jnp.dot(normed, wv_ref[...], preferred_element_type=F32).T.astype(BF)


def keys_values(tokens, gain, w_key, w_value, cosine, sine):
    rows, width = tokens.shape
    kv = w_key.shape[1]
    return pl.pallas_call(
        keys_values_kernel,
        in_specs=[vmem_spec()] * 6,
        out_specs=[vmem_spec()] * 2,
        out_shape=[
            jax.ShapeDtypeStruct((rows, width), BF),
            jax.ShapeDtypeStruct((2 * kv, rows), BF),
        ],
        name="keys_values",
        cost_estimate=cost(4 * rows * width * kv, 4 * rows * width + 4 * width * kv),
    )(tokens, gain, w_key, w_value, cosine, sine)


def window(lengths_ref, index):
    end = lengths_ref[0]
    start = jnp.zeros_like(index)
    for doc in range(1, DOCS):
        start = jnp.where(index >= end, end, start)
        if doc == DOCS - 1:
            last = end
        end = end + lengths_ref[doc]
    valid = index < last
    return jnp.where(valid, start, index), valid


def tile_state(ids_ref, edges, tile, half, q_rows, rows):
    me_wide = ids_ref[2]
    slot = tile // (rows // KT)
    block = (me_wide // 2 - slot // 2) * 2 + (ids_ref[1] ^ (slot % 2))
    key_base = block * rows + (tile % (rows // KT)) * KT
    q_base = me_wide * rows + half * q_rows
    low, high = edges[half]
    active = (key_base <= q_base + q_rows - 1) & (key_base + KT > low)
    whole = (key_base + KT - 1 <= q_base) & (key_base >= high)
    return active, active & whole, key_base, q_base


def window_edges(ids_ref, lengths_ref, rows):
    base = ids_ref[2] * rows
    step = rows // HALVES
    return [
        (
            window(lengths_ref, base + half * step)[0],
            window(lengths_ref, base + (half + 1) * step - 1)[0],
        )
        for half in range(HALVES)
    ]


def query_row(ids_ref, rows, half):
    step = rows // HALVES
    return ids_ref[2] * rows + half * step + lax.broadcasted_iota(jnp.int32, (1, step), 1)


def tile_mask(key_base, q_base, start_row):
    q_rows = start_row.shape[1]
    keys = key_base + lax.broadcasted_iota(jnp.int32, (KT, q_rows), 0)
    queries = q_base + lax.broadcasted_iota(jnp.int32, (KT, q_rows), 1)
    return (keys <= queries) & (keys >= start_row)


def both_ways(active, whole, run):
    pl.when(whole)(lambda: run(False))
    pl.when(active & jnp.logical_not(whole))(lambda: run(True))


def attend_kernel(slots, group, half, ids_ref, lengths_ref, q_ref, *refs):
    k_refs = refs[:slots]
    v_refs = refs[slots : 2 * slots]
    o_ref, mixed_ref, lse_ref, keys_s, values_s, top_s, sum_s, acc_s = refs[2 * slots :]
    q_rows = q_ref.shape[1]
    rows = k_refs[0].shape[1]
    per = rows // KT
    tiles = slots * per
    edges = window_edges(ids_ref, lengths_ref, rows)
    start_row, valid_row = window(lengths_ref, query_row(ids_ref, rows, half))
    for slot in range(slots):
        for part in range(per):
            tile = slot * per + part
            cut = slice(part * KT, (part + 1) * KT)

            @pl.when(tile_state(ids_ref, edges, tile, half, q_rows, rows)[0])
            def _(tile=tile, slot=slot, cut=cut):
                keys_s[tile] = k_refs[slot][:, cut].T
                values_s[tile] = v_refs[slot][:, cut]

    top_s[...] = jnp.full_like(top_s, MASKED_SCORE)
    sum_s[...] = jnp.zeros_like(sum_s)
    acc_s[...] = jnp.zeros_like(acc_s)
    heads = range(group)

    def step(tile, carry):
        active, whole, key_base, q_base = tile_state(ids_ref, edges, tile, half, q_rows, rows)

        def run(masked):
            keys = keys_s[tile]
            values = values_s[tile]
            scores = [
                jnp.dot(keys, q_ref[h * HD : (h + 1) * HD, :], preferred_element_type=F32)
                for h in heads
            ]
            if masked:
                allowed = tile_mask(key_base, q_base, start_row)
                scores = [jnp.where(allowed, s, MASKED_SCORE) for s in scores]
            tops, decays = [], []
            for h in heads:
                old = top_s[h : h + 1, :]
                new = jnp.maximum(old, jnp.max(scores[h], axis=0, keepdims=True))
                top_s[h : h + 1, :] = new
                tops.append(new)
                decays.append(jnp.exp2((old - new) * SCALE2))
            for h in heads:
                weight = jnp.exp2((scores[h] - tops[h]) * SCALE2)
                sum_s[h : h + 1, :] = sum_s[h : h + 1, :] * decays[h] + jnp.sum(
                    weight, axis=0, keepdims=True
                )
                acc_s[h] = acc_s[h] * decays[h] + jnp.dot(
                    values, weight.astype(BF), preferred_element_type=F32
                )

        both_ways(active, whole, run)
        return carry

    lax.fori_loop(0, tiles, step, 0)
    for h in heads:
        h_cut = slice(h * HD, (h + 1) * HD)
        total = sum_s[h : h + 1, :]
        out = acc_s[h] / total
        o_ref[h_cut, :] = out
        mixed_ref[h_cut, :] = jnp.where(valid_row, out, 0.0).astype(BF)
        lse_ref[0, h : h + 1, :] = top_s[h : h + 1, :] * SCALE2 + jnp.log(total) * LOG2E


def attend(half, ids, lengths, q_t, blocks, kv_heads):
    slots = len(blocks)
    heads = q_t.shape[0] // HD
    group = heads // kv_heads
    rows = q_t.shape[1]
    q_rows = rows // HALVES
    tiles = slots * (rows // KT)
    out_spec = pl.BlockSpec((group * HD, q_rows), lambda g: (g, 0))
    return pl.pallas_call(
        functools.partial(attend_kernel, slots, group, half),
        grid=(kv_heads,),
        in_specs=[
            smem_spec(),
            smem_spec(),
            pl.BlockSpec((group * HD, q_rows), lambda g: (g, half)),
        ]
        + [pl.BlockSpec((HD, rows), lambda g: (g, 0))] * slots
        + [pl.BlockSpec((HD, rows), lambda g: (kv_heads + g, 0))] * slots,
        out_specs=[out_spec, out_spec, pl.BlockSpec((1, group, q_rows), lambda g: (g, 0, 0))],
        out_shape=[
            jax.ShapeDtypeStruct((heads * HD, q_rows), F32),
            jax.ShapeDtypeStruct((heads * HD, q_rows), BF),
            jax.ShapeDtypeStruct((kv_heads, group, q_rows), F32),
        ],
        scratch_shapes=[
            pltpu.VMEM((tiles, KT, HD), BF),
            pltpu.VMEM((tiles, HD, KT), BF),
            pltpu.VMEM((group, q_rows), F32),
            pltpu.VMEM((group, q_rows), F32),
            pltpu.VMEM((group, HD, q_rows), F32),
        ],
        name="attend",
        cost_estimate=cost(
            16 * heads * q_rows * rows * HD, 8 * rows * heads * HD, heads * q_rows * rows * 4
        ),
    )(ids, lengths, q_t, *blocks, *blocks)


def attend_back_kernel(slots, group, members, ids_ref, lengths_ref, q_ref, *refs):
    do_refs, refs = refs[:members], refs[members:]
    o_refs, lse_refs, refs = refs[:HALVES], refs[HALVES : 2 * HALVES], refs[2 * HALVES :]
    k_refs, v_refs, refs = refs[:slots], refs[slots : 2 * slots], refs[2 * slots :]
    dq_ref, dkv_ref = refs[:2]
    keys_s, values_s, keys_t_s, dk_s, dv_s, q_s, do_s, do_t_s, dq_s, delta_s = refs[2:]
    rows = q_ref.shape[1]
    q_rows = rows // HALVES
    per = rows // KT
    tiles = slots * per
    heads = range(group)
    edges = window_edges(ids_ref, lengths_ref, rows)

    def any_active(tile):
        found = tile_state(ids_ref, edges, tile, 0, q_rows, rows)[0]
        for half in range(1, HALVES):
            found = found | tile_state(ids_ref, edges, tile, half, q_rows, rows)[0]
        return found

    for slot in range(slots):
        for part in range(per):
            tile = slot * per + part
            cut = slice(part * KT, (part + 1) * KT)

            @pl.when(any_active(tile))
            def _(tile=tile, slot=slot, cut=cut):
                keys_s[tile] = k_refs[slot][:, cut].T
                keys_t_s[tile] = k_refs[slot][:, cut]
                values_s[tile] = v_refs[slot][:, cut].T
                dk_s[tile] = jnp.zeros((KT, HD), F32)
                dv_s[tile] = jnp.zeros((KT, HD), F32)

    shard = do_refs[0].shape[0]
    for distance in range(members):
        at = pl.multiple_of((ids_ref[0] ^ distance) * shard, shard)
        do_s[pl.ds(at, shard), :] = do_refs[distance][...]
    do_t_s[...] = do_s[...].T

    for half in range(HALVES):
        q_cut = slice(half * q_rows, (half + 1) * q_rows)
        for h in heads:
            h_cut = slice(h * HD, (h + 1) * HD)
            q_s[h] = q_ref[h_cut, q_cut].T
            delta_s[h : h + 1, :] = jnp.sum(
                do_t_s[h_cut, q_cut].astype(F32) * o_refs[half][h_cut, :], axis=0, keepdims=True
            )
        dq_s[...] = jnp.zeros_like(dq_s)
        start_row = window(lengths_ref, query_row(ids_ref, rows, half))[0]

        def step(tile, carry, half=half, q_cut=q_cut, start_row=start_row):
            active, whole, key_base, q_base = tile_state(ids_ref, edges, tile, half, q_rows, rows)

            def run(masked):
                keys = keys_s[tile]
                values = values_s[tile]
                keys_t = keys_t_s[tile]
                scores = [
                    jnp.dot(keys, q_ref[h * HD : (h + 1) * HD, q_cut], preferred_element_type=F32)
                    for h in heads
                ]
                prob_grads = [
                    jnp.dot(values, do_t_s[h * HD : (h + 1) * HD, q_cut], preferred_element_type=F32)
                    for h in heads
                ]
                if masked:
                    allowed = tile_mask(key_base, q_base, start_row)
                probs, d_scores = [], []
                for h in heads:
                    scaled = scores[h] * SCALE2 - lse_refs[half][0, h : h + 1, :]
                    if masked:
                        scaled = jnp.where(allowed, scaled, MASKED_SCORE)
                    prob = jnp.exp2(scaled)
                    probs.append(prob.astype(BF))
                    d_scores.append((prob * (prob_grads[h] - delta_s[h : h + 1, :])).astype(BF))
                dk = dk_s[tile]
                dv = dv_s[tile]
                for h in heads:
                    dv = dv + jnp.dot(
                        probs[h],
                        do_s[q_cut, h * HD : (h + 1) * HD],
                        preferred_element_type=F32,
                    )
                    dk = dk + jnp.dot(d_scores[h], q_s[h], preferred_element_type=F32)
                    dq_s[h] += jnp.dot(keys_t, d_scores[h], preferred_element_type=F32)
                dk_s[tile] = dk
                dv_s[tile] = dv

            both_ways(active, whole, run)
            return carry

        lax.fori_loop(0, tiles, step, 0)
        for h in heads:
            dq_ref[h * HD : (h + 1) * HD, q_cut] = dq_s[h]
    for slot in range(slots):
        for part in range(per):
            cut = slice(part * KT, (part + 1) * KT)
            tile = slot * per + part
            active = any_active(tile)

            @pl.when(active)
            def _(tile=tile, slot=slot, cut=cut):
                dkv_ref[slot, 0, :, cut] = (dk_s[tile].T * (1.0 / math.sqrt(HD))).astype(BF)
                dkv_ref[slot, 1, :, cut] = dv_s[tile].T.astype(BF)

            @pl.when(jnp.logical_not(active))
            def _(slot=slot, cut=cut):
                dkv_ref[slot, 0, :, cut] = jnp.zeros((HD, KT), BF)
                dkv_ref[slot, 1, :, cut] = jnp.zeros((HD, KT), BF)


def attend_back(ids, lengths, q_t, do_pieces, outs, lses, blocks, kv_heads):
    slots = len(blocks)
    heads = q_t.shape[0] // HD
    group = heads // kv_heads
    rows = q_t.shape[1]
    q_rows = rows // HALVES
    tiles = slots * (rows // KT)
    members = len(do_pieces)
    wide = group * HD
    q_spec = pl.BlockSpec((wide, rows), lambda g: (g, 0))
    return pl.pallas_call(
        functools.partial(attend_back_kernel, slots, group, members),
        grid=(kv_heads,),
        in_specs=[smem_spec(), smem_spec(), q_spec]
        + [pl.BlockSpec((rows // members, wide), lambda g: (0, g))] * members
        + [pl.BlockSpec((wide, q_rows), lambda g: (g, 0))] * HALVES
        + [pl.BlockSpec((1, group, q_rows), lambda g: (g, 0, 0))] * HALVES
        + [pl.BlockSpec((HD, rows), lambda g: (g, 0))] * slots
        + [pl.BlockSpec((HD, rows), lambda g: (kv_heads + g, 0))] * slots,
        out_specs=[q_spec, pl.BlockSpec((slots, 2, HD, rows), lambda g: (0, 0, g, 0))],
        out_shape=[
            jax.ShapeDtypeStruct(q_t.shape, F32),
            jax.ShapeDtypeStruct((slots, 2, kv_heads * HD, rows), BF),
        ],
        scratch_shapes=[
            pltpu.VMEM((tiles, KT, HD), BF),
            pltpu.VMEM((tiles, KT, HD), BF),
            pltpu.VMEM((tiles, HD, KT), BF),
            pltpu.VMEM((tiles, KT, HD), F32),
            pltpu.VMEM((tiles, KT, HD), F32),
            pltpu.VMEM((group, q_rows, HD), BF),
            pltpu.VMEM((rows, wide), BF),
            pltpu.VMEM((wide, rows), BF),
            pltpu.VMEM((group, HD, q_rows), F32),
            pltpu.VMEM((group, q_rows), F32),
        ],
        name="attend_back",
        cost_estimate=cost(
            40 * heads * rows * rows * HD, 16 * rows * heads * HD, heads * rows * rows * 4
        ),
    )(ids, lengths, q_t, *do_pieces, *outs, *lses, *blocks, *blocks)


def fetch_weights(members, ids_ref, weights, held, sems):
    size = held.shape[0] // (2 * members)
    copies = []
    for distance in range(members):
        for other in range(2):
            index = 2 * distance + other
            source = pl.multiple_of((ids_ref[0] ^ distance) * size, size)
            copy = pltpu.make_async_copy(
                weights[other].at[pl.ds(source, size), :],
                held.at[index * size : (index + 1) * size, :],
                sems.at[index],
            )
            copy.start()
            first = pl.multiple_of((ids_ref[1] ^ other) * size, size)
            copies.append((copy, distance, index * size, first))
    return copies, size


def attn_out_kernel(members, ids_ref, x_ref, gain_ref, *refs):
    mixes, weights = refs[:members], refs[members : members + 2]
    hidden_ref, normed_ref, held, sems = refs[-4:]
    copies, size = fetch_weights(members, ids_ref, weights, held, sems)
    hidden_ref[...] = x_ref[...].astype(F32)
    for copy, distance, at, first in copies:
        copy.wait()
        hidden_ref[...] += dims(
            mixes[distance][pl.ds(first, size), :], held[at : at + size, :], 0, 0
        )
    rows = hidden_ref.shape[0]
    step = min(64, rows)
    for at in range(0, rows, step):
        hidden = hidden_ref[at : at + step, :]
        normed_ref[at : at + step, :] = (hidden * rms_scale(hidden) * gain_ref[...]).astype(BF)


def attn_out(half, ids, tokens, gain, mixes, weights, filled):
    rows, width = tokens.shape
    half_rows = rows // HALVES
    inner = sum(w.shape[0] for w in weights)
    out_spec = pl.BlockSpec((half_rows, width), lambda i: (half, 0))
    operands = [ids, tokens, gain, *mixes, *weights]
    extra = [] if filled is None else list(filled)
    return pl.pallas_call(
        functools.partial(attn_out_kernel, len(mixes)),
        grid=(1,),
        in_specs=[smem_spec(), out_spec, vmem_spec()]
        + [vmem_spec()] * len(mixes)
        + [any_spec()] * (len(weights) + len(extra)),
        out_specs=[out_spec, out_spec],
        out_shape=[
            jax.ShapeDtypeStruct((rows, width), F32),
            jax.ShapeDtypeStruct((rows, width), BF),
        ],
        scratch_shapes=[
            pltpu.VMEM((inner, width), BF),
            pltpu.SemaphoreType.DMA((2 * len(mixes),)),
        ],
        input_output_aliases={len(operands) + i: i for i in range(len(extra))},
        name="attn_out",
        cost_estimate=cost(
            2 * half_rows * inner * width, 2 * inner * width + 12 * half_rows * width
        ),
    )(*operands, *extra)


def row_sum(refs):
    total = refs[0][...].astype(F32)
    for ref in refs[1:]:
        total = total + ref[...].astype(F32)
    return total


def norm_back(grad_normed, gain, values, inverse):
    scaled = grad_normed * gain
    return inverse * scaled - values * inverse**3 * jnp.mean(
        scaled * values, axis=-1, keepdims=True
    )


def norm_two_back_kernel(members, ids_ref, lengths_ref, hidden_ref, cot_ref, gain_ref, *refs):
    pieces, refs = refs[:members], refs[members:]
    weights, refs = refs[:2], refs[2:]
    refs = refs[members - 1 :]
    sum_ref, low_ref, part_ref = refs[:3]
    d_mixed, refs = refs[3 : 3 + members], refs[3 + members :]
    sent, (held, sems) = refs[:-2], refs[-2:]
    copies, size = fetch_weights(members, ids_ref, weights, held, sems)
    grad = row_sum(pieces)
    hidden = hidden_ref[...]
    inverse = rms_scale(hidden)
    part_ref[...] = jnp.sum(grad * hidden * inverse, axis=0, keepdims=True)
    total = cot_ref[...].astype(F32) + norm_back(grad, gain_ref[...], hidden, inverse)
    sum_ref[...] = total
    low = total.astype(BF)
    low_ref[...] = low
    for ref in sent:
        ref[...] = low
    shard = hidden.shape[0]
    begin = (ids_ref[2] * members + ids_ref[0]) * shard
    keep = window(lengths_ref, begin + lax.broadcasted_iota(jnp.int32, (shard, 1), 0))[1]
    for copy, distance, at, first in copies:
        copy.wait()
        out = jnp.where(keep, dims(low, held[at : at + size, :], 1, 1), 0.0)
        d_mixed[distance][:, pl.ds(first, size)] = out.astype(BF)


def norm_two_back(ids, lengths, hidden, cotangent, gain, pieces, weights, travel):
    members = len(pieces)
    shard, width = pieces[0].shape
    inner = sum(w.shape[0] for w in weights)
    mine = pl.BlockSpec((shard, width), lambda i, ids, lengths: (ids[0], 0))
    whole = pl.BlockSpec((shard, width), lambda i, ids, lengths: (0, 0))
    line = pl.BlockSpec((1, width), lambda i, ids, lengths: (0, 0))
    head_spec = pl.BlockSpec((shard, inner // members), lambda i, ids, lengths: (0, 0))
    return pl.pallas_call(
        functools.partial(norm_two_back_kernel, members),
        grid_spec=pltpu.PrefetchScalarGridSpec(
            num_scalar_prefetch=2,
            grid=(1,),
            in_specs=[mine, mine, line]
            + [whole] * members
            + [any_spec()] * (len(weights) + len(travel)),
            out_specs=[whole, whole, line] + [head_spec] * members + [whole] * len(travel),
            scratch_shapes=[
                pltpu.VMEM((inner, width), BF),
                pltpu.SemaphoreType.DMA((2 * members,)),
            ],
        ),
        out_shape=[
            jax.ShapeDtypeStruct((shard, width), F32),
            jax.ShapeDtypeStruct((shard, width), BF),
            jax.ShapeDtypeStruct((1, width), F32),
        ]
        + [jax.ShapeDtypeStruct((shard, inner // members), BF)] * members
        + [jax.ShapeDtypeStruct(t.shape, BF) for t in travel],
        input_output_aliases={
            5 + members + len(weights) + i: 3 + members + i for i in range(len(travel))
        },
        name="norm_two_back",
        cost_estimate=cost(2 * shard * inner * width, 2 * inner * width + 24 * shard * width),
    )(ids, lengths, hidden, cotangent, gain, *pieces, *weights, *travel)


def last_rows_kernel(members, ids_ref, x_ref, hidden_ref, add_ref, gain_ref, *refs):
    pieces, ffn, (low_ref, part_ref) = refs[:members], refs[members:-2], refs[-2:]
    grad = row_sum(pieces)
    values = x_ref[...].astype(F32)
    shard = values.shape[0]
    inverse = rms_scale(values)
    part_ref[...] = jnp.sum(grad * values * inverse, axis=0, keepdims=True)
    low_ref[:shard, :] = (
        add_ref[...] + norm_back(grad, gain_ref[...], values, inverse)
    ).astype(BF)
    low_ref[shard:, :] = (hidden_ref[...] + row_sum(ffn)).astype(BF)


def last_rows(ids, tokens, hidden, add, gain, pieces, ffn_pieces):
    shard, width = pieces[0].shape
    mine = pl.BlockSpec((shard, width), lambda i, ids: (ids[0], 0))
    first = pl.BlockSpec((shard, width), lambda i, ids: (0, 0))
    second = pl.BlockSpec((shard, width), lambda i, ids: (1, 0))
    line = pl.BlockSpec((1, width), lambda i, ids: (0, 0))
    both = pl.BlockSpec((2 * shard, width), lambda i, ids: (0, 0))
    return pl.pallas_call(
        functools.partial(last_rows_kernel, len(pieces)),
        grid_spec=pltpu.PrefetchScalarGridSpec(
            num_scalar_prefetch=1,
            grid=(1,),
            in_specs=[mine, mine, first, line]
            + [first] * (len(pieces) + 1)
            + [second] * (len(ffn_pieces) - 1),
            out_specs=[both, line],
        ),
        out_shape=[
            jax.ShapeDtypeStruct((2 * shard, width), BF),
            jax.ShapeDtypeStruct((1, width), F32),
        ],
        name="last_rows",
        cost_estimate=cost(30 * shard * width, 32 * shard * width),
    )(ids, tokens, hidden, add, gain, *pieces, *ffn_pieces)


def in_order_kernel(shard, outs, ids_ref, *refs):
    pieces, out_refs = refs[:-outs], refs[-outs:]
    for distance, ref in enumerate(pieces):
        at = pl.multiple_of((ids_ref[0] ^ distance) * shard, shard)
        for index, out_ref in enumerate(out_refs):
            out_ref[pl.ds(at, shard), :] = ref[index * shard : (index + 1) * shard, :]


def in_order(ids, pieces, outs):
    width = pieces[0].shape[1]
    shard = pieces[0].shape[0] // outs if outs > 1 else pieces[0].shape[0]
    rows = shard * len(pieces)
    return pl.pallas_call(
        functools.partial(in_order_kernel, shard, outs),
        in_specs=[smem_spec()] + [vmem_spec()] * len(pieces),
        out_specs=[vmem_spec()] * outs,
        out_shape=[jax.ShapeDtypeStruct((rows, width), pieces[0].dtype)] * outs,
        name="token_order",
        cost_estimate=cost(0, 4 * rows * outs * width),
    )(ids, *pieces)


def ffn_kernel(n_ref, da_ref, wg_ref, wu_ref, act_ref, dg_ref, du_ref):
    normed = n_ref[...]
    gate = jnp.dot(normed, wg_ref[...], preferred_element_type=F32)
    up = jnp.dot(normed, wu_ref[...], preferred_element_type=F32)
    sig = jax.nn.sigmoid(gate)
    silu = gate * sig
    act_ref[...] = (silu * up).astype(BF)
    d_act = da_ref[...]
    dg_ref[...] = (d_act * up * sig * (1.0 + gate * (1.0 - sig))).astype(BF)
    du_ref[...] = (d_act * silu).astype(BF)


def ffn_forward(normed, d_act, w_gate, w_up):
    rows, width = normed.shape
    units = w_gate.shape[1]
    step = min(512, units)
    tile = pl.BlockSpec((rows, step), lambda j: (0, j))
    weight = pl.BlockSpec((width, step), lambda j: (0, j))
    return pl.pallas_call(
        ffn_kernel,
        grid=(units // step,),
        in_specs=[pl.BlockSpec((rows, width), lambda j: (0, 0)), tile, weight, weight],
        out_specs=[tile, tile, tile],
        out_shape=[jax.ShapeDtypeStruct((rows, units), BF)] * 3,
        name="gate_up",
        cost_estimate=cost(
            4 * rows * width * units,
            4 * width * units + 2 * rows * width + 10 * rows * units,
            rows * units,
        ),
    )(normed, d_act, w_gate, w_up)


def store_by_distance(ids_ref, out_refs, held, value):
    shard = value.shape[0] // len(out_refs)
    held[...] = value.astype(BF)
    for distance, out_ref in enumerate(out_refs):
        at = pl.multiple_of((ids_ref[0] ^ distance) * shard, shard)
        out_ref[...] = held[pl.ds(at, shard), :]


def pair_nt_kernel(ids_ref, a_ref, b_ref, wa_ref, wb_ref, *refs):
    value = dims(a_ref[...], wa_ref[...], 1, 1) + dims(b_ref[...], wb_ref[...], 1, 1)
    store_by_distance(ids_ref, refs[:-1], refs[-1], value)


def pair_nt(members, ids, a, b, w_a, w_b):
    rows, units = a.shape
    width = w_a.shape[0]
    step = min(512, width)
    full = pl.BlockSpec((rows, units), lambda j: (0, 0))
    weight = pl.BlockSpec((step, units), lambda j: (j, 0))
    return pl.pallas_call(
        pair_nt_kernel,
        grid=(width // step,),
        in_specs=[smem_spec(), full, full, weight, weight],
        out_specs=[pl.BlockSpec((rows // members, step), lambda j: (0, j))] * members,
        out_shape=[jax.ShapeDtypeStruct((rows // members, width), BF)] * members,
        scratch_shapes=[pltpu.VMEM((rows, step), BF)],
        name="d_normed_two",
        cost_estimate=cost(
            4 * rows * width * units, 4 * width * units + 4 * rows * units + 2 * rows * width
        ),
    )(ids, a, b, w_a, w_b)


def down_kernel(ids_ref, a_ref, w_ref, *refs):
    value = jnp.dot(a_ref[...], w_ref[...], preferred_element_type=F32)
    store_by_distance(ids_ref, refs[:-1], refs[-1], value)


def down_of(members, ids, act, w_down):
    rows, units = act.shape
    shard = rows // members
    width = w_down.shape[1]
    step = min(512, width)
    return pl.pallas_call(
        down_kernel,
        grid=(width // step,),
        in_specs=[
            smem_spec(),
            pl.BlockSpec((rows, units), lambda j: (0, 0)),
            pl.BlockSpec((units, step), lambda j: (0, j)),
        ],
        out_specs=[pl.BlockSpec((shard, step), lambda j: (0, j))]
        + [pl.BlockSpec((shard, step), lambda j: (1, j))] * (members - 1),
        out_shape=[jax.ShapeDtypeStruct((shard, width), BF)]
        + [jax.ShapeDtypeStruct((2 * shard, width), BF)] * (members - 1),
        scratch_shapes=[pltpu.VMEM((rows, step), BF)],
        name="ffn_down",
        cost_estimate=cost(
            2 * rows * width * units, 2 * width * units + 2 * rows * units + 2 * rows * width
        ),
    )(ids, act, w_down)


def column_specs(rows, part, count):
    return [
        pl.BlockSpec((rows, part), lambda j, ids, k=k: (0, 2 * k + ids[1])) for k in range(count)
    ]


def fill_columns(held, refs):
    count = len(refs) // 2
    rows, part = refs[0].shape
    for index, ref in enumerate(refs):
        top = (index // count) * rows
        left = (index % count) * part
        held[top : top + rows, left : left + part] = ref[...]


def grad_down_kernel(blocks, ids_ref, own_ref, other_ref, *refs):
    cots, (o_ref, held) = refs[: 2 * blocks], refs[2 * blocks :]

    @pl.when(pl.program_id(0) == 0)
    def _():
        fill_columns(held, cots)

    rows = own_ref.shape[0]
    o_ref[...] = (
        dims(own_ref[...], held[:rows, :], 0, 0) + dims(other_ref[...], held[rows:, :], 0, 0)
    ).astype(BF)


def grad_down_of(ids, act, act_other, cot, cot_other, part):
    rows, units = act.shape
    width = cot.shape[1]
    blocks = width // (2 * part)
    step = min(512, units)
    tile = pl.BlockSpec((rows, step), lambda j, ids: (0, j))
    columns = column_specs(rows, part, blocks)
    return pl.pallas_call(
        functools.partial(grad_down_kernel, blocks),
        grid_spec=pltpu.PrefetchScalarGridSpec(
            num_scalar_prefetch=1,
            grid=(units // step,),
            in_specs=[tile, tile] + columns + columns,
            out_specs=pl.BlockSpec((step, width // 2), lambda j, ids: (j, 0)),
            scratch_shapes=[pltpu.VMEM((2 * rows, width // 2), BF)],
        ),
        out_shape=jax.ShapeDtypeStruct((units, width // 2), BF),
        name="grad_down",
        cost_estimate=cost(
            2 * rows * width * units, 4 * rows * units + 2 * rows * width + width * units
        ),
    )(ids, act, act_other, *([cot] * blocks), *([cot_other] * blocks))


def grad_in_kernel(blocks, half, ids_ref, *refs):
    normeds, refs = refs[: 2 * blocks], refs[2 * blocks :]
    gates, ups, (o_ref, held) = refs[:2], refs[2:4], refs[4:]

    @pl.when(pl.program_id(0) == 0)
    def _():
        fill_columns(held, normeds)

    rows = gates[0].shape[0]

    def of(pair):
        o_ref[...] = (
            dims(held[:rows, :], pair[0][...], 0, 0) + dims(held[rows:, :], pair[1][...], 0, 0)
        ).astype(BF)

    pl.when(pl.program_id(0) < half)(lambda: of(gates))
    pl.when(pl.program_id(0) >= half)(lambda: of(ups))


def grad_in_of(ids, normed, normed_other, d_gates, d_ups, part):
    rows, width = normed.shape
    units = d_gates[0].shape[1]
    blocks = width // (2 * part)
    step = min(512, units)
    half = units // step
    columns = column_specs(rows, part, blocks)
    first = pl.BlockSpec((rows, step), lambda j, ids: (0, jnp.minimum(j, half - 1)))
    second = pl.BlockSpec((rows, step), lambda j, ids: (0, jnp.maximum(j - half, 0)))
    return pl.pallas_call(
        functools.partial(grad_in_kernel, blocks, half),
        grid_spec=pltpu.PrefetchScalarGridSpec(
            num_scalar_prefetch=1,
            grid=(2 * half,),
            in_specs=columns + columns + [first] * 2 + [second] * 2,
            out_specs=pl.BlockSpec((width // 2, step), lambda j, ids: (0, j)),
            scratch_shapes=[pltpu.VMEM((2 * rows, width // 2), BF)],
        ),
        out_shape=jax.ShapeDtypeStruct((width // 2, 2 * units), BF),
        name="grad_gate_up",
        cost_estimate=cost(
            4 * rows * width * units, 8 * rows * units + 2 * rows * width + 2 * width * units
        ),
    )(ids, *([normed] * blocks), *([normed_other] * blocks), *d_gates, *d_ups)


def grad_proj_kernel(lefts, ids_ref, *refs):
    own, other = refs[:lefts], refs[lefts : 2 * lefts]
    right_ref, right_other_ref, o_ref = refs[2 * lefts :]
    at = 0
    rows = right_ref.shape[0]
    part = rows // lefts
    total = 0.0
    for group, right in ((own, right_ref), (other, right_other_ref)):
        for index, left in enumerate(group):
            total = total + jnp.dot(
                left[...],
                right[index * part : (index + 1) * part, :],
                preferred_element_type=F32,
            )
    o_ref[...] = total.astype(BF)


def grad_proj_of(ids, lefts, lefts_other, right, right_other, part, name):
    inner = lefts[0].shape[0]
    rows, width = right.shape
    blocks = width // (2 * part)
    left_spec = pl.BlockSpec(lefts[0].shape, lambda k, ids: (0, 0))
    right_spec = pl.BlockSpec((rows, part), lambda k, ids: (0, 2 * k + ids[1]))
    return pl.pallas_call(
        functools.partial(grad_proj_kernel, len(lefts)),
        grid_spec=pltpu.PrefetchScalarGridSpec(
            num_scalar_prefetch=1,
            grid=(blocks,),
            in_specs=[left_spec] * (2 * len(lefts)) + [right_spec] * 2,
            out_specs=pl.BlockSpec((inner, part), lambda k, ids: (0, k)),
        ),
        out_shape=jax.ShapeDtypeStruct((inner, width // 2), BF),
        name=name,
        cost_estimate=cost(
            2 * rows * width * inner, 4 * inner * rows + 2 * rows * width + inner * width
        ),
    )(ids, *lefts, *lefts_other, right, right_other)


def finish_kernel(in_ref, out_ref, *refs):
    at = out_ref.shape[0]
    out_ref[...] = in_ref[:at, :].astype(F32)
    for ref in refs:
        count = ref.shape[1]
        ref[...] = in_ref[at : at + count, :].astype(F32).T
        at += count


def finish(grads, sizes):
    part = grads.shape[1]
    return pl.pallas_call(
        finish_kernel,
        in_specs=[vmem_spec()],
        out_specs=[vmem_spec()] * len(sizes),
        out_shape=[jax.ShapeDtypeStruct((sizes[0], part), F32)]
        + [jax.ShapeDtypeStruct((part, size), F32) for size in sizes[1:]],
        name="finish",
        cost_estimate=cost(0, 6 * sum(sizes) * part),
    )(grads)


def together(*values):
    return lax.optimization_barrier(values)


def body(
    tokens,
    attn_gain,
    w_query,
    w_key,
    w_value,
    w_out,
    ffn_gain,
    w_gate,
    w_up,
    w_down,
    doc_lengths,
    cotangent,
):
    rows, width = tokens.shape
    wide = lax.axis_size("wide")
    narrow = lax.axis_size("narrow")
    me_wide = lax.axis_index("wide")
    me = lax.axis_index("narrow")
    core = me_wide % 2
    kv_heads = w_key.shape[1] // HD
    half_rows = rows // HALVES
    shard = rows // narrow
    part = width // wide
    hops = wide // 4
    units = w_gate.shape[1]
    q_width = w_query.shape[1]
    k_width = w_key.shape[1]
    chip_groups = [list(range(0, wide, 2)), list(range(1, wide, 2))]
    ids = jnp.stack([me, core, me_wide]).astype(jnp.int32)

    def other_core(value):
        return lax.ppermute(value, "wide", [(i, i ^ 1) for i in range(wide)])

    def chips_up(value, hop):
        return lax.ppermute(value, "wide", [(i, i + 2 * hop) for i in range(wide - 2 * hop)])

    def chips_down(value, hop):
        return lax.ppermute(value, "wide", [(i + 2 * hop, i) for i in range(wide - 2 * hop)])

    def swap(value, distance):
        return lax.ppermute(value, "narrow", [(i, i ^ distance) for i in range(narrow)])

    def rows_of(value, distance):
        return lax.dynamic_slice_in_dim(value, (me ^ distance) * shard, shard, 0)

    def exchange(pieces):
        return [pieces[0]] + [swap(pieces[d], d) for d in range(1, narrow)]

    def gather_near(value):
        return [value] + [swap(value, d) for d in range(1, narrow)]

    def scatter(value, dimension):
        return lax.psum_scatter(
            value,
            "wide",
            scatter_dimension=dimension,
            axis_index_groups=chip_groups,
            tiled=True,
        )

    gain_one = attn_gain.astype(F32)[None, :]
    gain_two = ffn_gain.astype(F32)[None, :]

    w_half = w_out.shape[0] // 2
    w_mine = lax.dynamic_slice_in_dim(w_out, core * w_half, w_half, 0)
    w_all = lax.all_gather(w_mine, "narrow", axis=0, tiled=True)

    base = me_wide * rows
    index = base + jnp.arange(rows, dtype=jnp.int32)
    start = doc_offsets(doc_lengths, index)
    angle = jnp.asarray(inverse_frequencies(HD))[:, None] * (index - start).astype(F32)[None, :]
    cosine = jnp.cos(angle)
    sine = jnp.sin(angle)
    normed, packed = keys_values(tokens, gain_one, w_key, w_value, cosine, sine)
    ups = [chips_up(packed, hop) for hop in range(1, hops + 1)]
    beside = other_core(packed)
    query_t = rotate_t(dims(w_query, normed, 0, 1), cosine, sine).astype(BF)
    d_act = dims(cotangent, w_down, 1, 1)
    cot_other = other_core(cotangent)
    normed_other = other_core(normed)
    ups, query_t, d_act = together(ups, query_t, d_act)
    blocks = [packed, beside]
    for near in ups:
        blocks += [near, other_core(near)]

    outs, mixes, lses = [], [], []
    filled = None
    gathered = None
    for half in range(HALVES):
        out, mixed, lse = attend(half, ids, doc_lengths, query_t, blocks, kv_heads)
        outs.append(out)
        mixes.append(mixed)
        lses.append(lse)
        waiting = gathered
        if waiting is not None:
            waiting, mixed, w_all = together(waiting, mixed, w_all)
            out_weights = [w_all, other_core(w_all)]
        query_t, mixed = together(query_t, mixed)
        gathered = gather_near(mixed)
        if waiting is not None:
            filled = attn_out(half - 1, ids, tokens, gain_two, waiting, out_weights, filled)
            gathered, filled = together(gathered, filled)
    hidden_one, normed_two = attn_out(
        HALVES - 1, ids, tokens, gain_two, gathered, out_weights, filled
    )

    act, d_gate, d_up = ffn_forward(normed_two, d_act, w_gate, w_up)
    act_other = other_core(act)
    d_gates = [d_gate, other_core(d_gate)]
    d_ups = [d_up, other_core(d_up)]
    normed_two_other = other_core(normed_two)
    grad_down = grad_down_of(ids, act, act_other, cotangent, cot_other, part)
    d_gate_then, _ = together(d_gate, grad_down)
    grad_down = scatter(grad_down, 1)
    d_norm_pieces = pair_nt(narrow, ids, d_gate_then, d_up, w_gate, w_up)
    normed_two_then, d_norm_pieces = together(normed_two, d_norm_pieces)
    d_norm_pieces = exchange(d_norm_pieces)
    grad_gate_up = grad_in_of(ids, normed_two_then, normed_two_other, d_gates, d_ups, part)
    act_then, _ = together(act, grad_gate_up)
    ffn_pieces = down_of(narrow, ids, act_then, w_down)
    mixed_others = [other_core(m) for m in mixes]
    d_norm_pieces, ffn_pieces, mixed_others = together(d_norm_pieces, ffn_pieces, mixed_others)
    grad_gate_up = scatter(grad_gate_up, 0)

    d_hidden, d_hidden_b, gain_two_part, *made = norm_two_back(
        ids,
        doc_lengths,
        hidden_one,
        cotangent,
        gain_two,
        d_norm_pieces,
        out_weights,
        ffn_pieces[1:],
    )
    d_mixed, travel = made[:narrow], made[narrow:]
    d_mixed = exchange(d_mixed)
    d_mixed, travel = together(d_mixed, travel)
    travel = [swap(value, d + 1) for d, value in enumerate(travel)]

    d_query_r, d_blocks = attend_back(
        ids, doc_lengths, query_t, d_mixed, outs, lses, blocks, kv_heads
    )
    d_query_r, d_blocks, travel[:-1] = together(d_query_r, d_blocks, travel[:-1])
    d_blocks = d_blocks.reshape(2 * (hops + 1), 2 * k_width, rows)
    for_other = other_core(d_blocks[1::2])
    both = [
        d_blocks[2 * hop].astype(F32) + for_other[hop].astype(F32) for hop in range(hops + 1)
    ]
    down = chips_down(both[hops].astype(BF), 1)
    for hop in range(hops - 1, 0, -1):
        down = chips_down((both[hop] + down.astype(F32)).astype(BF), 1)
    d_kv = both[0]

    d_query = rotate_t(d_query_r * (1.0 / math.sqrt(HD)), cosine, -sine).astype(BF)
    (d_hidden_full,) = in_order(ids, [d_hidden_b, *travel], 1)
    grad_query = grad_proj_of(
        ids, [d_query], [other_core(d_query)], normed, normed_other, part, "grad_query"
    )
    grad_out = grad_proj_of(
        ids, mixes, mixed_others, d_hidden_full, other_core(d_hidden_full), part, "grad_out"
    )
    down, grad_out, grad_query, grad_down = together(down, grad_out, grad_query, grad_down)
    d_kv = d_kv + down.astype(F32)
    d_keys = rotate_t(d_kv[:k_width], cosine, -sine).astype(BF)
    d_values = d_kv[k_width:].astype(BF)
    norm_one_part = (
        dims(d_query, w_query, 0, 1) + dims(d_keys, w_key, 0, 1) + dims(d_values, w_value, 0, 1)
    ).astype(BF)
    norm_one_pieces = [rows_of(norm_one_part, d) for d in range(narrow)]
    d_pair = jnp.concatenate([d_keys, d_values], axis=0)
    d_pair, norm_one_pieces = together(d_pair, norm_one_pieces)
    norm_one_pieces = exchange(norm_one_pieces)
    grad_pair = grad_proj_of(
        ids, [d_pair], [other_core(d_pair)], normed, normed_other, part, "grad_key_value"
    )
    grads = jnp.concatenate([grad_out, grad_query, grad_pair], axis=0)
    norm_one_pieces, grads = together(norm_one_pieces, grads)
    last, gain_one_part = last_rows(
        ids,
        tokens,
        hidden_one,
        d_hidden,
        gain_one,
        norm_one_pieces,
        [ffn_pieces[0], *travel],
    )
    last_pieces = gather_near(last)
    gains = jnp.concatenate([gain_one_part, gain_two_part], axis=0)
    grads, grad_gate_up, last_pieces[1:-1] = together(grads, grad_gate_up, last_pieces[1:-1])
    grads = scatter(grads, 1)
    input_grad, output = in_order(ids, last_pieces, 2)
    gains, output = together(gains, output)
    gains = sum(gather_near(gains)[1:], gains)
    gains = gains + other_core(gains)
    gain_sum = 0.0
    for hop in range(wide // 2):
        target = lax.rem(me_wide + 2 * hop, wide)
        piece = lax.dynamic_slice_in_dim(gains, target * part, part, 1)
        if hop:
            piece = lax.ppermute(piece, "wide", [(i, (i + 2 * hop) % wide) for i in range(wide)])
        gain_sum = gain_sum + piece
    gains = gain_sum
    grad_gate = grad_gate_up[:, :units].astype(F32)
    grad_up = grad_gate_up[:, units:].astype(F32)
    grad_down = grad_down.astype(F32)
    grads, gains, input_grad, output, grad_gate, grad_up, grad_down = together(
        grads, gains, input_grad, output, grad_gate, grad_up, grad_down
    )
    grad_out, grad_query, grad_key, grad_value = finish(
        grads, (w_out.shape[0], q_width, k_width, k_width)
    )
    return (
        output,
        input_grad,
        gains[0],
        grad_query,
        grad_key,
        grad_value,
        grad_out,
        gains[1],
        grad_gate,
        grad_up,
        grad_down,
    )


def solution(mesh):
    in_specs = (
        P("wide", None),
        P(),
        P(None, "narrow"),
        P(None, "narrow"),
        P(None, "narrow"),
        P("narrow", None),
        P(),
        P(None, "narrow"),
        P(None, "narrow"),
        P("narrow", None),
        P(),
        P("wide", None),
    )
    out_specs = (
        P("wide", None),
        P("wide", None),
        P("wide"),
        P("wide", "narrow"),
        P("wide", "narrow"),
        P("wide", "narrow"),
        P("narrow", "wide"),
        P("wide"),
        P("wide", "narrow"),
        P("wide", "narrow"),
        P("narrow", "wide"),
    )
    return jax.shard_map(body, mesh=mesh, in_specs=in_specs, out_specs=out_specs, check_vma=False)
```

time: 579 us -> 439 us (0.76)
  blocking collectives: 78 us -> 0 us
  Pallas kernels: 77.3 us -> 150 us
  waiting for transfers between devices: 231 us -> 179 us
  local copies, waits for them, and re-layouts: 43.6 us -> 14.7 us
  other arithmetic: 41.4 us -> 15.5 us
  matrix products: 38.7 us -> 13.9 us
    psum x1 -> x0, blocking collectives: 78 us -> none  [body(): lax.psum(jnp.stack([gain_one_part, gain_two_part]), ('wide', 'narrow'))]
    reduce_scatter x4 -> x3, waiting for transfers between devices: 76.9 us -> 4.65 us  [scatter(): lax.psum_scatter(value, 'wide', scatter_dimension=dimension, axis_index_g...]
    pallas_call x5 -> x18, Pallas kernels: 61.4 us -> 133 us  [the longest x1 15.9 us: grad_in_of(): pl.pallas_call(functools.partial(grad_in_kernel, blocks, half), grid_spec...]
    dot_general x5 -> x0, matrix products: 16.1 us -> none  [the longest x1 8.06 us: body(): ffn_part = jnp.dot(act, w_down, preferred_element_type=F32).astype(BF)]
    dynamic_update_slice x9 -> x0, local copies, waits for them, and re-layouts: 12.8 us -> none  [in_order(): lax.dynamic_update_slice_in_dim(out, pieces[distance], (me ^ distance) *...]
    ppermute x2, waiting for transfers between devices: 17.9 us -> 28.5 us  [chips_down(): lax.ppermute(value, 'wide', [(i + 2 * hop, i) for i in range(wide - 2 * h...]
    dot_general x9 -> x5, matrix products: 22.6 us -> 13.9 us  [dims(): lax.dot_general(left, right, (((a,), (b,)), ((), ())), preferred_element_...]
    unnamed x109 -> x80, local copies, waits for them, and re-layouts: 14.4 us -> 6.8 us
  transfers between devices with their start and end apart: 45 -> 52, of which waited for: 24 -> 28; matrix products, arithmetic and copies ran while one was open for 14% -> 8% of each run, Pallas kernels for 6% -> 32%
where the time goes in v3:
time: 439 us; the launch traced here: 435 us
  waiting for transfers between devices  179 us (41%)
  Pallas kernels  150 us (34%)
  starting transfers between devices  47.1 us (11%)
  other arithmetic  15.5 us (4%)
  local copies, waits for them, and re-layouts  14.7 us (3%)
  between operations  14.6 us (3%)
  matrix products  13.9 us (3%)
    ppermute x24, waiting for transfers between devices, swap(): lax.ppermute(value, 'narrow', [(i, i ^ distance) for i in range(narrow)])  131 us
    ppermute x2, waiting for transfers between devices, chips_down(): lax.ppermute(value, 'wide', [(i + 2 * hop, i) for i in range(wide - 2 * h...  28.5 us
    ppermute x24, starting transfers between devices, swap(): lax.ppermute(value, 'narrow', [(i, i ^ distance) for i in range(narrow)])  28.1 us
    pallas_call x1, Pallas kernels, ffn_forward(): pl.pallas_call(ffn_kernel, grid=(units // step,), in_specs=[pl.BlockSpec(...  16.1 us
    pallas_call x1, Pallas kernels, grad_in_of(): pl.pallas_call(functools.partial(grad_in_kernel, blocks, half), grid_spec...  15.9 us
    pallas_call x3, Pallas kernels, grad_proj_of(): pl.pallas_call(functools.partial(grad_proj_kernel, len(lefts)), grid_spec...  15.7 us
    pallas_call x2, Pallas kernels, attn_out(): pl.pallas_call(functools.partial(attn_out_kernel, len(mixes)), grid=(1,),...  14.8 us
    pallas_call x1, Pallas kernels, pair_nt(): pl.pallas_call(pair_nt_kernel, grid=(width // step,), in_specs=[smem_spec...  14 us
  transfers between devices with their start and end apart: 52, of which 28 were waited for; matrix products, arithmetic and copies ran while one was open for 8% of the time, Pallas kernels for 32%

profile of v3, /device:TPU:0, one launch (start us, length us, event | category | flops | bytes accessed | tf_op | source)
XLA Modules:
  0.0 434.8 jit_solution(5832318754600278899)
XLA Ops:
  16.5 5.5 %collective-permute-start.1 = (bf16[256,512]{1,0:T(8,128)(2,1)}, bf16[256,512]{1,0:T(8,128)(2,1)S(1)}, u32[]{:S(2)}, u32[]{:S(2)}) collective-permute-start(bf16[256,512]{1,0:T(8,128)(2,1)} %get-tuple-element.129.refs_0_.refs_6_.refs_8_.refs_14_), channel_id=1, source_target_pairs={{0,16},{4,20},{8,24},{12,28},{1,17},{5,21},{9,25},{13,29},{2,18},{... | collective-permute-start | bytes 786440 | tf_op jit(solution)/shard_map/ppermute | solution.py:921
  30.7 6.1 %fusion.12.da_ref = f32[512,2048]{1,0:T(8,128)} fusion(bf16[512,2048]{1,0:T(8,128)(2,1)S(1)} %copy-done.1, bf16[2048,2048]{1,0:T(8,128)(2,1)S(1)} %copy-done.31), kind=kOutput, calls=%fused_computation.51 | convolution fusion | flops 4294967296 | bytes 14680064 | tf_op jit(solution)/shard_map/dot_general | solution.py:53
  49.6 6.2 %attend.3 = (f32[512,256]{1,0:T(8,128)}, bf16[512,256]{1,0:T(8,128)(2,1)}, f32[2,4,256]{2,1,0:T(4,128)}) custom-call(s32[3]{0:T(128)} %pad_add_fusion.ids_ref, s32[12]{0:T(128)} %lengths_ref.7, bf16[512,512]{1,0:T(8,128)(2,1)} %bitcast.61, bf16[256,512]{1,0:T(8,128)(2,1)} %get-tuple-element.129.refs_0_.refs_6_.refs_8_.refs_14_, bf16[256,512]{1,0:T(8,128)(2,1)} %copy-done.32, ...), custom_call_target="tpu_custom_call" | custom-call | flops 1073741824 | bytes 2097152 | tf_op jit(solution)/shard_map/attend/pallas_call | solution.py:241
  55.8 6.0 %collective-permute-done.7.refs_3_ = bf16[512,256]{1,0:T(8,128)(2,1)S(1)} collective-permute-done((bf16[512,256]{1,0:T(8,128)(2,1)}, bf16[512,256]{1,0:T(8,128)(2,1)S(1)}, u32[]{:S(2)}, u32[]{:S(2)}) %collective-permute-start.7) | collective-permute-done | bytes 262176 | tf_op jit(solution)/shard_map/ppermute | solution.py:927
  61.8 6.6 %collective-permute-done.6.refs_2_ = bf16[512,256]{1,0:T(8,128)(2,1)S(1)} collective-permute-done((bf16[512,256]{1,0:T(8,128)(2,1)}, bf16[512,256]{1,0:T(8,128)(2,1)S(1)}, u32[]{:S(2)}, u32[]{:S(2)}) %collective-permute-start.6) | collective-permute-done | bytes 262176 | tf_op jit(solution)/shard_map/ppermute | solution.py:927
  84.7 7.4 %attn_out.2 = (f32[512,2048]{1,0:T(8,128)}, bf16[512,2048]{1,0:T(8,128)(2,1)}) custom-call(s32[3]{0:T(128)} %pad_add_fusion.ids_ref, bf16[512,2048]{1,0:T(8,128)(2,1)} %x_ref.7, f32[1,2048]{1,0:T(1,128)} %bitcast.63, bf16[512,256]{1,0:T(8,128)(2,1)} %get-tuple-element.141.refs_0_, bf16[512,256]{1,0:T(8,128)(2,1)} %copy-done.24, bf16[512,256]{1,0:T(8,128)(2,1)} %copy-done.23, ...), custom_call_target="tpu_custom_call" | custom-call | flops 2147483648 | bytes 14680064 | tf_op jit(solution)/shard_map/attn_out/pallas_call | solution.py:466
  93.4 7.4 %attn_out.3 = (f32[512,2048]{1,0:T(8,128)}, bf16[512,2048]{1,0:T(8,128)(2,1)}) custom-call(s32[3]{0:T(128)} %pad_add_fusion.ids_ref, bf16[512,2048]{1,0:T(8,128)(2,1)} %x_ref.7, f32[1,2048]{1,0:T(1,128)} %bitcast.64, bf16[512,256]{1,0:T(8,128)(2,1)} %get-tuple-element.148.refs_0_.refs_1_, ...), custom_call_target="tpu_custom_call", output_to_operand_aliasing={{0}: (9, {}), {1}: (10, {})} | custom-call | flops 2147483648 | bytes 14680064 | tf_op jit(solution)/shard_map/attn_out/pallas_call | solution.py:466
  100.8 16.1 %gate_up.1 = (bf16[512,2048]{1,0:T(8,128)(2,1)}, bf16[512,2048]{1,0:T(8,128)(2,1)}, bf16[512,2048]{1,0:T(8,128)(2,1)}) custom-call(bf16[512,2048]{1,0:T(8,128)(2,1)} %get-tuple-element.169.n_ref.refs_0_.refs_1_.refs_2_.refs_3_, f32[512,2048]{1,0:T(8,128)} %fusion.12.da_ref, bf16[2048,2048]{1,0:T(8,128)(2,1)} %wa_ref.1, bf16[2048,2048]{1,0:T(8,128)(2,1)} %wb_ref.1), custom_call_target="tpu_custom_call" | custom-call | flops 8589934592 | bytes 29360128 | tf_op jit(solution)/shard_map/gate_up/pallas_call | solution.py:646
  121.4 9.4 %grad_down.1 = bf16[2048,1024]{1,0:T(8,128)(2,1)} custom-call(s32[3]{0:T(128)} %pad_add_fusion.ids_ref, bf16[512,2048]{1,0:T(8,128)(2,1)} %get-tuple-element.170.own_ref.a_ref, bf16[512,2048]{1,0:T(8,128)(2,1)} %collective-permute-done.12.other_ref, bf16[512,2048]{1,0:T(8,128)(2,1)} %cot_ref.1, bf16[512,2048]{1,0:T(8,128)(2,1)} %cot_ref.1, ...), custom_call_target="tpu_custom_call" | custom-call | flops 4294967296 | bytes 10485760 | tf_op jit(solution)/shard_map/grad_down/pallas_call | solution.py:759
  131.6 14.0 %d_normed_two.1 = (bf16[128,2048]{1,0:T(8,128)(2,1)}, bf16[128,2048]{1,0:T(8,128)(2,1)}, bf16[128,2048]{1,0:T(8,128)(2,1)}, bf16[128,2048]{1,0:T(8,128)(2,1)}) custom-call(s32[3]{0:T(128)} %pad_add_fusion.ids_ref, bf16[512,2048]{1,0:T(8,128)(2,1)} %get-tuple-element.159.a_ref.refs_8_, bf16[512,2048]{1,0:T(8,128)(2,1)} %get-tuple-element.160.b_ref.refs_10_, ...), custom_call_target="tpu_custom_call" | custom-call | flops 8589934592 | bytes 23068672 | tf_op jit(solution)/shard_map/d_normed_two/pallas_call | solution.py:680
  145.6 15.9 %grad_gate_up.1 = bf16[1024,4096]{1,0:T(8,128)(2,1)} custom-call(s32[3]{0:T(128)} %pad_add_fusion.ids_ref, bf16[512,2048]{1,0:T(8,128)(2,1)} %get-tuple-element.169.n_ref.refs_0_.refs_1_.refs_2_.refs_3_, bf16[512,2048]{1,0:T(8,128)(2,1)} %get-tuple-element.169.n_ref.refs_0_.refs_1_.refs_2_.refs_3_, ...), custom_call_target="tpu_custom_call" | custom-call | flops 8589934592 | bytes 18874368 | tf_op jit(solution)/shard_map/grad_gate_up/pallas_call | solution.py:804
  165.7 9.1 %ffn_down.1 = (bf16[128,2048]{1,0:T(8,128)(2,1)}, bf16[256,2048]{1,0:T(8,128)(2,1)}, bf16[256,2048]{1,0:T(8,128)(2,1)}, bf16[256,2048]{1,0:T(8,128)(2,1)}) custom-call(s32[3]{0:T(128)} %pad_add_fusion.ids_ref, bf16[512,2048]{1,0:T(8,128)(2,1)} %get-tuple-element.170.own_ref.a_ref, bf16[2048,2048]{1,0:T(8,128)(2,1)} %w_ref.1), custom_call_target="tpu_custom_call" | custom-call | flops 4294967296 | bytes 12582912 | tf_op jit(solution)/shard_map/ffn_down/pallas_call | solution.py:704
  176.6 12.0 %collective-permute-done.15.refs_2_ = bf16[128,2048]{1,0:T(8,128)(2,1)} collective-permute-done((bf16[128,2048]{1,0:T(8,128)(2,1)}, bf16[128,2048]{1,0:T(8,128)(2,1)}, u32[]{:S(2)}, u32[]{:S(2)}) %collective-permute-start.15) | collective-permute-done | bytes 524320 | tf_op jit(solution)/shard_map/ppermute | solution.py:927
  188.6 10.8 %norm_two_back.1 = (f32[128,2048]{1,0:T(8,128)}, bf16[128,2048]{1,0:T(8,128)(2,1)}, f32[1,2048]{1,0:T(1,128)}, bf16[128,512]{1,0:T(8,128)(2,1)}, bf16[128,512]{1...) custom-call(s32[3]{0:T(128)} %pad_add_fusion.ids_ref, ...), custom_call_target="tpu_custom_call", output_to_operand_aliasing={{7}: (11, {}), {8}: (12, {}), {9}: (13, {})} | custom-call | flops 1073741824 | bytes 14680064 | tf_op jit(solution)/shard_map/norm_two_back/pallas_call | solution.py:538
  212.3 11.6 %attend_back.1 = (f32[512,512]{1,0:T(8,128)}, bf16[6,2,128,512]{3,2,1,0:T(8,128)(2,1)}) custom-call(s32[3]{0:T(128)} %pad_add_fusion.ids_ref, s32[12]{0:T(128)} %lengths_ref.7, bf16[512,512]{1,0:T(8,128)(2,1)} %bitcast.62, bf16[128,512]{1,0:T(8,128)(2,1)} %get-tuple-element.189.refs_0_, bf16[128,512]{1,0:T(8,128)(2,1)} %copy-done.37, ...), custom_call_target="tpu_custom_call" | custom-call | flops 5368709120 | bytes 4194304 | tf_op jit(solution)/shard_map/attend_back/pallas_call | solution.py:391
  223.9 11.2 %collective-permute-done.25.refs_1_.refs_5_ = bf16[256,2048]{1,0:T(8,128)(2,1)S(1)} collective-permute-done((bf16[256,2048]{1,0:T(8,128)(2,1)}, bf16[256,2048]{1,0:T(8,128)(2,1)S(1)}, u32[]{:S(2)}, u32[]{:S(2)}) %collective-permute-start.25) | collective-permute-done | bytes 1048608 | tf_op jit(solution)/shard_map/ppermute | solution.py:927
  237.6 18.1 %collective-permute-done.30.refs_3_.refs_7_ = bf16[256,2048]{1,0:T(8,128)(2,1)} collective-permute-done((bf16[256,2048]{1,0:T(8,128)(2,1)}, bf16[256,2048]{1,0:T(8,128)(2,1)}, u32[]{:S(2)}, u32[]{:S(2)}) %collective-permute-start.30) | collective-permute-done | bytes 1048608 | tf_op jit(solution)/shard_map/ppermute | solution.py:927
  263.7 22.2 %collective-permute-done.28 = bf16[256,512]{1,0:T(8,128)(2,1)S(1)} collective-permute-done((bf16[256,512]{1,0:T(8,128)(2,1)S(1)}, bf16[256,512]{1,0:T(8,128)(2,1)S(1)}, u32[]{:S(2)}, u32[]{:S(2)}) %collective-permute-start.28) | collective-permute-done | bytes 262176 | tf_op jit(solution)/shard_map/ppermute | solution.py:924
  293.3 5.4 %grad_query.1 = bf16[512,1024]{1,0:T(8,128)(2,1)} custom-call(s32[3]{0:T(128)} %pad_add_fusion.ids_ref, bf16[512,512]{1,0:T(8,128)(2,1)} %bitcast.53, bf16[512,512]{1,0:T(8,128)(2,1)} %copy-done.17, bf16[512,2048]{1,0:T(8,128)(2,1)} %get-tuple-element.130.refs_2_, bf16[512,2048]{1,0:T(8,128)(2,1)} %collective-permute-done.33.refs_3_), custom_call_target="tpu_custom_call" | custom-call | flops 1073741824 | bytes 4194304 | tf_op jit(solution)/shard_map/grad_query/pallas_call | solution.py:844
  304.1 6.3 %collective-permute-done.29 = bf16[256,512]{1,0:T(8,128)(2,1)} collective-permute-done((bf16[256,512]{1,0:T(8,128)(2,1)}, bf16[256,512]{1,0:T(8,128)(2,1)}, u32[]{:S(2)}, u32[]{:S(2)}) %collective-permute-start.29) | collective-permute-done | bytes 262176 | tf_op jit(solution)/shard_map/ppermute | solution.py:924
  331.3 11.7 %collective-permute-done.35.refs_2_ = bf16[128,2048]{1,0:T(8,128)(2,1)} collective-permute-done((bf16[128,2048]{1,0:T(8,128)(2,1)}, bf16[128,2048]{1,0:T(8,128)(2,1)}, u32[]{:S(2)}, u32[]{:S(2)}) %collective-permute-start.35) | collective-permute-done | bytes 524320 | tf_op jit(solution)/shard_map/ppermute | solution.py:927
  343.1 6.2 %last_rows.1 = (bf16[256,2048]{1,0:T(8,128)(2,1)}, f32[1,2048]{1,0:T(1,128)}) custom-call(s32[3]{0:T(128)} %pad_add_fusion.ids_ref, bf16[512,2048]{1,0:T(8,128)(2,1)} %x_ref.7, f32[512,2048]{1,0:T(8,128)} %get-tuple-element.154.hidden_ref, f32[128,2048]{1,0:T(8,128)} %get-tuple-element.218.add_ref, f32[1,2048]{1,0:T(1,128)} %bitcast.67, ...), custom_call_target="tpu_custom_call" | custom-call | flops 7864320 | bytes 8388608 | tf_op jit(solution)/shard_map/last_rows/pallas_call | solution.py:587
  351.1 22.9 %collective-permute-done.39.refs_2_ = bf16[256,2048]{1,0:T(8,128)(2,1)} collective-permute-done((bf16[256,2048]{1,0:T(8,128)(2,1)}, bf16[256,2048]{1,0:T(8,128)(2,1)}, u32[]{:S(2)}, u32[]{:S(2)}) %collective-permute-start.39) | collective-permute-done | bytes 1048608 | tf_op jit(solution)/shard_map/ppermute | solution.py:927
  376.8 22.9 %collective-permute-done.40.refs_3_ = bf16[256,2048]{1,0:T(8,128)(2,1)} collective-permute-done((bf16[256,2048]{1,0:T(8,128)(2,1)}, bf16[256,2048]{1,0:T(8,128)(2,1)}, u32[]{:S(2)}, u32[]{:S(2)}) %collective-permute-start.40) | collective-permute-done | bytes 1048608 | tf_op jit(solution)/shard_map/ppermute | solution.py:927
  (222 shorter events, 149.2 us)
Async XLA Ops:
  7.2 69.9 %all-gather.2.cloned.1.call-start = ((), (), s32[]{:S(2)}) async-start(), calls=%async_computation.3 | async-start | bytes 5242880 | tf_op jit(solution)/shard_map/all_gather | solution.py:952
  9.8 300.6 %reduce-scatter.4.cloned.1.call-start = ((), (), s32[]{:S(2)}) async-start(), calls=%async_computation.4 | async-start | bytes 5242880 | tf_op jit(solution)/shard_map/reduce_scatter | solution.py:939
  16.0 23.0 %collective-permute-start.2 = (bf16[256,512]{1,0:T(8,128)(2,1)}, bf16[256,512]{1,0:T(8,128)(2,1)S(1)}, u32[]{:S(2)}, u32[]{:S(2)}) collective-permute-start(bf16[256,512]{1,0:T(8,128)(2,1)} %get-tuple-element.129.refs_0_.refs_6_.refs_8_.refs_14_), channel_id=1, source_target_pairs={{0,4},{4,0},{8,12},{12,8},{16,20},{20,16},{24,28},{28,24},{1,5},{5... | collective-permute-start | bytes 786440 | tf_op jit(solution)/shard_map/ppermute | solution.py:918
  16.5 21.4 %collective-permute-start.1 = (bf16[256,512]{1,0:T(8,128)(2,1)}, bf16[256,512]{1,0:T(8,128)(2,1)S(1)}, u32[]{:S(2)}, u32[]{:S(2)}) collective-permute-start(bf16[256,512]{1,0:T(8,128)(2,1)} %get-tuple-element.129.refs_0_.refs_6_.refs_8_.refs_14_), channel_id=1, source_target_pairs={{0,16},{4,20},{8,24},{12,28},{1,17},{5,21},{9,25},{13,29},{2,18},{... | collective-permute-start | bytes 786440 | tf_op jit(solution)/shard_map/ppermute | solution.py:921
  49.1 24.1 %collective-permute-start.5 = (bf16[512,256]{1,0:T(8,128)(2,1)}, bf16[512,256]{1,0:T(8,128)(2,1)S(1)}, u32[]{:S(2)}, u32[]{:S(2)}) collective-permute-start(bf16[512,256]{1,0:T(8,128)(2,1)} %get-tuple-element.141.refs_0_), channel_id=1, source_target_pairs={{0,1},{1,0},{2,3},{3,2},{4,5},{5,4},{6,7},{7,6},{8,9},{9,8},{10,11... | collective-permute-start | bytes 786440 | tf_op jit(solution)/shard_map/ppermute | solution.py:927
  80.6 36.3 %collective-permute-start.13 = (bf16[512,2048]{1,0:T(8,128)(2,1)}, bf16[512,2048]{1,0:T(8,128)(2,1)}, u32[]{:S(2)}, u32[]{:S(2)}) collective-permute-start(bf16[512,2048]{1,0:T(8,128)(2,1)} %cot_ref.1), channel_id=1, source_target_pairs={{0,4},{4,0},{8,12},{12,8},{16,20},{20,16},{24,28},{28,24},{1,5},{5... | collective-permute-start | bytes 6291464 | tf_op jit(solution)/shard_map/ppermute | solution.py:918
  130.8 244.4 %reduce-scatter.6.cloned.1.call-start = ((), (), s32[]{:S(2)}) async-start(), calls=%async_computation.5 | async-start | bytes 10485760 | tf_op jit(solution)/shard_map/reduce_scatter | solution.py:939
  161.5 263.6 %reduce-scatter.8.cloned.1.call-start = ((), (), s32[]{:S(2)}) async-start(), calls=%async_computation.6 | async-start | bytes 3276800 | tf_op jit(solution)/shard_map/reduce_scatter | solution.py:939
  163.2 25.4 %collective-permute-start.15 = (bf16[128,2048]{1,0:T(8,128)(2,1)}, bf16[128,2048]{1,0:T(8,128)(2,1)}, u32[]{:S(2)}, u32[]{:S(2)}) collective-permute-start(bf16[128,2048]{1,0:T(8,128)(2,1)} %get-tuple-element.167), channel_id=1, source_target_pairs={{0,2},{1,3},{2,0},{3,1},{4,6},{5,7},{6,4},{7,5},{8,10},{9,11},{10,... | collective-permute-start | bytes 1572872 | tf_op jit(solution)/shard_map/ppermute | solution.py:927
  164.2 24.4 %collective-permute-start.16 = (bf16[128,2048]{1,0:T(8,128)(2,1)}, bf16[128,2048]{1,0:T(8,128)(2,1)}, u32[]{:S(2)}, u32[]{:S(2)}) collective-permute-start(bf16[128,2048]{1,0:T(8,128)(2,1)} %get-tuple-element.168), channel_id=1, source_target_pairs={{0,3},{1,2},{2,1},{3,0},{4,7},{5,6},{6,5},{7,4},{8,11},{9,10},{10,... | collective-permute-start | bytes 1572872 | tf_op jit(solution)/shard_map/ppermute | solution.py:927
  208.8 26.3 %collective-permute-start.25 = (bf16[256,2048]{1,0:T(8,128)(2,1)}, bf16[256,2048]{1,0:T(8,128)(2,1)S(1)}, u32[]{:S(2)}, u32[]{:S(2)}) collective-permute-start(bf16[256,2048]{1,0:T(8,128)(2,1)} %get-tuple-element.199), channel_id=1, source_target_pairs={{0,1},{1,0},{2,3},{3,2},{4,5},{5,4},{6,7},{7,6},{8,9},{9,8},{10,11... | collective-permute-start | bytes 3145736 | tf_op jit(solution)/shard_map/ppermute | solution.py:927
  209.7 25.6 %collective-permute-start.26 = (bf16[256,2048]{1,0:T(8,128)(2,1)}, bf16[256,2048]{1,0:T(8,128)(2,1)}, u32[]{:S(2)}, u32[]{:S(2)}) collective-permute-start(bf16[256,2048]{1,0:T(8,128)(2,1)} %get-tuple-element.200), channel_id=1, source_target_pairs={{0,2},{1,3},{2,0},{3,1},{4,6},{5,7},{6,4},{7,5},{8,10},{9,11},{10,... | collective-permute-start | bytes 3145736 | tf_op jit(solution)/shard_map/ppermute | solution.py:927
  211.0 44.8 %collective-permute-start.30 = (bf16[256,2048]{1,0:T(8,128)(2,1)}, bf16[256,2048]{1,0:T(8,128)(2,1)}, u32[]{:S(2)}, u32[]{:S(2)}) collective-permute-start(bf16[256,2048]{1,0:T(8,128)(2,1)} %get-tuple-element.207), channel_id=1, source_target_pairs={{0,3},{1,2},{2,1},{3,0},{4,7},{5,6},{6,5},{7,4},{8,11},{9,10},{10,... | collective-permute-start | bytes 3145736 | tf_op jit(solution)/shard_map/ppermute | solution.py:927
  212.3 80.2 %collective-permute-start.33 = (bf16[512,2048]{1,0:T(8,128)(2,1)}, bf16[512,2048]{1,0:T(8,128)(2,1)}, u32[]{:S(2)}, u32[]{:S(2)}) collective-permute-start(bf16[512,2048]{1,0:T(8,128)(2,1)} %get-tuple-element.130.refs_2_), channel_id=1, source_target_pairs={{0,4},{4,0},{8,12},{12,8},{16,20},{20,16},{24,28},{28,24},{1,5},{5... | collective-permute-start | bytes 6291464 | tf_op jit(solution)/shard_map/ppermute | solution.py:918
  237.6 23.2 %collective-permute-start.27 = (bf16[3,256,512]{2,1,0:T(8,128)(2,1)}, bf16[3,256,512]{2,1,0:T(8,128)(2,1)}, u32[]{:S(2)}, u32[]{:S(2)}) collective-permute-start(bf16[3,256,512]{2,1,0:T(8,128)(2,1)} %slice.64), channel_id=1, source_target_pairs={{0,4},{4,0},{8,12},{12,8},{16,20},{20,16},{24,28},{28,24},{1,5},{5... | collective-permute-start | bytes 2359304 | tf_op jit(solution)/shard_map/ppermute | solution.py:918
  259.3 39.4 %collective-permute-start.31 = (bf16[512,2048]{1,0:T(8,128)(2,1)}, bf16[512,2048]{1,0:T(8,128)(2,1)}, u32[]{:S(2)}, u32[]{:S(2)}) collective-permute-start(bf16[512,2048]{1,0:T(8,128)(2,1)} %token_order.2.refs_4_), channel_id=1, source_target_pairs={{0,4},{4,0},{8,12},{12,8},{16,20},{20,16},{24,28},{28,24},{1,5},{5... | collective-permute-start | bytes 6291464 | tf_op jit(solution)/shard_map/ppermute | solution.py:918
  261.9 24.1 %collective-permute-start.28 = (bf16[256,512]{1,0:T(8,128)(2,1)S(1)}, bf16[256,512]{1,0:T(8,128)(2,1)S(1)}, u32[]{:S(2)}, u32[]{:S(2)}) collective-permute-start(bf16[256,512]{1,0:T(8,128)(2,1)S(1)} %fusion), channel_id=1, source_target_pairs={{8,0},{12,4},{16,8},{20,12},{24,16},{28,20},{9,1},{13,5},{17,9},{2... | collective-permute-start | bytes 786440 | tf_op jit(solution)/shard_map/ppermute | solution.py:924
  263.4 29.1 %collective-permute-start.32 = (bf16[512,512]{1,0:T(8,128)(2,1)S(1)}, bf16[512,512]{1,0:T(8,128)(2,1)S(1)}, u32[]{:S(2)}, u32[]{:S(2)}) collective-permute-start(bf16[512,512]{1,0:T(8,128)(2,1)S(1)} %bitcast.51), channel_id=1, source_target_pairs={{0,4},{4,0},{8,12},{12,8},{16,20},{20,16},{24,28},{28,24},{1,5},{5... | collective-permute-start | bytes 1572872 | tf_op jit(solution)/shard_map/ppermute | solution.py:918
  287.7 22.7 %collective-permute-start.29 = (bf16[256,512]{1,0:T(8,128)(2,1)}, bf16[256,512]{1,0:T(8,128)(2,1)}, u32[]{:S(2)}, u32[]{:S(2)}) collective-permute-start(bf16[256,512]{1,0:T(8,128)(2,1)} %fusion.2), channel_id=1, source_target_pairs={{8,0},{12,4},{16,8},{20,12},{24,16},{28,20},{9,1},{13,5},{17,9},{2... | collective-permute-start | bytes 786440 | tf_op jit(solution)/shard_map/ppermute | solution.py:924
  317.5 25.5 %collective-permute-start.35 = (bf16[128,2048]{1,0:T(8,128)(2,1)}, bf16[128,2048]{1,0:T(8,128)(2,1)}, u32[]{:S(2)}, u32[]{:S(2)}) collective-permute-start(bf16[128,2048]{1,0:T(8,128)(2,1)} %get-tuple-element.212), channel_id=1, source_target_pairs={{0,2},{1,3},{2,0},{3,1},{4,6},{5,7},{6,4},{7,5},{8,10},{9,11},{10,... | collective-permute-start | bytes 1572872 | tf_op jit(solution)/shard_map/ppermute | solution.py:927
  318.9 24.1 %collective-permute-start.36 = (bf16[128,2048]{1,0:T(8,128)(2,1)}, bf16[128,2048]{1,0:T(8,128)(2,1)}, u32[]{:S(2)}, u32[]{:S(2)}) collective-permute-start(bf16[128,2048]{1,0:T(8,128)(2,1)} %get-tuple-element.213), channel_id=1, source_target_pairs={{0,3},{1,2},{2,1},{3,0},{4,7},{5,6},{6,5},{7,4},{8,11},{9,10},{10,... | collective-permute-start | bytes 1572872 | tf_op jit(solution)/shard_map/ppermute | solution.py:927
  349.3 24.7 %collective-permute-start.39 = (bf16[256,2048]{1,0:T(8,128)(2,1)}, bf16[256,2048]{1,0:T(8,128)(2,1)}, u32[]{:S(2)}, u32[]{:S(2)}) collective-permute-start(bf16[256,2048]{1,0:T(8,128)(2,1)} %get-tuple-element.224.refs_0_), channel_id=1, source_target_pairs={{0,2},{1,3},{2,0},{3,1},{4,6},{5,7},{6,4},{7,5},{8,10},{9,11},{10,... | collective-permute-start | bytes 3145736 | tf_op jit(solution)/shard_map/ppermute | solution.py:927
  350.8 24.4 %collective-permute-start.38 = (bf16[256,2048]{1,0:T(8,128)(2,1)}, bf16[256,2048]{1,0:T(8,128)(2,1)}, u32[]{:S(2)}, u32[]{:S(2)}) collective-permute-start(bf16[256,2048]{1,0:T(8,128)(2,1)} %get-tuple-element.224.refs_0_), channel_id=1, source_target_pairs={{0,1},{1,0},{2,3},{3,2},{4,5},{5,4},{6,7},{7,6},{8,9},{9,8},{10,11... | collective-permute-start | bytes 3145736 | tf_op jit(solution)/shard_map/ppermute | solution.py:927
  375.2 24.5 %collective-permute-start.40 = (bf16[256,2048]{1,0:T(8,128)(2,1)}, bf16[256,2048]{1,0:T(8,128)(2,1)}, u32[]{:S(2)}, u32[]{:S(2)}) collective-permute-start(bf16[256,2048]{1,0:T(8,128)(2,1)} %get-tuple-element.224.refs_0_), channel_id=1, source_target_pairs={{0,3},{1,2},{2,1},{3,0},{4,7},{5,6},{6,5},{7,4},{8,11},{9,10},{10,... | collective-permute-start | bytes 3145736 | tf_op jit(solution)/shard_map/ppermute | solution.py:927
  (68 other events, 615.9 us)
Sparse Core Ops, SparseCore 0:
  10.5 66.6 all-gather.1
  130.9 76.8 reduce-scatter.3
  210.3 156.1 reduce-scatter.5
  375.3 49.7 reduce-scatter.7

commit v4 on v3

--- a/solution.py
+++ b/solution.py
@@ -979,7 +979,7 @@
         lses.append(lse)
         waiting = gathered
         if waiting is not None:
-            waiting, mixed, w_all = together(waiting, mixed, w_all)
+            waiting, mixed, w_all, normed_other = together(waiting, mixed, w_all, normed_other)
             out_weights = [w_all, other_core(w_all)]
         query_t, mixed = together(query_t, mixed)
         gathered = gather_near(mixed)
@@ -999,14 +999,17 @@
     d_gate_then, _ = together(d_gate, grad_down)
     grad_down = scatter(grad_down, 1)
     d_norm_pieces = pair_nt(narrow, ids, d_gate_then, d_up, w_gate, w_up)
-    normed_two_then, d_norm_pieces = together(normed_two, d_norm_pieces)
+    mixed_others = [other_core(m) for m in mixes]
+    act_then, d_norm_pieces, d_gates, d_ups, normed_two_other, mixed_others = together(
+        act, d_norm_pieces, d_gates, d_ups, normed_two_other, mixed_others
+    )
     d_norm_pieces = exchange(d_norm_pieces)
+    ffn_pieces = down_of(narrow, ids, act_then, w_down)
+    d_norm_pieces[1], ffn_pieces, normed_two_then = together(
+        d_norm_pieces[1], ffn_pieces, normed_two
+    )
     grad_gate_up = grad_in_of(ids, normed_two_then, normed_two_other, d_gates, d_ups, part)
-    act_then, _ = together(act, grad_gate_up)
-    ffn_pieces = down_of(narrow, ids, act_then, w_down)
-    mixed_others = [other_core(m) for m in mixes]
-    d_norm_pieces, ffn_pieces, mixed_others = together(d_norm_pieces, ffn_pieces, mixed_others)
-    grad_gate_up = scatter(grad_gate_up, 0)
+    d_norm_pieces, ffn_pieces, _ = together(d_norm_pieces, ffn_pieces, grad_gate_up)
 
     d_hidden, d_hidden_b, gain_two_part, *made = norm_two_back(
         ids,
@@ -1019,6 +1022,8 @@
         ffn_pieces[1:],
     )
     d_mixed, travel = made[:narrow], made[narrow:]
+    grad_gate_up, _ = together(grad_gate_up, d_hidden_b)
+    grad_gate_up = scatter(grad_gate_up, 0)
     d_mixed = exchange(d_mixed)
     d_mixed, travel = together(d_mixed, travel)
     travel = [swap(value, d + 1) for d, value in enumerate(travel)]
@@ -1026,7 +1031,7 @@
     d_query_r, d_blocks = attend_back(
         ids, doc_lengths, query_t, d_mixed, outs, lses, blocks, kv_heads
     )
-    d_query_r, d_blocks, travel[:-1] = together(d_query_r, d_blocks, travel[:-1])
+    d_query_r, d_blocks, travel[0] = together(d_query_r, d_blocks, travel[0])
     d_blocks = d_blocks.reshape(2 * (hops + 1), 2 * k_width, rows)
     for_other = other_core(d_blocks[1::2])
     both = [

time: 439 us -> 435 us (level)
  waiting for transfers between devices: 179 us -> 171 us
    ppermute x24, waiting for transfers between devices: 131 us -> 121 us  [swap(): lax.ppermute(value, 'narrow', [(i, i ^ distance) for i in range(narrow)])]
    reduce_scatter x3, waiting for transfers between devices: 4.65 us -> 10 us  [scatter(): lax.psum_scatter(value, 'wide', scatter_dimension=dimension, axis_index_g...]
    unnamed x80 -> x90, local copies, waits for them, and re-layouts: 6.8 us -> 8.97 us
  transfers between devices with their start and end apart: 52 -> 52, of which waited for: 28 -> 27; matrix products, arithmetic and copies ran while one was open for 8% -> 8% of each run, Pallas kernels for 32% -> 32%
where the time goes in v4:
time: 435 us; the launch traced here: 431 us
  waiting for transfers between devices  171 us (39%)
  Pallas kernels  149 us (34%)
  starting transfers between devices  50.1 us (12%)
  local copies, waits for them, and re-layouts  17.1 us (4%)
  other arithmetic  15.5 us (4%)
  between operations  14.7 us (3%)
  matrix products  14 us (3%)
    ppermute x24, waiting for transfers between devices, swap(): lax.ppermute(value, 'narrow', [(i, i ^ distance) for i in range(narrow)])  121 us
    ppermute x24, starting transfers between devices, swap(): lax.ppermute(value, 'narrow', [(i, i ^ distance) for i in range(narrow)])  29.2 us
    ppermute x2, waiting for transfers between devices, chips_down(): lax.ppermute(value, 'wide', [(i + 2 * hop, i) for i in range(wide - 2 * h...  26.2 us
    pallas_call x1, Pallas kernels, ffn_forward(): pl.pallas_call(ffn_kernel, grid=(units // step,), in_specs=[pl.BlockSpec(...  16.1 us
    pallas_call x1, Pallas kernels, grad_in_of(): pl.pallas_call(functools.partial(grad_in_kernel, blocks, half), grid_spec...  15.8 us
    pallas_call x3, Pallas kernels, grad_proj_of(): pl.pallas_call(functools.partial(grad_proj_kernel, len(lefts)), grid_spec...  15.8 us
    pallas_call x2, Pallas kernels, attn_out(): pl.pallas_call(functools.partial(attn_out_kernel, len(mixes)), grid=(1,),...  14.8 us
    pallas_call x1, Pallas kernels, pair_nt(): pl.pallas_call(pair_nt_kernel, grid=(width // step,), in_specs=[smem_spec...  14 us
  transfers between devices with their start and end apart: 52, of which 27 were waited for; matrix products, arithmetic and copies ran while one was open for 8% of the time, Pallas kernels for 32%

profile of v4, /device:TPU:0, one launch (start us, length us, event | category | flops | bytes accessed | tf_op | source)
XLA Modules:
  0.0 431.3 jit_solution(16428006568631509920)
XLA Ops:
  16.5 5.5 %collective-permute-start.1 = (bf16[256,512]{1,0:T(8,128)(2,1)}, bf16[256,512]{1,0:T(8,128)(2,1)S(1)}, u32[]{:S(2)}, u32[]{:S(2)}) collective-permute-start(bf16[256,512]{1,0:T(8,128)(2,1)} %get-tuple-element.140.refs_0_.refs_6_.refs_8_.refs_14_), channel_id=1, source_target_pairs={{0,16},{4,20},{8,24},{12,28},{1,17},{5,21},{9,25},{13,29},{2,18},{... | collective-permute-start | bytes 786440 | tf_op jit(solution)/shard_map/ppermute | solution.py:921
  30.7 6.2 %fusion.12.da_ref = f32[512,2048]{1,0:T(8,128)} fusion(bf16[512,2048]{1,0:T(8,128)(2,1)S(1)} %copy-done.1, bf16[2048,2048]{1,0:T(8,128)(2,1)S(1)} %copy-done.33), kind=kOutput, calls=%fused_computation.51 | convolution fusion | flops 4294967296 | bytes 14680064 | tf_op jit(solution)/shard_map/dot_general | solution.py:53
  49.7 6.2 %attend.3 = (f32[512,256]{1,0:T(8,128)}, bf16[512,256]{1,0:T(8,128)(2,1)}, f32[2,4,256]{2,1,0:T(4,128)}) custom-call(s32[3]{0:T(128)} %pad_add_fusion.ids_ref, s32[12]{0:T(128)} %lengths_ref.7, bf16[512,512]{1,0:T(8,128)(2,1)} %bitcast.61, bf16[256,512]{1,0:T(8,128)(2,1)} %get-tuple-element.140.refs_0_.refs_6_.refs_8_.refs_14_, bf16[256,512]{1,0:T(8,128)(2,1)} %copy-done.34, ...), custom_call_target="tpu_custom_call" | custom-call | flops 1073741824 | bytes 2097152 | tf_op jit(solution)/shard_map/attend/pallas_call | solution.py:241
  55.8 6.0 %collective-permute-done.7.refs_3_ = bf16[512,256]{1,0:T(8,128)(2,1)S(1)} collective-permute-done((bf16[512,256]{1,0:T(8,128)(2,1)}, bf16[512,256]{1,0:T(8,128)(2,1)S(1)}, u32[]{:S(2)}, u32[]{:S(2)}) %collective-permute-start.7) | collective-permute-done | bytes 262176 | tf_op jit(solution)/shard_map/ppermute | solution.py:927
  61.9 6.6 %collective-permute-done.6.refs_2_ = bf16[512,256]{1,0:T(8,128)(2,1)S(1)} collective-permute-done((bf16[512,256]{1,0:T(8,128)(2,1)}, bf16[512,256]{1,0:T(8,128)(2,1)S(1)}, u32[]{:S(2)}, u32[]{:S(2)}) %collective-permute-start.6) | collective-permute-done | bytes 262176 | tf_op jit(solution)/shard_map/ppermute | solution.py:927
  84.7 7.4 %attn_out.2 = (f32[512,2048]{1,0:T(8,128)}, bf16[512,2048]{1,0:T(8,128)(2,1)}) custom-call(s32[3]{0:T(128)} %pad_add_fusion.ids_ref, bf16[512,2048]{1,0:T(8,128)(2,1)} %x_ref.7, f32[1,2048]{1,0:T(1,128)} %bitcast.63, bf16[512,256]{1,0:T(8,128)(2,1)} %get-tuple-element.152.refs_0_, bf16[512,256]{1,0:T(8,128)(2,1)} %copy-done.26, bf16[512,256]{1,0:T(8,128)(2,1)} %copy-done.25, ...), custom_call_target="tpu_custom_call" | custom-call | flops 2147483648 | bytes 14680064 | tf_op jit(solution)/shard_map/attn_out/pallas_call | solution.py:466
  93.4 7.4 %attn_out.3 = (f32[512,2048]{1,0:T(8,128)}, bf16[512,2048]{1,0:T(8,128)(2,1)}) custom-call(s32[3]{0:T(128)} %pad_add_fusion.ids_ref, bf16[512,2048]{1,0:T(8,128)(2,1)} %x_ref.7, f32[1,2048]{1,0:T(1,128)} %bitcast.64, bf16[512,256]{1,0:T(8,128)(2,1)} %get-tuple-element.159.refs_0_.refs_1_, ...), custom_call_target="tpu_custom_call", output_to_operand_aliasing={{0}: (9, {}), {1}: (10, {})} | custom-call | flops 2147483648 | bytes 14680064 | tf_op jit(solution)/shard_map/attn_out/pallas_call | solution.py:466
  100.8 16.1 %gate_up.1 = (bf16[512,2048]{1,0:T(8,128)(2,1)}, bf16[512,2048]{1,0:T(8,128)(2,1)}, bf16[512,2048]{1,0:T(8,128)(2,1)}) custom-call(bf16[512,2048]{1,0:T(8,128)(2,1)} %get-tuple-element.190.n_ref.refs_0_.refs_1_.refs_2_.refs_3_, f32[512,2048]{1,0:T(8,128)} %fusion.12.da_ref, bf16[2048,2048]{1,0:T(8,128)(2,1)} %wa_ref.1, bf16[2048,2048]{1,0:T(8,128)(2,1)} %wb_ref.1), custom_call_target="tpu_custom_call" | custom-call | flops 8589934592 | bytes 29360128 | tf_op jit(solution)/shard_map/gate_up/pallas_call | solution.py:646
  121.4 9.4 %grad_down.1 = bf16[2048,1024]{1,0:T(8,128)(2,1)} custom-call(s32[3]{0:T(128)} %pad_add_fusion.ids_ref, bf16[512,2048]{1,0:T(8,128)(2,1)} %get-tuple-element.178.own_ref.a_ref, bf16[512,2048]{1,0:T(8,128)(2,1)} %collective-permute-done.13.other_ref, bf16[512,2048]{1,0:T(8,128)(2,1)} %cot_ref.1, bf16[512,2048]{1,0:T(8,128)(2,1)} %cot_ref.1, ...), custom_call_target="tpu_custom_call" | custom-call | flops 4294967296 | bytes 10485760 | tf_op jit(solution)/shard_map/grad_down/pallas_call | solution.py:759
  132.3 14.0 %d_normed_two.1 = (bf16[128,2048]{1,0:T(8,128)(2,1)}, bf16[128,2048]{1,0:T(8,128)(2,1)}, bf16[128,2048]{1,0:T(8,128)(2,1)}, bf16[128,2048]{1,0:T(8,128)(2,1)}) custom-call(s32[3]{0:T(128)} %pad_add_fusion.ids_ref, bf16[512,2048]{1,0:T(8,128)(2,1)} %get-tuple-element.192.a_ref.refs_8_, bf16[512,2048]{1,0:T(8,128)(2,1)} %get-tuple-element.194.b_ref.refs_10_, ...), custom_call_target="tpu_custom_call" | custom-call | flops 8589934592 | bytes 23068672 | tf_op jit(solution)/shard_map/d_normed_two/pallas_call | solution.py:680
  150.6 8.9 %ffn_down.1 = (bf16[128,2048]{1,0:T(8,128)(2,1)}, bf16[256,2048]{1,0:T(8,128)(2,1)}, bf16[256,2048]{1,0:T(8,128)(2,1)}, bf16[256,2048]{1,0:T(8,128)(2,1)}) custom-call(s32[3]{0:T(128)} %pad_add_fusion.ids_ref, bf16[512,2048]{1,0:T(8,128)(2,1)} %get-tuple-element.178.own_ref.a_ref, bf16[2048,2048]{1,0:T(8,128)(2,1)} %w_ref.1), custom_call_target="tpu_custom_call" | custom-call | flops 4294967296 | bytes 12582912 | tf_op jit(solution)/shard_map/ffn_down/pallas_call | solution.py:704
  162.0 15.8 %grad_gate_up.1 = bf16[1024,4096]{1,0:T(8,128)(2,1)} custom-call(s32[3]{0:T(128)} %pad_add_fusion.ids_ref, bf16[512,2048]{1,0:T(8,128)(2,1)} %get-tuple-element.190.n_ref.refs_0_.refs_1_.refs_2_.refs_3_, bf16[512,2048]{1,0:T(8,128)(2,1)} %get-tuple-element.190.n_ref.refs_0_.refs_1_.refs_2_.refs_3_, ...), custom_call_target="tpu_custom_call" | custom-call | flops 8589934592 | bytes 18874368 | tf_op jit(solution)/shard_map/grad_gate_up/pallas_call | solution.py:804
  178.6 10.8 %norm_two_back.1 = (f32[128,2048]{1,0:T(8,128)}, bf16[128,2048]{1,0:T(8,128)(2,1)}, f32[1,2048]{1,0:T(1,128)}, bf16[128,512]{1,0:T(8,128)(2,1)}, bf16[128,512]{1...) custom-call(s32[3]{0:T(128)} %pad_add_fusion.ids_ref, ...), custom_call_target="tpu_custom_call", output_to_operand_aliasing={{7}: (11, {}), {8}: (12, {}), {9}: (13, {})} | custom-call | flops 1073741824 | bytes 14680064 | tf_op jit(solution)/shard_map/norm_two_back/pallas_call | solution.py:538
  203.0 11.6 %attend_back.1 = (f32[512,512]{1,0:T(8,128)}, bf16[6,2,128,512]{3,2,1,0:T(8,128)(2,1)}) custom-call(s32[3]{0:T(128)} %pad_add_fusion.ids_ref, s32[12]{0:T(128)} %lengths_ref.7, bf16[512,512]{1,0:T(8,128)(2,1)} %bitcast.62, bf16[128,512]{1,0:T(8,128)(2,1)} %get-tuple-element.210.refs_0_, bf16[128,512]{1,0:T(8,128)(2,1)} %copy-done.39, ...), custom_call_target="tpu_custom_call" | custom-call | flops 5368709120 | bytes 4194304 | tf_op jit(solution)/shard_map/attend_back/pallas_call | solution.py:391
  214.5 11.2 %collective-permute-done.26.refs_1_.refs_5_ = bf16[256,2048]{1,0:T(8,128)(2,1)S(1)} collective-permute-done((bf16[256,2048]{1,0:T(8,128)(2,1)}, bf16[256,2048]{1,0:T(8,128)(2,1)S(1)}, u32[]{:S(2)}, u32[]{:S(2)}) %collective-permute-start.26) | collective-permute-done | bytes 1048608 | tf_op jit(solution)/shard_map/ppermute | solution.py:927
  228.2 18.2 %collective-permute-done.30.refs_2_.refs_6_ = bf16[256,2048]{1,0:T(8,128)(2,1)} collective-permute-done((bf16[256,2048]{1,0:T(8,128)(2,1)}, bf16[256,2048]{1,0:T(8,128)(2,1)}, u32[]{:S(2)}, u32[]{:S(2)}) %collective-permute-start.30) | collective-permute-done | bytes 1048608 | tf_op jit(solution)/shard_map/ppermute | solution.py:927
  254.4 20.4 %collective-permute-done.28 = bf16[256,512]{1,0:T(8,128)(2,1)S(1)} collective-permute-done((bf16[256,512]{1,0:T(8,128)(2,1)S(1)}, bf16[256,512]{1,0:T(8,128)(2,1)S(1)}, u32[]{:S(2)}, u32[]{:S(2)}) %collective-permute-start.28) | collective-permute-done | bytes 262176 | tf_op jit(solution)/shard_map/ppermute | solution.py:924
  282.1 5.5 %grad_query.1 = bf16[512,1024]{1,0:T(8,128)(2,1)} custom-call(s32[3]{0:T(128)} %pad_add_fusion.ids_ref, bf16[512,512]{1,0:T(8,128)(2,1)} %bitcast.53, bf16[512,512]{1,0:T(8,128)(2,1)} %copy-done.18, bf16[512,2048]{1,0:T(8,128)(2,1)} %get-tuple-element.141.refs_2_, bf16[512,2048]{1,0:T(8,128)(2,1)} %collective-permute-done.8.refs_3_), custom_call_target="tpu_custom_call" | custom-call | flops 1073741824 | bytes 4194304 | tf_op jit(solution)/shard_map/grad_query/pallas_call | solution.py:844
  293.0 5.8 %collective-permute-done.29 = bf16[256,512]{1,0:T(8,128)(2,1)} collective-permute-done((bf16[256,512]{1,0:T(8,128)(2,1)}, bf16[256,512]{1,0:T(8,128)(2,1)}, u32[]{:S(2)}, u32[]{:S(2)}) %collective-permute-start.29) | collective-permute-done | bytes 262176 | tf_op jit(solution)/shard_map/ppermute | solution.py:924
  319.8 12.1 %collective-permute-done.35.refs_2_ = bf16[128,2048]{1,0:T(8,128)(2,1)} collective-permute-done((bf16[128,2048]{1,0:T(8,128)(2,1)}, bf16[128,2048]{1,0:T(8,128)(2,1)}, u32[]{:S(2)}, u32[]{:S(2)}) %collective-permute-start.35) | collective-permute-done | bytes 524320 | tf_op jit(solution)/shard_map/ppermute | solution.py:927
  332.0 6.2 %last_rows.1 = (bf16[256,2048]{1,0:T(8,128)(2,1)}, f32[1,2048]{1,0:T(1,128)}) custom-call(s32[3]{0:T(128)} %pad_add_fusion.ids_ref, bf16[512,2048]{1,0:T(8,128)(2,1)} %x_ref.7, f32[512,2048]{1,0:T(8,128)} %get-tuple-element.165.hidden_ref, f32[128,2048]{1,0:T(8,128)} %get-tuple-element.240.add_ref, f32[1,2048]{1,0:T(1,128)} %bitcast.67, ...), custom_call_target="tpu_custom_call" | custom-call | flops 7864320 | bytes 8388608 | tf_op jit(solution)/shard_map/last_rows/pallas_call | solution.py:587
  340.4 22.7 %collective-permute-done.39.refs_2_ = bf16[256,2048]{1,0:T(8,128)(2,1)} collective-permute-done((bf16[256,2048]{1,0:T(8,128)(2,1)}, bf16[256,2048]{1,0:T(8,128)(2,1)}, u32[]{:S(2)}, u32[]{:S(2)}) %collective-permute-start.39) | collective-permute-done | bytes 1048608 | tf_op jit(solution)/shard_map/ppermute | solution.py:927
  368.9 23.5 %collective-permute-done.40.refs_3_ = bf16[256,2048]{1,0:T(8,128)(2,1)} collective-permute-done((bf16[256,2048]{1,0:T(8,128)(2,1)}, bf16[256,2048]{1,0:T(8,128)(2,1)}, u32[]{:S(2)}, u32[]{:S(2)}) %collective-permute-start.40) | collective-permute-done | bytes 1048608 | tf_op jit(solution)/shard_map/ppermute | solution.py:927
  413.8 7.8 %reduce-scatter.8.cloned.1.call-done.in_ref = bf16[1280,256]{1,0:T(8,128)(2,1)} async-done(((bf16[1280,1024]{1,0:T(8,128)(2,1)}), bf16[1280,256]{1,0:T(8,128)(2,1)}) %reduce-scatter.8.cloned.1.call-update) | async-done | bytes 655376 | tf_op jit(solution)/shard_map/reduce_scatter | solution.py:939
  (232 shorter events, 151.2 us)
Async XLA Ops:
  7.2 69.9 %all-gather.2.cloned.1.call-start = ((), (), s32[]{:S(2)}) async-start(), calls=%async_computation.3 | async-start | bytes 5242880 | tf_op jit(solution)/shard_map/all_gather | solution.py:952
  9.8 289.1 %reduce-scatter.4.cloned.1.call-start = ((), (), s32[]{:S(2)}) async-start(), calls=%async_computation.4 | async-start | bytes 5242880 | tf_op jit(solution)/shard_map/reduce_scatter | solution.py:939
  16.0 23.0 %collective-permute-start.2 = (bf16[256,512]{1,0:T(8,128)(2,1)}, bf16[256,512]{1,0:T(8,128)(2,1)S(1)}, u32[]{:S(2)}, u32[]{:S(2)}) collective-permute-start(bf16[256,512]{1,0:T(8,128)(2,1)} %get-tuple-element.140.refs_0_.refs_6_.refs_8_.refs_14_), channel_id=1, source_target_pairs={{0,4},{4,0},{8,12},{12,8},{16,20},{20,16},{24,28},{28,24},{1,5},{5... | collective-permute-start | bytes 786440 | tf_op jit(solution)/shard_map/ppermute | solution.py:918
  16.5 21.4 %collective-permute-start.1 = (bf16[256,512]{1,0:T(8,128)(2,1)}, bf16[256,512]{1,0:T(8,128)(2,1)S(1)}, u32[]{:S(2)}, u32[]{:S(2)}) collective-permute-start(bf16[256,512]{1,0:T(8,128)(2,1)} %get-tuple-element.140.refs_0_.refs_6_.refs_8_.refs_14_), channel_id=1, source_target_pairs={{0,16},{4,20},{8,24},{12,28},{1,17},{5,21},{9,25},{13,29},{2,18},{... | collective-permute-start | bytes 786440 | tf_op jit(solution)/shard_map/ppermute | solution.py:921
  26.0 47.1 %collective-permute-start.8 = (bf16[512,2048]{1,0:T(8,128)(2,1)}, bf16[512,2048]{1,0:T(8,128)(2,1)}, u32[]{:S(2)}, u32[]{:S(2)}) collective-permute-start(bf16[512,2048]{1,0:T(8,128)(2,1)} %get-tuple-element.141.refs_2_), channel_id=1, source_target_pairs={{0,4},{4,0},{8,12},{12,8},{16,20},{20,16},{24,28},{28,24},{1,5},{5... | collective-permute-start | bytes 6291464 | tf_op jit(solution)/shard_map/ppermute | solution.py:918
  49.1 24.0 %collective-permute-start.5 = (bf16[512,256]{1,0:T(8,128)(2,1)}, bf16[512,256]{1,0:T(8,128)(2,1)S(1)}, u32[]{:S(2)}, u32[]{:S(2)}) collective-permute-start(bf16[512,256]{1,0:T(8,128)(2,1)} %get-tuple-element.152.refs_0_), channel_id=1, source_target_pairs={{0,1},{1,0},{2,3},{3,2},{4,5},{5,4},{6,7},{7,6},{8,9},{9,8},{10,11... | collective-permute-start | bytes 786440 | tf_op jit(solution)/shard_map/ppermute | solution.py:927
  80.6 36.3 %collective-permute-start.14 = (bf16[512,2048]{1,0:T(8,128)(2,1)}, bf16[512,2048]{1,0:T(8,128)(2,1)}, u32[]{:S(2)}, u32[]{:S(2)}) collective-permute-start(bf16[512,2048]{1,0:T(8,128)(2,1)} %cot_ref.1), channel_id=1, source_target_pairs={{0,4},{4,0},{8,12},{12,8},{16,20},{20,16},{24,28},{28,24},{1,5},{5... | collective-permute-start | bytes 6291464 | tf_op jit(solution)/shard_map/ppermute | solution.py:918
  130.8 235.6 %reduce-scatter.6.cloned.1.call-start = ((), (), s32[]{:S(2)}) async-start(), calls=%async_computation.5 | async-start | bytes 10485760 | tf_op jit(solution)/shard_map/reduce_scatter | solution.py:939
  148.5 29.3 %collective-permute-start.21 = (bf16[128,2048]{1,0:T(8,128)(2,1)}, bf16[128,2048]{1,0:T(8,128)(2,1)S(1)}, u32[]{:S(2)}, u32[]{:S(2)}) collective-permute-start(bf16[128,2048]{1,0:T(8,128)(2,1)} %get-tuple-element.184), channel_id=1, source_target_pairs={{0,2},{1,3},{2,0},{3,1},{4,6},{5,7},{6,4},{7,5},{8,10},{9,11},{10,... | collective-permute-start | bytes 1572872 | tf_op jit(solution)/shard_map/ppermute | solution.py:927
  149.3 28.6 %collective-permute-start.22 = (bf16[128,2048]{1,0:T(8,128)(2,1)}, bf16[128,2048]{1,0:T(8,128)(2,1)}, u32[]{:S(2)}, u32[]{:S(2)}) collective-permute-start(bf16[128,2048]{1,0:T(8,128)(2,1)} %get-tuple-element.185), channel_id=1, source_target_pairs={{0,3},{1,2},{2,1},{3,0},{4,7},{5,6},{6,5},{7,4},{8,11},{9,10},{10,... | collective-permute-start | bytes 1572872 | tf_op jit(solution)/shard_map/ppermute | solution.py:927
  189.5 232.1 %reduce-scatter.8.cloned.1.call-start = ((), (), s32[]{:S(2)}) async-start(), calls=%async_computation.6 | async-start | bytes 3276800 | tf_op jit(solution)/shard_map/reduce_scatter | solution.py:939
  199.5 26.3 %collective-permute-start.26 = (bf16[256,2048]{1,0:T(8,128)(2,1)}, bf16[256,2048]{1,0:T(8,128)(2,1)S(1)}, u32[]{:S(2)}, u32[]{:S(2)}) collective-permute-start(bf16[256,2048]{1,0:T(8,128)(2,1)} %get-tuple-element.220), channel_id=1, source_target_pairs={{0,1},{1,0},{2,3},{3,2},{4,5},{5,4},{6,7},{7,6},{8,9},{9,8},{10,11... | collective-permute-start | bytes 3145736 | tf_op jit(solution)/shard_map/ppermute | solution.py:927
  200.6 45.8 %collective-permute-start.30 = (bf16[256,2048]{1,0:T(8,128)(2,1)}, bf16[256,2048]{1,0:T(8,128)(2,1)}, u32[]{:S(2)}, u32[]{:S(2)}) collective-permute-start(bf16[256,2048]{1,0:T(8,128)(2,1)} %get-tuple-element.226), channel_id=1, source_target_pairs={{0,2},{1,3},{2,0},{3,1},{4,6},{5,7},{6,4},{7,5},{8,10},{9,11},{10,... | collective-permute-start | bytes 3145736 | tf_op jit(solution)/shard_map/ppermute | solution.py:927
  201.3 45.1 %collective-permute-start.31 = (bf16[256,2048]{1,0:T(8,128)(2,1)}, bf16[256,2048]{1,0:T(8,128)(2,1)}, u32[]{:S(2)}, u32[]{:S(2)}) collective-permute-start(bf16[256,2048]{1,0:T(8,128)(2,1)} %get-tuple-element.227), channel_id=1, source_target_pairs={{0,3},{1,2},{2,1},{3,0},{4,7},{5,6},{6,5},{7,4},{8,11},{9,10},{10,... | collective-permute-start | bytes 3145736 | tf_op jit(solution)/shard_map/ppermute | solution.py:927
  228.2 23.3 %collective-permute-start.27 = (bf16[3,256,512]{2,1,0:T(8,128)(2,1)}, bf16[3,256,512]{2,1,0:T(8,128)(2,1)}, u32[]{:S(2)}, u32[]{:S(2)}) collective-permute-start(bf16[3,256,512]{2,1,0:T(8,128)(2,1)} %slice.64), channel_id=1, source_target_pairs={{0,4},{4,0},{8,12},{12,8},{16,20},{20,16},{24,28},{28,24},{1,5},{5... | collective-permute-start | bytes 2359304 | tf_op jit(solution)/shard_map/ppermute | solution.py:918
  249.9 37.7 %collective-permute-start.32 = (bf16[512,2048]{1,0:T(8,128)(2,1)}, bf16[512,2048]{1,0:T(8,128)(2,1)}, u32[]{:S(2)}, u32[]{:S(2)}) collective-permute-start(bf16[512,2048]{1,0:T(8,128)(2,1)} %token_order.2.refs_4_), channel_id=1, source_target_pairs={{0,4},{4,0},{8,12},{12,8},{16,20},{20,16},{24,28},{28,24},{1,5},{5... | collective-permute-start | bytes 6291464 | tf_op jit(solution)/shard_map/ppermute | solution.py:918
  252.5 22.2 %collective-permute-start.28 = (bf16[256,512]{1,0:T(8,128)(2,1)S(1)}, bf16[256,512]{1,0:T(8,128)(2,1)S(1)}, u32[]{:S(2)}, u32[]{:S(2)}) collective-permute-start(bf16[256,512]{1,0:T(8,128)(2,1)S(1)} %fusion), channel_id=1, source_target_pairs={{8,0},{12,4},{16,8},{20,12},{24,16},{28,20},{9,1},{13,5},{17,9},{2... | collective-permute-start | bytes 786440 | tf_op jit(solution)/shard_map/ppermute | solution.py:924
  254.1 27.3 %collective-permute-start.33 = (bf16[512,512]{1,0:T(8,128)(2,1)S(1)}, bf16[512,512]{1,0:T(8,128)(2,1)S(1)}, u32[]{:S(2)}, u32[]{:S(2)}) collective-permute-start(bf16[512,512]{1,0:T(8,128)(2,1)S(1)} %bitcast.51), channel_id=1, source_target_pairs={{0,4},{4,0},{8,12},{12,8},{16,20},{20,16},{24,28},{28,24},{1,5},{5... | collective-permute-start | bytes 1572872 | tf_op jit(solution)/shard_map/ppermute | solution.py:918
  276.5 22.4 %collective-permute-start.29 = (bf16[256,512]{1,0:T(8,128)(2,1)}, bf16[256,512]{1,0:T(8,128)(2,1)}, u32[]{:S(2)}, u32[]{:S(2)}) collective-permute-start(bf16[256,512]{1,0:T(8,128)(2,1)} %fusion.2), channel_id=1, source_target_pairs={{8,0},{12,4},{16,8},{20,12},{24,16},{28,20},{9,1},{13,5},{17,9},{2... | collective-permute-start | bytes 786440 | tf_op jit(solution)/shard_map/ppermute | solution.py:924
  306.4 25.5 %collective-permute-start.35 = (bf16[128,2048]{1,0:T(8,128)(2,1)}, bf16[128,2048]{1,0:T(8,128)(2,1)}, u32[]{:S(2)}, u32[]{:S(2)}) collective-permute-start(bf16[128,2048]{1,0:T(8,128)(2,1)} %get-tuple-element.233), channel_id=1, source_target_pairs={{0,2},{1,3},{2,0},{3,1},{4,6},{5,7},{6,4},{7,5},{8,10},{9,11},{10,... | collective-permute-start | bytes 1572872 | tf_op jit(solution)/shard_map/ppermute | solution.py:927
  307.9 24.1 %collective-permute-start.36 = (bf16[128,2048]{1,0:T(8,128)(2,1)}, bf16[128,2048]{1,0:T(8,128)(2,1)}, u32[]{:S(2)}, u32[]{:S(2)}) collective-permute-start(bf16[128,2048]{1,0:T(8,128)(2,1)} %get-tuple-element.234), channel_id=1, source_target_pairs={{0,3},{1,2},{2,1},{3,0},{4,7},{5,6},{6,5},{7,4},{8,11},{9,10},{10,... | collective-permute-start | bytes 1572872 | tf_op jit(solution)/shard_map/ppermute | solution.py:927
  338.2 24.9 %collective-permute-start.39 = (bf16[256,2048]{1,0:T(8,128)(2,1)}, bf16[256,2048]{1,0:T(8,128)(2,1)}, u32[]{:S(2)}, u32[]{:S(2)}) collective-permute-start(bf16[256,2048]{1,0:T(8,128)(2,1)} %get-tuple-element.246.refs_0_), channel_id=1, source_target_pairs={{0,2},{1,3},{2,0},{3,1},{4,6},{5,7},{6,4},{7,5},{8,10},{9,11},{10,... | collective-permute-start | bytes 3145736 | tf_op jit(solution)/shard_map/ppermute | solution.py:927
  339.8 24.4 %collective-permute-start.38 = (bf16[256,2048]{1,0:T(8,128)(2,1)}, bf16[256,2048]{1,0:T(8,128)(2,1)}, u32[]{:S(2)}, u32[]{:S(2)}) collective-permute-start(bf16[256,2048]{1,0:T(8,128)(2,1)} %get-tuple-element.246.refs_0_), channel_id=1, source_target_pairs={{0,1},{1,0},{2,3},{3,2},{4,5},{5,4},{6,7},{7,6},{8,9},{9,8},{10,11... | collective-permute-start | bytes 3145736 | tf_op jit(solution)/shard_map/ppermute | solution.py:927
  366.4 26.0 %collective-permute-start.40 = (bf16[256,2048]{1,0:T(8,128)(2,1)}, bf16[256,2048]{1,0:T(8,128)(2,1)}, u32[]{:S(2)}, u32[]{:S(2)}) collective-permute-start(bf16[256,2048]{1,0:T(8,128)(2,1)} %get-tuple-element.246.refs_0_), channel_id=1, source_target_pairs={{0,3},{1,2},{2,1},{3,0},{4,7},{5,6},{6,5},{7,4},{8,11},{9,10},{10,... | collective-permute-start | bytes 3145736 | tf_op jit(solution)/shard_map/ppermute | solution.py:927
  (73 other events, 615.3 us)
Sparse Core Ops, SparseCore 0:
  10.5 66.6 all-gather.1
  130.9 76.7 reduce-scatter.3
  210.2 156.1 reduce-scatter.5
  368.6 52.9 reduce-scatter.7

commit v5 on v4

--- a/solution.py
+++ b/solution.py
@@ -122,28 +122,25 @@
     return jnp.where(valid, start, index), valid
 
 
-def tile_state(ids_ref, edges, tile, half, q_rows, rows):
+def tile_state(ids_ref, edge, tile, half, q_rows, rows):
     me_wide = ids_ref[2]
     slot = tile // (rows // KT)
     block = (me_wide // 2 - slot // 2) * 2 + (ids_ref[1] ^ (slot % 2))
     key_base = block * rows + (tile % (rows // KT)) * KT
     q_base = me_wide * rows + half * q_rows
-    low, high = edges[half]
+    low, high = edge
     active = (key_base <= q_base + q_rows - 1) & (key_base + KT > low)
     whole = (key_base + KT - 1 <= q_base) & (key_base >= high)
     return active, active & whole, key_base, q_base
 
 
-def window_edges(ids_ref, lengths_ref, rows):
+def window_edge(ids_ref, lengths_ref, rows, half):
     base = ids_ref[2] * rows
     step = rows // HALVES
-    return [
-        (
-            window(lengths_ref, base + half * step)[0],
-            window(lengths_ref, base + (half + 1) * step - 1)[0],
-        )
-        for half in range(HALVES)
-    ]
+    return (
+        window(lengths_ref, base + half * step)[0],
+        window(lengths_ref, base + (half + 1) * step - 1)[0],
+    )
 
 
 def query_row(ids_ref, rows, half):
@@ -171,14 +168,14 @@
     rows = k_refs[0].shape[1]
     per = rows // KT
     tiles = slots * per
-    edges = window_edges(ids_ref, lengths_ref, rows)
+    edge = window_edge(ids_ref, lengths_ref, rows, half)
     start_row, valid_row = window(lengths_ref, query_row(ids_ref, rows, half))
     for slot in range(slots):
         for part in range(per):
             tile = slot * per + part
             cut = slice(part * KT, (part + 1) * KT)
 
-            @pl.when(tile_state(ids_ref, edges, tile, half, q_rows, rows)[0])
+            @pl.when(tile_state(ids_ref, edge, tile, half, q_rows, rows)[0])
             def _(tile=tile, slot=slot, cut=cut):
                 keys_s[tile] = k_refs[slot][:, cut].T
                 values_s[tile] = v_refs[slot][:, cut]
@@ -189,7 +186,7 @@
     heads = range(group)
 
     def step(tile, carry):
-        active, whole, key_base, q_base = tile_state(ids_ref, edges, tile, half, q_rows, rows)
+        active, whole, key_base, q_base = tile_state(ids_ref, edge, tile, half, q_rows, rows)
 
         def run(masked):
             keys = keys_s[tile]
@@ -273,18 +270,18 @@
     o_refs, lse_refs, refs = refs[:HALVES], refs[HALVES : 2 * HALVES], refs[2 * HALVES :]
     k_refs, v_refs, refs = refs[:slots], refs[slots : 2 * slots], refs[2 * slots :]
     dq_ref, dkv_ref = refs[:2]
-    keys_s, values_s, keys_t_s, dk_s, dv_s, q_s, do_s, do_t_s, dq_s, delta_s = refs[2:]
+    keys_s, values_s, keys_t_s, dk_s, dv_s, q_s, do_s, do_t_s, dq_s, delta_s, lse_s = refs[2:]
     rows = q_ref.shape[1]
     q_rows = rows // HALVES
     per = rows // KT
     tiles = slots * per
     heads = range(group)
-    edges = window_edges(ids_ref, lengths_ref, rows)
+    edges = [window_edge(ids_ref, lengths_ref, rows, half) for half in range(HALVES)]
 
     def any_active(tile):
-        found = tile_state(ids_ref, edges, tile, 0, q_rows, rows)[0]
+        found = tile_state(ids_ref, edges[0], tile, 0, q_rows, rows)[0]
         for half in range(1, HALVES):
-            found = found | tile_state(ids_ref, edges, tile, half, q_rows, rows)[0]
+            found = found | tile_state(ids_ref, edges[half], tile, half, q_rows, rows)[0]
         return found
 
     for slot in range(slots):
@@ -307,18 +304,24 @@
     do_t_s[...] = do_s[...].T
 
     for half in range(HALVES):
-        q_cut = slice(half * q_rows, (half + 1) * q_rows)
         for h in heads:
             h_cut = slice(h * HD, (h + 1) * HD)
-            q_s[h] = q_ref[h_cut, q_cut].T
-            delta_s[h : h + 1, :] = jnp.sum(
-                do_t_s[h_cut, q_cut].astype(F32) * o_refs[half][h_cut, :], axis=0, keepdims=True
+            do_h = do_t_s[h_cut, half * q_rows : (half + 1) * q_rows].astype(F32)
+            delta_s[half, h : h + 1, :] = jnp.sum(
+                do_h * o_refs[half][h_cut, :], axis=0, keepdims=True
             )
+            lse_s[half, h : h + 1, :] = lse_refs[half][0, h : h + 1, :]
+
+    def half_step(half, carry):
+        q_cut = pl.ds(pl.multiple_of(half * q_rows, q_rows), q_rows)
+        edge = window_edge(ids_ref, lengths_ref, rows, half)
+        for h in heads:
+            q_s[h] = q_ref[h * HD : (h + 1) * HD, q_cut].T
         dq_s[...] = jnp.zeros_like(dq_s)
         start_row = window(lengths_ref, query_row(ids_ref, rows, half))[0]
 
-        def step(tile, carry, half=half, q_cut=q_cut, start_row=start_row):
-            active, whole, key_base, q_base = tile_state(ids_ref, edges, tile, half, q_rows, rows)
+        def step(tile, carry):
+            active, whole, key_base, q_base = tile_state(ids_ref, edge, tile, half, q_rows, rows)
 
             def run(masked):
                 keys = keys_s[tile]
@@ -336,12 +339,14 @@
                     allowed = tile_mask(key_base, q_base, start_row)
                 probs, d_scores = [], []
                 for h in heads:
-                    scaled = scores[h] * SCALE2 - lse_refs[half][0, h : h + 1, :]
+                    scaled = scores[h] * SCALE2 - lse_s[half, h : h + 1, :]
                     if masked:
                         scaled = jnp.where(allowed, scaled, MASKED_SCORE)
                     prob = jnp.exp2(scaled)
                     probs.append(prob.astype(BF))
-                    d_scores.append((prob * (prob_grads[h] - delta_s[h : h + 1, :])).astype(BF))
+                    d_scores.append(
+                        (prob * (prob_grads[h] - delta_s[half, h : h + 1, :])).astype(BF)
+                    )
                 dk = dk_s[tile]
                 dv = dv_s[tile]
                 for h in heads:
@@ -361,6 +366,9 @@
         lax.fori_loop(0, tiles, step, 0)
         for h in heads:
             dq_ref[h * HD : (h + 1) * HD, q_cut] = dq_s[h]
+        return carry
+
+    lax.fori_loop(0, HALVES, half_step, 0)
     for slot in range(slots):
         for part in range(per):
             cut = slice(part * KT, (part + 1) * KT)
@@ -412,7 +420,8 @@
             pltpu.VMEM((rows, wide), BF),
             pltpu.VMEM((wide, rows), BF),
             pltpu.VMEM((group, HD, q_rows), F32),
-            pltpu.VMEM((group, q_rows), F32),
+            pltpu.VMEM((HALVES, group, q_rows), F32),
+            pltpu.VMEM((HALVES, group, q_rows), F32),
         ],
         name="attend_back",
         cost_estimate=cost(
@@ -421,69 +430,93 @@
     )(ids, lengths, q_t, *do_pieces, *outs, *lses, *blocks, *blocks)
 
 
-def fetch_weights(members, ids_ref, weights, held, sems):
+def weight_copies(members, ids_ref, weights, held, sems, distance):
     size = held.shape[0] // (2 * members)
     copies = []
+    for other in range(2):
+        index = 2 * distance + other
+        source = pl.multiple_of((ids_ref[0] ^ distance) * size, size)
+        at = pl.multiple_of(index * size, size)
+        copy = pltpu.make_async_copy(
+            weights[other].at[pl.ds(source, size), :], held.at[pl.ds(at, size), :], sems.at[index]
+        )
+        copies.append((copy, at, pl.multiple_of((ids_ref[1] ^ other) * size, size)))
+    return copies
+
+
+def project(members, ids_ref, x_ref, gain_ref, mixes, weights, hidden_ref, normed_ref, scratch):
+    held, left, sems = scratch
+    size = held.shape[0] // (2 * members)
+    for distance in range(members):
+        for copy, _, _ in weight_copies(members, ids_ref, weights, held, sems, distance):
+            copy.start()
     for distance in range(members):
         for other in range(2):
-            index = 2 * distance + other
-            source = pl.multiple_of((ids_ref[0] ^ distance) * size, size)
-            copy = pltpu.make_async_copy(
-                weights[other].at[pl.ds(source, size), :],
-                held.at[index * size : (index + 1) * size, :],
-                sems.at[index],
-            )
-            copy.start()
+            at = (2 * distance + other) * size
             first = pl.multiple_of((ids_ref[1] ^ other) * size, size)
-            copies.append((copy, distance, index * size, first))
-    return copies, size
-
-
-def attn_out_kernel(members, ids_ref, x_ref, gain_ref, *refs):
-    mixes, weights = refs[:members], refs[members : members + 2]
-    hidden_ref, normed_ref, held, sems = refs[-4:]
-    copies, size = fetch_weights(members, ids_ref, weights, held, sems)
+            left[at : at + size, :] = mixes[distance][pl.ds(first, size), :]
     hidden_ref[...] = x_ref[...].astype(F32)
-    for copy, distance, at, first in copies:
-        copy.wait()
-        hidden_ref[...] += dims(
-            mixes[distance][pl.ds(first, size), :], held[at : at + size, :], 0, 0
-        )
+
+    def add(distance, carry):
+        for copy, _, _ in weight_copies(members, ids_ref, weights, held, sems, distance):
+            copy.wait()
+        at = pl.ds(pl.multiple_of(2 * distance * size, size), 2 * size)
+        hidden_ref[...] += dims(left[at, :], held[at, :], 0, 0)
+        return carry
+
+    lax.fori_loop(0, members, add, 0)
     rows = hidden_ref.shape[0]
     step = min(64, rows)
-    for at in range(0, rows, step):
-        hidden = hidden_ref[at : at + step, :]
-        normed_ref[at : at + step, :] = (hidden * rms_scale(hidden) * gain_ref[...]).astype(BF)
-
-
-def attn_out(half, ids, tokens, gain, mixes, weights, filled):
+
+    def norm(index, carry):
+        at = pl.ds(pl.multiple_of(index * step, step), step)
+        hidden = hidden_ref[at, :]
+        normed_ref[at, :] = (hidden * rms_scale(hidden) * gain_ref[...]).astype(BF)
+        return carry
+
+    lax.fori_loop(0, rows // step, norm, 0)
+
+
+def project_scratch(inner, width, half_rows, members):
+    return [
+        pltpu.VMEM((inner, width), BF),
+        pltpu.VMEM((inner, half_rows), BF),
+        pltpu.SemaphoreType.DMA((2 * members,)),
+    ]
+
+
+def attn_out_kernel(members, ids_ref, x_ref, gain_ref, *refs):
+    mixes, weights, refs = refs[:members], refs[members : members + 2], refs[members + 2 :]
+    hidden_ref, normed_ref = refs[:2]
+    project(members, ids_ref, x_ref, gain_ref, mixes, weights, hidden_ref, normed_ref, refs[2:])
+
+
+def attn_out(half, ids, tokens, gain, mixes, weights):
     rows, width = tokens.shape
     half_rows = rows // HALVES
-    inner = sum(w.shape[0] for w in weights)
-    out_spec = pl.BlockSpec((half_rows, width), lambda i: (half, 0))
-    operands = [ids, tokens, gain, *mixes, *weights]
-    extra = [] if filled is None else list(filled)
-    return pl.pallas_call(
-        functools.partial(attn_out_kernel, len(mixes)),
+    members = len(mixes)
+    inner = 2 * weights[0].shape[0]
+    return pl.pallas_call(
+        functools.partial(attn_out_kernel, members),
         grid=(1,),
-        in_specs=[smem_spec(), out_spec, vmem_spec()]
-        + [vmem_spec()] * len(mixes)
-        + [any_spec()] * (len(weights) + len(extra)),
-        out_specs=[out_spec, out_spec],
+        in_specs=[
+            smem_spec(),
+            pl.BlockSpec((half_rows, width), lambda i: (half, 0)),
+            vmem_spec(),
+        ]
+        + [vmem_spec()] * members
+        + [any_spec()] * len(weights),
+        out_specs=[vmem_spec()] * 2,
         out_shape=[
-            jax.ShapeDtypeStruct((rows, width), F32),
-            jax.ShapeDtypeStruct((rows, width), BF),
+            jax.ShapeDtypeStruct((half_rows, width), F32),
+            jax.ShapeDtypeStruct((half_rows, width), BF),
         ],
-        scratch_shapes=[
-            pltpu.VMEM((inner, width), BF),
-            pltpu.SemaphoreType.DMA((2 * len(mixes),)),
-        ],
-        input_output_aliases={len(operands) + i: i for i in range(len(extra))},
+        scratch_shapes=project_scratch(inner, width, half_rows, members),
         name="attn_out",
         cost_estimate=cost(
             2 * half_rows * inner * width, 2 * inner * width + 12 * half_rows * width
         ),
-    )(*operands, *extra)
+    )(ids, tokens, gain, *mixes, *weights)
 
 
 def row_sum(refs):
@@ -500,38 +533,67 @@
     )
 
 
-def norm_two_back_kernel(members, ids_ref, lengths_ref, hidden_ref, cot_ref, gain_ref, *refs):
+def pick_half(members, ids_ref, refs, at):
+    per = members // HALVES
+    value = refs[0][at, :]
+    for half in range(1, HALVES):
+        value = jnp.where(ids_ref[0] // per == half, refs[half][at, :], value)
+    return value
+
+
+def norm_two_back_kernel(members, ids_ref, lengths_ref, *refs):
+    hiddens, (cot_ref, gain_ref), refs = refs[:HALVES], refs[HALVES : HALVES + 2], refs[HALVES + 2 :]
     pieces, refs = refs[:members], refs[members:]
     weights, refs = refs[:2], refs[2:]
     refs = refs[members - 1 :]
     sum_ref, low_ref, part_ref = refs[:3]
     d_mixed, refs = refs[3 : 3 + members], refs[3 + members :]
-    sent, (held, sems) = refs[:-2], refs[-2:]
-    copies, size = fetch_weights(members, ids_ref, weights, held, sems)
-    grad = row_sum(pieces)
-    hidden = hidden_ref[...]
-    inverse = rms_scale(hidden)
-    part_ref[...] = jnp.sum(grad * hidden * inverse, axis=0, keepdims=True)
-    total = cot_ref[...].astype(F32) + norm_back(grad, gain_ref[...], hidden, inverse)
-    sum_ref[...] = total
-    low = total.astype(BF)
-    low_ref[...] = low
-    for ref in sent:
-        ref[...] = low
-    shard = hidden.shape[0]
+    sent, (held, made, sems) = refs[:-3], refs[-3:]
+    for distance in range(members):
+        for copy, _, _ in weight_copies(members, ids_ref, weights, held, sems, distance):
+            copy.start()
+    shard = low_ref.shape[0]
+    step = min(32, shard)
+    part_ref[...] = jnp.zeros_like(part_ref)
+
+    def rows_at(index, carry):
+        at = pl.ds(pl.multiple_of(index * step, step), step)
+        grad = row_sum([r.at[at, :] for r in pieces])
+        hidden = pick_half(members, ids_ref, hiddens, at)
+        inverse = rms_scale(hidden)
+        part_ref[...] += jnp.sum(grad * hidden * inverse, axis=0, keepdims=True)
+        total = cot_ref[at, :].astype(F32) + norm_back(grad, gain_ref[...], hidden, inverse)
+        sum_ref[at, :] = total
+        low = total.astype(BF)
+        low_ref[at, :] = low
+        for ref in sent:
+            ref[at, :] = low
+        return carry
+
+    lax.fori_loop(0, shard // step, rows_at, 0)
     begin = (ids_ref[2] * members + ids_ref[0]) * shard
     keep = window(lengths_ref, begin + lax.broadcasted_iota(jnp.int32, (shard, 1), 0))[1]
-    for copy, distance, at, first in copies:
-        copy.wait()
-        out = jnp.where(keep, dims(low, held[at : at + size, :], 1, 1), 0.0)
-        d_mixed[distance][:, pl.ds(first, size)] = out.astype(BF)
-
-
-def norm_two_back(ids, lengths, hidden, cotangent, gain, pieces, weights, travel):
+    size = held.shape[0] // (2 * members)
+
+    def heads_of(distance, carry):
+        for copy, at, first in weight_copies(members, ids_ref, weights, held, sems, distance):
+            copy.wait()
+            out = dims(low_ref[...], held[pl.ds(at, size), :], 1, 1)
+            made[distance, :, pl.ds(first, size)] = jnp.where(keep, out, 0.0).astype(BF)
+        return carry
+
+    lax.fori_loop(0, members, heads_of, 0)
+    for distance, ref in enumerate(d_mixed):
+        ref[...] = made[distance]
+
+
+def norm_two_back(ids, lengths, hiddens, cotangent, gain, pieces, weights, travel):
     members = len(pieces)
     shard, width = pieces[0].shape
     inner = sum(w.shape[0] for w in weights)
+    per = members // HALVES
     mine = pl.BlockSpec((shard, width), lambda i, ids, lengths: (ids[0], 0))
+    mine_half = pl.BlockSpec((shard, width), lambda i, ids, lengths: (ids[0] % per, 0))
     whole = pl.BlockSpec((shard, width), lambda i, ids, lengths: (0, 0))
     line = pl.BlockSpec((1, width), lambda i, ids, lengths: (0, 0))
     head_spec = pl.BlockSpec((shard, inner // members), lambda i, ids, lengths: (0, 0))
@@ -540,12 +602,14 @@
         grid_spec=pltpu.PrefetchScalarGridSpec(
             num_scalar_prefetch=2,
             grid=(1,),
-            in_specs=[mine, mine, line]
+            in_specs=[mine_half] * HALVES
+            + [mine, line]
             + [whole] * members
             + [any_spec()] * (len(weights) + len(travel)),
             out_specs=[whole, whole, line] + [head_spec] * members + [whole] * len(travel),
             scratch_shapes=[
                 pltpu.VMEM((inner, width), BF),
+                pltpu.VMEM((members, shard, inner // members), BF),
                 pltpu.SemaphoreType.DMA((2 * members,)),
             ],
         ),
@@ -557,29 +621,44 @@
         + [jax.ShapeDtypeStruct((shard, inner // members), BF)] * members
         + [jax.ShapeDtypeStruct(t.shape, BF) for t in travel],
         input_output_aliases={
-            5 + members + len(weights) + i: 3 + members + i for i in range(len(travel))
+            4 + HALVES + members + len(weights) + i: 3 + members + i for i in range(len(travel))
         },
         name="norm_two_back",
         cost_estimate=cost(2 * shard * inner * width, 2 * inner * width + 24 * shard * width),
-    )(ids, lengths, hidden, cotangent, gain, *pieces, *weights, *travel)
-
-
-def last_rows_kernel(members, ids_ref, x_ref, hidden_ref, add_ref, gain_ref, *refs):
+    )(ids, lengths, *hiddens, cotangent, gain, *pieces, *weights, *travel)
+
+
+def last_rows_kernel(members, ids_ref, x_ref, *refs):
+    hiddens, (add_ref, gain_ref), refs = refs[:HALVES], refs[HALVES : HALVES + 2], refs[HALVES + 2 :]
     pieces, ffn, (low_ref, part_ref) = refs[:members], refs[members:-2], refs[-2:]
-    grad = row_sum(pieces)
-    values = x_ref[...].astype(F32)
-    shard = values.shape[0]
-    inverse = rms_scale(values)
-    part_ref[...] = jnp.sum(grad * values * inverse, axis=0, keepdims=True)
-    low_ref[:shard, :] = (
-        add_ref[...] + norm_back(grad, gain_ref[...], values, inverse)
-    ).astype(BF)
-    low_ref[shard:, :] = (hidden_ref[...] + row_sum(ffn)).astype(BF)
-
-
-def last_rows(ids, tokens, hidden, add, gain, pieces, ffn_pieces):
+    shard = x_ref.shape[0]
+    step = min(32, shard)
+    part_ref[...] = jnp.zeros_like(part_ref)
+
+    def rows_at(index, carry):
+        first = pl.multiple_of(index * step, step)
+        at = pl.ds(first, step)
+        grad = row_sum([r.at[at, :] for r in pieces])
+        values = x_ref[at, :].astype(F32)
+        inverse = rms_scale(values)
+        part_ref[...] += jnp.sum(grad * values * inverse, axis=0, keepdims=True)
+        low_ref[at, :] = (
+            add_ref[at, :] + norm_back(grad, gain_ref[...], values, inverse)
+        ).astype(BF)
+        hidden = pick_half(members, ids_ref, hiddens, at)
+        low_ref[pl.ds(shard + first, step), :] = (
+            hidden + row_sum([r.at[at, :] for r in ffn])
+        ).astype(BF)
+        return carry
+
+    lax.fori_loop(0, shard // step, rows_at, 0)
+
+
+def last_rows(ids, tokens, hiddens, add, gain, pieces, ffn_pieces):
     shard, width = pieces[0].shape
+    per = len(pieces) // HALVES
     mine = pl.BlockSpec((shard, width), lambda i, ids: (ids[0], 0))
+    mine_half = pl.BlockSpec((shard, width), lambda i, ids: (ids[0] % per, 0))
     first = pl.BlockSpec((shard, width), lambda i, ids: (0, 0))
     second = pl.BlockSpec((shard, width), lambda i, ids: (1, 0))
     line = pl.BlockSpec((1, width), lambda i, ids: (0, 0))
@@ -589,7 +668,7 @@
         grid_spec=pltpu.PrefetchScalarGridSpec(
             num_scalar_prefetch=1,
             grid=(1,),
-            in_specs=[mine, mine, first, line]
+            in_specs=[mine] + [mine_half] * HALVES + [first, line]
             + [first] * (len(pieces) + 1)
             + [second] * (len(ffn_pieces) - 1),
             out_specs=[both, line],
@@ -600,7 +679,7 @@
         ],
         name="last_rows",
         cost_estimate=cost(30 * shard * width, 32 * shard * width),
-    )(ids, tokens, hidden, add, gain, *pieces, *ffn_pieces)
+    )(ids, tokens, *hiddens, add, gain, *pieces, *ffn_pieces)
 
 
 def in_order_kernel(shard, outs, ids_ref, *refs):
@@ -625,8 +704,21 @@
     )(ids, *pieces)
 
 
-def ffn_kernel(n_ref, da_ref, wg_ref, wu_ref, act_ref, dg_ref, du_ref):
-    normed = n_ref[...]
+def ffn_kernel(members, ids_ref, x_ref, gain_ref, before_ref, da_ref, wg_ref, wu_ref, *refs):
+    mixes, refs = refs[:members], refs[members:]
+    weights, refs = refs[:2], refs[2:]
+    hidden_ref, normed_ref, act_ref, dg_ref, du_ref, full_s = refs[:6]
+    half_rows = before_ref.shape[0]
+
+    @pl.when(pl.program_id(0) == 0)
+    def _():
+        full_s[:half_rows, :] = before_ref[...]
+        project(
+            members, ids_ref, x_ref, gain_ref, mixes, weights, hidden_ref, normed_ref, refs[6:]
+        )
+        full_s[half_rows:, :] = normed_ref[...]
+
+    normed = full_s[...]
     gate = jnp.dot(normed, wg_ref[...], preferred_element_type=F32)
     up = jnp.dot(normed, wu_ref[...], preferred_element_type=F32)
     sig = jax.nn.sigmoid(gate)
@@ -637,25 +729,45 @@
     du_ref[...] = (d_act * silu).astype(BF)
 
 
-def ffn_forward(normed, d_act, w_gate, w_up):
-    rows, width = normed.shape
+def ffn_forward(ids, tokens, gain, mixes, weights, before, d_act, w_gate, w_up):
+    rows, width = tokens.shape
+    half_rows = rows // HALVES
+    members = len(mixes)
+    inner = 2 * weights[0].shape[0]
     units = w_gate.shape[1]
     step = min(512, units)
     tile = pl.BlockSpec((rows, step), lambda j: (0, j))
     weight = pl.BlockSpec((width, step), lambda j: (0, j))
-    return pl.pallas_call(
-        ffn_kernel,
+    half_spec = pl.BlockSpec((half_rows, width), lambda j: (0, 0))
+    return pl.pallas_call(
+        functools.partial(ffn_kernel, members),
         grid=(units // step,),
-        in_specs=[pl.BlockSpec((rows, width), lambda j: (0, 0)), tile, weight, weight],
-        out_specs=[tile, tile, tile],
-        out_shape=[jax.ShapeDtypeStruct((rows, units), BF)] * 3,
+        in_specs=[
+            smem_spec(),
+            pl.BlockSpec((half_rows, width), lambda j: (HALVES - 1, 0)),
+            pl.BlockSpec((1, width), lambda j: (0, 0)),
+            half_spec,
+            tile,
+            weight,
+            weight,
+        ]
+        + [pl.BlockSpec(m.shape, lambda j: (0, 0)) for m in mixes]
+        + [any_spec()] * len(weights),
+        out_specs=[half_spec, half_spec, tile, tile, tile],
+        out_shape=[
+            jax.ShapeDtypeStruct((half_rows, width), F32),
+            jax.ShapeDtypeStruct((half_rows, width), BF),
+        ]
+        + [jax.ShapeDtypeStruct((rows, units), BF)] * 3,
+        scratch_shapes=[pltpu.VMEM((rows, width), BF)]
+        + project_scratch(inner, width, half_rows, members),
         name="gate_up",
         cost_estimate=cost(
-            4 * rows * width * units,
-            4 * width * units + 2 * rows * width + 10 * rows * units,
+            4 * rows * width * units + 2 * half_rows * inner * width,
+            4 * width * units + 2 * rows * width + 10 * rows * units + 2 * inner * width,
             rows * units,
         ),
-    )(normed, d_act, w_gate, w_up)
+    )(ids, tokens, gain, before, d_act, w_gate, w_up, *mixes, *weights)
 
 
 def store_by_distance(ids_ref, out_refs, held, value):
@@ -727,8 +839,8 @@
     ]
 
 
-def fill_columns(held, refs):
-    count = len(refs) // 2
+def fill_columns(held, refs, groups):
+    count = len(refs) // groups
     rows, part = refs[0].shape
     for index, ref in enumerate(refs):
         top = (index // count) * rows
@@ -741,7 +853,7 @@
 
     @pl.when(pl.program_id(0) == 0)
     def _():
-        fill_columns(held, cots)
+        fill_columns(held, cots, 2)
 
     rows = own_ref.shape[0]
     o_ref[...] = (
@@ -773,13 +885,13 @@
     )(ids, act, act_other, *([cot] * blocks), *([cot_other] * blocks))
 
 
-def grad_in_kernel(blocks, half, ids_ref, *refs):
-    normeds, refs = refs[: 2 * blocks], refs[2 * blocks :]
+def grad_in_kernel(groups, blocks, half, ids_ref, *refs):
+    normeds, refs = refs[: groups * blocks], refs[groups * blocks :]
     gates, ups, (o_ref, held) = refs[:2], refs[2:4], refs[4:]
 
     @pl.when(pl.program_id(0) == 0)
     def _():
-        fill_columns(held, normeds)
+        fill_columns(held, normeds, groups)
 
     rows = gates[0].shape[0]
 
@@ -792,21 +904,21 @@
     pl.when(pl.program_id(0) >= half)(lambda: of(ups))
 
 
-def grad_in_of(ids, normed, normed_other, d_gates, d_ups, part):
-    rows, width = normed.shape
-    units = d_gates[0].shape[1]
+def grad_in_of(ids, normeds, d_gates, d_ups, part):
+    width = normeds[0].shape[1]
+    rows, units = d_gates[0].shape
     blocks = width // (2 * part)
     step = min(512, units)
     half = units // step
-    columns = column_specs(rows, part, blocks)
+    columns = column_specs(normeds[0].shape[0], part, blocks)
     first = pl.BlockSpec((rows, step), lambda j, ids: (0, jnp.minimum(j, half - 1)))
     second = pl.BlockSpec((rows, step), lambda j, ids: (0, jnp.maximum(j - half, 0)))
     return pl.pallas_call(
-        functools.partial(grad_in_kernel, blocks, half),
+        functools.partial(grad_in_kernel, len(normeds), blocks, half),
         grid_spec=pltpu.PrefetchScalarGridSpec(
             num_scalar_prefetch=1,
             grid=(2 * half,),
-            in_specs=columns + columns + [first] * 2 + [second] * 2,
+            in_specs=columns * len(normeds) + [first] * 2 + [second] * 2,
             out_specs=pl.BlockSpec((width // 2, step), lambda j, ids: (0, j)),
             scratch_shapes=[pltpu.VMEM((2 * rows, width // 2), BF)],
         ),
@@ -815,7 +927,7 @@
         cost_estimate=cost(
             4 * rows * width * units, 8 * rows * units + 2 * rows * width + 2 * width * units
         ),
-    )(ids, *([normed] * blocks), *([normed_other] * blocks), *d_gates, *d_ups)
+    )(ids, *[n for n in normeds for _ in range(blocks)], *d_gates, *d_ups)
 
 
 def grad_proj_kernel(lefts, ids_ref, *refs):
@@ -969,52 +1081,52 @@
     for near in ups:
         blocks += [near, other_core(near)]
 
-    outs, mixes, lses = [], [], []
-    filled = None
-    gathered = None
+    outs, mixes, lses, gathered = [], [], [], []
     for half in range(HALVES):
         out, mixed, lse = attend(half, ids, doc_lengths, query_t, blocks, kv_heads)
+        if gathered:
+            mixed_others = [other_core(mixes[0])]
+            gathered[-1], mixed, w_all, normed_other, mixed_others = together(
+                gathered[-1], mixed, w_all, normed_other, mixed_others
+            )
+            out_weights = [w_all, other_core(w_all)]
         outs.append(out)
         mixes.append(mixed)
         lses.append(lse)
-        waiting = gathered
-        if waiting is not None:
-            waiting, mixed, w_all, normed_other = together(waiting, mixed, w_all, normed_other)
-            out_weights = [w_all, other_core(w_all)]
         query_t, mixed = together(query_t, mixed)
-        gathered = gather_near(mixed)
-        if waiting is not None:
-            filled = attn_out(half - 1, ids, tokens, gain_two, waiting, out_weights, filled)
-            gathered, filled = together(gathered, filled)
-    hidden_one, normed_two = attn_out(
-        HALVES - 1, ids, tokens, gain_two, gathered, out_weights, filled
-    )
-
-    act, d_gate, d_up = ffn_forward(normed_two, d_act, w_gate, w_up)
+        gathered.append(gather_near(mixed))
+    hidden_first, normed_first = attn_out(0, ids, tokens, gain_two, gathered[0], out_weights)
+    gathered[1], normed_first = together(gathered[1], normed_first)
+
+    hidden_last, normed_last, act, d_gate, d_up = ffn_forward(
+        ids, tokens, gain_two, gathered[1], out_weights, normed_first, d_act, w_gate, w_up
+    )
+    hiddens = [hidden_first, hidden_last]
     act_other = other_core(act)
     d_gates = [d_gate, other_core(d_gate)]
     d_ups = [d_up, other_core(d_up)]
-    normed_two_other = other_core(normed_two)
+    normed_twos = [normed_first, normed_last]
+    normed_others = [other_core(n) for n in normed_twos]
     grad_down = grad_down_of(ids, act, act_other, cotangent, cot_other, part)
     d_gate_then, _ = together(d_gate, grad_down)
     grad_down = scatter(grad_down, 1)
     d_norm_pieces = pair_nt(narrow, ids, d_gate_then, d_up, w_gate, w_up)
-    mixed_others = [other_core(m) for m in mixes]
-    act_then, d_norm_pieces, d_gates, d_ups, normed_two_other, mixed_others = together(
-        act, d_norm_pieces, d_gates, d_ups, normed_two_other, mixed_others
+    mixed_others += [other_core(m) for m in mixes[1:]]
+    act_then, d_norm_pieces, d_gates, d_ups, normed_others, mixed_others = together(
+        act, d_norm_pieces, d_gates, d_ups, normed_others, mixed_others
     )
     d_norm_pieces = exchange(d_norm_pieces)
     ffn_pieces = down_of(narrow, ids, act_then, w_down)
-    d_norm_pieces[1], ffn_pieces, normed_two_then = together(
-        d_norm_pieces[1], ffn_pieces, normed_two
-    )
-    grad_gate_up = grad_in_of(ids, normed_two_then, normed_two_other, d_gates, d_ups, part)
+    d_norm_pieces[1], ffn_pieces, normed_twos = together(
+        d_norm_pieces[1], ffn_pieces, normed_twos
+    )
+    grad_gate_up = grad_in_of(ids, normed_twos + normed_others, d_gates, d_ups, part)
     d_norm_pieces, ffn_pieces, _ = together(d_norm_pieces, ffn_pieces, grad_gate_up)
 
     d_hidden, d_hidden_b, gain_two_part, *made = norm_two_back(
         ids,
         doc_lengths,
-        hidden_one,
+        hiddens,
         cotangent,
         gain_two,
         d_norm_pieces,
@@ -1069,7 +1181,7 @@
     last, gain_one_part = last_rows(
         ids,
         tokens,
-        hidden_one,
+        hiddens,
         d_hidden,
         gain_one,
         norm_one_pieces,

time: 435 us -> 430 us (0.989)
    unnamed x90 -> x82, local copies, waits for them, and re-layouts: 8.97 us -> 8.15 us
    pallas_call x4 -> x3, Pallas kernels: 46.7 us -> 46.3 us  [the longest x1 21.9 us: ffn_forward(): pl.pallas_call(functools.partial(ffn_kernel, members), grid=(units // ste...]
    ppermute x17 -> x18, waiting for transfers between devices: 8.71 us -> 8.62 us  [other_core(): return lax.ppermute(value, 'wide', [(i, i ^ 1) for i in range(wide)])]
  transfers between devices with their start and end apart: 52 -> 53, of which waited for: 27 -> 26; matrix products, arithmetic and copies ran while one was open for 8% -> 8% of each run, Pallas kernels for 32% -> 32%
where the time goes in v5:
time: 430 us; the launch traced here: 429 us
  waiting for transfers between devices  169 us (39%)
  Pallas kernels  150 us (35%)
  starting transfers between devices  50.2 us (12%)
  local copies, waits for them, and re-layouts  16.3 us (4%)
  other arithmetic  15.5 us (4%)
  between operations  14.4 us (3%)
  matrix products  13.9 us (3%)
    ppermute x24, waiting for transfers between devices, swap(): lax.ppermute(value, 'narrow', [(i, i ^ distance) for i in range(narrow)])  119 us
    ppermute x24, starting transfers between devices, swap(): lax.ppermute(value, 'narrow', [(i, i ^ distance) for i in range(narrow)])  29.2 us
    ppermute x2, waiting for transfers between devices, chips_down(): lax.ppermute(value, 'wide', [(i + 2 * hop, i) for i in range(wide - 2 * h...  26 us
    pallas_call x1, Pallas kernels, ffn_forward(): pl.pallas_call(functools.partial(ffn_kernel, members), grid=(units // ste...  21.9 us
    pallas_call x1, Pallas kernels, grad_in_of(): pl.pallas_call(functools.partial(grad_in_kernel, len(normeds), blocks, ha...  16.1 us
    pallas_call x3, Pallas kernels, grad_proj_of(): pl.pallas_call(functools.partial(grad_proj_kernel, len(lefts)), grid_spec...  15.8 us
    pallas_call x1, Pallas kernels, pair_nt(): pl.pallas_call(pair_nt_kernel, grid=(width // step,), in_specs=[smem_spec...  14.2 us
    dot_general x5, matrix products, dims(): lax.dot_general(left, right, (((a,), (b,)), ((), ())), preferred_element_...  13.9 us
  transfers between devices with their start and end apart: 53, of which 26 were waited for; matrix products, arithmetic and copies ran while one was open for 8% of the time, Pallas kernels for 32%

profile of v5, /device:TPU:0, one launch (start us, length us, event | category | flops | bytes accessed | tf_op | source)
XLA Modules:
  0.0 429.1 jit_solution(3891087465552469966)
XLA Ops:
  16.5 5.5 %collective-permute-start.1 = (bf16[256,512]{1,0:T(8,128)(2,1)}, bf16[256,512]{1,0:T(8,128)(2,1)S(1)}, u32[]{:S(2)}, u32[]{:S(2)}) collective-permute-start(bf16[256,512]{1,0:T(8,128)(2,1)} %get-tuple-element.142.refs_0_.refs_6_.refs_8_.refs_14_), channel_id=1, source_target_pairs={{0,16},{4,20},{8,24},{12,28},{1,17},{5,21},{9,25},{13,29},{2,18},{... | collective-permute-start | bytes 786440 | tf_op jit(solution)/shard_map/ppermute | solution.py:1033
  30.2 6.2 %fusion.12.da_ref = f32[512,2048]{1,0:T(8,128)} fusion(bf16[512,2048]{1,0:T(8,128)(2,1)S(1)} %copy-done.1, bf16[2048,2048]{1,0:T(8,128)(2,1)S(1)} %copy-done.29), kind=kOutput, calls=%fused_computation.51 | convolution fusion | flops 4294967296 | bytes 14680064 | tf_op jit(solution)/shard_map/dot_general | solution.py:53
  49.8 6.2 %attend.3 = (f32[512,256]{1,0:T(8,128)}, bf16[512,256]{1,0:T(8,128)(2,1)}, f32[2,4,256]{2,1,0:T(4,128)}) custom-call(s32[3]{0:T(128)} %pad_add_fusion.ids_ref, s32[12]{0:T(128)} %lengths_ref.7, bf16[512,512]{1,0:T(8,128)(2,1)} %bitcast.61, bf16[256,512]{1,0:T(8,128)(2,1)} %get-tuple-element.142.refs_0_.refs_6_.refs_8_.refs_14_, bf16[256,512]{1,0:T(8,128)(2,1)} %copy-done.30, ...), custom_call_target="tpu_custom_call" | custom-call | flops 1073741824 | bytes 2097152 | tf_op jit(solution)/shard_map/attend/pallas_call | solution.py:238
  56.0 5.4 %collective-permute-done.7.refs_3_ = bf16[512,256]{1,0:T(8,128)(2,1)S(1)} collective-permute-done((bf16[512,256]{1,0:T(8,128)(2,1)}, bf16[512,256]{1,0:T(8,128)(2,1)S(1)}, u32[]{:S(2)}, u32[]{:S(2)}) %collective-permute-start.7) | collective-permute-done | bytes 262176 | tf_op jit(solution)/shard_map/ppermute | solution.py:1039
  61.4 6.5 %collective-permute-done.6.refs_2_ = bf16[512,256]{1,0:T(8,128)(2,1)S(1)} collective-permute-done((bf16[512,256]{1,0:T(8,128)(2,1)}, bf16[512,256]{1,0:T(8,128)(2,1)S(1)}, u32[]{:S(2)}, u32[]{:S(2)}) %collective-permute-start.6) | collective-permute-done | bytes 262176 | tf_op jit(solution)/shard_map/ppermute | solution.py:1039
  84.7 8.3 %attn_out.1 = (f32[256,2048]{1,0:T(8,128)}, bf16[256,2048]{1,0:T(8,128)(2,1)}) custom-call(s32[3]{0:T(128)} %pad_add_fusion.ids_ref, bf16[512,2048]{1,0:T(8,128)(2,1)} %x_ref.7, f32[1,2048]{1,0:T(1,128)} %bitcast.63, bf16[512,256]{1,0:T(8,128)(2,1)} %get-tuple-element.153.refs_0_, bf16[512,256]{1,0:T(8,128)(2,1)} %copy-done.22, bf16[512,256]{1,0:T(8,128)(2,1)} %copy-done.21, ...), custom_call_target="tpu_custom_call" | custom-call | flops 2147483648 | bytes 14680064 | tf_op jit(solution)/shard_map/attn_out/pallas_call | solution.py:499
  93.0 21.9 %gate_up.1 = (f32[256,2048]{1,0:T(8,128)}, bf16[256,2048]{1,0:T(8,128)(2,1)}, bf16[512,2048]{1,0:T(8,128)(2,1)}, bf16[512,2048]{1,0:T(8,128)(2,1)}, bf16[512,2048]{1,0:T(8,128)(2,1)}) custom-call(s32[3]{0:T(128)} %pad_add_fusion.ids_ref, bf16[512,2048]{1,0:T(8,128)(2,1)} %x_ref.7, f32[1,2048]{1,0:T(1,128)} %bitcast.64, ...), custom_call_target="tpu_custom_call" | custom-call | flops 10737418240 | bytes 37748736 | tf_op jit(solution)/shard_map/gate_up/pallas_call | solution.py:742
  119.5 9.4 %grad_down.1 = bf16[2048,1024]{1,0:T(8,128)(2,1)} custom-call(s32[3]{0:T(128)} %pad_add_fusion.ids_ref, bf16[512,2048]{1,0:T(8,128)(2,1)} %get-tuple-element.180.own_ref.a_ref, bf16[512,2048]{1,0:T(8,128)(2,1)} %collective-permute-done.14.other_ref, bf16[512,2048]{1,0:T(8,128)(2,1)} %refs_2_.3, bf16[512,2048]{1,0:T(8,128)(2,1)} %refs_2_.3, ...), custom_call_target="tpu_custom_call" | custom-call | flops 4294967296 | bytes 10485760 | tf_op jit(solution)/shard_map/grad_down/pallas_call | solution.py:871
  130.7 14.2 %d_normed_two.1 = (bf16[128,2048]{1,0:T(8,128)(2,1)}, bf16[128,2048]{1,0:T(8,128)(2,1)}, bf16[128,2048]{1,0:T(8,128)(2,1)}, bf16[128,2048]{1,0:T(8,128)(2,1)}) custom-call(s32[3]{0:T(128)} %pad_add_fusion.ids_ref, bf16[512,2048]{1,0:T(8,128)(2,1)} %get-tuple-element.196.a_ref.refs_16_, bf16[512,2048]{1,0:T(8,128)(2,1)} %get-tuple-element.198.b_ref.refs_18_, ...), custom_call_target="tpu_custom_call" | custom-call | flops 8589934592 | bytes 23068672 | tf_op jit(solution)/shard_map/d_normed_two/pallas_call | solution.py:792
  148.5 8.9 %ffn_down.1 = (bf16[128,2048]{1,0:T(8,128)(2,1)}, bf16[256,2048]{1,0:T(8,128)(2,1)}, bf16[256,2048]{1,0:T(8,128)(2,1)}, bf16[256,2048]{1,0:T(8,128)(2,1)}) custom-call(s32[3]{0:T(128)} %pad_add_fusion.ids_ref, bf16[512,2048]{1,0:T(8,128)(2,1)} %get-tuple-element.180.own_ref.a_ref, bf16[2048,2048]{1,0:T(8,128)(2,1)} %w_ref.1), custom_call_target="tpu_custom_call" | custom-call | flops 4294967296 | bytes 12582912 | tf_op jit(solution)/shard_map/ffn_down/pallas_call | solution.py:816
  160.0 16.1 %grad_gate_up.1 = bf16[1024,4096]{1,0:T(8,128)(2,1)} custom-call(s32[3]{0:T(128)} %pad_add_fusion.ids_ref, bf16[256,2048]{1,0:T(8,128)(2,1)} %get-tuple-element.192.before_ref.refs_0_.refs_1_.refs_2_.refs_3_, bf16[256,2048]{1,0:T(8,128)(2,1)} %get-tuple-element.192.before_ref.refs_0_.refs_1_.refs_2_.refs_3_, ...), custom_call_target="tpu_custom_call" | custom-call | flops 8589934592 | bytes 18874368 | tf_op jit(solution)/shard_map/grad_gate_up/pallas_call | solution.py:916
  176.9 11.2 %norm_two_back.1 = (f32[128,2048]{1,0:T(8,128)}, bf16[128,2048]{1,0:T(8,128)(2,1)}, f32[1,2048]{1,0:T(1,128)}, bf16[128,512]{1,0:T(8,128)(2,1)}, bf16[128,512]{1...) custom-call(s32[3]{0:T(128)} %pad_add_fusion.ids_ref, ...), custom_call_target="tpu_custom_call", output_to_operand_aliasing={{7}: (12, {}), {8}: (13, {}), {9}: (14, {})} | custom-call | flops 1073741824 | bytes 14680064 | tf_op jit(solution)/shard_map/norm_two_back/pallas_call | solution.py:600
  201.6 11.6 %attend_back.1 = (f32[512,512]{1,0:T(8,128)}, bf16[6,2,128,512]{3,2,1,0:T(8,128)(2,1)}) custom-call(s32[3]{0:T(128)} %pad_add_fusion.ids_ref, s32[12]{0:T(128)} %lengths_ref.7, bf16[512,512]{1,0:T(8,128)(2,1)} %bitcast.62, bf16[128,512]{1,0:T(8,128)(2,1)} %get-tuple-element.214.refs_0_, bf16[128,512]{1,0:T(8,128)(2,1)} %copy-done.35, ...), custom_call_target="tpu_custom_call" | custom-call | flops 5368709120 | bytes 4194304 | tf_op jit(solution)/shard_map/attend_back/pallas_call | solution.py:399
  213.2 11.2 %collective-permute-done.27.refs_1_.refs_9_ = bf16[256,2048]{1,0:T(8,128)(2,1)S(1)} collective-permute-done((bf16[256,2048]{1,0:T(8,128)(2,1)}, bf16[256,2048]{1,0:T(8,128)(2,1)S(1)}, u32[]{:S(2)}, u32[]{:S(2)}) %collective-permute-start.27) | collective-permute-done | bytes 1048608 | tf_op jit(solution)/shard_map/ppermute | solution.py:1039
  226.8 18.2 %collective-permute-done.31.refs_2_.refs_10_ = bf16[256,2048]{1,0:T(8,128)(2,1)} collective-permute-done((bf16[256,2048]{1,0:T(8,128)(2,1)}, bf16[256,2048]{1,0:T(8,128)(2,1)}, u32[]{:S(2)}, u32[]{:S(2)}) %collective-permute-start.31) | collective-permute-done | bytes 1048608 | tf_op jit(solution)/shard_map/ppermute | solution.py:1039
  253.0 20.3 %collective-permute-done.29 = bf16[256,512]{1,0:T(8,128)(2,1)S(1)} collective-permute-done((bf16[256,512]{1,0:T(8,128)(2,1)S(1)}, bf16[256,512]{1,0:T(8,128)(2,1)S(1)}, u32[]{:S(2)}, u32[]{:S(2)}) %collective-permute-start.29) | collective-permute-done | bytes 262176 | tf_op jit(solution)/shard_map/ppermute | solution.py:1036
  280.7 5.4 %grad_query.1 = bf16[512,1024]{1,0:T(8,128)(2,1)} custom-call(s32[3]{0:T(128)} %pad_add_fusion.ids_ref, bf16[512,512]{1,0:T(8,128)(2,1)} %bitcast.53, bf16[512,512]{1,0:T(8,128)(2,1)} %copy-done.17, bf16[512,2048]{1,0:T(8,128)(2,1)} %get-tuple-element.143.refs_2_, bf16[512,2048]{1,0:T(8,128)(2,1)} %collective-permute-done.8.refs_3_), custom_call_target="tpu_custom_call" | custom-call | flops 1073741824 | bytes 4194304 | tf_op jit(solution)/shard_map/grad_query/pallas_call | solution.py:956
  286.1 5.5 %grad_out.1 = bf16[512,1024]{1,0:T(8,128)(2,1)} custom-call(s32[3]{0:T(128)} %pad_add_fusion.ids_ref, bf16[512,256]{1,0:T(8,128)(2,1)} %get-tuple-element.153.refs_0_, bf16[512,256]{1,0:T(8,128)(2,1)} %get-tuple-element.163.refs_0_.refs_1_, bf16[512,256]{1,0:T(8,128)(2,1)} %copy-done.18, bf16[512,256]{1,0:T(8,128)(2,1)} %collective-permute-done.20.refs_3_, ...), custom_call_target="tpu_custom_call" | custom-call | flops 1073741824 | bytes 4194304 | tf_op jit(solution)/shard_map/grad_out/pallas_call | solution.py:956
  291.6 5.7 %collective-permute-done.30 = bf16[256,512]{1,0:T(8,128)(2,1)} collective-permute-done((bf16[256,512]{1,0:T(8,128)(2,1)}, bf16[256,512]{1,0:T(8,128)(2,1)}, u32[]{:S(2)}, u32[]{:S(2)}) %collective-permute-start.30) | collective-permute-done | bytes 262176 | tf_op jit(solution)/shard_map/ppermute | solution.py:1036
  318.3 11.5 %collective-permute-done.36.refs_6_ = bf16[128,2048]{1,0:T(8,128)(2,1)} collective-permute-done((bf16[128,2048]{1,0:T(8,128)(2,1)}, bf16[128,2048]{1,0:T(8,128)(2,1)}, u32[]{:S(2)}, u32[]{:S(2)}) %collective-permute-start.36) | collective-permute-done | bytes 524320 | tf_op jit(solution)/shard_map/ppermute | solution.py:1039
  329.8 6.5 %last_rows.1 = (bf16[256,2048]{1,0:T(8,128)(2,1)}, f32[1,2048]{1,0:T(1,128)}) custom-call(s32[3]{0:T(128)} %pad_add_fusion.ids_ref, bf16[512,2048]{1,0:T(8,128)(2,1)} %x_ref.7, f32[256,2048]{1,0:T(8,128)} %get-tuple-element.158.refs_0_, f32[256,2048]{1,0:T(8,128)} %get-tuple-element.167.refs_1_, f32[128,2048]{1,0:T(8,128)} %get-tuple-element.244.refs_2_, ...), custom_call_target="tpu_custom_call" | custom-call | flops 7864320 | bytes 8388608 | tf_op jit(solution)/shard_map/last_rows/pallas_call | solution.py:666
  338.5 22.7 %collective-permute-done.40.refs_2_ = bf16[256,2048]{1,0:T(8,128)(2,1)} collective-permute-done((bf16[256,2048]{1,0:T(8,128)(2,1)}, bf16[256,2048]{1,0:T(8,128)(2,1)}, u32[]{:S(2)}, u32[]{:S(2)}) %collective-permute-start.40) | collective-permute-done | bytes 1048608 | tf_op jit(solution)/shard_map/ppermute | solution.py:1039
  367.0 23.6 %collective-permute-done.41.refs_3_ = bf16[256,2048]{1,0:T(8,128)(2,1)} collective-permute-done((bf16[256,2048]{1,0:T(8,128)(2,1)}, bf16[256,2048]{1,0:T(8,128)(2,1)}, u32[]{:S(2)}, u32[]{:S(2)}) %collective-permute-start.41) | collective-permute-done | bytes 1048608 | tf_op jit(solution)/shard_map/ppermute | solution.py:1039
  411.9 7.8 %reduce-scatter.8.cloned.1.call-done.in_ref = bf16[1280,256]{1,0:T(8,128)(2,1)} async-done(((bf16[1280,1024]{1,0:T(8,128)(2,1)}), bf16[1280,256]{1,0:T(8,128)(2,1)}) %reduce-scatter.8.cloned.1.call-update) | async-done | bytes 655376 | tf_op jit(solution)/shard_map/reduce_scatter | solution.py:1051
  (225 shorter events, 144.9 us)
Async XLA Ops:
  7.2 69.9 %all-gather.2.cloned.1.call-start = ((), (), s32[]{:S(2)}) async-start(), calls=%async_computation.3 | async-start | bytes 5242880 | tf_op jit(solution)/shard_map/all_gather | solution.py:1064
  9.8 287.6 %reduce-scatter.4.cloned.1.call-start = ((), (), s32[]{:S(2)}) async-start(), calls=%async_computation.4 | async-start | bytes 5242880 | tf_op jit(solution)/shard_map/reduce_scatter | solution.py:1051
  16.1 22.5 %collective-permute-start.2 = (bf16[256,512]{1,0:T(8,128)(2,1)}, bf16[256,512]{1,0:T(8,128)(2,1)S(1)}, u32[]{:S(2)}, u32[]{:S(2)}) collective-permute-start(bf16[256,512]{1,0:T(8,128)(2,1)} %get-tuple-element.142.refs_0_.refs_6_.refs_8_.refs_14_), channel_id=1, source_target_pairs={{0,4},{4,0},{8,12},{12,8},{16,20},{20,16},{24,28},{28,24},{1,5},{5... | collective-permute-start | bytes 786440 | tf_op jit(solution)/shard_map/ppermute | solution.py:1030
  25.6 47.0 %collective-permute-start.8 = (bf16[512,2048]{1,0:T(8,128)(2,1)}, bf16[512,2048]{1,0:T(8,128)(2,1)}, u32[]{:S(2)}, u32[]{:S(2)}) collective-permute-start(bf16[512,2048]{1,0:T(8,128)(2,1)} %get-tuple-element.143.refs_2_), channel_id=1, source_target_pairs={{0,4},{4,0},{8,12},{12,8},{16,20},{20,16},{24,28},{28,24},{1,5},{5... | collective-permute-start | bytes 6291464 | tf_op jit(solution)/shard_map/ppermute | solution.py:1030
  48.5 24.1 %collective-permute-start.5 = (bf16[512,256]{1,0:T(8,128)(2,1)}, bf16[512,256]{1,0:T(8,128)(2,1)S(1)}, u32[]{:S(2)}, u32[]{:S(2)}) collective-permute-start(bf16[512,256]{1,0:T(8,128)(2,1)} %get-tuple-element.153.refs_0_), channel_id=1, source_target_pairs={{0,1},{1,0},{2,3},{3,2},{4,5},{5,4},{6,7},{7,6},{8,9},{9,8},{10,11... | collective-permute-start | bytes 786440 | tf_op jit(solution)/shard_map/ppermute | solution.py:1039
  49.2 23.4 %collective-permute-start.9 = (bf16[512,256]{1,0:T(8,128)(2,1)}, bf16[512,256]{1,0:T(8,128)(2,1)S(1)}, u32[]{:S(2)}, u32[]{:S(2)}) collective-permute-start(bf16[512,256]{1,0:T(8,128)(2,1)} %get-tuple-element.153.refs_0_), channel_id=1, source_target_pairs={{0,4},{4,0},{8,12},{12,8},{16,20},{20,16},{24,28},{28,24},{1,5},{5... | collective-permute-start | bytes 786440 | tf_op jit(solution)/shard_map/ppermute | solution.py:1030
  80.6 34.5 %collective-permute-start.15 = (bf16[512,2048]{1,0:T(8,128)(2,1)}, bf16[512,2048]{1,0:T(8,128)(2,1)}, u32[]{:S(2)}, u32[]{:S(2)}) collective-permute-start(bf16[512,2048]{1,0:T(8,128)(2,1)} %refs_2_.3), channel_id=1, source_target_pairs={{0,4},{4,0},{8,12},{12,8},{16,20},{20,16},{24,28},{28,24},{1,5},{5... | collective-permute-start | bytes 6291464 | tf_op jit(solution)/shard_map/ppermute | solution.py:1030
  128.9 235.6 %reduce-scatter.6.cloned.1.call-start = ((), (), s32[]{:S(2)}) async-start(), calls=%async_computation.5 | async-start | bytes 10485760 | tf_op jit(solution)/shard_map/reduce_scatter | solution.py:1051
  146.5 29.6 %collective-permute-start.22 = (bf16[128,2048]{1,0:T(8,128)(2,1)}, bf16[128,2048]{1,0:T(8,128)(2,1)S(1)}, u32[]{:S(2)}, u32[]{:S(2)}) collective-permute-start(bf16[128,2048]{1,0:T(8,128)(2,1)} %get-tuple-element.186), channel_id=1, source_target_pairs={{0,2},{1,3},{2,0},{3,1},{4,6},{5,7},{6,4},{7,5},{8,10},{9,11},{10,... | collective-permute-start | bytes 1572872 | tf_op jit(solution)/shard_map/ppermute | solution.py:1039
  147.1 29.1 %collective-permute-start.23 = (bf16[128,2048]{1,0:T(8,128)(2,1)}, bf16[128,2048]{1,0:T(8,128)(2,1)}, u32[]{:S(2)}, u32[]{:S(2)}) collective-permute-start(bf16[128,2048]{1,0:T(8,128)(2,1)} %get-tuple-element.187), channel_id=1, source_target_pairs={{0,3},{1,2},{2,1},{3,0},{4,7},{5,6},{6,5},{7,4},{8,11},{9,10},{10,... | collective-permute-start | bytes 1572872 | tf_op jit(solution)/shard_map/ppermute | solution.py:1039
  188.2 231.5 %reduce-scatter.8.cloned.1.call-start = ((), (), s32[]{:S(2)}) async-start(), calls=%async_computation.6 | async-start | bytes 3276800 | tf_op jit(solution)/shard_map/reduce_scatter | solution.py:1051
  198.1 26.3 %collective-permute-start.27 = (bf16[256,2048]{1,0:T(8,128)(2,1)}, bf16[256,2048]{1,0:T(8,128)(2,1)S(1)}, u32[]{:S(2)}, u32[]{:S(2)}) collective-permute-start(bf16[256,2048]{1,0:T(8,128)(2,1)} %get-tuple-element.224), channel_id=1, source_target_pairs={{0,1},{1,0},{2,3},{3,2},{4,5},{5,4},{6,7},{7,6},{8,9},{9,8},{10,11... | collective-permute-start | bytes 3145736 | tf_op jit(solution)/shard_map/ppermute | solution.py:1039
  199.4 45.7 %collective-permute-start.31 = (bf16[256,2048]{1,0:T(8,128)(2,1)}, bf16[256,2048]{1,0:T(8,128)(2,1)}, u32[]{:S(2)}, u32[]{:S(2)}) collective-permute-start(bf16[256,2048]{1,0:T(8,128)(2,1)} %get-tuple-element.230), channel_id=1, source_target_pairs={{0,2},{1,3},{2,0},{3,1},{4,6},{5,7},{6,4},{7,5},{8,10},{9,11},{10,... | collective-permute-start | bytes 3145736 | tf_op jit(solution)/shard_map/ppermute | solution.py:1039
  200.1 44.9 %collective-permute-start.32 = (bf16[256,2048]{1,0:T(8,128)(2,1)}, bf16[256,2048]{1,0:T(8,128)(2,1)}, u32[]{:S(2)}, u32[]{:S(2)}) collective-permute-start(bf16[256,2048]{1,0:T(8,128)(2,1)} %get-tuple-element.231), channel_id=1, source_target_pairs={{0,3},{1,2},{2,1},{3,0},{4,7},{5,6},{6,5},{7,4},{8,11},{9,10},{10,... | collective-permute-start | bytes 3145736 | tf_op jit(solution)/shard_map/ppermute | solution.py:1039
  226.8 23.3 %collective-permute-start.28 = (bf16[3,256,512]{2,1,0:T(8,128)(2,1)}, bf16[3,256,512]{2,1,0:T(8,128)(2,1)}, u32[]{:S(2)}, u32[]{:S(2)}) collective-permute-start(bf16[3,256,512]{2,1,0:T(8,128)(2,1)} %slice.64), channel_id=1, source_target_pairs={{0,4},{4,0},{8,12},{12,8},{16,20},{20,16},{24,28},{28,24},{1,5},{5... | collective-permute-start | bytes 2359304 | tf_op jit(solution)/shard_map/ppermute | solution.py:1030
  248.5 37.6 %collective-permute-start.33 = (bf16[512,2048]{1,0:T(8,128)(2,1)}, bf16[512,2048]{1,0:T(8,128)(2,1)}, u32[]{:S(2)}, u32[]{:S(2)}) collective-permute-start(bf16[512,2048]{1,0:T(8,128)(2,1)} %token_order.2.refs_4_), channel_id=1, source_target_pairs={{0,4},{4,0},{8,12},{12,8},{16,20},{20,16},{24,28},{28,24},{1,5},{5... | collective-permute-start | bytes 6291464 | tf_op jit(solution)/shard_map/ppermute | solution.py:1030
  251.1 22.1 %collective-permute-start.29 = (bf16[256,512]{1,0:T(8,128)(2,1)S(1)}, bf16[256,512]{1,0:T(8,128)(2,1)S(1)}, u32[]{:S(2)}, u32[]{:S(2)}) collective-permute-start(bf16[256,512]{1,0:T(8,128)(2,1)S(1)} %fusion), channel_id=1, source_target_pairs={{8,0},{12,4},{16,8},{20,12},{24,16},{28,20},{9,1},{13,5},{17,9},{2... | collective-permute-start | bytes 786440 | tf_op jit(solution)/shard_map/ppermute | solution.py:1036
  252.7 27.2 %collective-permute-start.34 = (bf16[512,512]{1,0:T(8,128)(2,1)S(1)}, bf16[512,512]{1,0:T(8,128)(2,1)S(1)}, u32[]{:S(2)}, u32[]{:S(2)}) collective-permute-start(bf16[512,512]{1,0:T(8,128)(2,1)S(1)} %bitcast.51), channel_id=1, source_target_pairs={{0,4},{4,0},{8,12},{12,8},{16,20},{20,16},{24,28},{28,24},{1,5},{5... | collective-permute-start | bytes 1572872 | tf_op jit(solution)/shard_map/ppermute | solution.py:1030
  275.1 22.3 %collective-permute-start.30 = (bf16[256,512]{1,0:T(8,128)(2,1)}, bf16[256,512]{1,0:T(8,128)(2,1)}, u32[]{:S(2)}, u32[]{:S(2)}) collective-permute-start(bf16[256,512]{1,0:T(8,128)(2,1)} %fusion.2), channel_id=1, source_target_pairs={{8,0},{12,4},{16,8},{20,12},{24,16},{28,20},{9,1},{13,5},{17,9},{2... | collective-permute-start | bytes 786440 | tf_op jit(solution)/shard_map/ppermute | solution.py:1036
  304.3 25.5 %collective-permute-start.36 = (bf16[128,2048]{1,0:T(8,128)(2,1)}, bf16[128,2048]{1,0:T(8,128)(2,1)}, u32[]{:S(2)}, u32[]{:S(2)}) collective-permute-start(bf16[128,2048]{1,0:T(8,128)(2,1)} %get-tuple-element.237), channel_id=1, source_target_pairs={{0,2},{1,3},{2,0},{3,1},{4,6},{5,7},{6,4},{7,5},{8,10},{9,11},{10,... | collective-permute-start | bytes 1572872 | tf_op jit(solution)/shard_map/ppermute | solution.py:1039
  305.8 24.1 %collective-permute-start.37 = (bf16[128,2048]{1,0:T(8,128)(2,1)}, bf16[128,2048]{1,0:T(8,128)(2,1)}, u32[]{:S(2)}, u32[]{:S(2)}) collective-permute-start(bf16[128,2048]{1,0:T(8,128)(2,1)} %get-tuple-element.238), channel_id=1, source_target_pairs={{0,3},{1,2},{2,1},{3,0},{4,7},{5,6},{6,5},{7,4},{8,11},{9,10},{10,... | collective-permute-start | bytes 1572872 | tf_op jit(solution)/shard_map/ppermute | solution.py:1039
  336.3 24.9 %collective-permute-start.40 = (bf16[256,2048]{1,0:T(8,128)(2,1)}, bf16[256,2048]{1,0:T(8,128)(2,1)}, u32[]{:S(2)}, u32[]{:S(2)}) collective-permute-start(bf16[256,2048]{1,0:T(8,128)(2,1)} %get-tuple-element.250.refs_0_), channel_id=1, source_target_pairs={{0,2},{1,3},{2,0},{3,1},{4,6},{5,7},{6,4},{7,5},{8,10},{9,11},{10,... | collective-permute-start | bytes 3145736 | tf_op jit(solution)/shard_map/ppermute | solution.py:1039
  337.9 24.1 %collective-permute-start.39 = (bf16[256,2048]{1,0:T(8,128)(2,1)}, bf16[256,2048]{1,0:T(8,128)(2,1)}, u32[]{:S(2)}, u32[]{:S(2)}) collective-permute-start(bf16[256,2048]{1,0:T(8,128)(2,1)} %get-tuple-element.250.refs_0_), channel_id=1, source_target_pairs={{0,1},{1,0},{2,3},{3,2},{4,5},{5,4},{6,7},{7,6},{8,9},{9,8},{10,11... | collective-permute-start | bytes 3145736 | tf_op jit(solution)/shard_map/ppermute | solution.py:1039
  364.5 26.0 %collective-permute-start.41 = (bf16[256,2048]{1,0:T(8,128)(2,1)}, bf16[256,2048]{1,0:T(8,128)(2,1)}, u32[]{:S(2)}, u32[]{:S(2)}) collective-permute-start(bf16[256,2048]{1,0:T(8,128)(2,1)} %get-tuple-element.250.refs_0_), channel_id=1, source_target_pairs={{0,3},{1,2},{2,1},{3,0},{4,7},{5,6},{6,5},{7,4},{8,11},{9,10},{10,... | collective-permute-start | bytes 3145736 | tf_op jit(solution)/shard_map/ppermute | solution.py:1039
  (70 other events, 665.2 us)
Sparse Core Ops, SparseCore 0:
  10.5 66.6 all-gather.1
  129.0 76.8 reduce-scatter.3
  208.3 156.1 reduce-scatter.5
  366.8 52.9 reduce-scatter.7

commit v6 on v5

--- a/solution.py
+++ b/solution.py
@@ -848,41 +848,50 @@
         held[top : top + rows, left : left + part] = ref[...]
 
 
-def grad_down_kernel(blocks, ids_ref, own_ref, other_ref, *refs):
-    cots, (o_ref, held) = refs[: 2 * blocks], refs[2 * blocks :]
-
-    @pl.when(pl.program_id(0) == 0)
-    def _():
-        fill_columns(held, cots, 2)
-
+def pick_columns_kernel(blocks, ids_ref, *refs):
+    fill_columns(refs[-1], refs[:-1], len(refs[:-1]) // blocks)
+
+
+def pick_columns(ids, values, part):
+    rows, width = values[0].shape
+    blocks = width // (2 * part)
+    return pl.pallas_call(
+        functools.partial(pick_columns_kernel, blocks),
+        grid_spec=pltpu.PrefetchScalarGridSpec(
+            num_scalar_prefetch=1,
+            grid=(1,),
+            in_specs=column_specs(rows, part, blocks) * len(values),
+            out_specs=pl.BlockSpec((len(values) * rows, width // 2), lambda j, ids: (0, 0)),
+        ),
+        out_shape=jax.ShapeDtypeStruct((len(values) * rows, width // 2), BF),
+        name="pick_columns",
+        cost_estimate=cost(0, 4 * len(values) * rows * width // 2),
+    )(ids, *[v for v in values for _ in range(blocks)])
+
+
+def grad_down_kernel(own_ref, other_ref, cot_ref, o_ref):
     rows = own_ref.shape[0]
     o_ref[...] = (
-        dims(own_ref[...], held[:rows, :], 0, 0) + dims(other_ref[...], held[rows:, :], 0, 0)
+        dims(own_ref[...], cot_ref[:rows, :], 0, 0) + dims(other_ref[...], cot_ref[rows:, :], 0, 0)
     ).astype(BF)
 
 
-def grad_down_of(ids, act, act_other, cot, cot_other, part):
+def grad_down_of(act, act_other, cots):
     rows, units = act.shape
-    width = cot.shape[1]
-    blocks = width // (2 * part)
+    width = cots.shape[1]
     step = min(512, units)
-    tile = pl.BlockSpec((rows, step), lambda j, ids: (0, j))
-    columns = column_specs(rows, part, blocks)
-    return pl.pallas_call(
-        functools.partial(grad_down_kernel, blocks),
-        grid_spec=pltpu.PrefetchScalarGridSpec(
-            num_scalar_prefetch=1,
-            grid=(units // step,),
-            in_specs=[tile, tile] + columns + columns,
-            out_specs=pl.BlockSpec((step, width // 2), lambda j, ids: (j, 0)),
-            scratch_shapes=[pltpu.VMEM((2 * rows, width // 2), BF)],
-        ),
-        out_shape=jax.ShapeDtypeStruct((units, width // 2), BF),
+    tile = pl.BlockSpec((rows, step), lambda j: (0, j))
+    return pl.pallas_call(
+        grad_down_kernel,
+        grid=(units // step,),
+        in_specs=[tile, tile, pl.BlockSpec((2 * rows, width), lambda j: (0, 0))],
+        out_specs=pl.BlockSpec((step, width), lambda j: (j, 0)),
+        out_shape=jax.ShapeDtypeStruct((units, width), BF),
         name="grad_down",
         cost_estimate=cost(
-            2 * rows * width * units, 4 * rows * units + 2 * rows * width + width * units
-        ),
-    )(ids, act, act_other, *([cot] * blocks), *([cot_other] * blocks))
+            4 * rows * width * units, 4 * rows * units + 4 * rows * width + 2 * width * units
+        ),
+    )(act, act_other, cots)
 
 
 def grad_in_kernel(groups, blocks, half, ids_ref, *refs):
@@ -1107,7 +1116,10 @@
     d_ups = [d_up, other_core(d_up)]
     normed_twos = [normed_first, normed_last]
     normed_others = [other_core(n) for n in normed_twos]
-    grad_down = grad_down_of(ids, act, act_other, cotangent, cot_other, part)
+    act, cot_other, cot_mine = together(act, cot_other, cotangent)
+    cots = pick_columns(ids, [cot_mine, cot_other], part)
+    act_other, cots = together(act_other, cots)
+    grad_down = grad_down_of(act, act_other, cots)
     d_gate_then, _ = together(d_gate, grad_down)
     grad_down = scatter(grad_down, 1)
     d_norm_pieces = pair_nt(narrow, ids, d_gate_then, d_up, w_gate, w_up)

time: 430 us -> 429 us (level)
    pallas_call x1 -> x2, Pallas kernels: 9.37 us -> 12.2 us  [the longest x1 8.43 us: grad_down_of(): pl.pallas_call(grad_down_kernel, grid=(units // step,), in_specs=[tile, t...]
  transfers between devices with their start and end apart: 53 -> 53, of which waited for: 26 -> 26; matrix products, arithmetic and copies ran while one was open for 8% -> 8% of each run, Pallas kernels for 32% -> 33%
where the time goes in v6:
time: 429 us; the launch traced here: 428 us
  waiting for transfers between devices  165 us (38%)
  Pallas kernels  153 us (36%)
  starting transfers between devices  50.2 us (12%)
  local copies, waits for them, and re-layouts  16.4 us (4%)
  other arithmetic  15.5 us (4%)
  between operations  14.4 us (3%)
  matrix products  13.9 us (3%)
    ppermute x24, waiting for transfers between devices, swap(): lax.ppermute(value, 'narrow', [(i, i ^ distance) for i in range(narrow)])  119 us
    ppermute x24, starting transfers between devices, swap(): lax.ppermute(value, 'narrow', [(i, i ^ distance) for i in range(narrow)])  29.2 us
    ppermute x2, waiting for transfers between devices, chips_down(): lax.ppermute(value, 'wide', [(i + 2 * hop, i) for i in range(wide - 2 * h...  26 us
    pallas_call x1, Pallas kernels, ffn_forward(): pl.pallas_call(functools.partial(ffn_kernel, members), grid=(units // ste...  21.9 us
    pallas_call x1, Pallas kernels, grad_in_of(): pl.pallas_call(functools.partial(grad_in_kernel, len(normeds), blocks, ha...  16.1 us
    pallas_call x3, Pallas kernels, grad_proj_of(): pl.pallas_call(functools.partial(grad_proj_kernel, len(lefts)), grid_spec...  15.9 us
    pallas_call x1, Pallas kernels, pair_nt(): pl.pallas_call(pair_nt_kernel, grid=(width // step,), in_specs=[smem_spec...  14.2 us
    dot_general x5, matrix products, dims(): lax.dot_general(left, right, (((a,), (b,)), ((), ())), preferred_element_...  13.9 us
  transfers between devices with their start and end apart: 53, of which 26 were waited for; matrix products, arithmetic and copies ran while one was open for 8% of the time, Pallas kernels for 33%

profile of v6, /device:TPU:0, one launch (start us, length us, event | category | flops | bytes accessed | tf_op | source)
XLA Modules:
  0.0 428.1 jit_solution(4482137418588731568)
XLA Ops:
  16.5 5.5 %collective-permute-start.1 = (bf16[256,512]{1,0:T(8,128)(2,1)}, bf16[256,512]{1,0:T(8,128)(2,1)S(1)}, u32[]{:S(2)}, u32[]{:S(2)}) collective-permute-start(bf16[256,512]{1,0:T(8,128)(2,1)} %get-tuple-element.147.refs_0_.refs_6_.refs_8_.refs_14_), channel_id=1, source_target_pairs={{0,16},{4,20},{8,24},{12,28},{1,17},{5,21},{9,25},{13,29},{2,18},{... | collective-permute-start | bytes 786440 | tf_op jit(solution)/shard_map/ppermute | solution.py:1042
  30.2 6.2 %fusion.12.da_ref = f32[512,2048]{1,0:T(8,128)} fusion(bf16[512,2048]{1,0:T(8,128)(2,1)S(1)} %copy-done.1, bf16[2048,2048]{1,0:T(8,128)(2,1)S(1)} %copy-done.29), kind=kOutput, calls=%fused_computation.51 | convolution fusion | flops 4294967296 | bytes 14680064 | tf_op jit(solution)/shard_map/dot_general | solution.py:53
  49.8 6.2 %attend.3 = (f32[512,256]{1,0:T(8,128)}, bf16[512,256]{1,0:T(8,128)(2,1)}, f32[2,4,256]{2,1,0:T(4,128)}) custom-call(s32[3]{0:T(128)} %pad_add_fusion.ids_ref, s32[12]{0:T(128)} %lengths_ref.7, bf16[512,512]{1,0:T(8,128)(2,1)} %bitcast.61, bf16[256,512]{1,0:T(8,128)(2,1)} %get-tuple-element.147.refs_0_.refs_6_.refs_8_.refs_14_, bf16[256,512]{1,0:T(8,128)(2,1)} %copy-done.30, ...), custom_call_target="tpu_custom_call" | custom-call | flops 1073741824 | bytes 2097152 | tf_op jit(solution)/shard_map/attend/pallas_call | solution.py:238
  56.0 5.4 %collective-permute-done.7.refs_3_ = bf16[512,256]{1,0:T(8,128)(2,1)S(1)} collective-permute-done((bf16[512,256]{1,0:T(8,128)(2,1)}, bf16[512,256]{1,0:T(8,128)(2,1)S(1)}, u32[]{:S(2)}, u32[]{:S(2)}) %collective-permute-start.7) | collective-permute-done | bytes 262176 | tf_op jit(solution)/shard_map/ppermute | solution.py:1048
  61.4 6.5 %collective-permute-done.6.refs_2_ = bf16[512,256]{1,0:T(8,128)(2,1)S(1)} collective-permute-done((bf16[512,256]{1,0:T(8,128)(2,1)}, bf16[512,256]{1,0:T(8,128)(2,1)S(1)}, u32[]{:S(2)}, u32[]{:S(2)}) %collective-permute-start.6) | collective-permute-done | bytes 262176 | tf_op jit(solution)/shard_map/ppermute | solution.py:1048
  84.7 8.3 %attn_out.1 = (f32[256,2048]{1,0:T(8,128)}, bf16[256,2048]{1,0:T(8,128)(2,1)}) custom-call(s32[3]{0:T(128)} %pad_add_fusion.ids_ref, bf16[512,2048]{1,0:T(8,128)(2,1)} %x_ref.7, f32[1,2048]{1,0:T(1,128)} %bitcast.63, bf16[512,256]{1,0:T(8,128)(2,1)} %get-tuple-element.158.refs_0_, bf16[512,256]{1,0:T(8,128)(2,1)} %copy-done.22, bf16[512,256]{1,0:T(8,128)(2,1)} %copy-done.21, ...), custom_call_target="tpu_custom_call" | custom-call | flops 2147483648 | bytes 14680064 | tf_op jit(solution)/shard_map/attn_out/pallas_call | solution.py:499
  93.0 21.9 %gate_up.1 = (f32[256,2048]{1,0:T(8,128)}, bf16[256,2048]{1,0:T(8,128)(2,1)}, bf16[512,2048]{1,0:T(8,128)(2,1)}, bf16[512,2048]{1,0:T(8,128)(2,1)}, bf16[512,2048]{1,0:T(8,128)(2,1)}) custom-call(s32[3]{0:T(128)} %pad_add_fusion.ids_ref, bf16[512,2048]{1,0:T(8,128)(2,1)} %x_ref.7, f32[1,2048]{1,0:T(1,128)} %bitcast.64, ...), custom_call_target="tpu_custom_call" | custom-call | flops 10737418240 | bytes 37748736 | tf_op jit(solution)/shard_map/gate_up/pallas_call | solution.py:742
  119.5 8.4 %grad_down.1 = bf16[2048,1024]{1,0:T(8,128)(2,1)} custom-call(bf16[512,2048]{1,0:T(8,128)(2,1)} %get-tuple-element.190.own_ref.a_ref, bf16[512,2048]{1,0:T(8,128)(2,1)} %collective-permute-done.15.other_ref, bf16[1024,1024]{1,0:T(8,128)(2,1)} %pick_columns.1.cot_ref), custom_call_target="tpu_custom_call" | custom-call | flops 4294967296 | bytes 10485760 | tf_op jit(solution)/shard_map/grad_down/pallas_call | solution.py:884
  129.8 14.2 %d_normed_two.1 = (bf16[128,2048]{1,0:T(8,128)(2,1)}, bf16[128,2048]{1,0:T(8,128)(2,1)}, bf16[128,2048]{1,0:T(8,128)(2,1)}, bf16[128,2048]{1,0:T(8,128)(2,1)}) custom-call(s32[3]{0:T(128)} %pad_add_fusion.ids_ref, bf16[512,2048]{1,0:T(8,128)(2,1)} %get-tuple-element.206.a_ref.refs_16_, bf16[512,2048]{1,0:T(8,128)(2,1)} %get-tuple-element.208.b_ref.refs_18_, ...), custom_call_target="tpu_custom_call" | custom-call | flops 8589934592 | bytes 23068672 | tf_op jit(solution)/shard_map/d_normed_two/pallas_call | solution.py:792
  147.6 8.9 %ffn_down.1 = (bf16[128,2048]{1,0:T(8,128)(2,1)}, bf16[256,2048]{1,0:T(8,128)(2,1)}, bf16[256,2048]{1,0:T(8,128)(2,1)}, bf16[256,2048]{1,0:T(8,128)(2,1)}) custom-call(s32[3]{0:T(128)} %pad_add_fusion.ids_ref, bf16[512,2048]{1,0:T(8,128)(2,1)} %get-tuple-element.190.own_ref.a_ref, bf16[2048,2048]{1,0:T(8,128)(2,1)} %w_ref.1), custom_call_target="tpu_custom_call" | custom-call | flops 4294967296 | bytes 12582912 | tf_op jit(solution)/shard_map/ffn_down/pallas_call | solution.py:816
  159.1 16.1 %grad_gate_up.1 = bf16[1024,4096]{1,0:T(8,128)(2,1)} custom-call(s32[3]{0:T(128)} %pad_add_fusion.ids_ref, bf16[256,2048]{1,0:T(8,128)(2,1)} %get-tuple-element.202.before_ref.refs_0_.refs_1_.refs_2_.refs_3_, bf16[256,2048]{1,0:T(8,128)(2,1)} %get-tuple-element.202.before_ref.refs_0_.refs_1_.refs_2_.refs_3_, ...), custom_call_target="tpu_custom_call" | custom-call | flops 8589934592 | bytes 18874368 | tf_op jit(solution)/shard_map/grad_gate_up/pallas_call | solution.py:925
  176.0 11.2 %norm_two_back.1 = (f32[128,2048]{1,0:T(8,128)}, bf16[128,2048]{1,0:T(8,128)(2,1)}, f32[1,2048]{1,0:T(1,128)}, bf16[128,512]{1,0:T(8,128)(2,1)}, bf16[128,512]{1...) custom-call(s32[3]{0:T(128)} %pad_add_fusion.ids_ref, ...), custom_call_target="tpu_custom_call", output_to_operand_aliasing={{7}: (12, {}), {8}: (13, {}), {9}: (14, {})} | custom-call | flops 1073741824 | bytes 14680064 | tf_op jit(solution)/shard_map/norm_two_back/pallas_call | solution.py:600
  200.6 11.6 %attend_back.1 = (f32[512,512]{1,0:T(8,128)}, bf16[6,2,128,512]{3,2,1,0:T(8,128)(2,1)}) custom-call(s32[3]{0:T(128)} %pad_add_fusion.ids_ref, s32[12]{0:T(128)} %lengths_ref.7, bf16[512,512]{1,0:T(8,128)(2,1)} %bitcast.62, bf16[128,512]{1,0:T(8,128)(2,1)} %get-tuple-element.224.refs_0_, bf16[128,512]{1,0:T(8,128)(2,1)} %copy-done.35, ...), custom_call_target="tpu_custom_call" | custom-call | flops 5368709120 | bytes 4194304 | tf_op jit(solution)/shard_map/attend_back/pallas_call | solution.py:399
  212.3 11.2 %collective-permute-done.27.refs_1_.refs_9_ = bf16[256,2048]{1,0:T(8,128)(2,1)S(1)} collective-permute-done((bf16[256,2048]{1,0:T(8,128)(2,1)}, bf16[256,2048]{1,0:T(8,128)(2,1)S(1)}, u32[]{:S(2)}, u32[]{:S(2)}) %collective-permute-start.27) | collective-permute-done | bytes 1048608 | tf_op jit(solution)/shard_map/ppermute | solution.py:1048
  225.9 18.2 %collective-permute-done.31.refs_2_.refs_10_ = bf16[256,2048]{1,0:T(8,128)(2,1)} collective-permute-done((bf16[256,2048]{1,0:T(8,128)(2,1)}, bf16[256,2048]{1,0:T(8,128)(2,1)}, u32[]{:S(2)}, u32[]{:S(2)}) %collective-permute-start.31) | collective-permute-done | bytes 1048608 | tf_op jit(solution)/shard_map/ppermute | solution.py:1048
  252.0 20.3 %collective-permute-done.29 = bf16[256,512]{1,0:T(8,128)(2,1)S(1)} collective-permute-done((bf16[256,512]{1,0:T(8,128)(2,1)S(1)}, bf16[256,512]{1,0:T(8,128)(2,1)S(1)}, u32[]{:S(2)}, u32[]{:S(2)}) %collective-permute-start.29) | collective-permute-done | bytes 262176 | tf_op jit(solution)/shard_map/ppermute | solution.py:1045
  279.7 5.4 %grad_query.1 = bf16[512,1024]{1,0:T(8,128)(2,1)} custom-call(s32[3]{0:T(128)} %pad_add_fusion.ids_ref, bf16[512,512]{1,0:T(8,128)(2,1)} %bitcast.53, bf16[512,512]{1,0:T(8,128)(2,1)} %copy-done.17, bf16[512,2048]{1,0:T(8,128)(2,1)} %get-tuple-element.148.refs_2_, bf16[512,2048]{1,0:T(8,128)(2,1)} %collective-permute-done.8.refs_3_), custom_call_target="tpu_custom_call" | custom-call | flops 1073741824 | bytes 4194304 | tf_op jit(solution)/shard_map/grad_query/pallas_call | solution.py:965
  285.2 5.6 %grad_out.1 = bf16[512,1024]{1,0:T(8,128)(2,1)} custom-call(s32[3]{0:T(128)} %pad_add_fusion.ids_ref, bf16[512,256]{1,0:T(8,128)(2,1)} %get-tuple-element.158.refs_0_, bf16[512,256]{1,0:T(8,128)(2,1)} %get-tuple-element.168.refs_0_.refs_1_, bf16[512,256]{1,0:T(8,128)(2,1)} %copy-done.18, bf16[512,256]{1,0:T(8,128)(2,1)} %collective-permute-done.20.refs_3_, ...), custom_call_target="tpu_custom_call" | custom-call | flops 1073741824 | bytes 4194304 | tf_op jit(solution)/shard_map/grad_out/pallas_call | solution.py:965
  290.7 5.7 %collective-permute-done.30 = bf16[256,512]{1,0:T(8,128)(2,1)} collective-permute-done((bf16[256,512]{1,0:T(8,128)(2,1)}, bf16[256,512]{1,0:T(8,128)(2,1)}, u32[]{:S(2)}, u32[]{:S(2)}) %collective-permute-start.30) | collective-permute-done | bytes 262176 | tf_op jit(solution)/shard_map/ppermute | solution.py:1045
  317.4 11.4 %collective-permute-done.36.refs_6_ = bf16[128,2048]{1,0:T(8,128)(2,1)} collective-permute-done((bf16[128,2048]{1,0:T(8,128)(2,1)}, bf16[128,2048]{1,0:T(8,128)(2,1)}, u32[]{:S(2)}, u32[]{:S(2)}) %collective-permute-start.36) | collective-permute-done | bytes 524320 | tf_op jit(solution)/shard_map/ppermute | solution.py:1048
  328.8 6.5 %last_rows.1 = (bf16[256,2048]{1,0:T(8,128)(2,1)}, f32[1,2048]{1,0:T(1,128)}) custom-call(s32[3]{0:T(128)} %pad_add_fusion.ids_ref, bf16[512,2048]{1,0:T(8,128)(2,1)} %x_ref.7, f32[256,2048]{1,0:T(8,128)} %get-tuple-element.163.refs_0_, f32[256,2048]{1,0:T(8,128)} %get-tuple-element.172.refs_1_, f32[128,2048]{1,0:T(8,128)} %get-tuple-element.254.refs_2_, ...), custom_call_target="tpu_custom_call" | custom-call | flops 7864320 | bytes 8388608 | tf_op jit(solution)/shard_map/last_rows/pallas_call | solution.py:666
  337.4 22.7 %collective-permute-done.40.refs_2_ = bf16[256,2048]{1,0:T(8,128)(2,1)} collective-permute-done((bf16[256,2048]{1,0:T(8,128)(2,1)}, bf16[256,2048]{1,0:T(8,128)(2,1)}, u32[]{:S(2)}, u32[]{:S(2)}) %collective-permute-start.40) | collective-permute-done | bytes 1048608 | tf_op jit(solution)/shard_map/ppermute | solution.py:1048
  365.9 23.6 %collective-permute-done.41.refs_3_ = bf16[256,2048]{1,0:T(8,128)(2,1)} collective-permute-done((bf16[256,2048]{1,0:T(8,128)(2,1)}, bf16[256,2048]{1,0:T(8,128)(2,1)}, u32[]{:S(2)}, u32[]{:S(2)}) %collective-permute-start.41) | collective-permute-done | bytes 1048608 | tf_op jit(solution)/shard_map/ppermute | solution.py:1048
  410.9 7.8 %reduce-scatter.8.cloned.1.call-done.in_ref = bf16[1280,256]{1,0:T(8,128)(2,1)} async-done(((bf16[1280,1024]{1,0:T(8,128)(2,1)}), bf16[1280,256]{1,0:T(8,128)(2,1)}) %reduce-scatter.8.cloned.1.call-update) | async-done | bytes 655376 | tf_op jit(solution)/shard_map/reduce_scatter | solution.py:1060
  (226 shorter events, 145.0 us)
Async XLA Ops:
  7.2 69.9 %all-gather.2.cloned.1.call-start = ((), (), s32[]{:S(2)}) async-start(), calls=%async_computation.3 | async-start | bytes 5242880 | tf_op jit(solution)/shard_map/all_gather | solution.py:1073
  9.8 286.7 %reduce-scatter.4.cloned.1.call-start = ((), (), s32[]{:S(2)}) async-start(), calls=%async_computation.4 | async-start | bytes 5242880 | tf_op jit(solution)/shard_map/reduce_scatter | solution.py:1060
  16.1 22.5 %collective-permute-start.2 = (bf16[256,512]{1,0:T(8,128)(2,1)}, bf16[256,512]{1,0:T(8,128)(2,1)S(1)}, u32[]{:S(2)}, u32[]{:S(2)}) collective-permute-start(bf16[256,512]{1,0:T(8,128)(2,1)} %get-tuple-element.147.refs_0_.refs_6_.refs_8_.refs_14_), channel_id=1, source_target_pairs={{0,4},{4,0},{8,12},{12,8},{16,20},{20,16},{24,28},{28,24},{1,5},{5... | collective-permute-start | bytes 786440 | tf_op jit(solution)/shard_map/ppermute | solution.py:1039
  25.6 47.0 %collective-permute-start.8 = (bf16[512,2048]{1,0:T(8,128)(2,1)}, bf16[512,2048]{1,0:T(8,128)(2,1)}, u32[]{:S(2)}, u32[]{:S(2)}) collective-permute-start(bf16[512,2048]{1,0:T(8,128)(2,1)} %get-tuple-element.148.refs_2_), channel_id=1, source_target_pairs={{0,4},{4,0},{8,12},{12,8},{16,20},{20,16},{24,28},{28,24},{1,5},{5... | collective-permute-start | bytes 6291464 | tf_op jit(solution)/shard_map/ppermute | solution.py:1039
  48.5 24.1 %collective-permute-start.5 = (bf16[512,256]{1,0:T(8,128)(2,1)}, bf16[512,256]{1,0:T(8,128)(2,1)S(1)}, u32[]{:S(2)}, u32[]{:S(2)}) collective-permute-start(bf16[512,256]{1,0:T(8,128)(2,1)} %get-tuple-element.158.refs_0_), channel_id=1, source_target_pairs={{0,1},{1,0},{2,3},{3,2},{4,5},{5,4},{6,7},{7,6},{8,9},{9,8},{10,11... | collective-permute-start | bytes 786440 | tf_op jit(solution)/shard_map/ppermute | solution.py:1048
  49.2 23.4 %collective-permute-start.9 = (bf16[512,256]{1,0:T(8,128)(2,1)}, bf16[512,256]{1,0:T(8,128)(2,1)S(1)}, u32[]{:S(2)}, u32[]{:S(2)}) collective-permute-start(bf16[512,256]{1,0:T(8,128)(2,1)} %get-tuple-element.158.refs_0_), channel_id=1, source_target_pairs={{0,4},{4,0},{8,12},{12,8},{16,20},{20,16},{24,28},{28,24},{1,5},{5... | collective-permute-start | bytes 786440 | tf_op jit(solution)/shard_map/ppermute | solution.py:1039
  80.6 34.5 %collective-permute-start.14 = (bf16[512,2048]{1,0:T(8,128)(2,1)}, bf16[512,2048]{1,0:T(8,128)(2,1)}, u32[]{:S(2)}, u32[]{:S(2)}) collective-permute-start(bf16[512,2048]{1,0:T(8,128)(2,1)} %refs_2_.2), channel_id=1, source_target_pairs={{0,4},{4,0},{8,12},{12,8},{16,20},{20,16},{24,28},{28,24},{1,5},{5... | collective-permute-start | bytes 6291464 | tf_op jit(solution)/shard_map/ppermute | solution.py:1039
  127.9 235.5 %reduce-scatter.6.cloned.1.call-start = ((), (), s32[]{:S(2)}) async-start(), calls=%async_computation.5 | async-start | bytes 10485760 | tf_op jit(solution)/shard_map/reduce_scatter | solution.py:1060
  145.5 29.6 %collective-permute-start.22 = (bf16[128,2048]{1,0:T(8,128)(2,1)}, bf16[128,2048]{1,0:T(8,128)(2,1)S(1)}, u32[]{:S(2)}, u32[]{:S(2)}) collective-permute-start(bf16[128,2048]{1,0:T(8,128)(2,1)} %get-tuple-element.196), channel_id=1, source_target_pairs={{0,2},{1,3},{2,0},{3,1},{4,6},{5,7},{6,4},{7,5},{8,10},{9,11},{10,... | collective-permute-start | bytes 1572872 | tf_op jit(solution)/shard_map/ppermute | solution.py:1048
  146.1 29.1 %collective-permute-start.23 = (bf16[128,2048]{1,0:T(8,128)(2,1)}, bf16[128,2048]{1,0:T(8,128)(2,1)}, u32[]{:S(2)}, u32[]{:S(2)}) collective-permute-start(bf16[128,2048]{1,0:T(8,128)(2,1)} %get-tuple-element.197), channel_id=1, source_target_pairs={{0,3},{1,2},{2,1},{3,0},{4,7},{5,6},{6,5},{7,4},{8,11},{9,10},{10,... | collective-permute-start | bytes 1572872 | tf_op jit(solution)/shard_map/ppermute | solution.py:1048
  187.3 231.4 %reduce-scatter.8.cloned.1.call-start = ((), (), s32[]{:S(2)}) async-start(), calls=%async_computation.6 | async-start | bytes 3276800 | tf_op jit(solution)/shard_map/reduce_scatter | solution.py:1060
  197.1 26.3 %collective-permute-start.27 = (bf16[256,2048]{1,0:T(8,128)(2,1)}, bf16[256,2048]{1,0:T(8,128)(2,1)S(1)}, u32[]{:S(2)}, u32[]{:S(2)}) collective-permute-start(bf16[256,2048]{1,0:T(8,128)(2,1)} %get-tuple-element.234), channel_id=1, source_target_pairs={{0,1},{1,0},{2,3},{3,2},{4,5},{5,4},{6,7},{7,6},{8,9},{9,8},{10,11... | collective-permute-start | bytes 3145736 | tf_op jit(solution)/shard_map/ppermute | solution.py:1048
  198.4 45.6 %collective-permute-start.31 = (bf16[256,2048]{1,0:T(8,128)(2,1)}, bf16[256,2048]{1,0:T(8,128)(2,1)}, u32[]{:S(2)}, u32[]{:S(2)}) collective-permute-start(bf16[256,2048]{1,0:T(8,128)(2,1)} %get-tuple-element.240), channel_id=1, source_target_pairs={{0,2},{1,3},{2,0},{3,1},{4,6},{5,7},{6,4},{7,5},{8,10},{9,11},{10,... | collective-permute-start | bytes 3145736 | tf_op jit(solution)/shard_map/ppermute | solution.py:1048
  199.1 44.9 %collective-permute-start.32 = (bf16[256,2048]{1,0:T(8,128)(2,1)}, bf16[256,2048]{1,0:T(8,128)(2,1)}, u32[]{:S(2)}, u32[]{:S(2)}) collective-permute-start(bf16[256,2048]{1,0:T(8,128)(2,1)} %get-tuple-element.241), channel_id=1, source_target_pairs={{0,3},{1,2},{2,1},{3,0},{4,7},{5,6},{6,5},{7,4},{8,11},{9,10},{10,... | collective-permute-start | bytes 3145736 | tf_op jit(solution)/shard_map/ppermute | solution.py:1048
  225.9 23.3 %collective-permute-start.28 = (bf16[3,256,512]{2,1,0:T(8,128)(2,1)}, bf16[3,256,512]{2,1,0:T(8,128)(2,1)}, u32[]{:S(2)}, u32[]{:S(2)}) collective-permute-start(bf16[3,256,512]{2,1,0:T(8,128)(2,1)} %slice.64), channel_id=1, source_target_pairs={{0,4},{4,0},{8,12},{12,8},{16,20},{20,16},{24,28},{28,24},{1,5},{5... | collective-permute-start | bytes 2359304 | tf_op jit(solution)/shard_map/ppermute | solution.py:1039
  247.6 37.6 %collective-permute-start.33 = (bf16[512,2048]{1,0:T(8,128)(2,1)}, bf16[512,2048]{1,0:T(8,128)(2,1)}, u32[]{:S(2)}, u32[]{:S(2)}) collective-permute-start(bf16[512,2048]{1,0:T(8,128)(2,1)} %token_order.2.refs_4_), channel_id=1, source_target_pairs={{0,4},{4,0},{8,12},{12,8},{16,20},{20,16},{24,28},{28,24},{1,5},{5... | collective-permute-start | bytes 6291464 | tf_op jit(solution)/shard_map/ppermute | solution.py:1039
  250.2 22.1 %collective-permute-start.29 = (bf16[256,512]{1,0:T(8,128)(2,1)S(1)}, bf16[256,512]{1,0:T(8,128)(2,1)S(1)}, u32[]{:S(2)}, u32[]{:S(2)}) collective-permute-start(bf16[256,512]{1,0:T(8,128)(2,1)S(1)} %fusion), channel_id=1, source_target_pairs={{8,0},{12,4},{16,8},{20,12},{24,16},{28,20},{9,1},{13,5},{17,9},{2... | collective-permute-start | bytes 786440 | tf_op jit(solution)/shard_map/ppermute | solution.py:1045
  251.7 27.2 %collective-permute-start.34 = (bf16[512,512]{1,0:T(8,128)(2,1)S(1)}, bf16[512,512]{1,0:T(8,128)(2,1)S(1)}, u32[]{:S(2)}, u32[]{:S(2)}) collective-permute-start(bf16[512,512]{1,0:T(8,128)(2,1)S(1)} %bitcast.51), channel_id=1, source_target_pairs={{0,4},{4,0},{8,12},{12,8},{16,20},{20,16},{24,28},{28,24},{1,5},{5... | collective-permute-start | bytes 1572872 | tf_op jit(solution)/shard_map/ppermute | solution.py:1039
  274.1 22.3 %collective-permute-start.30 = (bf16[256,512]{1,0:T(8,128)(2,1)}, bf16[256,512]{1,0:T(8,128)(2,1)}, u32[]{:S(2)}, u32[]{:S(2)}) collective-permute-start(bf16[256,512]{1,0:T(8,128)(2,1)} %fusion.2), channel_id=1, source_target_pairs={{8,0},{12,4},{16,8},{20,12},{24,16},{28,20},{9,1},{13,5},{17,9},{2... | collective-permute-start | bytes 786440 | tf_op jit(solution)/shard_map/ppermute | solution.py:1045
  303.2 25.5 %collective-permute-start.36 = (bf16[128,2048]{1,0:T(8,128)(2,1)}, bf16[128,2048]{1,0:T(8,128)(2,1)}, u32[]{:S(2)}, u32[]{:S(2)}) collective-permute-start(bf16[128,2048]{1,0:T(8,128)(2,1)} %get-tuple-element.247), channel_id=1, source_target_pairs={{0,2},{1,3},{2,0},{3,1},{4,6},{5,7},{6,4},{7,5},{8,10},{9,11},{10,... | collective-permute-start | bytes 1572872 | tf_op jit(solution)/shard_map/ppermute | solution.py:1048
  304.7 24.0 %collective-permute-start.37 = (bf16[128,2048]{1,0:T(8,128)(2,1)}, bf16[128,2048]{1,0:T(8,128)(2,1)}, u32[]{:S(2)}, u32[]{:S(2)}) collective-permute-start(bf16[128,2048]{1,0:T(8,128)(2,1)} %get-tuple-element.248), channel_id=1, source_target_pairs={{0,3},{1,2},{2,1},{3,0},{4,7},{5,6},{6,5},{7,4},{8,11},{9,10},{10,... | collective-permute-start | bytes 1572872 | tf_op jit(solution)/shard_map/ppermute | solution.py:1048
  335.3 24.9 %collective-permute-start.40 = (bf16[256,2048]{1,0:T(8,128)(2,1)}, bf16[256,2048]{1,0:T(8,128)(2,1)}, u32[]{:S(2)}, u32[]{:S(2)}) collective-permute-start(bf16[256,2048]{1,0:T(8,128)(2,1)} %get-tuple-element.260.refs_0_), channel_id=1, source_target_pairs={{0,2},{1,3},{2,0},{3,1},{4,6},{5,7},{6,4},{7,5},{8,10},{9,11},{10,... | collective-permute-start | bytes 3145736 | tf_op jit(solution)/shard_map/ppermute | solution.py:1048
  336.8 24.2 %collective-permute-start.39 = (bf16[256,2048]{1,0:T(8,128)(2,1)}, bf16[256,2048]{1,0:T(8,128)(2,1)}, u32[]{:S(2)}, u32[]{:S(2)}) collective-permute-start(bf16[256,2048]{1,0:T(8,128)(2,1)} %get-tuple-element.260.refs_0_), channel_id=1, source_target_pairs={{0,1},{1,0},{2,3},{3,2},{4,5},{5,4},{6,7},{7,6},{8,9},{9,8},{10,11... | collective-permute-start | bytes 3145736 | tf_op jit(solution)/shard_map/ppermute | solution.py:1048
  363.5 26.0 %collective-permute-start.41 = (bf16[256,2048]{1,0:T(8,128)(2,1)}, bf16[256,2048]{1,0:T(8,128)(2,1)}, u32[]{:S(2)}, u32[]{:S(2)}) collective-permute-start(bf16[256,2048]{1,0:T(8,128)(2,1)} %get-tuple-element.260.refs_0_), channel_id=1, source_target_pairs={{0,3},{1,2},{2,1},{3,0},{4,7},{5,6},{6,5},{7,4},{8,11},{9,10},{10,... | collective-permute-start | bytes 3145736 | tf_op jit(solution)/shard_map/ppermute | solution.py:1048
  (70 other events, 665.3 us)
Sparse Core Ops, SparseCore 0:
  10.5 66.6 all-gather.1
  128.0 76.7 reduce-scatter.3
  207.3 156.1 reduce-scatter.5
  365.7 52.9 reduce-scatter.7

commit v7 on v6

--- a/solution.py
+++ b/solution.py
@@ -1094,10 +1094,7 @@
     for half in range(HALVES):
         out, mixed, lse = attend(half, ids, doc_lengths, query_t, blocks, kv_heads)
         if gathered:
-            mixed_others = [other_core(mixes[0])]
-            gathered[-1], mixed, w_all, normed_other, mixed_others = together(
-                gathered[-1], mixed, w_all, normed_other, mixed_others
-            )
+            gathered[-1], mixed, w_all = together(gathered[-1], mixed, w_all)
             out_weights = [w_all, other_core(w_all)]
         outs.append(out)
         mixes.append(mixed)
@@ -1105,7 +1102,8 @@
         query_t, mixed = together(query_t, mixed)
         gathered.append(gather_near(mixed))
     hidden_first, normed_first = attn_out(0, ids, tokens, gain_two, gathered[0], out_weights)
-    gathered[1], normed_first = together(gathered[1], normed_first)
+    mixed_others = [other_core(mixes[0])]
+    gathered[1], normed_first, mixed_others = together(gathered[1], normed_first, mixed_others)
 
     hidden_last, normed_last, act, d_gate, d_up = ffn_forward(
         ids, tokens, gain_two, gathered[1], out_weights, normed_first, d_act, w_gate, w_up

time: 429 us -> 430 us (level)
  no operation moved by 1% of the time
where the time goes in v7:
time: 430 us; the launch traced here: 429 us
  waiting for transfers between devices  165 us (38%)
  Pallas kernels  153 us (36%)
  starting transfers between devices  50.5 us (12%)
  local copies, waits for them, and re-layouts  16.4 us (4%)
  other arithmetic  15.5 us (4%)
  between operations  14.5 us (3%)
  matrix products  13.9 us (3%)
    ppermute x24, waiting for transfers between devices, swap(): lax.ppermute(value, 'narrow', [(i, i ^ distance) for i in range(narrow)])  118 us
    ppermute x24, starting transfers between devices, swap(): lax.ppermute(value, 'narrow', [(i, i ^ distance) for i in range(narrow)])  29.2 us
    ppermute x2, waiting for transfers between devices, chips_down(): lax.ppermute(value, 'wide', [(i + 2 * hop, i) for i in range(wide - 2 * h...  26.1 us
    pallas_call x1, Pallas kernels, ffn_forward(): pl.pallas_call(functools.partial(ffn_kernel, members), grid=(units // ste...  21.9 us
    pallas_call x1, Pallas kernels, grad_in_of(): pl.pallas_call(functools.partial(grad_in_kernel, len(normeds), blocks, ha...  16.1 us
    pallas_call x3, Pallas kernels, grad_proj_of(): pl.pallas_call(functools.partial(grad_proj_kernel, len(lefts)), grid_spec...  15.8 us
    pallas_call x1, Pallas kernels, pair_nt(): pl.pallas_call(pair_nt_kernel, grid=(width // step,), in_specs=[smem_spec...  14.1 us
    dot_general x5, matrix products, dims(): lax.dot_general(left, right, (((a,), (b,)), ((), ())), preferred_element_...  13.9 us
  transfers between devices with their start and end apart: 53, of which 26 were waited for; matrix products, arithmetic and copies ran while one was open for 8% of the time, Pallas kernels for 33%

profile of v7, /device:TPU:0, one launch (start us, length us, event | category | flops | bytes accessed | tf_op | source)
XLA Modules:
  0.0 428.7 jit_solution(18249002870128227740)
XLA Ops:
  16.5 5.5 %collective-permute-start.1 = (bf16[256,512]{1,0:T(8,128)(2,1)}, bf16[256,512]{1,0:T(8,128)(2,1)S(1)}, u32[]{:S(2)}, u32[]{:S(2)}) collective-permute-start(bf16[256,512]{1,0:T(8,128)(2,1)} %get-tuple-element.146.refs_0_.refs_6_.refs_8_.refs_14_), channel_id=1, source_target_pairs={{0,16},{4,20},{8,24},{12,28},{1,17},{5,21},{9,25},{13,29},{2,18},{... | collective-permute-start | bytes 786440 | tf_op jit(solution)/shard_map/ppermute | solution.py:1042
  30.2 6.1 %fusion.12.da_ref = f32[512,2048]{1,0:T(8,128)} fusion(bf16[512,2048]{1,0:T(8,128)(2,1)S(1)} %copy-done.1, bf16[2048,2048]{1,0:T(8,128)(2,1)S(1)} %copy-done.30), kind=kOutput, calls=%fused_computation.51 | convolution fusion | flops 4294967296 | bytes 14680064 | tf_op jit(solution)/shard_map/dot_general | solution.py:53
  49.1 6.2 %attend.3 = (f32[512,256]{1,0:T(8,128)}, bf16[512,256]{1,0:T(8,128)(2,1)}, f32[2,4,256]{2,1,0:T(4,128)}) custom-call(s32[3]{0:T(128)} %pad_add_fusion.ids_ref, s32[12]{0:T(128)} %lengths_ref.7, bf16[512,512]{1,0:T(8,128)(2,1)} %bitcast.61, bf16[256,512]{1,0:T(8,128)(2,1)} %get-tuple-element.146.refs_0_.refs_6_.refs_8_.refs_14_, bf16[256,512]{1,0:T(8,128)(2,1)} %copy-done.31, ...), custom_call_target="tpu_custom_call" | custom-call | flops 1073741824 | bytes 2097152 | tf_op jit(solution)/shard_map/attend/pallas_call | solution.py:238
  55.2 5.6 %collective-permute-done.7.refs_3_ = bf16[512,256]{1,0:T(8,128)(2,1)S(1)} collective-permute-done((bf16[512,256]{1,0:T(8,128)(2,1)}, bf16[512,256]{1,0:T(8,128)(2,1)S(1)}, u32[]{:S(2)}, u32[]{:S(2)}) %collective-permute-start.7) | collective-permute-done | bytes 262176 | tf_op jit(solution)/shard_map/ppermute | solution.py:1048
  60.9 6.8 %collective-permute-done.6.refs_2_ = bf16[512,256]{1,0:T(8,128)(2,1)S(1)} collective-permute-done((bf16[512,256]{1,0:T(8,128)(2,1)}, bf16[512,256]{1,0:T(8,128)(2,1)S(1)}, u32[]{:S(2)}, u32[]{:S(2)}) %collective-permute-start.6) | collective-permute-done | bytes 262176 | tf_op jit(solution)/shard_map/ppermute | solution.py:1048
  85.2 8.2 %attn_out.1 = (f32[256,2048]{1,0:T(8,128)}, bf16[256,2048]{1,0:T(8,128)(2,1)}) custom-call(s32[3]{0:T(128)} %pad_add_fusion.ids_ref, bf16[512,2048]{1,0:T(8,128)(2,1)} %x_ref.7, f32[1,2048]{1,0:T(1,128)} %bitcast.63, bf16[512,256]{1,0:T(8,128)(2,1)} %get-tuple-element.157.refs_0_, bf16[512,256]{1,0:T(8,128)(2,1)} %copy-done.23, bf16[512,256]{1,0:T(8,128)(2,1)} %copy-done.22, ...), custom_call_target="tpu_custom_call" | custom-call | flops 2147483648 | bytes 14680064 | tf_op jit(solution)/shard_map/attn_out/pallas_call | solution.py:499
  93.5 21.9 %gate_up.1 = (f32[256,2048]{1,0:T(8,128)}, bf16[256,2048]{1,0:T(8,128)(2,1)}, bf16[512,2048]{1,0:T(8,128)(2,1)}, bf16[512,2048]{1,0:T(8,128)(2,1)}, bf16[512,2048]{1,0:T(8,128)(2,1)}) custom-call(s32[3]{0:T(128)} %pad_add_fusion.ids_ref, bf16[512,2048]{1,0:T(8,128)(2,1)} %x_ref.7, f32[1,2048]{1,0:T(1,128)} %bitcast.64, ...), custom_call_target="tpu_custom_call" | custom-call | flops 10737418240 | bytes 37748736 | tf_op jit(solution)/shard_map/gate_up/pallas_call | solution.py:742
  120.0 8.4 %grad_down.1 = bf16[2048,1024]{1,0:T(8,128)(2,1)} custom-call(bf16[512,2048]{1,0:T(8,128)(2,1)} %get-tuple-element.189.own_ref.a_ref, bf16[512,2048]{1,0:T(8,128)(2,1)} %collective-permute-done.14.other_ref, bf16[1024,1024]{1,0:T(8,128)(2,1)} %pick_columns.1.cot_ref), custom_call_target="tpu_custom_call" | custom-call | flops 4294967296 | bytes 10485760 | tf_op jit(solution)/shard_map/grad_down/pallas_call | solution.py:884
  130.5 14.1 %d_normed_two.1 = (bf16[128,2048]{1,0:T(8,128)(2,1)}, bf16[128,2048]{1,0:T(8,128)(2,1)}, bf16[128,2048]{1,0:T(8,128)(2,1)}, bf16[128,2048]{1,0:T(8,128)(2,1)}) custom-call(s32[3]{0:T(128)} %pad_add_fusion.ids_ref, bf16[512,2048]{1,0:T(8,128)(2,1)} %get-tuple-element.205.a_ref.refs_16_, bf16[512,2048]{1,0:T(8,128)(2,1)} %get-tuple-element.207.b_ref.refs_18_, ...), custom_call_target="tpu_custom_call" | custom-call | flops 8589934592 | bytes 23068672 | tf_op jit(solution)/shard_map/d_normed_two/pallas_call | solution.py:792
  148.2 9.0 %ffn_down.1 = (bf16[128,2048]{1,0:T(8,128)(2,1)}, bf16[256,2048]{1,0:T(8,128)(2,1)}, bf16[256,2048]{1,0:T(8,128)(2,1)}, bf16[256,2048]{1,0:T(8,128)(2,1)}) custom-call(s32[3]{0:T(128)} %pad_add_fusion.ids_ref, bf16[512,2048]{1,0:T(8,128)(2,1)} %get-tuple-element.189.own_ref.a_ref, bf16[2048,2048]{1,0:T(8,128)(2,1)} %w_ref.1), custom_call_target="tpu_custom_call" | custom-call | flops 4294967296 | bytes 12582912 | tf_op jit(solution)/shard_map/ffn_down/pallas_call | solution.py:816
  159.7 16.1 %grad_gate_up.1 = bf16[1024,4096]{1,0:T(8,128)(2,1)} custom-call(s32[3]{0:T(128)} %pad_add_fusion.ids_ref, bf16[256,2048]{1,0:T(8,128)(2,1)} %get-tuple-element.201.before_ref.refs_0_.refs_1_.refs_2_.refs_3_, bf16[256,2048]{1,0:T(8,128)(2,1)} %get-tuple-element.201.before_ref.refs_0_.refs_1_.refs_2_.refs_3_, ...), custom_call_target="tpu_custom_call" | custom-call | flops 8589934592 | bytes 18874368 | tf_op jit(solution)/shard_map/grad_gate_up/pallas_call | solution.py:925
  176.6 11.2 %norm_two_back.1 = (f32[128,2048]{1,0:T(8,128)}, bf16[128,2048]{1,0:T(8,128)(2,1)}, f32[1,2048]{1,0:T(1,128)}, bf16[128,512]{1,0:T(8,128)(2,1)}, bf16[128,512]{1...) custom-call(s32[3]{0:T(128)} %pad_add_fusion.ids_ref, ...), custom_call_target="tpu_custom_call", output_to_operand_aliasing={{7}: (12, {}), {8}: (13, {}), {9}: (14, {})} | custom-call | flops 1073741824 | bytes 14680064 | tf_op jit(solution)/shard_map/norm_two_back/pallas_call | solution.py:600
  201.3 11.7 %attend_back.1 = (f32[512,512]{1,0:T(8,128)}, bf16[6,2,128,512]{3,2,1,0:T(8,128)(2,1)}) custom-call(s32[3]{0:T(128)} %pad_add_fusion.ids_ref, s32[12]{0:T(128)} %lengths_ref.7, bf16[512,512]{1,0:T(8,128)(2,1)} %bitcast.62, bf16[128,512]{1,0:T(8,128)(2,1)} %get-tuple-element.223.refs_0_, bf16[128,512]{1,0:T(8,128)(2,1)} %copy-done.36, ...), custom_call_target="tpu_custom_call" | custom-call | flops 5368709120 | bytes 4194304 | tf_op jit(solution)/shard_map/attend_back/pallas_call | solution.py:399
  213.0 11.1 %collective-permute-done.26.refs_1_.refs_9_ = bf16[256,2048]{1,0:T(8,128)(2,1)S(1)} collective-permute-done((bf16[256,2048]{1,0:T(8,128)(2,1)}, bf16[256,2048]{1,0:T(8,128)(2,1)S(1)}, u32[]{:S(2)}, u32[]{:S(2)}) %collective-permute-start.26) | collective-permute-done | bytes 1048608 | tf_op jit(solution)/shard_map/ppermute | solution.py:1048
  226.6 18.1 %collective-permute-done.30.refs_2_.refs_10_ = bf16[256,2048]{1,0:T(8,128)(2,1)} collective-permute-done((bf16[256,2048]{1,0:T(8,128)(2,1)}, bf16[256,2048]{1,0:T(8,128)(2,1)}, u32[]{:S(2)}, u32[]{:S(2)}) %collective-permute-start.30) | collective-permute-done | bytes 1048608 | tf_op jit(solution)/shard_map/ppermute | solution.py:1048
  252.6 20.3 %collective-permute-done.28 = bf16[256,512]{1,0:T(8,128)(2,1)S(1)} collective-permute-done((bf16[256,512]{1,0:T(8,128)(2,1)S(1)}, bf16[256,512]{1,0:T(8,128)(2,1)S(1)}, u32[]{:S(2)}, u32[]{:S(2)}) %collective-permute-start.28) | collective-permute-done | bytes 262176 | tf_op jit(solution)/shard_map/ppermute | solution.py:1045
  280.3 5.4 %grad_query.1 = bf16[512,1024]{1,0:T(8,128)(2,1)} custom-call(s32[3]{0:T(128)} %pad_add_fusion.ids_ref, bf16[512,512]{1,0:T(8,128)(2,1)} %bitcast.53, bf16[512,512]{1,0:T(8,128)(2,1)} %copy-done.18, bf16[512,2048]{1,0:T(8,128)(2,1)} %get-tuple-element.147.refs_2_, bf16[512,2048]{1,0:T(8,128)(2,1)} %collective-permute-done.34.refs_3_), custom_call_target="tpu_custom_call" | custom-call | flops 1073741824 | bytes 4194304 | tf_op jit(solution)/shard_map/grad_query/pallas_call | solution.py:965
  285.7 5.5 %grad_out.1 = bf16[512,1024]{1,0:T(8,128)(2,1)} custom-call(s32[3]{0:T(128)} %pad_add_fusion.ids_ref, bf16[512,256]{1,0:T(8,128)(2,1)} %get-tuple-element.157.refs_0_, bf16[512,256]{1,0:T(8,128)(2,1)} %get-tuple-element.167.refs_0_.refs_1_, bf16[512,256]{1,0:T(8,128)(2,1)} %copy-done.20, bf16[512,256]{1,0:T(8,128)(2,1)} %collective-permute-done.19.refs_3_, ...), custom_call_target="tpu_custom_call" | custom-call | flops 1073741824 | bytes 4194304 | tf_op jit(solution)/shard_map/grad_out/pallas_call | solution.py:965
  291.2 5.8 %collective-permute-done.29 = bf16[256,512]{1,0:T(8,128)(2,1)} collective-permute-done((bf16[256,512]{1,0:T(8,128)(2,1)}, bf16[256,512]{1,0:T(8,128)(2,1)}, u32[]{:S(2)}, u32[]{:S(2)}) %collective-permute-start.29) | collective-permute-done | bytes 262176 | tf_op jit(solution)/shard_map/ppermute | solution.py:1045
  317.9 11.4 %collective-permute-done.36.refs_6_ = bf16[128,2048]{1,0:T(8,128)(2,1)} collective-permute-done((bf16[128,2048]{1,0:T(8,128)(2,1)}, bf16[128,2048]{1,0:T(8,128)(2,1)}, u32[]{:S(2)}, u32[]{:S(2)}) %collective-permute-start.36) | collective-permute-done | bytes 524320 | tf_op jit(solution)/shard_map/ppermute | solution.py:1048
  329.4 6.5 %last_rows.1 = (bf16[256,2048]{1,0:T(8,128)(2,1)}, f32[1,2048]{1,0:T(1,128)}) custom-call(s32[3]{0:T(128)} %pad_add_fusion.ids_ref, bf16[512,2048]{1,0:T(8,128)(2,1)} %x_ref.7, f32[256,2048]{1,0:T(8,128)} %get-tuple-element.162.refs_0_, f32[256,2048]{1,0:T(8,128)} %get-tuple-element.171.refs_1_, f32[128,2048]{1,0:T(8,128)} %get-tuple-element.252.refs_2_, ...), custom_call_target="tpu_custom_call" | custom-call | flops 7864320 | bytes 8388608 | tf_op jit(solution)/shard_map/last_rows/pallas_call | solution.py:666
  338.0 22.7 %collective-permute-done.40.refs_2_ = bf16[256,2048]{1,0:T(8,128)(2,1)} collective-permute-done((bf16[256,2048]{1,0:T(8,128)(2,1)}, bf16[256,2048]{1,0:T(8,128)(2,1)}, u32[]{:S(2)}, u32[]{:S(2)}) %collective-permute-start.40) | collective-permute-done | bytes 1048608 | tf_op jit(solution)/shard_map/ppermute | solution.py:1048
  366.6 23.6 %collective-permute-done.41.refs_3_ = bf16[256,2048]{1,0:T(8,128)(2,1)} collective-permute-done((bf16[256,2048]{1,0:T(8,128)(2,1)}, bf16[256,2048]{1,0:T(8,128)(2,1)}, u32[]{:S(2)}, u32[]{:S(2)}) %collective-permute-start.41) | collective-permute-done | bytes 1048608 | tf_op jit(solution)/shard_map/ppermute | solution.py:1048
  411.5 7.9 %reduce-scatter.8.cloned.1.call-done.in_ref = bf16[1280,256]{1,0:T(8,128)(2,1)} async-done(((bf16[1280,1024]{1,0:T(8,128)(2,1)}), bf16[1280,256]{1,0:T(8,128)(2,1)}) %reduce-scatter.8.cloned.1.call-update) | async-done | bytes 655376 | tf_op jit(solution)/shard_map/reduce_scatter | solution.py:1060
  (228 shorter events, 145.2 us)
Async XLA Ops:
  7.2 69.9 %all-gather.2.cloned.1.call-start = ((), (), s32[]{:S(2)}) async-start(), calls=%async_computation.3 | async-start | bytes 5242880 | tf_op jit(solution)/shard_map/all_gather | solution.py:1073
  9.8 287.2 %reduce-scatter.4.cloned.1.call-start = ((), (), s32[]{:S(2)}) async-start(), calls=%async_computation.4 | async-start | bytes 5242880 | tf_op jit(solution)/shard_map/reduce_scatter | solution.py:1060
  16.0 22.4 %collective-permute-start.2 = (bf16[256,512]{1,0:T(8,128)(2,1)}, bf16[256,512]{1,0:T(8,128)(2,1)S(1)}, u32[]{:S(2)}, u32[]{:S(2)}) collective-permute-start(bf16[256,512]{1,0:T(8,128)(2,1)} %get-tuple-element.146.refs_0_.refs_6_.refs_8_.refs_14_), channel_id=1, source_target_pairs={{0,4},{4,0},{8,12},{12,8},{16,20},{20,16},{24,28},{28,24},{1,5},{5... | collective-permute-start | bytes 786440 | tf_op jit(solution)/shard_map/ppermute | solution.py:1039
  16.5 20.8 %collective-permute-start.1 = (bf16[256,512]{1,0:T(8,128)(2,1)}, bf16[256,512]{1,0:T(8,128)(2,1)S(1)}, u32[]{:S(2)}, u32[]{:S(2)}) collective-permute-start(bf16[256,512]{1,0:T(8,128)(2,1)} %get-tuple-element.146.refs_0_.refs_6_.refs_8_.refs_14_), channel_id=1, source_target_pairs={{0,16},{4,20},{8,24},{12,28},{1,17},{5,21},{9,25},{13,29},{2,18},{... | collective-permute-start | bytes 786440 | tf_op jit(solution)/shard_map/ppermute | solution.py:1042
  48.2 23.6 %collective-permute-start.5 = (bf16[512,256]{1,0:T(8,128)(2,1)}, bf16[512,256]{1,0:T(8,128)(2,1)S(1)}, u32[]{:S(2)}, u32[]{:S(2)}) collective-permute-start(bf16[512,256]{1,0:T(8,128)(2,1)} %get-tuple-element.157.refs_0_), channel_id=1, source_target_pairs={{0,1},{1,0},{2,3},{3,2},{4,5},{5,4},{6,7},{7,6},{8,9},{9,8},{10,11... | collective-permute-start | bytes 786440 | tf_op jit(solution)/shard_map/ppermute | solution.py:1048
  85.0 30.8 %collective-permute-start.13 = (bf16[512,2048]{1,0:T(8,128)(2,1)}, bf16[512,2048]{1,0:T(8,128)(2,1)}, u32[]{:S(2)}, u32[]{:S(2)}) collective-permute-start(bf16[512,2048]{1,0:T(8,128)(2,1)} %refs_2_.2), channel_id=1, source_target_pairs={{0,4},{4,0},{8,12},{12,8},{16,20},{20,16},{24,28},{28,24},{1,5},{5... | collective-permute-start | bytes 6291464 | tf_op jit(solution)/shard_map/ppermute | solution.py:1039
  128.4 235.7 %reduce-scatter.6.cloned.1.call-start = ((), (), s32[]{:S(2)}) async-start(), calls=%async_computation.5 | async-start | bytes 10485760 | tf_op jit(solution)/shard_map/reduce_scatter | solution.py:1060
  146.2 29.6 %collective-permute-start.21 = (bf16[128,2048]{1,0:T(8,128)(2,1)}, bf16[128,2048]{1,0:T(8,128)(2,1)S(1)}, u32[]{:S(2)}, u32[]{:S(2)}) collective-permute-start(bf16[128,2048]{1,0:T(8,128)(2,1)} %get-tuple-element.195), channel_id=1, source_target_pairs={{0,2},{1,3},{2,0},{3,1},{4,6},{5,7},{6,4},{7,5},{8,10},{9,11},{10,... | collective-permute-start | bytes 1572872 | tf_op jit(solution)/shard_map/ppermute | solution.py:1048
  146.7 29.0 %collective-permute-start.22 = (bf16[128,2048]{1,0:T(8,128)(2,1)}, bf16[128,2048]{1,0:T(8,128)(2,1)}, u32[]{:S(2)}, u32[]{:S(2)}) collective-permute-start(bf16[128,2048]{1,0:T(8,128)(2,1)} %get-tuple-element.196), channel_id=1, source_target_pairs={{0,3},{1,2},{2,1},{3,0},{4,7},{5,6},{6,5},{7,4},{8,11},{9,10},{10,... | collective-permute-start | bytes 1572872 | tf_op jit(solution)/shard_map/ppermute | solution.py:1048
  187.9 231.5 %reduce-scatter.8.cloned.1.call-start = ((), (), s32[]{:S(2)}) async-start(), calls=%async_computation.6 | async-start | bytes 3276800 | tf_op jit(solution)/shard_map/reduce_scatter | solution.py:1060
  197.8 26.3 %collective-permute-start.26 = (bf16[256,2048]{1,0:T(8,128)(2,1)}, bf16[256,2048]{1,0:T(8,128)(2,1)S(1)}, u32[]{:S(2)}, u32[]{:S(2)}) collective-permute-start(bf16[256,2048]{1,0:T(8,128)(2,1)} %get-tuple-element.233), channel_id=1, source_target_pairs={{0,1},{1,0},{2,3},{3,2},{4,5},{5,4},{6,7},{7,6},{8,9},{9,8},{10,11... | collective-permute-start | bytes 3145736 | tf_op jit(solution)/shard_map/ppermute | solution.py:1048
  199.1 45.6 %collective-permute-start.30 = (bf16[256,2048]{1,0:T(8,128)(2,1)}, bf16[256,2048]{1,0:T(8,128)(2,1)}, u32[]{:S(2)}, u32[]{:S(2)}) collective-permute-start(bf16[256,2048]{1,0:T(8,128)(2,1)} %get-tuple-element.239), channel_id=1, source_target_pairs={{0,2},{1,3},{2,0},{3,1},{4,6},{5,7},{6,4},{7,5},{8,10},{9,11},{10,... | collective-permute-start | bytes 3145736 | tf_op jit(solution)/shard_map/ppermute | solution.py:1048
  199.8 44.9 %collective-permute-start.31 = (bf16[256,2048]{1,0:T(8,128)(2,1)}, bf16[256,2048]{1,0:T(8,128)(2,1)}, u32[]{:S(2)}, u32[]{:S(2)}) collective-permute-start(bf16[256,2048]{1,0:T(8,128)(2,1)} %get-tuple-element.240), channel_id=1, source_target_pairs={{0,3},{1,2},{2,1},{3,0},{4,7},{5,6},{6,5},{7,4},{8,11},{9,10},{10,... | collective-permute-start | bytes 3145736 | tf_op jit(solution)/shard_map/ppermute | solution.py:1048
  201.3 78.2 %collective-permute-start.34 = (bf16[512,2048]{1,0:T(8,128)(2,1)}, bf16[512,2048]{1,0:T(8,128)(2,1)}, u32[]{:S(2)}, u32[]{:S(2)}) collective-permute-start(bf16[512,2048]{1,0:T(8,128)(2,1)} %get-tuple-element.147.refs_2_), channel_id=1, source_target_pairs={{0,4},{4,0},{8,12},{12,8},{16,20},{20,16},{24,28},{28,24},{1,5},{5... | collective-permute-start | bytes 6291464 | tf_op jit(solution)/shard_map/ppermute | solution.py:1039
  226.6 23.2 %collective-permute-start.27 = (bf16[3,256,512]{2,1,0:T(8,128)(2,1)}, bf16[3,256,512]{2,1,0:T(8,128)(2,1)}, u32[]{:S(2)}, u32[]{:S(2)}) collective-permute-start(bf16[3,256,512]{2,1,0:T(8,128)(2,1)} %slice.64), channel_id=1, source_target_pairs={{0,4},{4,0},{8,12},{12,8},{16,20},{20,16},{24,28},{28,24},{1,5},{5... | collective-permute-start | bytes 2359304 | tf_op jit(solution)/shard_map/ppermute | solution.py:1039
  248.2 37.6 %collective-permute-start.32 = (bf16[512,2048]{1,0:T(8,128)(2,1)}, bf16[512,2048]{1,0:T(8,128)(2,1)}, u32[]{:S(2)}, u32[]{:S(2)}) collective-permute-start(bf16[512,2048]{1,0:T(8,128)(2,1)} %token_order.2.refs_4_), channel_id=1, source_target_pairs={{0,4},{4,0},{8,12},{12,8},{16,20},{20,16},{24,28},{28,24},{1,5},{5... | collective-permute-start | bytes 6291464 | tf_op jit(solution)/shard_map/ppermute | solution.py:1039
  250.8 22.1 %collective-permute-start.28 = (bf16[256,512]{1,0:T(8,128)(2,1)S(1)}, bf16[256,512]{1,0:T(8,128)(2,1)S(1)}, u32[]{:S(2)}, u32[]{:S(2)}) collective-permute-start(bf16[256,512]{1,0:T(8,128)(2,1)S(1)} %fusion), channel_id=1, source_target_pairs={{8,0},{12,4},{16,8},{20,12},{24,16},{28,20},{9,1},{13,5},{17,9},{2... | collective-permute-start | bytes 786440 | tf_op jit(solution)/shard_map/ppermute | solution.py:1045
  252.3 27.2 %collective-permute-start.33 = (bf16[512,512]{1,0:T(8,128)(2,1)S(1)}, bf16[512,512]{1,0:T(8,128)(2,1)S(1)}, u32[]{:S(2)}, u32[]{:S(2)}) collective-permute-start(bf16[512,512]{1,0:T(8,128)(2,1)S(1)} %bitcast.51), channel_id=1, source_target_pairs={{0,4},{4,0},{8,12},{12,8},{16,20},{20,16},{24,28},{28,24},{1,5},{5... | collective-permute-start | bytes 1572872 | tf_op jit(solution)/shard_map/ppermute | solution.py:1039
  274.7 22.3 %collective-permute-start.29 = (bf16[256,512]{1,0:T(8,128)(2,1)}, bf16[256,512]{1,0:T(8,128)(2,1)}, u32[]{:S(2)}, u32[]{:S(2)}) collective-permute-start(bf16[256,512]{1,0:T(8,128)(2,1)} %fusion.2), channel_id=1, source_target_pairs={{8,0},{12,4},{16,8},{20,12},{24,16},{28,20},{9,1},{13,5},{17,9},{2... | collective-permute-start | bytes 786440 | tf_op jit(solution)/shard_map/ppermute | solution.py:1045
  303.8 25.5 %collective-permute-start.36 = (bf16[128,2048]{1,0:T(8,128)(2,1)}, bf16[128,2048]{1,0:T(8,128)(2,1)}, u32[]{:S(2)}, u32[]{:S(2)}) collective-permute-start(bf16[128,2048]{1,0:T(8,128)(2,1)} %get-tuple-element.245), channel_id=1, source_target_pairs={{0,2},{1,3},{2,0},{3,1},{4,6},{5,7},{6,4},{7,5},{8,10},{9,11},{10,... | collective-permute-start | bytes 1572872 | tf_op jit(solution)/shard_map/ppermute | solution.py:1048
  305.3 24.0 %collective-permute-start.37 = (bf16[128,2048]{1,0:T(8,128)(2,1)}, bf16[128,2048]{1,0:T(8,128)(2,1)}, u32[]{:S(2)}, u32[]{:S(2)}) collective-permute-start(bf16[128,2048]{1,0:T(8,128)(2,1)} %get-tuple-element.246), channel_id=1, source_target_pairs={{0,3},{1,2},{2,1},{3,0},{4,7},{5,6},{6,5},{7,4},{8,11},{9,10},{10,... | collective-permute-start | bytes 1572872 | tf_op jit(solution)/shard_map/ppermute | solution.py:1048
  335.9 24.9 %collective-permute-start.40 = (bf16[256,2048]{1,0:T(8,128)(2,1)}, bf16[256,2048]{1,0:T(8,128)(2,1)}, u32[]{:S(2)}, u32[]{:S(2)}) collective-permute-start(bf16[256,2048]{1,0:T(8,128)(2,1)} %get-tuple-element.258.refs_0_), channel_id=1, source_target_pairs={{0,2},{1,3},{2,0},{3,1},{4,6},{5,7},{6,4},{7,5},{8,10},{9,11},{10,... | collective-permute-start | bytes 3145736 | tf_op jit(solution)/shard_map/ppermute | solution.py:1048
  337.4 24.1 %collective-permute-start.39 = (bf16[256,2048]{1,0:T(8,128)(2,1)}, bf16[256,2048]{1,0:T(8,128)(2,1)}, u32[]{:S(2)}, u32[]{:S(2)}) collective-permute-start(bf16[256,2048]{1,0:T(8,128)(2,1)} %get-tuple-element.258.refs_0_), channel_id=1, source_target_pairs={{0,1},{1,0},{2,3},{3,2},{4,5},{5,4},{6,7},{7,6},{8,9},{9,8},{10,11... | collective-permute-start | bytes 3145736 | tf_op jit(solution)/shard_map/ppermute | solution.py:1048
  364.1 26.0 %collective-permute-start.41 = (bf16[256,2048]{1,0:T(8,128)(2,1)}, bf16[256,2048]{1,0:T(8,128)(2,1)}, u32[]{:S(2)}, u32[]{:S(2)}) collective-permute-start(bf16[256,2048]{1,0:T(8,128)(2,1)} %get-tuple-element.258.refs_0_), channel_id=1, source_target_pairs={{0,3},{1,2},{2,1},{3,0},{4,7},{5,6},{6,5},{7,4},{8,11},{9,10},{10,... | collective-permute-start | bytes 3145736 | tf_op jit(solution)/shard_map/ppermute | solution.py:1048
  (71 other events, 700.7 us)
Sparse Core Ops, SparseCore 0:
  10.5 66.6 all-gather.1
  128.6 76.8 reduce-scatter.3
  207.9 156.1 reduce-scatter.5
  366.4 52.8 reduce-scatter.7
